TPU v7x, 32 devices: a whole 2x2x4 slice. The times are simulated.
32 devices in a mesh: context: 8 (over y, x, core), tensor: 4 (over z).
Axes of the slice: x: 2, y: 2, z: 4, core: 2. Of those that a mesh axis runs over, the one named last changes fastest.
Arguments:
- block_input: bfloat16 [4, 4096, 2048], P(None, 'context'), may hold values from -6 to 6
- doc_lengths: int32 [4, 8], replicated, may hold values from 0 to 4096, as said below
- norm_gains: bfloat16 [2, 2048], P(None, 'context'), may hold values from 0.099609375 to 1.8984375
- qkv_weight: bfloat16 [3, 2048, 2048], P(None, 'context', 'tensor'), may hold values from -0.125 to 0.125
- out_weight: bfloat16 [2048, 2048], P('tensor', 'context'), may hold values from -1 to 1
- gateup_weight: bfloat16 [2, 2048, 4096], P(None, 'context', 'tensor'), may hold values from -0.125 to 0.125
- down_weight: bfloat16 [4096, 2048], P('tensor', 'context'), may hold values from -0.09375 to 0.09375
- cotangent: bfloat16 [4, 4096, 2048], P(None, 'context'), may hold values from -6 to 6
Outputs:
- block_output: bfloat16 [4, 4096, 2048], P(None, 'context')
- input_grad: float32 [4, 4096, 2048], P(None, 'context')
- gains_grad: float32 [2, 2048], P(None, 'context')
- qkv_grad: float32 [3, 2048, 2048], P(None, 'context', 'tensor')
- out_grad: float32 [2048, 2048], P('tensor', 'context')
- gateup_grad: float32 [2, 2048, 4096], P(None, 'context', 'tensor')
- down_grad: float32 [4096, 2048], P('tensor', 'context')
Inputs may be any that keep to these rules, and one draw needn't show every extreme that they name: `doc_lengths`: each row sums to 4096. In each micro-batch, rows m * 2 to m * 2 + 1, one row drawn from the seed is a single document of 4096 tokens followed by zeros; every other row holds 8 documents of one token or more.
All inputs are finite; a program needn't handle non-finite values.
Results may differ from a plain program's by a relative error of at most 0.024.
Values may be sent and summed in bfloat16 or wider, within the bound.
No kernel may reach another device: no remote copies, remote signals or barrier semaphores. Data moves between devices by JAX's collectives and lax.ppermute only.
A program may use at most 576 MiB of HBM per device.

v0:
```python
import math

import jax
import jax.numpy as jnp
from jax import lax
from jax.sharding import PartitionSpec as P

HEAD_DIM = 64
WINDOW = 2048
SEQ_LEN = 4096
SB = 2


epsilon = 1e-05
rope_base = 10000.0
masked_fill = -1e30


def rope_tables(positions, head_dim):
    half_dim = head_dim // 2
    counter = jnp.arange(half_dim, dtype=jnp.float32)
    frequency = jnp.exp(counter * (-2.0 * math.log(rope_base) / head_dim))
    angles = positions.astype(jnp.float32)[:, None] * frequency[None, :]
    return (jnp.cos(angles)[:, None, :], jnp.sin(angles)[:, None, :])


def rotate(values, cosine, sine):
    half_dim = values.shape[-1] // 2
    front_half = values[..., :half_dim]
    back_half = values[..., half_dim:]
    return jnp.concatenate(
        [front_half * cosine - back_half * sine, back_half * cosine + front_half * sine], axis=-1
    )


def unrotate(values, cosine, sine):
    half_dim = values.shape[-1] // 2
    front_half = values[..., :half_dim]
    back_half = values[..., half_dim:]
    return jnp.concatenate(
        [front_half * cosine + back_half * sine, back_half * cosine - front_half * sine], axis=-1
    )


def norm_forward(rows, gain):
    inverse = lax.rsqrt(jnp.mean(rows * rows, axis=-1, keepdims=True) + epsilon)
    normal = rows * inverse
    return (normal, inverse, normal * gain)


def norm_backward(grad_normed, normal, inverse, gain):
    grad_normal = grad_normed * gain
    inner = jnp.mean(grad_normal * normal, axis=-1, keepdims=True)
    return (inverse * (grad_normal - normal * inner), jnp.sum(grad_normed * normal, axis=(0, 1)))


def shards(
    block_input,
    doc_lengths,
    norm_gains,
    qkv_weight,
    out_weight,
    gateup_weight,
    down_weight,
    cotangent,
):
    local_len = block_input.shape[1]
    model_width = block_input.shape[2]
    device_index = lax.axis_index("context")
    key_span = WINDOW + local_len
    head_width = qkv_weight.shape[2]
    local_heads = head_width // HEAD_DIM
    hidden_width = gateup_weight.shape[2]
    micro_count = block_input.shape[0] // SB
    score_scale = HEAD_DIM ** (-0.5)
    local_start = device_index * local_len
    query_pos = local_start + jnp.arange(local_len, dtype=jnp.int32)
    key_pos = local_start - WINDOW + jnp.arange(key_span, dtype=jnp.int32)
    cosine, sine = rope_tables(query_pos, HEAD_DIM)
    seq_positions = jnp.arange(SEQ_LEN, dtype=jnp.int32)
    distance = query_pos[:, None] - key_pos[None, :]
    in_window = (distance >= 0) & (distance < WINDOW)

    def micro_step(micro_index, carried):
        output_all, input_grads, total_qkv, total_out, total_gateup, total_down, total_gains = (
            carried
        )
        qkv_full, out_full, gateup_full, down_full, gains_full = (
            lax.all_gather(qkv_weight, "context", axis=1, tiled=True),
            lax.all_gather(out_weight, "context", axis=1, tiled=True),
            lax.all_gather(gateup_weight, "context", axis=1, tiled=True),
            lax.all_gather(down_weight, "context", axis=1, tiled=True),
            lax.all_gather(norm_gains, "context", axis=1, tiled=True),
        )
        gains_value = gains_full.astype(jnp.float32)
        first_row = micro_index * SB
        rows_in = lax.dynamic_slice_in_dim(block_input, first_row, SB, 0).astype(jnp.float32)
        incoming = lax.dynamic_slice_in_dim(cotangent, first_row, SB, 0)
        lengths = lax.dynamic_slice_in_dim(doc_lengths, first_row, SB, 0)
        doc_ends = jnp.cumsum(lengths, axis=1)
        segment = jnp.sum(
            (seq_positions[None, :, None] >= doc_ends[:, None, :]).astype(jnp.int32), axis=-1
        )
        padded_seg = jnp.concatenate([jnp.full((SB, WINDOW), -1, jnp.int32), segment], axis=1)
        key_seg = lax.dynamic_slice_in_dim(padded_seg, local_start, key_span, 1)
        query_seg = lax.dynamic_slice_in_dim(segment, local_start, local_len, 1)
        visible = ((query_seg[:, :, None] == key_seg[:, None, :]) & in_window[None])[:, None]
        normal_one, inverse_one, normed_one = norm_forward(rows_in, gains_value[0])
        normed_one = normed_one.astype(jnp.bfloat16)
        projected = jnp.einsum(
            "snd,kde->ksne", normed_one, qkv_full, preferred_element_type=jnp.float32
        )
        projected = projected.reshape(3, SB, local_len, local_heads, HEAD_DIM)
        queries = rotate(projected[0], cosine, sine).astype(jnp.bfloat16)
        key_rows = rotate(projected[1], cosine, sine).astype(jnp.bfloat16)
        value_rows = projected[2].astype(jnp.bfloat16)
        key_value = jnp.stack([key_rows, value_rows]).reshape(2, SB, local_len, head_width)
        all_pairs = lax.all_gather(key_value, "context", axis=2, tiled=True)
        padded_pairs = jnp.concatenate(
            [jnp.zeros((2, SB, WINDOW, head_width), jnp.bfloat16), all_pairs], axis=2
        )
        window_pairs = lax.dynamic_slice_in_dim(padded_pairs, local_start, key_span, 2)
        window_pairs = window_pairs.reshape(2, SB, key_span, local_heads, HEAD_DIM)
        key_buffer = window_pairs[0]
        value_buffer = window_pairs[1]
        scores = (
            jnp.einsum("sqhe,skhe->shqk", queries, key_buffer, preferred_element_type=jnp.float32)
            * score_scale
        )
        scores = jnp.where(visible, scores, masked_fill)
        row_max = jnp.max(scores, axis=-1, keepdims=True)
        exp_scores = jnp.exp(scores - row_max)
        row_total = jnp.sum(exp_scores, axis=-1, keepdims=True)
        log_total = row_max + jnp.log(row_total)
        probs_low = (exp_scores / row_total).astype(jnp.bfloat16)
        attended = jnp.einsum(
            "shqk,skhe->sqhe", probs_low, value_buffer, preferred_element_type=jnp.float32
        )
        attended = attended.reshape(SB, local_len, head_width).astype(jnp.bfloat16)
        attention_part = jnp.einsum(
            "snc,cd->snd", attended, out_full, preferred_element_type=jnp.float32
        )
        attention_branch = lax.psum(attention_part.astype(jnp.bfloat16), "tensor").astype(
            jnp.float32
        )
        hidden = rows_in + attention_branch
        normal_two, inverse_two, normed_two = norm_forward(hidden, gains_value[1])
        normed_two = normed_two.astype(jnp.bfloat16)
        gate_up = jnp.einsum(
            "snd,kdf->ksnf", normed_two, gateup_full, preferred_element_type=jnp.float32
        )
        gate_sigmoid = jax.nn.sigmoid(gate_up[0])
        gate_silu = gate_up[0] * gate_sigmoid
        activation = (gate_silu * gate_up[1]).astype(jnp.bfloat16)
        feedforward_part = jnp.einsum(
            "snf,fd->snd", activation, down_full, preferred_element_type=jnp.float32
        )
        feedforward_branch = lax.psum(feedforward_part.astype(jnp.bfloat16), "tensor").astype(
            jnp.float32
        )
        result = (hidden + feedforward_branch).astype(jnp.bfloat16)
        total_down = total_down + jnp.einsum(
            "snf,snd->fd", activation, incoming, preferred_element_type=jnp.float32
        )
        grad_activation = jnp.einsum(
            "snd,fd->snf", incoming, down_full, preferred_element_type=jnp.float32
        )
        grad_gate = (
            grad_activation * gate_up[1] * gate_sigmoid * (1.0 + gate_up[0] * (1.0 - gate_sigmoid))
        )
        grad_up = grad_activation * gate_silu
        grad_gateup = jnp.stack([grad_gate, grad_up]).astype(jnp.bfloat16)
        total_gateup = total_gateup + jnp.einsum(
            "snd,ksnf->kdf", normed_two, grad_gateup, preferred_element_type=jnp.float32
        )
        second_part = jnp.einsum(
            "ksnf,kdf->snd", grad_gateup, gateup_full, preferred_element_type=jnp.float32
        )
        grad_normed_two = lax.psum(second_part.astype(jnp.bfloat16), "tensor").astype(jnp.float32)
        grad_rows_two, gain_two = norm_backward(
            grad_normed_two, normal_two, inverse_two, gains_value[1]
        )
        grad_hidden = incoming.astype(jnp.float32) + grad_rows_two
        grad_hidden_low = grad_hidden.astype(jnp.bfloat16)
        total_out = total_out + jnp.einsum(
            "snc,snd->cd", attended, grad_hidden_low, preferred_element_type=jnp.float32
        )
        grad_attended = jnp.einsum(
            "snd,cd->snc", grad_hidden_low, out_full, preferred_element_type=jnp.float32
        )
        grad_attended = grad_attended.astype(jnp.bfloat16).reshape(
            SB, local_len, local_heads, HEAD_DIM
        )
        again = (
            jnp.einsum("sqhe,skhe->shqk", queries, key_buffer, preferred_element_type=jnp.float32)
            * score_scale
        )
        again = jnp.where(visible, again, masked_fill)
        probs = jnp.exp(again - log_total)
        probs_again = probs.astype(jnp.bfloat16)
        grad_probs = jnp.einsum(
            "sqhe,skhe->shqk", grad_attended, value_buffer, preferred_element_type=jnp.float32
        )
        row_dot = jnp.sum(probs * grad_probs, axis=-1, keepdims=True)
        grad_scores = (probs * (grad_probs - row_dot)).astype(jnp.bfloat16)
        grad_queries = (
            jnp.einsum(
                "shqk,skhe->sqhe", grad_scores, key_buffer, preferred_element_type=jnp.float32
            )
            * score_scale
        )
        grad_keys = (
            jnp.einsum("shqk,sqhe->skhe", grad_scores, queries, preferred_element_type=jnp.float32)
            * score_scale
        )
        grad_values = jnp.einsum(
            "shqk,sqhe->skhe", probs_again, grad_attended, preferred_element_type=jnp.float32
        )
        grad_pairs = jnp.stack([grad_keys, grad_values]).reshape(2, SB, key_span, head_width)
        spread = jnp.zeros((2, SB, WINDOW + SEQ_LEN, head_width), jnp.float32)
        spread = lax.dynamic_update_slice_in_dim(spread, grad_pairs, local_start, 2)[:, :, WINDOW:]
        grad_own = lax.psum_scatter(
            spread.astype(jnp.bfloat16), "context", scatter_dimension=2, tiled=True
        ).astype(jnp.float32)
        grad_own = grad_own.reshape(2, SB, local_len, local_heads, HEAD_DIM)
        grad_projected = jnp.stack(
            [unrotate(grad_queries, cosine, sine), unrotate(grad_own[0], cosine, sine), grad_own[1]]
        )
        grad_projected = grad_projected.reshape(3, SB, local_len, head_width).astype(jnp.bfloat16)
        total_qkv = total_qkv + jnp.einsum(
            "snd,ksne->kde", normed_one, grad_projected, preferred_element_type=jnp.float32
        )
        first_part = jnp.einsum(
            "ksne,kde->snd", grad_projected, qkv_full, preferred_element_type=jnp.float32
        )
        grad_normed_one = lax.psum(first_part.astype(jnp.bfloat16), "tensor").astype(jnp.float32)
        grad_rows_one, gain_one = norm_backward(
            grad_normed_one, normal_one, inverse_one, gains_value[0]
        )
        grad_input = grad_hidden + grad_rows_one
        total_gains = total_gains + jnp.stack([gain_one, gain_two])
        output_all = lax.dynamic_update_slice_in_dim(output_all, result, first_row, 0)
        input_grads = lax.dynamic_update_slice_in_dim(input_grads, grad_input, first_row, 0)
        return (
            output_all,
            input_grads,
            total_qkv,
            total_out,
            total_gateup,
            total_down,
            total_gains,
        )

    initial = (
        jnp.zeros(block_input.shape, jnp.bfloat16),
        jnp.zeros(block_input.shape, jnp.float32),
        jnp.zeros((3, model_width, head_width), jnp.float32),
        jnp.zeros((head_width, model_width), jnp.float32),
        jnp.zeros((2, model_width, hidden_width), jnp.float32),
        jnp.zeros((hidden_width, model_width), jnp.float32),
        jnp.zeros((2, model_width), jnp.float32),
    )
    final = lax.fori_loop(0, micro_count, micro_step, initial)
    gains_grad, qkv_grad, out_grad, gateup_grad, down_grad = (
        lax.psum_scatter(
            final[6].astype(jnp.bfloat16), "context", scatter_dimension=1, tiled=True
        ).astype(jnp.float32),
        lax.psum_scatter(
            final[2].astype(jnp.bfloat16), "context", scatter_dimension=1, tiled=True
        ).astype(jnp.float32),
        lax.psum_scatter(
            final[3].astype(jnp.bfloat16), "context", scatter_dimension=1, tiled=True
        ).astype(jnp.float32),
        lax.psum_scatter(
            final[4].astype(jnp.bfloat16), "context", scatter_dimension=1, tiled=True
        ).astype(jnp.float32),
        lax.psum_scatter(
            final[5].astype(jnp.bfloat16), "context", scatter_dimension=1, tiled=True
        ).astype(jnp.float32),
    )
    return (final[0], final[1], gains_grad, qkv_grad, out_grad, gateup_grad, down_grad)


def solution(mesh):
    in_specs = (
        P(None, "context", None),
        P(),
        P(None, "context"),
        P(None, "context", "tensor"),
        P("tensor", "context"),
        P(None, "context", "tensor"),
        P("tensor", "context"),
        P(None, "context", None),
    )
    out_specs = (
        P(None, "context", None),
        P(None, "context", None),
        P(None, "context"),
        P(None, "context", "tensor"),
        P("tensor", "context"),
        P(None, "context", "tensor"),
        P("tensor", "context"),
    )
    return jax.shard_map(shards, mesh=mesh, in_specs=in_specs, out_specs=out_specs, check_vma=False)
```

profile of v0, /device:TPU:0, one launch (start us, length us, event | category | flops | bytes accessed | tf_op | source)
XLA Modules:
  0.0 3081.6 jit_solution(3677816356305977269)
XLA Ops:
  24.9 2769.0 %while.30 = (s32[]{:T(128)}, bf16[4,512,2048]{2,1,0:T(8,128)(2,1)}, f32[4,512,2048]{2,1,0:T(8,128)}, f32[3,2048,512]{1,2,0:T(8,128)}, f32[512,2048]{1,0:T(8,128)...) while((s32[]{:T(128)}, bf16[4,512,2048]{2,1,0:T(8,128)(2,1)}, ...), condition=%wide.region_17.18_spmd.clone.clone.clone, body=%wide.region_0.17_spmd.clone.clone.clone.sunk | while | flops 81181999104 | bytes 1911083520 | solution.py:263
  25.7 10.5 all_gather.80
  41.3 35.8 %all-gather.8.cloned.1.call-done = bf16[3,2048,512]{1,2,0:T(8,128)(2,1)} async-done(((bf16[3,256,512]{1,2,0:T(8,128)(2,1)}), bf16[3,2048,512]{1,2,0:T(8,128)(2,1)}) %all-gather.8.cloned.1.call-update) | async-done | bytes 6291472 | tf_op jit(solution)/shard_map/while/body/eval_jaxpr/all_gather | solution.py:89
  77.2 10.2 fusion.190
  97.3 87.0 %all-gather.10.cloned.1.call-done = bf16[2,2,4096,512]{2,3,0,1:T(8,128)(2,1)} async-done(((bf16[2,2,512,512]{2,3,0,1:T(8,128)(2,1)}), bf16[2,2,4096,512]{2,3,0,1:T(8,128)(2,1)}) %all-gather.10.cloned.1.call-update) | async-done | bytes 16777232 | tf_op jit(solution)/shard_map/while/body/eval_jaxpr/all_gather | solution.py:118
  191.6 32.9 %fusion.193 = (f32[2,8,512]{2,1,0:T(8,128)S(1)}, f32[2,8,512,2560]{3,2,1,0:T(8,128)}) fusion(bf16[2,2560,8,64]{1,3,2,0:T(8,128)(2,1)} %bitcast.256, bf16[2,512,8,32]{1,3,2,0:T(8,128)(2,1)} %get-tuple-element.1009, bf16[2,512,8,32]{1,3,2,0:T(8,128)(2,1)S(1)} %get-tuple-element.1010, pred[2,512,2560]{2,1,0:T(8,128)(4,1)S(1)} %compare_and_fusion.2), kind=kOutput, calls=%fused_computation.143.clone.1 | convolution fusion | flops 2749358080 | bytes 92831744 | tf_op jit(solution)/shard_map/while/body/eval_jaxpr/sqhe,skhe->shqk/dot_general | solution.py:127
  224.5 26.5 fusion.194
  251.0 30.2 fusion.195
  288.7 156.5 %all-reduce.9.cloned.1.call-done = bf16[2,512,2048]{2,1,0:T(8,128)(2,1)} async-done(((bf16[2,512,2048]{2,1,0:T(8,128)(2,1)}), bf16[2,512,2048]{2,1,0:T(8,128)(2,1)}) %all-reduce.9.cloned.1.call-update) | async-done | bytes 4194320 | tf_op jit(solution)/shard_map/while/body/eval_jaxpr/psum | solution.py:143
  450.1 50.3 %all-gather.6.cloned.1.call-done = bf16[2,2048,1024]{2,1,0:T(8,128)(2,1)} async-done(((bf16[2,256,1024]{2,1,0:T(8,128)(2,1)}), bf16[2,2048,1024]{2,1,0:T(8,128)(2,1)}) %all-gather.6.cloned.1.call-update) | async-done | bytes 8388624 | tf_op jit(solution)/shard_map/while/body/eval_jaxpr/all_gather | solution.py:91
  500.4 16.1 fusion.196
  516.5 23.1 all-gather.14.cloned.1.call-done
  539.6 13.3 fusion.197
  554.9 10.5 bitcast_convert_fusion.4
  565.4 155.1 %all-reduce.11.cloned.1.call-done = bf16[2,512,2048]{2,1,0:T(8,128)(2,1)} async-done(((bf16[2,512,2048]{2,1,0:T(8,128)(2,1)}), bf16[2,512,2048]{2,1,0:T(8,128)(2,1)}) %all-reduce.11.cloned.1.call-update) | async-done | bytes 4194320 | tf_op jit(solution)/shard_map/while/body/eval_jaxpr/psum | solution.py:179
  738.5 53.9 %multiply_reduce_fusion.5 = (f32[2,8,512]{2,1,0:T(8,128)S(1)}, f32[2,8,512,2560]{3,2,1,0:T(8,128)}) fusion(f32[2,8,512,2560]{3,2,1,0:T(8,128)} %get-tuple-element.1011, f32[2,8,512]{2,1,0:T(8,128)S(1)} %log_add_fusion.2, bf16[2,512,8,64]{1,3,2,0:T(8,128)(2,1)S(1)} %bitcast.269, bf16[2,2560,8,64]{1,3,2,0:T(8,128)(2,1)S(1)} %bitcast.265), kind=kOutput, calls=%fused_computation.5.clone.1 | convolution fusion | flops 2747260928 | bytes 174129152 | tf_op jit(solution)/shard_map/while/body/eval_jaxpr/sqhe,skhe->shqk/dot_general | solution.py:201
  792.4 31.0 %fusion.202 = bf16[2,8,64,2560]{3,2,1,0:T(8,128)(2,1)} fusion(bf16[2,512,8,64]{1,3,2,0:T(8,128)(2,1)S(1)} %bitcast.270, f32[2,8,512,2560]{3,2,1,0:T(8,128)} %get-tuple-element.1011, f32[2,8,512]{2,1,0:T(8,128)S(1)} %log_add_fusion.2), kind=kOutput, calls=%fused_computation.12.clone.1 | convolution fusion | flops 2726297600 | bytes 90210304 | tf_op jit(solution)/shard_map/while/body/eval_jaxpr/shqk,sqhe->skhe/dot_general | solution.py:216
  823.4 66.5 %multiply_convert_fusion.8 = bf16[2,8,512,2560]{3,2,1,0:T(8,128)(2,1)} fusion(f32[2,8,512,2560]{3,2,1,0:T(8,128)} %get-tuple-element.1018, f32[2,8,512,2560]{3,2,1,0:T(8,128)} %get-tuple-element.1011, f32[2,8,512]{2,1,0:T(8,128)S(1)} %get-tuple-element.1019, f32[2,8,512]{2,1,0:T(8,128)S(1)} %log_add_fusion.2), kind=kLoop, calls=%fused_computation.4.clone.1 | loop fusion | flops 83886080 | bytes 209780736 | tf_op jit(solution)/shard_map/while/body/eval_jaxpr/convert_element_type | solution.py:205
  889.9 19.1 convolution_multiply_fusion.2
  924.9 8.4 broadcast.302
  933.4 8.7 maximum_dynamic-update-slice_fusion.2
  942.0 13.8 slice.353
  965.8 22.6 multiply_bitcast_fusion.2
  988.4 82.6 %reduce-scatter.19.cloned.1.call-done = bf16[2,2,512,512]{3,2,0,1:T(8,128)(2,1)} async-done(((bf16[2,2,4096,512]{3,2,0,1:T(8,128)(2,1)}), bf16[2,2,512,512]{3,2,0,1:T(8,128)(2,1)}) %reduce-scatter.19.cloned.1.call-update) | async-done | bytes 2097168 | tf_op jit(solution)/shard_map/while/body/eval_jaxpr/reduce_scatter | solution.py:222
  1082.0 11.2 bitcast_convert_fusion.5
  1094.7 9.1 bitcast_add_fusion.11
  1103.8 16.7 bitcast_add_fusion.10
  1127.2 10.2 bitcast_add_fusion.8
  1137.4 247.5 %all-reduce.13.cloned.1.call-done = (bf16[2,512,2048]{2,1,0:T(8,128)(2,1)}, bf16[2,512,2048]{2,1,0:T(8,128)(2,1)}) async-done(((bf16[2,512,2048]{2,1,0:T(8,128)(2,1)}, bf16[2,512,2048]{2,1,0:T(8,128)(2,1)}), (bf16[2,512,2048]{2,1,0:T(8,128)(2,1)}, bf16[2,512,2048]{2,1,0:T(8,128)(2,1)})) %all-reduce.13.cloned.1.call-update) | async-done | bytes 8388624 | tf_op jit(solution)/shard_map/while/body/eval_jaxpr/psum | solution.py:158
  1390.7 12.4 fusion.205
  1411.1 9.0 all_gather.80
  1425.0 33.7 %all-gather.8.cloned.1.call-done = bf16[3,2048,512]{1,2,0:T(8,128)(2,1)} async-done(((bf16[3,256,512]{1,2,0:T(8,128)(2,1)}), bf16[3,2048,512]{1,2,0:T(8,128)(2,1)}) %all-gather.8.cloned.1.call-update) | async-done | bytes 6291472 | tf_op jit(solution)/shard_map/while/body/eval_jaxpr/all_gather | solution.py:89
  1458.7 10.2 fusion.190
  1478.8 87.1 %all-gather.10.cloned.1.call-done = bf16[2,2,4096,512]{2,3,0,1:T(8,128)(2,1)} async-done(((bf16[2,2,512,512]{2,3,0,1:T(8,128)(2,1)}), bf16[2,2,4096,512]{2,3,0,1:T(8,128)(2,1)}) %all-gather.10.cloned.1.call-update) | async-done | bytes 16777232 | tf_op jit(solution)/shard_map/while/body/eval_jaxpr/all_gather | solution.py:118
  1573.2 32.9 %fusion.193 = (f32[2,8,512]{2,1,0:T(8,128)S(1)}, f32[2,8,512,2560]{3,2,1,0:T(8,128)}) fusion(bf16[2,2560,8,64]{1,3,2,0:T(8,128)(2,1)} %bitcast.256, bf16[2,512,8,32]{1,3,2,0:T(8,128)(2,1)} %get-tuple-element.1009, bf16[2,512,8,32]{1,3,2,0:T(8,128)(2,1)S(1)} %get-tuple-element.1010, pred[2,512,2560]{2,1,0:T(8,128)(4,1)S(1)} %compare_and_fusion.2), kind=kOutput, calls=%fused_computation.143.clone.1 | convolution fusion | flops 2749358080 | bytes 92831744 | tf_op jit(solution)/shard_map/while/body/eval_jaxpr/sqhe,skhe->shqk/dot_general | solution.py:127
  1606.0 26.5 fusion.194
  1632.5 30.2 fusion.195
  1670.3 156.4 %all-reduce.9.cloned.1.call-done = bf16[2,512,2048]{2,1,0:T(8,128)(2,1)} async-done(((bf16[2,512,2048]{2,1,0:T(8,128)(2,1)}), bf16[2,512,2048]{2,1,0:T(8,128)(2,1)}) %all-reduce.9.cloned.1.call-update) | async-done | bytes 4194320 | tf_op jit(solution)/shard_map/while/body/eval_jaxpr/psum | solution.py:143
  1831.7 50.3 %all-gather.6.cloned.1.call-done = bf16[2,2048,1024]{2,1,0:T(8,128)(2,1)} async-done(((bf16[2,256,1024]{2,1,0:T(8,128)(2,1)}), bf16[2,2048,1024]{2,1,0:T(8,128)(2,1)}) %all-gather.6.cloned.1.call-update) | async-done | bytes 8388624 | tf_op jit(solution)/shard_map/while/body/eval_jaxpr/all_gather | solution.py:91
  1881.9 16.2 fusion.196
  1898.2 23.0 all-gather.14.cloned.1.call-done
  1921.1 13.3 fusion.197
  1936.4 10.5 bitcast_convert_fusion.4
  1947.0 155.0 %all-reduce.11.cloned.1.call-done = bf16[2,512,2048]{2,1,0:T(8,128)(2,1)} async-done(((bf16[2,512,2048]{2,1,0:T(8,128)(2,1)}), bf16[2,512,2048]{2,1,0:T(8,128)(2,1)}) %all-reduce.11.cloned.1.call-update) | async-done | bytes 4194320 | tf_op jit(solution)/shard_map/while/body/eval_jaxpr/psum | solution.py:179
  2119.7 53.9 %multiply_reduce_fusion.5 = (f32[2,8,512]{2,1,0:T(8,128)S(1)}, f32[2,8,512,2560]{3,2,1,0:T(8,128)}) fusion(f32[2,8,512,2560]{3,2,1,0:T(8,128)} %get-tuple-element.1011, f32[2,8,512]{2,1,0:T(8,128)S(1)} %log_add_fusion.2, bf16[2,512,8,64]{1,3,2,0:T(8,128)(2,1)S(1)} %bitcast.269, bf16[2,2560,8,64]{1,3,2,0:T(8,128)(2,1)S(1)} %bitcast.265), kind=kOutput, calls=%fused_computation.5.clone.1 | convolution fusion | flops 2747260928 | bytes 174129152 | tf_op jit(solution)/shard_map/while/body/eval_jaxpr/sqhe,skhe->shqk/dot_general | solution.py:201
  2173.6 31.0 %fusion.202 = bf16[2,8,64,2560]{3,2,1,0:T(8,128)(2,1)} fusion(bf16[2,512,8,64]{1,3,2,0:T(8,128)(2,1)S(1)} %bitcast.270, f32[2,8,512,2560]{3,2,1,0:T(8,128)} %get-tuple-element.1011, f32[2,8,512]{2,1,0:T(8,128)S(1)} %log_add_fusion.2), kind=kOutput, calls=%fused_computation.12.clone.1 | convolution fusion | flops 2726297600 | bytes 90210304 | tf_op jit(solution)/shard_map/while/body/eval_jaxpr/shqk,sqhe->skhe/dot_general | solution.py:216
  2204.6 66.6 %multiply_convert_fusion.8 = bf16[2,8,512,2560]{3,2,1,0:T(8,128)(2,1)} fusion(f32[2,8,512,2560]{3,2,1,0:T(8,128)} %get-tuple-element.1018, f32[2,8,512,2560]{3,2,1,0:T(8,128)} %get-tuple-element.1011, f32[2,8,512]{2,1,0:T(8,128)S(1)} %get-tuple-element.1019, f32[2,8,512]{2,1,0:T(8,128)S(1)} %log_add_fusion.2), kind=kLoop, calls=%fused_computation.4.clone.1 | loop fusion | flops 83886080 | bytes 209780736 | tf_op jit(solution)/shard_map/while/body/eval_jaxpr/convert_element_type | solution.py:205
  2271.2 19.1 convolution_multiply_fusion.2
  2314.7 8.7 maximum_dynamic-update-slice_fusion.2
  2323.3 13.8 slice.353
  2347.1 22.6 multiply_bitcast_fusion.2
  2369.7 82.6 %reduce-scatter.19.cloned.1.call-done = bf16[2,2,512,512]{3,2,0,1:T(8,128)(2,1)} async-done(((bf16[2,2,4096,512]{3,2,0,1:T(8,128)(2,1)}), bf16[2,2,512,512]{3,2,0,1:T(8,128)(2,1)}) %reduce-scatter.19.cloned.1.call-update) | async-done | bytes 2097168 | tf_op jit(solution)/shard_map/while/body/eval_jaxpr/reduce_scatter | solution.py:222
  2463.2 11.2 bitcast_convert_fusion.5
  2476.0 10.3 bitcast_add_fusion.11
  2486.3 19.1 bitcast_add_fusion.10
  2513.4 13.0 bitcast_add_fusion.8
  2526.5 239.7 %all-reduce.13.cloned.1.call-done = (bf16[2,512,2048]{2,1,0:T(8,128)(2,1)}, bf16[2,512,2048]{2,1,0:T(8,128)(2,1)}) async-done(((bf16[2,512,2048]{2,1,0:T(8,128)(2,1)}, bf16[2,512,2048]{2,1,0:T(8,128)(2,1)}), (bf16[2,512,2048]{2,1,0:T(8,128)(2,1)}, bf16[2,512,2048]{2,1,0:T(8,128)(2,1)})) %all-reduce.13.cloned.1.call-update) | async-done | bytes 8388624 | tf_op jit(solution)/shard_map/while/body/eval_jaxpr/psum | solution.py:158
  2772.1 12.1 fusion.205
  2805.9 10.0 copy.57
  2816.0 14.2 copy.58
  2832.8 43.7 %reduce-scatter.11.cloned.1.call-done = bf16[512,256]{1,0:T(8,128)(2,1)} async-done(((bf16[512,2048]{1,0:T(8,128)(2,1)}), bf16[512,256]{1,0:T(8,128)(2,1)}) %reduce-scatter.11.cloned.1.call-update) | async-done | bytes 262160 | tf_op jit(solution)/shard_map/reduce_scatter | solution.py:271
  2878.2 52.7 %reduce-scatter.15.cloned.1.call-done = bf16[1024,256]{1,0:T(8,128)(2,1)} async-done(((bf16[1024,2048]{1,0:T(8,128)(2,1)}), bf16[1024,256]{1,0:T(8,128)(2,1)}) %reduce-scatter.15.cloned.1.call-update) | async-done | bytes 524304 | tf_op jit(solution)/shard_map/reduce_scatter | solution.py:277
  2933.0 63.3 %reduce-scatter.9.cloned.1.call-done = bf16[3,256,512]{2,1,0:T(8,128)(2,1)} async-done(((bf16[3,2048,512]{2,1,0:T(8,128)(2,1)}), bf16[3,256,512]{2,1,0:T(8,128)(2,1)}) %reduce-scatter.9.cloned.1.call-update) | async-done | bytes 786448 | tf_op jit(solution)/shard_map/reduce_scatter | solution.py:268
  2998.7 72.2 %reduce-scatter.13.cloned.1.call-done = bf16[2,256,1024]{2,1,0:T(8,128)(2,1)} async-done(((bf16[2,2048,1024]{2,1,0:T(8,128)(2,1)}), bf16[2,256,1024]{2,1,0:T(8,128)(2,1)}) %reduce-scatter.13.cloned.1.call-update) | async-done | bytes 1048592 | tf_op jit(solution)/shard_map/reduce_scatter | solution.py:274
  (333 shorter events, 276.2 us)
Async XLA Ops:
  24.9 52.3 %all-gather.8.cloned.1.call-start = ((), (), s32[]{:S(2)}) async-start(), calls=%async_computation.12 | async-start | bytes 7077888 | tf_op jit(solution)/shard_map/while/body/eval_jaxpr/all_gather | solution.py:89
  25.6 158.7 %all-gather.10.cloned.1.call-start = ((), (), s32[]{:S(2)}) async-start(), calls=%async_computation.13 | async-start | bytes 18874368 | tf_op jit(solution)/shard_map/while/body/eval_jaxpr/all_gather | solution.py:118
  39.7 47.7 %copy-start.23 = (f32[2,512]{1,0:T(2,128)}, f32[2,512]{1,0:T(2,128)S(1)}, u32[]{:S(2)}) copy-start(f32[2,512]{1,0:T(2,128)S(1)} %add_rsqrt_fusion.4) | copy-start | bytes 12292 | tf_op jit(solution)/shard_map/while
  40.7 47.3 %copy-start.13 = (f32[512,32]{0,1:T(8,128)}, f32[512,32]{0,1:T(8,128)S(1)}, u32[]{:S(2)}) copy-start(f32[512,32]{0,1:T(8,128)S(1)} %get-tuple-element.1003) | copy-start | bytes 196612 | tf_op jit(solution)/shard_map/while
  40.7 47.3 %copy-start.15 = (f32[512,32]{0,1:T(8,128)}, f32[512,32]{0,1:T(8,128)S(1)}, u32[]{:S(2)}) copy-start(f32[512,32]{0,1:T(8,128)S(1)} %get-tuple-element.1002) | copy-start | bytes 196612 | tf_op jit(solution)/shard_map/while
  41.3 46.1 %copy-start.19 = (f32[1,2048]{1,0:T(1,128)}, f32[1,2048]{1,0:T(1,128)S(1)}, u32[]{:S(2)}) copy-start(f32[1,2048]{1,0:T(1,128)S(1)} %get-tuple-element.1000) | copy-start | bytes 24580 | tf_op jit(solution)/shard_map/while
  89.5 102.1 %copy-start.4 = (bf16[2,512,8,32]{1,3,2,0:T(8,128)(2,1)}, bf16[2,512,8,32]{1,3,2,0:T(8,128)(2,1)S(1)}, u32[]{:S(2)}) copy-start(bf16[2,512,8,32]{1,3,2,0:T(8,128)(2,1)S(1)} %get-tuple-element.1010) | copy-start | bytes 1572868 | tf_op jit(solution)/shard_map/while
  91.1 190.1 %all-gather.12.cloned.1.call-start = ((), (), s32[]{:S(2)}) async-start(), calls=%async_computation.14 | async-start | bytes 2359296 | tf_op jit(solution)/shard_map/while/body/eval_jaxpr/all_gather | solution.py:90
  91.8 353.3 %all-reduce.9.cloned.1.call-start = ((), (), s32[]{:S(2)}) async-start(), calls=%async_computation.15 | async-start | bytes 8388608 | tf_op jit(solution)/shard_map/while/body/eval_jaxpr/psum | solution.py:143
  287.5 212.9 %copy-start.17 = (f32[1,2048]{1,0:T(1,128)S(1)}, f32[1,2048]{1,0:T(1,128)}, u32[]{:S(2)}) copy-start(f32[1,2048]{1,0:T(1,128)} %get-tuple-element.1013) | copy-start | bytes 24580 | tf_op jit(solution)/shard_map/while
  287.5 212.9 %all-gather.6.cloned.1.call-start = ((), (), s32[]{:S(2)}) async-start(), calls=%async_computation.11 | async-start | bytes 9437184 | tf_op jit(solution)/shard_map/while/body/eval_jaxpr/all_gather | solution.py:91
  288.1 251.5 %all-gather.14.cloned.1.call-start = ((), (), s32[]{:S(2)}) async-start(), calls=%async_computation.16 | async-start | bytes 4718592 | tf_op jit(solution)/shard_map/while/body/eval_jaxpr/all_gather | solution.py:92
  288.7 431.9 %all-reduce.11.cloned.1.call-start = ((), (), s32[]{:S(2)}) async-start(), calls=%async_computation.17 | async-start | bytes 8388608 | tf_op jit(solution)/shard_map/while/body/eval_jaxpr/psum | solution.py:179
  450.1 278.3 %copy-start.21 = (f32[2,512]{1,0:T(2,128)}, f32[2,512]{1,0:T(2,128)S(1)}, u32[]{:S(2)}) copy-start(f32[2,512]{1,0:T(2,128)S(1)} %add_rsqrt_fusion.5) | copy-start | bytes 12292 | tf_op jit(solution)/shard_map/while
  539.6 15.3 copy-start.30
  565.4 505.6 %reduce-scatter.19.cloned.1.call-start = ((), (), s32[]{:S(2)}) async-start(), calls=%async_computation.18 | async-start | bytes 18874368 | tf_op jit(solution)/shard_map/while/body/eval_jaxpr/reduce_scatter | solution.py:222
  823.4 66.5 %copy-start.5 = (bf16[2,512,8,32]{1,3,2,0:T(8,128)(2,1)S(1)}, bf16[2,512,8,32]{1,3,2,0:T(8,128)(2,1)}, u32[]{:S(2)}) copy-start(bf16[2,512,8,32]{1,3,2,0:T(8,128)(2,1)} %copy-done.4) | copy-start | bytes 1572868 | tf_op jit(solution)/shard_map/while
  823.4 66.5 %copy-start.6 = (bf16[2,512,8,32]{1,3,2,0:T(8,128)(2,1)S(1)}, bf16[2,512,8,32]{1,3,2,0:T(8,128)(2,1)}, u32[]{:S(2)}) copy-start(bf16[2,512,8,32]{1,3,2,0:T(8,128)(2,1)} %get-tuple-element.1009) | copy-start | bytes 1572868 | tf_op jit(solution)/shard_map/while
  955.8 429.0 %all-reduce.13.cloned.1.call-start = ((), (), s32[]{:S(2)}) async-start(), calls=%async_computation.19 | async-start | bytes 16777216 | tf_op jit(solution)/shard_map/while/body/eval_jaxpr/psum | solution.py:158
  988.4 89.1 %copy-start.14 = (f32[512,32]{0,1:T(8,128)S(1)}, f32[512,32]{0,1:T(8,128)}, u32[]{:S(2)}) copy-start(f32[512,32]{0,1:T(8,128)} %copy-done.13) | copy-start | bytes 196612 | tf_op jit(solution)/shard_map/while
  988.4 89.1 %copy-start.16 = (f32[512,32]{0,1:T(8,128)S(1)}, f32[512,32]{0,1:T(8,128)}, u32[]{:S(2)}) copy-start(f32[512,32]{0,1:T(8,128)} %copy-done.15) | copy-start | bytes 196612 | tf_op jit(solution)/shard_map/while
  1103.8 16.7 copy-start.33
  1137.4 252.9 %copy-start.27 = (f32[2048]{0:T(1024)S(1)}, f32[2048]{0:T(1024)}, u32[]{:S(2)}) copy-start(f32[2048]{0:T(1024)} %get-tuple-element.1031) | copy-start | bytes 24580 | tf_op jit(solution)/shard_map/while
  1137.4 252.9 %copy-start.28 = (f32[2,2048]{1,0:T(2,128)S(1)}, f32[2,2048]{1,0:T(2,128)}, u32[]{:S(2)}) copy-start(f32[2,2048]{1,0:T(2,128)} %get-tuple-element.1068) | copy-start | bytes 49156 | tf_op jit(solution)/shard_map/while
  1137.4 253.0 %copy-start.26 = (f32[2,512]{1,0:T(2,128)S(1)}, f32[2,512]{1,0:T(2,128)}, u32[]{:S(2)}) copy-start(f32[2,512]{1,0:T(2,128)} %copy-done.25) | copy-start | bytes 12292 | tf_op jit(solution)/shard_map/while
  1384.8 18.3 slice-start.2
  1390.3 12.8 copy-start.29
  1390.7 12.4 slice-start.3
  1410.4 48.3 %all-gather.8.cloned.1.call-start = ((), (), s32[]{:S(2)}) async-start(), calls=%async_computation.12 | async-start | bytes 7077888 | tf_op jit(solution)/shard_map/while/body/eval_jaxpr/all_gather | solution.py:89
  1411.0 154.9 %all-gather.10.cloned.1.call-start = ((), (), s32[]{:S(2)}) async-start(), calls=%async_computation.13 | async-start | bytes 18874368 | tf_op jit(solution)/shard_map/while/body/eval_jaxpr/all_gather | solution.py:118
  1423.4 45.6 %copy-start.23 = (f32[2,512]{1,0:T(2,128)}, f32[2,512]{1,0:T(2,128)S(1)}, u32[]{:S(2)}) copy-start(f32[2,512]{1,0:T(2,128)S(1)} %add_rsqrt_fusion.4) | copy-start | bytes 12292 | tf_op jit(solution)/shard_map/while
  1424.4 45.2 %copy-start.13 = (f32[512,32]{0,1:T(8,128)}, f32[512,32]{0,1:T(8,128)S(1)}, u32[]{:S(2)}) copy-start(f32[512,32]{0,1:T(8,128)S(1)} %get-tuple-element.1003) | copy-start | bytes 196612 | tf_op jit(solution)/shard_map/while
  1424.4 45.2 %copy-start.15 = (f32[512,32]{0,1:T(8,128)}, f32[512,32]{0,1:T(8,128)S(1)}, u32[]{:S(2)}) copy-start(f32[512,32]{0,1:T(8,128)S(1)} %get-tuple-element.1002) | copy-start | bytes 196612 | tf_op jit(solution)/shard_map/while
  1425.0 44.0 %copy-start.19 = (f32[1,2048]{1,0:T(1,128)}, f32[1,2048]{1,0:T(1,128)S(1)}, u32[]{:S(2)}) copy-start(f32[1,2048]{1,0:T(1,128)S(1)} %get-tuple-element.1000) | copy-start | bytes 24580 | tf_op jit(solution)/shard_map/while
  1471.1 102.1 %copy-start.4 = (bf16[2,512,8,32]{1,3,2,0:T(8,128)(2,1)}, bf16[2,512,8,32]{1,3,2,0:T(8,128)(2,1)S(1)}, u32[]{:S(2)}) copy-start(bf16[2,512,8,32]{1,3,2,0:T(8,128)(2,1)S(1)} %get-tuple-element.1010) | copy-start | bytes 1572868 | tf_op jit(solution)/shard_map/while
  1472.7 190.1 %all-gather.12.cloned.1.call-start = ((), (), s32[]{:S(2)}) async-start(), calls=%async_computation.14 | async-start | bytes 2359296 | tf_op jit(solution)/shard_map/while/body/eval_jaxpr/all_gather | solution.py:90
  1473.2 353.5 %all-reduce.9.cloned.1.call-start = ((), (), s32[]{:S(2)}) async-start(), calls=%async_computation.15 | async-start | bytes 8388608 | tf_op jit(solution)/shard_map/while/body/eval_jaxpr/psum | solution.py:143
  1669.0 212.9 %copy-start.17 = (f32[1,2048]{1,0:T(1,128)S(1)}, f32[1,2048]{1,0:T(1,128)}, u32[]{:S(2)}) copy-start(f32[1,2048]{1,0:T(1,128)} %get-tuple-element.1013) | copy-start | bytes 24580 | tf_op jit(solution)/shard_map/while
  1669.1 212.9 %all-gather.6.cloned.1.call-start = ((), (), s32[]{:S(2)}) async-start(), calls=%async_computation.11 | async-start | bytes 9437184 | tf_op jit(solution)/shard_map/while/body/eval_jaxpr/all_gather | solution.py:91
  1669.7 251.5 %all-gather.14.cloned.1.call-start = ((), (), s32[]{:S(2)}) async-start(), calls=%async_computation.16 | async-start | bytes 4718592 | tf_op jit(solution)/shard_map/while/body/eval_jaxpr/all_gather | solution.py:92
  1670.3 431.8 %all-reduce.11.cloned.1.call-start = ((), (), s32[]{:S(2)}) async-start(), calls=%async_computation.17 | async-start | bytes 8388608 | tf_op jit(solution)/shard_map/while/body/eval_jaxpr/psum | solution.py:179
  1831.6 277.9 %copy-start.21 = (f32[2,512]{1,0:T(2,128)}, f32[2,512]{1,0:T(2,128)S(1)}, u32[]{:S(2)}) copy-start(f32[2,512]{1,0:T(2,128)S(1)} %add_rsqrt_fusion.5) | copy-start | bytes 12292 | tf_op jit(solution)/shard_map/while
  1921.1 15.3 copy-start.30
  1946.9 505.3 %reduce-scatter.19.cloned.1.call-start = ((), (), s32[]{:S(2)}) async-start(), calls=%async_computation.18 | async-start | bytes 18874368 | tf_op jit(solution)/shard_map/while/body/eval_jaxpr/reduce_scatter | solution.py:222
  2204.6 66.6 %copy-start.5 = (bf16[2,512,8,32]{1,3,2,0:T(8,128)(2,1)S(1)}, bf16[2,512,8,32]{1,3,2,0:T(8,128)(2,1)}, u32[]{:S(2)}) copy-start(bf16[2,512,8,32]{1,3,2,0:T(8,128)(2,1)} %copy-done.4) | copy-start | bytes 1572868 | tf_op jit(solution)/shard_map/while
  2204.6 66.6 %copy-start.6 = (bf16[2,512,8,32]{1,3,2,0:T(8,128)(2,1)S(1)}, bf16[2,512,8,32]{1,3,2,0:T(8,128)(2,1)}, u32[]{:S(2)}) copy-start(bf16[2,512,8,32]{1,3,2,0:T(8,128)(2,1)} %get-tuple-element.1009) | copy-start | bytes 1572868 | tf_op jit(solution)/shard_map/while
  2337.1 10.0 slice-start.4
  2337.1 429.0 %all-reduce.13.cloned.1.call-start = ((), (), s32[]{:S(2)}) async-start(), calls=%async_computation.19 | async-start | bytes 16777216 | tf_op jit(solution)/shard_map/while/body/eval_jaxpr/psum | solution.py:158
  2369.7 89.1 %copy-start.14 = (f32[512,32]{0,1:T(8,128)S(1)}, f32[512,32]{0,1:T(8,128)}, u32[]{:S(2)}) copy-start(f32[512,32]{0,1:T(8,128)} %copy-done.13) | copy-start | bytes 196612 | tf_op jit(solution)/shard_map/while
  2369.7 89.1 %copy-start.16 = (f32[512,32]{0,1:T(8,128)S(1)}, f32[512,32]{0,1:T(8,128)}, u32[]{:S(2)}) copy-start(f32[512,32]{0,1:T(8,128)} %copy-done.15) | copy-start | bytes 196612 | tf_op jit(solution)/shard_map/while
  2476.0 10.3 copy-start.18
  2476.0 10.3 copy-start.22
  2486.3 19.2 copy-start.33
  2526.5 245.1 %copy-start.27 = (f32[2048]{0:T(1024)S(1)}, f32[2048]{0:T(1024)}, u32[]{:S(2)}) copy-start(f32[2048]{0:T(1024)} %get-tuple-element.1031) | copy-start | bytes 24580 | tf_op jit(solution)/shard_map/while
  2526.5 245.1 %copy-start.28 = (f32[2,2048]{1,0:T(2,128)S(1)}, f32[2,2048]{1,0:T(2,128)}, u32[]{:S(2)}) copy-start(f32[2,2048]{1,0:T(2,128)} %get-tuple-element.1068) | copy-start | bytes 49156 | tf_op jit(solution)/shard_map/while
  2526.5 245.2 %copy-start.26 = (f32[2,512]{1,0:T(2,128)S(1)}, f32[2,512]{1,0:T(2,128)}, u32[]{:S(2)}) copy-start(f32[2,512]{1,0:T(2,128)} %copy-done.25) | copy-start | bytes 12292 | tf_op jit(solution)/shard_map/while
  2766.1 18.1 slice-start.2
  2771.6 12.6 copy-start.29
  2772.1 12.1 slice-start.3
  2793.9 37.3 %reduce-scatter.17.cloned.1.call-start = ((), (), s32[]{:S(2)}) async-start(), calls=%async_computation.10 | async-start | bytes 589824
  2795.8 80.6 %reduce-scatter.11.cloned.1.call-start = ((), (), s32[]{:S(2)}) async-start(), calls=%async_computation.7 | async-start | bytes 2359296 | tf_op jit(solution)/shard_map/reduce_scatter | solution.py:271
  2799.7 131.2 %reduce-scatter.15.cloned.1.call-start = ((), (), s32[]{:S(2)}) async-start(), calls=%async_computation.9 | async-start | bytes 4718592 | tf_op jit(solution)/shard_map/reduce_scatter | solution.py:277
  2805.8 190.4 %reduce-scatter.9.cloned.1.call-start = ((), (), s32[]{:S(2)}) async-start(), calls=%async_computation.6 | async-start | bytes 7077888 | tf_op jit(solution)/shard_map/reduce_scatter | solution.py:268
  2816.0 254.9 %reduce-scatter.13.cloned.1.call-start = ((), (), s32[]{:S(2)}) async-start(), calls=%async_computation.8 | async-start | bytes 9437184 | tf_op jit(solution)/shard_map/reduce_scatter | solution.py:274
  (47 other events, 261.3 us)
Sparse Core Ops, SparseCore 0:
  27.8 49.3 all-gather.7
  91.2 93.1 all-gather.9
  186.4 28.1 all-gather.11
  287.6 157.5 all-reduce.8
  446.9 53.3 all-gather.5
  502.1 37.4 all-gather.13
  565.5 154.9 all-reduce.10
  956.0 114.9 reduce-scatter.18
  1093.3 291.5 all-reduce.12
  1413.0 45.6 all-gather.7
  1472.8 93.0 all-gather.9
  1567.8 28.1 all-gather.11
  1669.2 157.4 all-reduce.8
  1828.5 53.3 all-gather.5
  1883.7 37.4 all-gather.13
  1947.1 154.9 all-reduce.10
  2337.2 114.9 reduce-scatter.18
  2474.6 291.5 all-reduce.12
Sparse Core Ops, SparseCore 1:
  2798.1 33.1 reduce-scatter.16
  2835.3 41.1 reduce-scatter.10
  2879.7 51.2 reduce-scatter.14
  2934.7 61.5 reduce-scatter.8
  2999.7 71.1 reduce-scatter.12
where the time goes:
time: 3090 us; the launch traced here: 3080 us
  waiting for transfers between devices  1900 us (61%)
  matrix products  629 us (20%)
  other arithmetic  351 us (11%)
  local copies, waits for them, and re-layouts  158 us (5%)
    psum x2, waiting for transfers between devices, micro_step(): lax.psum(feedforward_part.astype(jnp.bfloat16), 'tensor')  487 us
    psum x2, waiting for transfers between devices, micro_step(): lax.psum(attention_part.astype(jnp.bfloat16), 'tensor').astype(jnp.float32)  313 us
    psum x2, waiting for transfers between devices, micro_step(): lax.psum(second_part.astype(jnp.bfloat16), 'tensor').astype(jnp.float32)  310 us
    all_gather x2, waiting for transfers between devices, micro_step(): all_pairs = lax.all_gather(key_value, 'context', axis=2, tiled=True)  174 us
    reduce_scatter x2, waiting for transfers between devices, micro_step(): lax.psum_scatter(spread.astype(jnp.bfloat16), 'context', scatter_dimensio...  165 us
    convert_element_type x2, other arithmetic, micro_step(): grad_scores = (probs * (grad_probs - row_dot)).astype(jnp.bfloat16)  133 us
    dot_general x2, matrix products, micro_step(): jnp.einsum('sqhe,skhe->shqk', grad_attended, value_buffer, preferred_elem...  108 us
    all_gather x2, waiting for transfers between devices, micro_step(): lax.all_gather(gateup_weight, 'context', axis=1, tiled=True)  101 us
  transfers between devices with their start and end apart: 23, of which 21 were waited for; matrix products, arithmetic and copies ran while one was open for 15% of the time, Pallas kernels for 0%

commit v1 on v0

v1 whole, which is shorter than its diff:
```python
import functools
import math

import jax
import jax.numpy as jnp
from jax import lax
from jax.experimental import pallas as pl
from jax.experimental.pallas import tpu as pltpu
from jax.sharding import Mesh
from jax.sharding import PartitionSpec as P

HEAD_DIM = 64
WINDOW = 2048
BLOCK = 256

epsilon = 1e-05
rope_base = 10000.0
masked_fill = -1e30

f32 = jnp.float32
bf16 = jnp.bfloat16
VMEM_BYTES = 56 * 1024 * 1024


def dot(a, b, ca, cb):
    return lax.dot_general(a, b, (((ca,), (cb,)), ((), ())), preferred_element_type=f32)


def visible_block(low_row, q0, k0, block):
    key = k0 + lax.broadcasted_iota(jnp.int32, (block, block), 0)
    query = q0 + lax.broadcasted_iota(jnp.int32, (block, block), 1)
    return (key >= low_row) & (key <= query)


def key_loops(lo_ref, full_ref, step, carry):
    qb = pl.program_id(0)
    lo = lo_ref[qb]
    full = jnp.minimum(jnp.maximum(full_ref[qb], lo), qb)
    carry = lax.fori_loop(lo, full, functools.partial(step, True), carry)
    carry = lax.fori_loop(full, qb, functools.partial(step, False), carry)
    return step(True, qb, carry)


def attend_kernel(lo_ref, full_ref, low_ref, q_ref, k_ref, v_ref, o_ref, lse_ref, acc_ref):
    heads = k_ref.shape[0]
    block = q_ref.shape[1]
    q0 = pl.program_id(0) * block
    acc_ref[...] = jnp.zeros_like(acc_ref)

    def step(masked, kb, carry):
        k0 = pl.multiple_of(kb * block, block)
        if masked:
            visible = visible_block(low_ref[...], q0, k0, block)
        out = []
        for h in range(heads):
            top, total = carry[h]
            rows = pl.ds(h * HEAD_DIM, HEAD_DIM)
            scores = dot(k_ref[h, pl.ds(k0, block), :], q_ref[rows, :], 1, 0)
            if masked:
                scores = jnp.where(visible, scores, masked_fill)
            new_top = jnp.maximum(top, jnp.max(scores, axis=0, keepdims=True))
            weights = jnp.exp(scores - new_top)
            fade = jnp.exp(top - new_top)
            total = total * fade + jnp.sum(weights, axis=0, keepdims=True)
            acc_ref[rows, :] = acc_ref[rows, :] * fade + dot(
                v_ref[rows, pl.ds(k0, block)], weights.astype(bf16), 1, 0
            )
            out.append((new_top, total))
        return tuple(out)

    start = tuple(
        (jnp.full((1, block), masked_fill, f32), jnp.zeros((1, block), f32)) for _ in range(heads)
    )
    final = key_loops(lo_ref, full_ref, step, start)
    for h in range(heads):
        top, total = final[h]
        rows = pl.ds(h * HEAD_DIM, HEAD_DIM)
        o_ref[rows, :] = (acc_ref[rows, :] / total).astype(bf16)
        lse_ref[h : h + 1, :] = top + jnp.log(total)


def attend_back_kernel(
    lo_ref,
    full_ref,
    low_ref,
    q_ref,
    g_ref,
    o_ref,
    lse_ref,
    k_ref,
    v_ref,
    kt_ref,
    dq_ref,
    dk_ref,
    dv_ref,
):
    heads = k_ref.shape[0]
    block = q_ref.shape[1]
    q0 = pl.program_id(0) * block

    @pl.when(pl.program_id(0) == 0)
    def _():
        dk_ref[...] = jnp.zeros_like(dk_ref)
        dv_ref[...] = jnp.zeros_like(dv_ref)

    dq_ref[...] = jnp.zeros_like(dq_ref)
    inner = []
    for h in range(heads):
        rows = pl.ds(h * HEAD_DIM, HEAD_DIM)
        inner.append(
            jnp.sum(
                g_ref[rows, :].astype(f32) * o_ref[rows, :].astype(f32), axis=0, keepdims=True
            )
        )

    def step(masked, kb, carry):
        k0 = pl.multiple_of(kb * block, block)
        cols = pl.ds(k0, block)
        if masked:
            visible = visible_block(low_ref[...], q0, k0, block)
        for h in range(heads):
            rows = pl.ds(h * HEAD_DIM, HEAD_DIM)
            scores = dot(k_ref[h, cols, :], q_ref[rows, :], 1, 0)
            if masked:
                scores = jnp.where(visible, scores, masked_fill)
            probs = jnp.exp(scores - lse_ref[h : h + 1, :])
            grad_probs = dot(v_ref[h, cols, :], g_ref[rows, :], 1, 0)
            grad_scores = (probs * (grad_probs - inner[h])).astype(bf16)
            dv_ref[rows, cols] += dot(g_ref[rows, :], probs.astype(bf16), 1, 1)
            dk_ref[rows, cols] += dot(q_ref[rows, :], grad_scores, 1, 1)
            dq_ref[rows, :] += dot(kt_ref[rows, cols], grad_scores, 1, 0)
        return carry

    key_loops(lo_ref, full_ref, step, 0)


def attention_specs(heads, length, block):
    width = heads * HEAD_DIM
    whole_t = pl.BlockSpec((width, length), lambda i, *_: (0, 0))
    whole_h = pl.BlockSpec((heads, length, HEAD_DIM), lambda i, *_: (0, 0, 0))
    tile = pl.BlockSpec((width, block), lambda i, *_: (0, i))
    low = pl.BlockSpec((1, block), lambda i, *_: (0, i))
    stat = pl.BlockSpec((heads, block), lambda i, *_: (0, i))
    return whole_t, whole_h, tile, low, stat


def attend(bounds, q_t, k_h, v_t):
    heads, length, _ = k_h.shape
    width = heads * HEAD_DIM
    block = math.gcd(BLOCK, length)
    whole_t, whole_h, tile, low, stat = attention_specs(heads, length, block)
    pairs = length * WINDOW * heads
    return pl.pallas_call(
        attend_kernel,
        out_shape=(
            jax.ShapeDtypeStruct((width, length), bf16),
            jax.ShapeDtypeStruct((heads, length), f32),
        ),
        grid_spec=pltpu.PrefetchScalarGridSpec(
            num_scalar_prefetch=2,
            grid=(length // block,),
            in_specs=[low, tile, whole_h, whole_t],
            out_specs=[tile, stat],
            scratch_shapes=[pltpu.VMEM((width, block), f32)],
        ),
        compiler_params=pltpu.CompilerParams(vmem_limit_bytes=VMEM_BYTES),
        cost_estimate=pl.CostEstimate(
            flops=pairs * 4 * 256, transcendentals=pairs, bytes_accessed=length * width * 8
        ),
        name="attend",
    )(*bounds, q_t, k_h, v_t)


def attend_back(bounds, q_t, g_t, o_t, lse, k_h, v_h, k_t):
    heads, length, _ = k_h.shape
    width = heads * HEAD_DIM
    block = math.gcd(BLOCK, length)
    whole_t, whole_h, tile, low, stat = attention_specs(heads, length, block)
    pairs = length * WINDOW * heads
    return pl.pallas_call(
        attend_back_kernel,
        out_shape=tuple(jax.ShapeDtypeStruct((width, length), f32) for _ in range(3)),
        grid_spec=pltpu.PrefetchScalarGridSpec(
            num_scalar_prefetch=2,
            grid=(length // block,),
            in_specs=[low, tile, tile, tile, stat, whole_h, whole_h, whole_t],
            out_specs=[tile, whole_t, whole_t],
        ),
        compiler_params=pltpu.CompilerParams(vmem_limit_bytes=VMEM_BYTES),
        cost_estimate=pl.CostEstimate(
            flops=pairs * 10 * 256, transcendentals=pairs, bytes_accessed=length * width * 24
        ),
        name="attend_back",
    )(*bounds, q_t, g_t, o_t, lse, k_h, v_h, k_t)


def attention_bounds(lengths, length):
    docs = lengths.shape[0]
    upto = jnp.arange(docs)[:, None] >= jnp.arange(docs)[None, :]
    ends = jnp.sum(jnp.where(upto, lengths[None, :], 0), axis=1)
    position = jnp.arange(length, dtype=jnp.int32)
    starts = jnp.max(jnp.where(ends[:, None] <= position[None, :], ends[:, None], 0), axis=0)
    low = jnp.maximum(starts, position - (WINDOW - 1)).astype(jnp.int32)
    block = math.gcd(BLOCK, length)
    by_block = low.reshape(length // block, block)
    first = by_block[:, 0] // block
    full = (by_block[:, -1] + block - 1) // block
    return first, full, low.reshape(1, length)


def rope_tables(length):
    half_dim = HEAD_DIM // 2
    counter = jnp.arange(half_dim, dtype=f32)
    frequency = jnp.exp(counter * (-2.0 * math.log(rope_base) / HEAD_DIM))
    angles = frequency[:, None] * jnp.arange(length, dtype=f32)[None, :]
    return jnp.cos(angles)[None], jnp.sin(angles)[None]


def rotate(values, cosine, sine):
    heads = values.shape[0] // HEAD_DIM
    v = values.reshape(heads, 2, HEAD_DIM // 2, values.shape[1])
    a, b = v[:, 0], v[:, 1]
    out = jnp.stack([a * cosine - b * sine, b * cosine + a * sine], axis=1)
    return out.reshape(values.shape)


def norm_inverse(rows):
    return lax.rsqrt(jnp.mean(rows * rows, axis=-1, keepdims=True) + epsilon)


def norm_backward(grad_normed, normal, inverse, gain):
    grad_normal = grad_normed * gain
    inner = jnp.mean(grad_normal * normal, axis=-1, keepdims=True)
    return inverse * (grad_normal - normal * inner), jnp.sum(grad_normed * normal, axis=0)


def shards(
    parts,
    block_input,
    doc_lengths,
    norm_gains,
    qkv_weight,
    out_weight,
    gateup_weight,
    down_weight,
    cotangent,
):
    n_context, seqs, n_extra = parts
    plane = ("context", "extra")
    model = block_input.shape[2]
    local_len = block_input.shape[1]
    length = local_len * n_context
    own_len = local_len // n_extra
    rows = model // n_context
    block_heads = qkv_weight.shape[2] // HEAD_DIM
    heads = seqs * block_heads // n_context
    block_hidden = gateup_weight.shape[2] // n_context
    hidden_width = seqs * block_hidden
    width = heads * HEAD_DIM
    seq = lax.axis_index("seq")
    first_row = lax.axis_index("extra") * own_len

    def exchange(a):
        return lax.all_to_all(a, "context", split_axis=0, concat_axis=0, tiled=True)

    def gather_plane(a):
        return lax.all_gather(a, plane, axis=0, tiled=True)

    def scatter_plane(a):
        return lax.psum_scatter(a.astype(bf16), plane, scatter_dimension=0, tiled=True).astype(f32)

    def own(a):
        return lax.dynamic_slice(a, (seq, first_row, 0), (1, own_len, model))[0]

    def gather_heads(a):
        m = a.shape[1]
        if block_heads % n_context == 0:
            a = exchange(a.reshape(n_context, -1, rows))
            a = lax.all_gather(a, "seq", axis=0, tiled=False)
            a = a.reshape(seqs, n_context, block_heads // n_context, m, rows)
            return a.transpose(0, 2, 3, 1, 4).reshape(heads, m, model)
        a = lax.all_gather(a, "seq", axis=0, tiled=True)
        a = exchange(a.reshape(n_context, -1, rows))
        return a.reshape(n_context, heads, m, rows).transpose(1, 2, 0, 3).reshape(heads, m, model)

    def scatter_heads(a):
        m = a.shape[1]
        a = a.astype(bf16)
        if block_heads % n_context == 0:
            a = a.reshape(seqs, block_heads // n_context, m, n_context, rows)
            a = a.transpose(0, 3, 1, 2, 4).reshape(seqs, n_context, -1, rows)
            a = lax.psum_scatter(a, "seq", scatter_dimension=0, tiled=False)
            return exchange(a).reshape(block_heads, m, rows).astype(f32)
        a = a.reshape(heads, m, n_context, rows).transpose(2, 0, 1, 3)
        a = exchange(a.reshape(n_context, -1, rows)).reshape(seqs * block_heads, m, rows)
        return lax.psum_scatter(a, "seq", scatter_dimension=0, tiled=True).astype(f32)

    def gather_hidden(a):
        a = lax.all_gather(exchange(a), "seq", axis=0, tiled=False)
        return a.transpose(0, 2, 1, 3).reshape(seqs, a.shape[2], model)

    def scatter_hidden(a):
        m = a.shape[1]
        a = a.astype(bf16).reshape(seqs, m, n_context, rows).transpose(0, 2, 1, 3)
        return exchange(lax.psum_scatter(a, "seq", scatter_dimension=0, tiled=False)).astype(f32)

    gains = lax.all_gather(norm_gains, "context", axis=1, tiled=True).astype(f32)
    rows_in = own(block_input).astype(f32)
    incoming = own(cotangent)

    qkv_local = qkv_weight.reshape(3, rows, block_heads, HEAD_DIM).transpose(2, 0, 3, 1)
    qkv_full = gather_heads(qkv_local.reshape(block_heads, 3 * HEAD_DIM, rows))
    qkv_t = qkv_full.reshape(heads, 3, HEAD_DIM, model).transpose(1, 0, 2, 3)
    qkv_t = qkv_t.reshape(3 * width, model)
    inverse_one = norm_inverse(rows_in)
    normal_one = rows_in * inverse_one
    normed_one = gather_plane((normal_one * gains[0]).astype(bf16))
    out_full = gather_heads(out_weight.reshape(block_heads, HEAD_DIM, rows)).reshape(width, model)
    gateup_local = gateup_weight.reshape(2, rows, n_context, block_hidden).transpose(2, 0, 3, 1)
    gateup_full = gather_hidden(gateup_local.reshape(n_context, 2 * block_hidden, rows))
    gateup_t = gateup_full.reshape(seqs, 2, block_hidden, model).transpose(1, 0, 2, 3)
    gateup_t = gateup_t.reshape(2 * hidden_width, model)
    down_full = gather_hidden(down_weight.reshape(n_context, block_hidden, rows))
    down_full = down_full.reshape(hidden_width, model)
    incoming_all = gather_plane(incoming)

    bounds = attention_bounds(lax.dynamic_slice_in_dim(doc_lengths, seq, 1, 0)[0], length)
    cosine, sine = rope_tables(length)
    score_scale = HEAD_DIM ** (-0.5)

    projected = dot(qkv_t, normed_one, 1, 1)
    q_t = rotate(projected[:width], cosine, sine).astype(bf16) * bf16(score_scale)
    k_t = rotate(projected[width : 2 * width], cosine, sine).astype(bf16)
    v_t = projected[2 * width :].astype(bf16)
    k_h = k_t.reshape(heads, HEAD_DIM, length).transpose(0, 2, 1)
    v_h = v_t.reshape(heads, HEAD_DIM, length).transpose(0, 2, 1)
    o_t, lse = attend(bounds, q_t, k_h, v_t)

    attention_branch = scatter_plane(dot(o_t, out_full, 0, 0))
    hidden = rows_in + attention_branch
    inverse_two = norm_inverse(hidden)
    normal_two = hidden * inverse_two
    normed_two = gather_plane((normal_two * gains[1]).astype(bf16))

    grad_activation = dot(incoming_all, down_full, 1, 1)
    gate_up = dot(normed_two, gateup_t, 1, 1)
    gate, up = gate_up[:, :hidden_width], gate_up[:, hidden_width:]
    gate_sigmoid = jax.nn.sigmoid(gate)
    gate_silu = gate * gate_sigmoid
    activation = (gate_silu * up).astype(bf16)
    grad_gate = grad_activation * up * gate_sigmoid * (1.0 + gate * (1.0 - gate_sigmoid))
    grad_up = grad_activation * gate_silu
    grad_gateup = jnp.concatenate([grad_gate, grad_up], axis=1).astype(bf16)
    grad_normed_two = scatter_plane(dot(grad_gateup, gateup_t, 1, 0))
    feedforward_branch = scatter_plane(dot(activation, down_full, 1, 0))
    result = (hidden + feedforward_branch).astype(bf16)

    grad_rows_two, gain_two = norm_backward(grad_normed_two, normal_two, inverse_two, gains[1])
    grad_hidden = incoming.astype(f32) + grad_rows_two
    grad_hidden_all = gather_plane(grad_hidden.astype(bf16))

    down_grad = dot(activation, incoming_all, 0, 0)
    gateup_grad = dot(grad_gateup, normed_two, 0, 0)
    down_grad = scatter_hidden(down_grad.reshape(seqs, block_hidden, model))
    gateup_grad = gateup_grad.reshape(2, seqs, block_hidden, model).transpose(1, 0, 2, 3)
    gateup_grad = scatter_hidden(gateup_grad.reshape(seqs, 2 * block_hidden, model))

    g_t = dot(out_full, grad_hidden_all, 1, 1).astype(bf16)
    out_grad = scatter_heads(dot(o_t, grad_hidden_all, 1, 0).reshape(heads, HEAD_DIM, model))
    dq_t, dk_t, dv_t = attend_back(bounds, q_t, g_t, o_t, lse, k_h, v_h, k_t)
    grad_projected = jnp.concatenate(
        [rotate(dq_t * score_scale, cosine, -sine), rotate(dk_t, cosine, -sine), dv_t], axis=0
    ).astype(bf16)
    grad_normed_one = scatter_plane(dot(grad_projected, qkv_t, 0, 0))
    qkv_grad = dot(grad_projected, normed_one, 1, 0)
    qkv_grad = qkv_grad.reshape(3, heads, HEAD_DIM, model).transpose(1, 0, 2, 3)
    qkv_grad = scatter_heads(qkv_grad.reshape(heads, 3 * HEAD_DIM, model))

    grad_rows_one, gain_one = norm_backward(grad_normed_one, normal_one, inverse_one, gains[0])
    grad_input = (grad_hidden + grad_rows_one).astype(bf16)

    def everywhere(a):
        a = lax.all_gather(a, ("seq", "extra"), axis=0, tiled=True)
        return a.reshape(seqs, local_len, model)

    gains_grad = lax.psum_scatter(
        jnp.stack([gain_one, gain_two]), "context", scatter_dimension=1, tiled=True
    )
    gains_grad = lax.psum(gains_grad, ("seq", "extra"))
    qkv_grad = qkv_grad.reshape(block_heads, 3, HEAD_DIM, rows).transpose(1, 3, 0, 2)
    gateup_grad = gateup_grad.reshape(n_context, 2, block_hidden, rows).transpose(1, 3, 0, 2)
    return (
        everywhere(result),
        everywhere(grad_input).astype(f32),
        gains_grad,
        qkv_grad.reshape(qkv_weight.shape),
        out_grad.reshape(out_weight.shape),
        gateup_grad.reshape(gateup_weight.shape),
        down_grad.reshape(down_weight.shape),
    )


def solution(mesh):
    n_context, n_tensor = mesh.shape["context"], mesh.shape["tensor"]
    tensor = ("seq", "extra")

    def program(block_input, *others):
        seqs = block_input.shape[0]
        n_extra = n_tensor // seqs
        assert n_extra * seqs == n_tensor
        split = Mesh(
            mesh.devices.reshape(n_context, seqs, n_extra), ("context", "seq", "extra")
        )
        in_specs = (
            P(None, "context", None),
            P(),
            P(None, "context"),
            P(None, "context", tensor),
            P(tensor, "context"),
            P(None, "context", tensor),
            P(tensor, "context"),
            P(None, "context", None),
        )
        out_specs = (
            P(None, "context", None),
            P(None, "context", None),
            P(None, "context"),
            P(None, "context", tensor),
            P(tensor, "context"),
            P(None, "context", tensor),
            P(tensor, "context"),
        )
        return jax.shard_map(
            functools.partial(shards, (n_context, seqs, n_extra)),
            mesh=split,
            in_specs=in_specs,
            out_specs=out_specs,
            check_vma=False,
        )(block_input, *others)

    return program
```

time: 3090 us -> 2060 us (0.67)
  waiting for transfers between devices: 1900 us -> 1440 us
  matrix products: 629 us -> 213 us
  other arithmetic: 351 us -> 68.6 us
  Pallas kernels: 0 us -> 118 us
  blocking collectives: 19.5 us -> 98.2 us
  local copies, waits for them, and re-layouts: 158 us -> 91.3 us
    psum x6 -> x0, waiting for transfers between devices: 1110 us -> none  [the longest x2 487 us: micro_step(): lax.psum(feedforward_part.astype(jnp.bfloat16), 'tensor')]
    dot_general x36 -> x12, matrix products: 629 us -> 213 us  [dot(): lax.dot_general(a, b, (((ca,), (cb,)), ((), ())), preferred_element_type=...]
    all_gather x10, waiting for transfers between devices: 390 us -> 746 us  [the longest x4 305 us: gather_plane(): return lax.all_gather(a, plane, axis=0, tiled=True)]
    reduce_scatter x6 -> x8, waiting for transfers between devices: 397 us -> 662 us  [the longest x4 482 us: scatter_plane(): lax.psum_scatter(a.astype(bf16), plane, scatter_dimension=0, tiled=True)]
    convert_element_type x12 -> x6, other arithmetic: 168 us -> 34.7 us  [the longest x1 13.1 us: shards(): everywhere(grad_input).astype(f32)]
    pallas_call x0 -> x2, Pallas kernels: none -> 118 us  [the longest x1 59 us: attend_back(): pl.pallas_call(attend_back_kernel, out_shape=tuple((jax.ShapeDtypeStruct(...]
    reduce_sum x12 -> x5, other arithmetic: 96 us -> 13.4 us  [the longest x2 8.09 us: norm_backward(): jnp.sum(grad_normed * normal, axis=0)]
    all_to_all x0 -> x5, blocking collectives: none -> 78 us  [exchange(): return lax.all_to_all(a, 'context', split_axis=0, concat_axis=0, tiled=True)]
  transfers between devices with their start and end apart: 23 -> 22, of which waited for: 21 -> 19; matrix products, arithmetic and copies ran while one was open for 15% -> 10% of each run, Pallas kernels for 0% -> 0%
where the time goes in v1:
time: 2060 us; the launch traced here: 2050 us
  waiting for transfers between devices  1440 us (70%)
  matrix products  213 us (10%)
  Pallas kernels  118 us (6%)
  blocking collectives  98.2 us (5%)
  local copies, waits for them, and re-layouts  91.3 us (4%)
  other arithmetic  68.6 us (3%)
    reduce_scatter x4, waiting for transfers between devices, scatter_plane(): lax.psum_scatter(a.astype(bf16), plane, scatter_dimension=0, tiled=True)  482 us
    all_gather x4, waiting for transfers between devices, gather_plane(): return lax.all_gather(a, plane, axis=0, tiled=True)  305 us
    all_gather x2, waiting for transfers between devices, everywhere(): a = lax.all_gather(a, ('seq', 'extra'), axis=0, tiled=True)  275 us
    dot_general x12, matrix products, dot(): lax.dot_general(a, b, (((ca,), (cb,)), ((), ())), preferred_element_type=...  213 us
    all_gather x2, waiting for transfers between devices, gather_hidden(): a = lax.all_gather(exchange(a), 'seq', axis=0, tiled=False)  113 us
    reduce_scatter x2, waiting for transfers between devices, scatter_hidden(): lax.psum_scatter(a, 'seq', scatter_dimension=0, tiled=False)  112 us
    all_to_all x5, blocking collectives, exchange(): return lax.all_to_all(a, 'context', split_axis=0, concat_axis=0, tiled=True)  78 us
    reduce_scatter x2, waiting for transfers between devices, scatter_heads(): a = lax.psum_scatter(a, 'seq', scatter_dimension=0, tiled=False)  67.7 us
  transfers between devices with their start and end apart: 22, of which 19 were waited for; matrix products, arithmetic and copies ran while one was open for 10% of the time, Pallas kernels for 0%

profile of v1, /device:TPU:0, one launch (start us, length us, event | category | flops | bytes accessed | tf_op | source)
XLA Modules:
  0.0 2053.0 jit_solution(14267555890666887572)
XLA Ops:
  7.2 12.2 all_to_all.40
  21.0 15.7 all_to_all.41
  36.7 7.9 all_gather.45
  47.4 3.5 fusion.21
  52.6 3.0 fusion.32
  58.8 53.0 %all-gather.26.cloned.1.call-done = bf16[32,192,256]{2,1,0:T(8,128)(2,1)} async-done(((bf16[8,192,256]{2,1,0:T(8,128)(2,1)}), bf16[32,192,256]{2,1,0:T(8,128)(2,1)}) %all-gather.26.cloned.1.call-update) | async-done | bytes 3145744 | tf_op jit(solution)/shard_map/all_gather | solution.py:279
  111.7 3.7 copy.119
  115.4 3.4 reshape_reshape.12
  121.5 81.3 %all-gather.16.cloned.1.call-done = bf16[4096,2048]{1,0:T(8,128)(2,1)} async-done(((bf16[512,2048]{1,0:T(8,128)(2,1)}), bf16[4096,2048]{1,0:T(8,128)(2,1)}) %all-gather.16.cloned.1.call-update) | async-done | bytes 16777232 | tf_op jit(solution)/shard_map/all_gather | solution.py:267
  202.7 16.0 convolution_bitcast_fusion
  218.8 2.8 fusion.40
  224.0 3.4 copy.86
  227.4 2.8 subtract_convert_fusion.2
  231.8 58.5 %attend.1 = (bf16[256,4096]{1,0:T(8,128)(2,1)}, f32[4,4096]{1,0:T(4,128)}) custom-call(s32[16]{0:T(128)} %get-tuple-element.74.lo_ref, s32[16]{0:T(128)} %get-tuple-element.73.full_ref, s32[1,4096]{1,0:T(1,128)} %add_maximum_fusion.low_ref, bf16[256,4096]{1,0:T(8,128)(2,1)} %bitcast.223, bf16[4,4096,64]{2,1,0:T(8,128)(2,1)} %bitcast.202, ...), custom_call_target="tpu_custom_call" | custom-call | flops 34359738368 | bytes 8388608 | tf_op jit(solution)/shard_map/attend/pallas_call | solution.py:153
  290.4 10.2 convolution_convert_fusion.3
  301.6 12.8 all_to_all.42
  315.1 18.5 all_to_all.43
  333.7 159.7 %reduce-scatter.12.cloned.1.call-done = bf16[512,2048]{1,0:T(8,128)(2,1)} async-done(((bf16[4096,2048]{1,0:T(8,128)(2,1)}), bf16[512,2048]{1,0:T(8,128)(2,1)}) %reduce-scatter.12.cloned.1.call-update) | async-done | bytes 2097168 | tf_op jit(solution)/shard_map/reduce_scatter | solution.py:270
  493.4 3.1 multiply_reduce_fusion
  496.6 4.1 multiply_convert_fusion.3
  500.7 3.3 constant_dynamic-slice_fusion
  504.1 36.7 %all-gather.32.cloned.1.call-done = bf16[32,128,256]{2,1,0:T(8,128)(2,1)} async-done(((bf16[8,128,256]{2,1,0:T(8,128)(2,1)}), bf16[32,128,256]{2,1,0:T(8,128)(2,1)}) %all-gather.32.cloned.1.call-update) | async-done | bytes 2097168 | tf_op jit(solution)/shard_map/all_gather | solution.py:299
  540.8 2.8 copy.92
  545.6 76.1 %all-gather.30.cloned.1.call-done = bf16[32,256,256]{2,1,0:T(8,128)(2,1)} async-done(((bf16[8,256,256]{2,1,0:T(8,128)(2,1)}), bf16[32,256,256]{2,1,0:T(8,128)(2,1)}) %all-gather.30.cloned.1.call-update) | async-done | bytes 4194320 | tf_op jit(solution)/shard_map/all_gather | solution.py:299
  621.7 6.6 copy.118
  628.3 8.0 reshape_reshape.14
  636.3 4.8 copy.91
  641.1 70.9 %all-gather.18.cloned.1.call-done = bf16[4096,2048]{1,0:T(8,128)(2,1)} async-done(((bf16[512,2048]{1,0:T(8,128)(2,1)}), bf16[4096,2048]{1,0:T(8,128)(2,1)}) %all-gather.18.cloned.1.call-update) | async-done | bytes 16777232 | tf_op jit(solution)/shard_map/all_gather | solution.py:267
  712.0 23.6 %fusion.42 = f32[4096,1024]{0,1:T(8,128)} fusion(bf16[4096,2048]{1,0:T(8,128)(2,1)} %all-gather.18.cloned.1.call-done, bf16[1024,2048]{1,0:T(8,128)(2,1)} %bitcast.207), kind=kOutput, calls=%fused_computation.112 | convolution fusion | flops 17179869184 | bytes 37748736 | tf_op jit(solution)/shard_map/dot_general | solution.py:26
  735.6 68.2 %all-gather.34.cloned.1.call-done = bf16[1,4096,2048]{2,1,0:T(8,128)(2,1)} async-done(((bf16[1,512,2048]{2,1,0:T(8,128)(2,1)}), bf16[1,4096,2048]{2,1,0:T(8,128)(2,1)}) %all-gather.34.cloned.1.call-update) | async-done | bytes 16777232 | tf_op jit(solution)/shard_map/all_gather | solution.py:267
  803.8 22.0 %multiply_convert_fusion.1 = (bf16[4096,512]{0,1:T(8,128)(2,1)}, bf16[4096,512]{0,1:T(8,128)(2,1)}, bf16[4096,512]{0,1:T(8,128)(2,1)}) fusion(f32[4096,1024]{0,1:T(8,128)} %fusion.42, bf16[512,2048]{1,0:T(8,128)(2,1)} %bitcast.225, bf16[1,4096,2048]{2,1,0:T(8,128)(2,1)} %all-gather.34.cloned.1.call-done), kind=kOutput, calls=%fused_computation.10 | convolution fusion | flops 8621391872 | bytes 48234496 | tf_op jit(solution)/shard_map/dot_general | solution.py:26
  825.8 25.0 %convolution_convert_fusion.1 = bf16[4096,2048]{1,0:T(8,128)(2,1)} fusion(bf16[1024,2048]{1,0:T(8,128)(2,1)} %bitcast.208, bf16[4096,512]{0,1:T(8,128)(2,1)} %get-tuple-element.52, bf16[4096,512]{0,1:T(8,128)(2,1)} %get-tuple-element.51), kind=kOutput, calls=%fused_computation.5 | convolution fusion | flops 17205035008 | bytes 29360128 | tf_op jit(solution)/shard_map/dot_general | solution.py:26
  850.8 116.1 %reduce-scatter.16.cloned.1.call-done = bf16[512,2048]{1,0:T(8,128)(2,1)} async-done(((bf16[4096,2048]{1,0:T(8,128)(2,1)}), bf16[512,2048]{1,0:T(8,128)(2,1)}) %reduce-scatter.16.cloned.1.call-update) | async-done | bytes 2097168 | tf_op jit(solution)/shard_map/reduce_scatter | solution.py:270
  966.9 4.5 fusion.20
  972.0 5.7 fusion.39
  978.0 4.8 copy.94
  982.8 85.0 %all-gather.22.cloned.1.call-done = bf16[4096,2048]{1,0:T(8,128)(2,1)} async-done(((bf16[512,2048]{1,0:T(8,128)(2,1)}), bf16[4096,2048]{1,0:T(8,128)(2,1)}) %all-gather.22.cloned.1.call-update) | async-done | bytes 16777232 | tf_op jit(solution)/shard_map/all_gather | solution.py:267
  1067.8 18.1 fusion.13.g_ref
  1085.9 59.0 %attend_back.1 = (f32[256,4096]{1,0:T(8,128)}, f32[256,4096]{1,0:T(8,128)}, f32[256,4096]{1,0:T(8,128)}) custom-call(s32[16]{0:T(128)} %get-tuple-element.74.lo_ref, s32[16]{0:T(128)} %get-tuple-element.73.full_ref, s32[1,4096]{1,0:T(1,128)} %add_maximum_fusion.low_ref, bf16[256,4096]{1,0:T(8,128)(2,1)} %bitcast.224, bf16[256,4096]{1,0:T(8,128)(2,1)} %fusion.13.g_ref, ...), custom_call_target="tpu_custom_call" | custom-call | flops 85899345920 | bytes 25165824 | tf_op jit(solution)/shard_map/attend_back/pallas_call | solution.py:180
  1155.3 20.3 convolution_convert_fusion
  1177.2 14.7 convolution_convert_fusion.2
  1191.9 13.8 fusion.27
  1208.3 22.7 %fusion.25 = bf16[1024,2048]{1,0:T(8,128)(2,1)S(1)} fusion(bf16[4096,2048]{1,0:T(8,128)(2,1)} %all-gather.18.cloned.1.call-done, bf16[4096,512]{0,1:T(8,128)(2,1)} %get-tuple-element.52, bf16[4096,512]{0,1:T(8,128)(2,1)} %get-tuple-element.51), kind=kOutput, calls=%fused_computation.50 | convolution fusion | flops 17198743552 | bytes 29360128 | tf_op jit(solution)/shard_map/dot_general | solution.py:26
  1236.7 8.3 convolution_convert_fusion.6
  1246.7 18.8 convolution_convert_fusion.5
  1268.8 91.9 %reduce-scatter.18.cloned.1.call-done = bf16[512,2048]{1,0:T(8,128)(2,1)} async-done(((bf16[4096,2048]{1,0:T(8,128)(2,1)}), bf16[512,2048]{1,0:T(8,128)(2,1)}) %reduce-scatter.18.cloned.1.call-update) | async-done | bytes 2097168 | tf_op jit(solution)/shard_map/reduce_scatter | solution.py:270
  1360.7 3.6 fusion.23
  1365.7 114.4 %reduce-scatter.14.cloned.1.call-done = bf16[512,2048]{1,0:T(8,128)(2,1)} async-done(((bf16[4096,2048]{1,0:T(8,128)(2,1)}), bf16[512,2048]{1,0:T(8,128)(2,1)}) %reduce-scatter.14.cloned.1.call-update) | async-done | bytes 2097168 | tf_op jit(solution)/shard_map/reduce_scatter | solution.py:270
  1480.1 8.2 fusion.16
  1489.1 37.2 %reduce-scatter.26.cloned.1.call-done = bf16[1,8,128,256]{3,2,1,0:T(8,128)(2,1)} async-done(((bf16[4,8,128,256]{3,2,1,0:T(8,128)(2,1)}), bf16[1,8,128,256]{3,2,1,0:T(8,128)(2,1)}) %reduce-scatter.26.cloned.1.call-update) | async-done | bytes 524304 | tf_op jit(solution)/shard_map/reduce_scatter | solution.py:305
  1526.3 3.7 all-to-all-start.7
  1529.9 75.3 %reduce-scatter.24.cloned.1.call-done = bf16[1,8,256,256]{3,1,2,0:T(8,128)(2,1)} async-done(((bf16[4,8,256,256]{3,1,2,0:T(8,128)(2,1)}), bf16[1,8,256,256]{3,1,2,0:T(8,128)(2,1)}) %reduce-scatter.24.cloned.1.call-update) | async-done | bytes 1048592 | tf_op jit(solution)/shard_map/reduce_scatter | solution.py:305
  1606.7 18.8 all_to_all.44
  1625.5 10.1 reduce-scatter.22.cloned.1.call-done
  1635.6 3.7 all-to-all-start.5
  1639.3 57.5 %reduce-scatter.20.cloned.1.call-done = bf16[1,8,192,256]{3,1,2,0:T(8,128)(2,1)} async-done(((bf16[4,8,192,256]{3,1,2,0:T(8,128)(2,1)}), bf16[1,8,192,256]{3,1,2,0:T(8,128)(2,1)}) %reduce-scatter.20.cloned.1.call-update) | async-done | bytes 786448 | tf_op jit(solution)/shard_map/reduce_scatter | solution.py:292
  1699.0 3.9 all-to-all-start.4
  1707.1 8.4 all-to-all-done.4
  1717.5 18.8 reduce-scatter.28.cloned.1.call-done
  1737.2 12.3 psum.7
  1749.5 138.5 %all-gather.24.cloned.1.call-done = bf16[2048,2048]{1,0:T(8,128)(2,1)} async-done(((bf16[512,2048]{1,0:T(8,128)(2,1)}), bf16[2048,2048]{1,0:T(8,128)(2,1)}) %all-gather.24.cloned.1.call-update) | async-done | bytes 8388624 | tf_op jit(solution)/shard_map/all_gather | solution.py:383
  1888.0 13.1 convert.56
  1901.1 136.5 %all-gather.20.cloned.1.call-done = bf16[2048,2048]{1,0:T(8,128)(2,1)} async-done(((bf16[512,2048]{1,0:T(8,128)(2,1)}), bf16[2048,2048]{1,0:T(8,128)(2,1)}) %all-gather.20.cloned.1.call-update) | async-done | bytes 8388624 | tf_op jit(solution)/shard_map/all_gather | solution.py:383
  2037.5 8.5 copy.123
  (163 shorter events, 58.5 us)
Async XLA Ops:
  7.2 43.8 %copy-start = (s32[4,8]{1,0:T(4,128)S(1)}, s32[4,8]{1,0:T(4,128)}, u32[]{:S(2)}) copy-start(s32[4,8]{1,0:T(4,128)} %param.9) | copy-start | bytes 388
  7.2 29.6 %copy-start.33 = (bf16[2,256]{1,0:T(2,128)(2,1)S(1)}, bf16[2,256]{1,0:T(2,128)(2,1)}, u32[]{:S(2)}) copy-start(bf16[2,256]{1,0:T(2,128)(2,1)} %param.10) | copy-start | bytes 3076
  7.2 48.4 %all-gather.28.cloned.1.call-start = ((), (), s32[]{:S(2)}) async-start(), calls=%async_computation.31 | async-start | bytes 1310720 | tf_op jit(solution)/shard_map/all_gather | solution.py:279
  19.5 92.3 %all-gather.26.cloned.1.call-start = ((), (), s32[]{:S(2)}) async-start(), calls=%async_computation.30 | async-start | bytes 3932160 | tf_op jit(solution)/shard_map/all_gather | solution.py:279
  36.7 166.1 %all-gather.16.cloned.1.call-start = ((), (), s32[]{:S(2)}) async-start(), calls=%async_computation.17 | async-start | bytes 18874368 | tf_op jit(solution)/shard_map/all_gather | solution.py:267
  46.8 0.6 copy-start.29
  46.8 0.6 copy-start.24
  46.8 924.6 %copy-start.22 = (f32[1,2048]{1,0:T(1,128)}, f32[1,2048]{1,0:T(1,128)S(1)}, u32[]{:S(2)}) copy-start(f32[1,2048]{1,0:T(1,128)S(1)} %get-tuple-element.68) | copy-start | bytes 24580
  50.9 442.5 %reduce-scatter.12.cloned.1.call-start = ((), (), s32[]{:S(2)}) async-start(), calls=%async_computation.18 | async-start | bytes 18874368 | tf_op jit(solution)/shard_map/reduce_scatter | solution.py:270
  121.5 97.3 %copy-start.12 = (bf16[3,4,64,2048]{3,2,1,0:T(8,128)(2,1)}, bf16[3,4,64,2048]{3,2,1,0:T(8,128)(2,1)S(1)}, u32[]{:S(2)}) copy-start(bf16[3,4,64,2048]{3,2,1,0:T(8,128)(2,1)S(1)} %copy.85) | copy-start | bytes 9437188
  221.5 1.6 copy-start.5
  221.5 1.6 copy-start.8
  224.0 6.2 copy-start.7
  231.8 58.5 %copy-start.9 = (bf16[32,8,8,256]{3,1,2,0:T(8,128)(2,1)S(1)}, bf16[32,8,8,256]{3,1,2,0:T(8,128)(2,1)}, u32[]{:S(2)}) copy-start(bf16[32,8,8,256]{3,1,2,0:T(8,128)(2,1)} %copy.108) | copy-start | bytes 3145732
  300.5 1.0 copy-start.21
  300.5 13.9 copy-start.20
  300.6 240.2 %all-gather.32.cloned.1.call-start = ((), (), s32[]{:S(2)}) async-start(), calls=%async_computation.33 | async-start | bytes 2621440 | tf_op jit(solution)/shard_map/all_gather | solution.py:299
  314.4 307.3 %all-gather.30.cloned.1.call-start = ((), (), s32[]{:S(2)}) async-start(), calls=%async_computation.32 | async-start | bytes 5242880 | tf_op jit(solution)/shard_map/all_gather | solution.py:299
  333.6 378.4 %all-gather.18.cloned.1.call-start = ((), (), s32[]{:S(2)}) async-start(), calls=%async_computation.19 | async-start | bytes 18874368 | tf_op jit(solution)/shard_map/all_gather | solution.py:267
  493.4 3.1 copy-start.2
  496.5 474.9 %copy-start.26 = (f32[512]{0:T(512)}, f32[512]{0:T(512)S(1)}, u32[]{:S(2)}) copy-start(f32[512]{0:T(512)S(1)} %add_rsqrt_fusion) | copy-start | bytes 6148
  500.7 303.1 %all-gather.34.cloned.1.call-start = ((), (), s32[]{:S(2)}) async-start(), calls=%async_computation.34 | async-start | bytes 18874368 | tf_op jit(solution)/shard_map/all_gather | solution.py:267
  504.0 462.9 %reduce-scatter.16.cloned.1.call-start = ((), (), s32[]{:S(2)}) async-start(), calls=%async_computation.22 | async-start | bytes 18874368 | tf_op jit(solution)/shard_map/reduce_scatter | solution.py:270
  850.8 217.0 %all-gather.22.cloned.1.call-start = ((), (), s32[]{:S(2)}) async-start(), calls=%async_computation.23 | async-start | bytes 18874368 | tf_op jit(solution)/shard_map/all_gather | solution.py:267
  966.9 5.1 copy-start.4
  971.5 0.6 copy-start.31
  977.8 382.9 %reduce-scatter.18.cloned.1.call-start = ((), (), s32[]{:S(2)}) async-start(), calls=%async_computation.24 | async-start | bytes 18874368 | tf_op jit(solution)/shard_map/reduce_scatter | solution.py:270
  1144.9 3.4 copy-start.10
  1147.5 2.4 copy-start.6
  1147.5 3.1 copy-start.11
  1147.5 3.3 copy-start.17
  1152.2 3.1 copy-start.13
  1175.6 1.6 copy-start.16
  1175.6 304.5 %reduce-scatter.14.cloned.1.call-start = ((), (), s32[]{:S(2)}) async-start(), calls=%async_computation.20 | async-start | bytes 18874368 | tf_op jit(solution)/shard_map/reduce_scatter | solution.py:270
  1191.9 334.4 %reduce-scatter.26.cloned.1.call-start = ((), (), s32[]{:S(2)}) async-start(), calls=%async_computation.29 | async-start | bytes 2621440 | tf_op jit(solution)/shard_map/reduce_scatter | solution.py:305
  1208.2 397.0 %reduce-scatter.24.cloned.1.call-start = ((), (), s32[]{:S(2)}) async-start(), calls=%async_computation.28 | async-start | bytes 5242880 | tf_op jit(solution)/shard_map/reduce_scatter | solution.py:305
  1235.1 1.6 copy-start.14
  1235.1 400.5 %reduce-scatter.22.cloned.1.call-start = ((), (), s32[]{:S(2)}) async-start(), calls=%async_computation.27 | async-start | bytes 1310720 | tf_op jit(solution)/shard_map/reduce_scatter | solution.py:292
  1245.0 1.7 copy-start.15
  1246.5 450.3 %reduce-scatter.20.cloned.1.call-start = ((), (), s32[]{:S(2)}) async-start(), calls=%async_computation.26 | async-start | bytes 3932160 | tf_op jit(solution)/shard_map/reduce_scatter | solution.py:292
  1265.9 94.7 %copy-start.25 = (f32[1,2048]{1,0:T(1,128)S(1)}, f32[1,2048]{1,0:T(1,128)}, u32[]{:S(2)}) copy-start(f32[1,2048]{1,0:T(1,128)} %copy-done.24) | copy-start | bytes 24580
  1265.9 94.7 %copy-start.30 = (f32[512]{0:T(512)S(1)}, f32[512]{0:T(512)}, u32[]{:S(2)}) copy-start(f32[512]{0:T(512)} %copy-done.29) | copy-start | bytes 6148
  1268.7 95.5 %copy-start.28 = (f32[2048]{0:T(1024)S(1)}, f32[2048]{0:T(1024)}, u32[]{:S(2)}) copy-start(f32[2048]{0:T(1024)} %get-tuple-element.45) | copy-start | bytes 24580
  1268.7 211.4 %copy-start.3 = (bf16[512,2048]{1,0:T(8,128)(2,1)S(1)}, bf16[512,2048]{1,0:T(8,128)(2,1)}, u32[]{:S(2)}) copy-start(bf16[512,2048]{1,0:T(8,128)(2,1)} %reduce-scatter.12.cloned.1.call-done) | copy-start | bytes 6291460
  1268.7 211.4 %copy-start.23 = (f32[1,2048]{1,0:T(1,128)S(1)}, f32[1,2048]{1,0:T(1,128)}, u32[]{:S(2)}) copy-start(f32[1,2048]{1,0:T(1,128)} %copy-done.22) | copy-start | bytes 24580
  1268.7 211.4 %copy-start.27 = (f32[512]{0:T(512)S(1)}, f32[512]{0:T(512)}, u32[]{:S(2)}) copy-start(f32[512]{0:T(512)} %copy-done.26) | copy-start | bytes 6148
  1268.7 211.4 %copy-start.32 = (f32[512]{0:T(512)S(1)}, f32[512]{0:T(512)}, u32[]{:S(2)}) copy-start(f32[512]{0:T(512)} %copy-done.31) | copy-start | bytes 6148
  1268.7 467.5 %reduce-scatter.28.cloned.1.call-start = ((), (), s32[]{:S(2)}) async-start(), calls=%async_computation.35 | async-start | bytes 1179648
  1365.6 522.4 %all-gather.24.cloned.1.call-start = ((), (), s32[]{:S(2)}) async-start(), calls=%async_computation.25 | async-start | bytes 10485760 | tf_op jit(solution)/shard_map/all_gather | solution.py:383
  1488.3 549.2 %all-gather.20.cloned.1.call-start = ((), (), s32[]{:S(2)}) async-start(), calls=%async_computation.21 | async-start | bytes 10485760 | tf_op jit(solution)/shard_map/all_gather | solution.py:383
  1526.3 80.4 %all-to-all-start.7 = ((bf16[8,128,256]{2,1,0:T(8,128)(2,1)}), bf16[8,128,256]{2,1,0:T(8,128)(2,1)S(1)}, u32[]{:S(2)}, u32[]{:S(2)}) async-start(bf16[8,128,256]{2,1,0:T(8,128)(2,1)} %bitcast.238), calls=%async_computation.15 | async-start | bytes 1048576 | tf_op jit(solution)/shard_map/all_to_all | solution.py:264
  1635.6 63.4 %all-to-all-start.5 = ((bf16[8,64,256]{2,1,0:T(8,128)(2,1)}), bf16[8,64,256]{2,1,0:T(8,128)(2,1)S(1)}, u32[]{:S(2)}, u32[]{:S(2)}) async-start(bf16[8,64,256]{2,1,0:T(8,128)(2,1)} %bitcast.240), calls=%async_computation.11 | async-start | bytes 524288 | tf_op jit(solution)/shard_map/all_to_all | solution.py:264
  1699.0 5.0 copy-start.18
  1699.0 16.5 all-to-all-start.4
  1704.2 2.0 copy-start.19
  2037.5 8.5 copy-start.1
Sparse Core Ops, SparseCore 0:
  19.6 27.4 all-gather.27
  48.7 62.9 all-gather.25
  114.2 88.4 all-gather.15
  300.7 192.6 reduce-scatter.11
  494.8 45.8 all-gather.31
  542.2 79.4 all-gather.29
  623.6 88.3 all-gather.17
  713.9 89.8 all-gather.33
  850.9 115.9 reduce-scatter.15
  977.9 89.8 all-gather.21
  1175.7 184.9 reduce-scatter.17
  1364.1 115.9 reduce-scatter.13
  1482.4 43.8 reduce-scatter.25
  1529.1 76.0 reduce-scatter.23
  1607.9 27.6 reduce-scatter.21
  1637.9 58.8 reduce-scatter.19
  1700.2 36.0 reduce-scatter.27
  1738.3 149.6 all-gather.23
  1889.7 147.8 all-gather.19

commit v2 on v1

v2 whole, which is shorter than its diff:
```python
import functools
import math

import jax
import jax.numpy as jnp
from jax import lax
from jax.experimental import pallas as pl
from jax.experimental.pallas import tpu as pltpu
from jax.sharding import Mesh
from jax.sharding import PartitionSpec as P

HEAD_DIM = 64
WINDOW = 2048
BLOCK = 512
TAIL_CHUNKS = 2

epsilon = 1e-05
rope_base = 10000.0
masked_fill = -1e30

f32 = jnp.float32
bf16 = jnp.bfloat16
VMEM_BYTES = 56 * 1024 * 1024


def dot(a, b, ca, cb):
    return lax.dot_general(a, b, (((ca,), (cb,)), ((), ())), preferred_element_type=f32)


def visible_block(low_row, q0, k0, q_block, k_block):
    key = k0 + lax.broadcasted_iota(jnp.int32, (k_block, q_block), 0)
    query = q0 + lax.broadcasted_iota(jnp.int32, (k_block, q_block), 1)
    return (key >= low_row) & (key <= query)


def key_loops(lo_ref, full_ref, q_block, k_block, step, carry):
    qb = pl.program_id(0)
    lo = lo_ref[qb]
    diagonal = qb * q_block // k_block
    full = jnp.minimum(jnp.maximum(full_ref[qb], lo), diagonal)
    carry = lax.fori_loop(lo, full, functools.partial(step, True), carry)
    carry = lax.fori_loop(full, diagonal, functools.partial(step, False), carry)
    for extra in range(max(1, q_block // k_block)):
        carry = step(True, diagonal + extra, carry)
    return carry


def attend_kernel(k_block, lo_ref, full_ref, low_ref, q_ref, k_ref, v_ref, o_ref, lse_ref, acc_ref):
    heads = range(k_ref.shape[0])
    q_block = q_ref.shape[1]
    q0 = pl.program_id(0) * q_block
    rows = [pl.ds(h * HEAD_DIM, HEAD_DIM) for h in heads]
    acc_ref[...] = jnp.zeros_like(acc_ref)

    def step(masked, kb, carry):
        k0 = pl.multiple_of(kb * k_block, k_block)
        cols = pl.ds(k0, k_block)
        scores = [dot(k_ref[h, cols, :], q_ref[rows[h], :], 1, 0) for h in heads]
        if masked:
            visible = visible_block(low_ref[...], q0, k0, q_block, k_block)
            scores = [jnp.where(visible, v, masked_fill) for v in scores]
        top = [jnp.maximum(carry[h][0], jnp.max(scores[h], axis=0, keepdims=True)) for h in heads]
        weights = [jnp.exp(scores[h] - top[h]) for h in heads]
        added = [dot(v_ref[rows[h], cols], weights[h].astype(bf16), 1, 0) for h in heads]
        out = []
        for h in heads:
            fade = jnp.exp(carry[h][0] - top[h])
            total = carry[h][1] * fade + jnp.sum(weights[h], axis=0, keepdims=True)
            acc_ref[rows[h], :] = acc_ref[rows[h], :] * fade + added[h]
            out.append((top[h], total))
        return tuple(out)

    start = tuple(
        (jnp.full((1, q_block), masked_fill, f32), jnp.zeros((1, q_block), f32)) for _ in heads
    )
    final = key_loops(lo_ref, full_ref, q_block, k_block, step, start)
    for h in heads:
        top, total = final[h]
        o_ref[rows[h], :] = (acc_ref[rows[h], :] / total).astype(bf16)
        lse_ref[h : h + 1, :] = top + jnp.log(total)


def attend_back_kernel(
    k_block,
    lo_ref,
    full_ref,
    low_ref,
    q_ref,
    g_ref,
    o_ref,
    lse_ref,
    k_ref,
    v_ref,
    kt_ref,
    dq_ref,
    dk_ref,
    dv_ref,
):
    heads = range(k_ref.shape[0])
    q_block = q_ref.shape[1]
    q0 = pl.program_id(0) * q_block
    rows = [pl.ds(h * HEAD_DIM, HEAD_DIM) for h in heads]

    @pl.when(pl.program_id(0) == 0)
    def _():
        dk_ref[...] = jnp.zeros_like(dk_ref)
        dv_ref[...] = jnp.zeros_like(dv_ref)

    dq_ref[...] = jnp.zeros_like(dq_ref)
    inner = [
        jnp.sum(g_ref[r, :].astype(f32) * o_ref[r, :].astype(f32), axis=0, keepdims=True)
        for r in rows
    ]

    def step(masked, kb, carry):
        k0 = pl.multiple_of(kb * k_block, k_block)
        cols = pl.ds(k0, k_block)
        if masked:
            visible = visible_block(low_ref[...], q0, k0, q_block, k_block)
        for h in heads:
            r = rows[h]
            scores = dot(k_ref[h, cols, :], q_ref[r, :], 1, 0)
            grad_probs = dot(v_ref[h, cols, :], g_ref[r, :], 1, 0)
            if masked:
                scores = jnp.where(visible, scores, masked_fill)
            probs = jnp.exp(scores - lse_ref[h : h + 1, :])
            grad_scores = (probs * (grad_probs - inner[h])).astype(bf16)
            dv = dot(g_ref[r, :], probs.astype(bf16), 1, 1)
            dk = dot(q_ref[r, :], grad_scores, 1, 1)
            dq = dot(kt_ref[r, cols], grad_scores, 1, 0)
            dv_ref[r, cols] += dv
            dk_ref[r, cols] += dk
            dq_ref[r, :] += dq
        return carry

    key_loops(lo_ref, full_ref, q_block, k_block, step, 0)


def attention_specs(heads, length, q_block):
    width = heads * HEAD_DIM
    once = pl.Buffered(1)
    whole_t = pl.BlockSpec((width, length), lambda i, *_: (0, 0), pipeline_mode=once)
    whole_h = pl.BlockSpec((heads, length, HEAD_DIM), lambda i, *_: (0, 0, 0), pipeline_mode=once)
    tile = pl.BlockSpec((width, q_block), lambda i, *_: (0, i))
    low = pl.BlockSpec((1, q_block), lambda i, *_: (0, i))
    stat = pl.BlockSpec((heads, q_block), lambda i, *_: (0, i))
    return whole_t, whole_h, tile, low, stat


def attend(bounds, q_t, k_h, v_t):
    heads, length, _ = k_h.shape
    width = heads * HEAD_DIM
    block = math.gcd(BLOCK, length)
    whole_t, whole_h, tile, low, stat = attention_specs(heads, length, block)
    pairs = length * WINDOW * heads
    return pl.pallas_call(
        functools.partial(attend_kernel, block),
        out_shape=(
            jax.ShapeDtypeStruct((width, length), bf16),
            jax.ShapeDtypeStruct((heads, length), f32),
        ),
        grid_spec=pltpu.PrefetchScalarGridSpec(
            num_scalar_prefetch=2,
            grid=(length // block,),
            in_specs=[low, tile, whole_h, whole_t],
            out_specs=[tile, stat],
            scratch_shapes=[pltpu.VMEM((width, block), f32)],
        ),
        compiler_params=pltpu.CompilerParams(vmem_limit_bytes=VMEM_BYTES),
        cost_estimate=pl.CostEstimate(
            flops=pairs * 6 * 256, transcendentals=pairs, bytes_accessed=length * width * 8
        ),
        name="attend",
    )(*bounds, q_t, k_h, v_t)


def attend_back(bounds, q_t, g_t, o_t, lse, k_h, v_h, k_t):
    heads, length, _ = k_h.shape
    width = heads * HEAD_DIM
    block = math.gcd(BLOCK, length)
    whole_t, whole_h, tile, low, stat = attention_specs(heads, length, block)
    pairs = length * WINDOW * heads
    return pl.pallas_call(
        functools.partial(attend_back_kernel, block),
        out_shape=tuple(jax.ShapeDtypeStruct((width, length), f32) for _ in range(3)),
        grid_spec=pltpu.PrefetchScalarGridSpec(
            num_scalar_prefetch=2,
            grid=(length // block,),
            in_specs=[low, tile, tile, tile, stat, whole_h, whole_h, whole_t],
            out_specs=[tile, whole_t, whole_t],
        ),
        compiler_params=pltpu.CompilerParams(vmem_limit_bytes=VMEM_BYTES),
        cost_estimate=pl.CostEstimate(
            flops=pairs * 12 * 256, transcendentals=pairs, bytes_accessed=length * width * 24
        ),
        name="attend_back",
    )(*bounds, q_t, g_t, o_t, lse, k_h, v_h, k_t)


def attention_bounds(lengths, length):
    docs = lengths.shape[0]
    upto = jnp.arange(docs)[:, None] >= jnp.arange(docs)[None, :]
    ends = jnp.sum(jnp.where(upto, lengths[None, :], 0), axis=1)
    position = jnp.arange(length, dtype=jnp.int32)
    starts = jnp.max(jnp.where(ends[:, None] <= position[None, :], ends[:, None], 0), axis=0)
    low = jnp.maximum(starts, position - (WINDOW - 1)).astype(jnp.int32)
    block = math.gcd(BLOCK, length)
    by_block = low.reshape(length // block, block)
    first = by_block[:, 0] // block
    full = (by_block[:, -1] + block - 1) // block
    return first, full, low.reshape(1, length)


def rope_tables(length):
    half_dim = HEAD_DIM // 2
    counter = jnp.arange(half_dim, dtype=f32)
    frequency = jnp.exp(counter * (-2.0 * math.log(rope_base) / HEAD_DIM))
    angles = frequency[:, None] * jnp.arange(length, dtype=f32)[None, :]
    return jnp.cos(angles)[None], jnp.sin(angles)[None]


def rotate(values, cosine, sine):
    heads = values.shape[0] // HEAD_DIM
    v = values.reshape(heads, 2, HEAD_DIM // 2, values.shape[1])
    a, b = v[:, 0], v[:, 1]
    out = jnp.stack([a * cosine - b * sine, b * cosine + a * sine], axis=1)
    return out.reshape(values.shape)


def norm_inverse(rows):
    return lax.rsqrt(jnp.mean(rows * rows, axis=-1, keepdims=True) + epsilon)


def norm_backward(grad_normed, normal, inverse, gain):
    grad_normal = grad_normed * gain
    inner = jnp.mean(grad_normal * normal, axis=-1, keepdims=True)
    return inverse * (grad_normal - normal * inner), jnp.sum(grad_normed * normal, axis=0)


def swap(a, axis):
    return lax.ppermute(a, axis, [(0, 1), (1, 0)])


def halve(a, axis, dim):
    index = lax.axis_index(axis)
    mine = lax.dynamic_index_in_dim(a, index, dim, False)
    other = lax.dynamic_index_in_dim(a, 1 - index, dim, False)
    return mine.astype(f32) + swap(other, axis).astype(f32)


def after(a, *others):
    return lax.optimization_barrier((a, *others))[0]


def shards(
    parts,
    block_input,
    doc_lengths,
    norm_gains,
    qkv_weight,
    out_weight,
    gateup_weight,
    down_weight,
    cotangent,
):
    n_chips, n_pair, n_core, seqs, n_extra = parts
    n_context = n_chips * n_pair * n_core
    context = ("chips", "pair", "core")
    plane = (*context, "extra")
    everyone = (*plane, "seq")
    cube = n_chips == n_pair == n_core == 2 and n_extra == 1
    model = block_input.shape[2]
    local_len = block_input.shape[1]
    length = local_len * n_context
    own_len = local_len // n_extra
    rows = model // n_context
    block_heads = qkv_weight.shape[2] // HEAD_DIM
    heads = seqs * block_heads // n_context
    split_heads = block_heads % n_context == 0
    block_hidden = gateup_weight.shape[2] // n_context
    hidden_width = seqs * block_hidden
    width = heads * HEAD_DIM
    seq = lax.axis_index("seq")
    first_row = lax.axis_index("extra") * own_len

    def exchange(a):
        return lax.all_to_all(a, context, split_axis=0, concat_axis=0, tiled=True)

    def send(a, *pairs):
        return lax.ppermute(a, "seq", pairs)

    def up(a, first=0):
        return send(a, *((i, i + 1) for i in range(first, seqs - 1)))

    def down(a, last=None):
        return send(a, *((i, i - 1) for i in range(1, seqs if last is None else last)))

    def spread_near(a):
        return [up(a), down(a)]

    def spread_far(near):
        across = jnp.where(seq == 1, near[0], near[1])
        return [up(near[0], 1), down(near[1], seqs - 1), send(across, (1, 3), (2, 0))]

    def spread_blocks(a, near, far):
        return [
            a,
            jnp.where(seq == 0, far[2], near[0]),
            jnp.where(seq >= 2, far[0], far[1]),
            jnp.where(seq == seqs - 1, far[2], near[1]),
        ]

    def spread_line(a, near, far):
        line = jnp.stack([far[2], far[0], near[0], a, near[1], far[1], far[2]])
        return lax.dynamic_slice_in_dim(line, seqs - 1 - seq, seqs, 0)

    def collect_far(blocks):
        across = jnp.where(seq == 0, blocks[1], blocks[3])
        return [
            send(blocks[2], *((i, i + 1) for i in range(seqs - 2))),
            send(blocks[2], *((i, i - 1) for i in range(2, seqs))),
            send(across, (0, 2), (3, 1)),
        ]

    def collect_near(blocks, far):
        above = blocks[3].astype(f32) + far[0].astype(f32) + jnp.where(seq == 2, far[2], 0)
        below = blocks[1].astype(f32) + far[1].astype(f32) + jnp.where(seq == 1, far[2], 0)
        return [blocks[0], up(above.astype(bf16)), down(below.astype(bf16))]

    def total(blocks):
        return sum((b.astype(f32) for b in blocks[1:]), blocks[0].astype(f32))

    def gather_plane(a):
        return lax.all_gather(a, plane, axis=0, tiled=True)

    def scatter_plane(a):
        return lax.psum_scatter(a.astype(bf16), plane, scatter_dimension=0, tiled=True).astype(f32)

    def scatter_start(part):
        part = part.astype(bf16)
        if not cube:
            return [scatter_plane(part)]
        size = part.shape[0] // n_context
        a = halve(part.reshape(n_chips, n_pair, n_core, size, model), "core", 2).astype(bf16)
        one, two = a[:, :, : size // 2], a[:, :, size // 2 :]
        return [halve(one, "pair", 1).astype(bf16), halve(two, "chips", 0).astype(bf16)]

    def scatter_end(halves):
        if not cube:
            return halves[0]
        return jnp.concatenate([halve(halves[0], "chips", 0), halve(halves[1], "pair", 0)], axis=0)

    def scatter_rows(part):
        return scatter_end(scatter_start(part))

    def own(a):
        return lax.dynamic_slice(a, (seq, first_row, 0), (1, own_len, model))[0]

    def heads_out(a):
        if split_heads:
            return exchange(a.reshape(n_context, -1, rows))
        m = a.shape[1]
        a = lax.all_gather(a, "seq", axis=0, tiled=True)
        return exchange(a.reshape(n_context, heads * m, rows))

    def heads_spread(a):
        near = spread_near(a)
        return spread_blocks(a, near, spread_far(near))

    def heads_whole(blocks, m):
        a = jnp.stack(blocks).reshape(len(blocks), n_context, heads // len(blocks), m, rows)
        return a.transpose(0, 2, 3, 1, 4).reshape(heads, m, model)

    def heads_split(a):
        a = a.astype(bf16).reshape(seqs, heads // seqs, a.shape[1], n_context, rows)
        return list(a.transpose(0, 3, 1, 2, 4).reshape(seqs, n_context, -1, rows))

    def heads_back(a):
        m = a.shape[1]
        if split_heads:
            blocks = heads_split(a)
            blocks = collect_near(blocks, collect_far(blocks))
            return exchange(total(blocks).astype(bf16)).reshape(block_heads, m, rows).astype(f32)
        a = a.astype(bf16).reshape(heads, m, n_context, rows).transpose(2, 0, 1, 3)
        a = exchange(a.reshape(n_context, -1, rows)).reshape(seqs * block_heads, m, rows)
        return lax.psum_scatter(a, "seq", scatter_dimension=0, tiled=True).astype(f32)

    gains = lax.all_gather(norm_gains, context, axis=1, tiled=True).astype(f32)
    rows_in = own(block_input).astype(f32)
    incoming = own(cotangent)
    inverse_one = norm_inverse(rows_in)
    normal_one = rows_in * inverse_one
    normed_one = gather_plane((normal_one * gains[0]).astype(bf16))

    qkv_local = qkv_weight.reshape(3, rows, block_heads, HEAD_DIM).transpose(2, 0, 3, 1)
    qkv_block = heads_out(qkv_local.reshape(block_heads, 3 * HEAD_DIM, rows))
    qkv_block, out_local, gateup_local, down_local = lax.optimization_barrier(
        (qkv_block, out_weight, gateup_weight, down_weight)
    )
    qkv_blocks = heads_spread(qkv_block) if split_heads else [qkv_block]
    qkv_t = heads_whole(qkv_blocks, 3 * HEAD_DIM).reshape(heads, 3, HEAD_DIM, model)
    qkv_t = qkv_t.transpose(1, 0, 2, 3).reshape(3 * width, model)
    out_block = heads_out(out_local.reshape(block_heads, HEAD_DIM, rows))
    gateup_local = gateup_local.reshape(2, rows, n_context, block_hidden).transpose(2, 0, 3, 1)
    hidden_block = exchange(
        jnp.concatenate(
            [
                gateup_local.reshape(n_context, 2 * block_hidden, rows),
                down_local.reshape(n_context, block_hidden, rows),
            ],
            axis=1,
        )
    )
    cosine, sine = rope_tables(length)
    bounds = attention_bounds(lax.dynamic_slice_in_dim(doc_lengths, seq, 1, 0)[0], length)
    normed_one, incoming_now, qkv_t, out_block, hidden_block, cosine, sine, bounds = (
        lax.optimization_barrier(
            (normed_one, incoming, qkv_t, out_block, hidden_block, cosine, sine, bounds)
        )
    )

    incoming_all = gather_plane(incoming_now)
    hidden_near = spread_near(hidden_block)
    out_blocks = heads_spread(out_block) if split_heads else [out_block]
    score_scale = HEAD_DIM ** (-0.5)
    projected = dot(qkv_t, normed_one, 1, 1)
    q_t = rotate(projected[:width], cosine, sine).astype(bf16) * bf16(score_scale)
    k_t = rotate(projected[width : 2 * width], cosine, sine).astype(bf16)
    v_t = projected[2 * width :].astype(bf16)
    k_h = k_t.reshape(heads, HEAD_DIM, length).transpose(0, 2, 1)
    v_h = v_t.reshape(heads, HEAD_DIM, length).transpose(0, 2, 1)
    q_t, hidden_near, out_blocks = lax.optimization_barrier((q_t, hidden_near, out_blocks))
    hidden_far = spread_far(hidden_near)
    o_t, lse = attend(bounds, q_t, k_h, v_t)
    o_t, incoming_all, hidden_far = lax.optimization_barrier((o_t, incoming_all, hidden_far))

    out_full = heads_whole(out_blocks, HEAD_DIM).reshape(width, model)
    attention_branch = scatter_rows(dot(o_t, out_full, 0, 0))
    hidden = rows_in + attention_branch
    inverse_two = norm_inverse(hidden)
    normal_two = hidden * inverse_two
    normed_two = gather_plane((normal_two * gains[1]).astype(bf16))

    hidden_full = jnp.stack(spread_blocks(hidden_block, hidden_near, hidden_far))
    hidden_full = hidden_full.reshape(seqs, n_context, 3, block_hidden, rows)
    hidden_full = hidden_full.transpose(2, 0, 3, 1, 4).reshape(3 * hidden_width, model)
    gateup_t = hidden_full[: 2 * hidden_width]
    down_full = hidden_full[2 * hidden_width :]
    grad_activation = dot(incoming_all, down_full, 1, 1)
    normed_two, grad_activation = lax.optimization_barrier((normed_two, grad_activation))

    gate_up = dot(normed_two, gateup_t, 1, 1)
    gate, raised = gate_up[:, :hidden_width], gate_up[:, hidden_width:]
    gate_sigmoid = jax.nn.sigmoid(gate)
    gate_silu = gate * gate_sigmoid
    activation = (gate_silu * raised).astype(bf16)
    grad_gate = grad_activation * raised * gate_sigmoid * (1.0 + gate * (1.0 - gate_sigmoid))
    grad_up = grad_activation * gate_silu
    grad_gateup = jnp.concatenate([grad_gate, grad_up], axis=1).astype(bf16)
    feedforward_halves = scatter_start(dot(activation, down_full, 1, 0))
    second_halves = scatter_start(dot(grad_gateup, gateup_t, 1, 0))
    down_grad = dot(activation, incoming_all, 0, 0).astype(bf16)
    gateup_grad = dot(grad_gateup, normed_two, 0, 0).astype(bf16)
    hidden_grads = jnp.concatenate(
        [
            gateup_grad.reshape(2, seqs, block_hidden, n_context, rows),
            down_grad.reshape(1, seqs, block_hidden, n_context, rows),
        ],
        axis=0,
    )
    hidden_grads = list(hidden_grads.transpose(1, 3, 0, 2, 4).reshape(seqs, n_context, -1, rows))
    second_halves, hidden_grads = lax.optimization_barrier((second_halves, hidden_grads))
    hidden_grads_far = collect_far(hidden_grads)
    feedforward_branch = scatter_end(feedforward_halves)
    result = (hidden + feedforward_branch).astype(bf16)
    if n_extra > 1:
        result = lax.all_gather(result, "extra", axis=0, tiled=True)
    grad_normed_two = scatter_end(second_halves)
    grad_normed_two, result, hidden_grads_far = lax.optimization_barrier(
        (grad_normed_two, result, hidden_grads_far)
    )

    hidden_grads = collect_near(hidden_grads, hidden_grads_far)
    result_near = spread_near(result)
    grad_rows_two, gain_two = norm_backward(grad_normed_two, normal_two, inverse_two, gains[1])
    grad_hidden = incoming.astype(f32) + grad_rows_two
    grad_hidden_all = gather_plane(grad_hidden.astype(bf16))
    grad_hidden_all, hidden_grads, result_near = lax.optimization_barrier(
        (grad_hidden_all, hidden_grads, result_near)
    )

    result_far = spread_far(result_near)
    g_t = dot(out_full, grad_hidden_all, 1, 1).astype(bf16)
    dq_t, dk_t, dv_t = attend_back(bounds, q_t, g_t, o_t, lse, k_h, v_h, k_t)
    dq_t, dk_t, dv_t, result_far = lax.optimization_barrier((dq_t, dk_t, dv_t, result_far))
    grad_projected = jnp.concatenate(
        [rotate(dq_t * score_scale, cosine, -sine), rotate(dk_t, cosine, -sine), dv_t], axis=0
    ).astype(bf16)

    piece = own_len // TAIL_CHUNKS
    first_part = dot(grad_projected, qkv_t, 0, 0).astype(bf16)
    first_part = first_part.reshape(n_context * n_extra, own_len, model)
    input_pieces = []
    gain_one = jnp.zeros((model,), f32)
    for i in range(TAIL_CHUNKS):
        part = slice(i * piece, (i + 1) * piece)
        grad_normed_one = scatter_rows(first_part[:, part].reshape(-1, model))
        grad_rows_one, gain_part = norm_backward(
            grad_normed_one, normal_one[part], inverse_one[part], gains[0]
        )
        gain_one = gain_one + gain_part
        grad_input = (grad_hidden[part] + grad_rows_one).astype(bf16)
        gathered = lax.all_gather(grad_input, ("seq", "extra"), axis=0, tiled=False)
        input_pieces.append(gathered.reshape(seqs, n_extra, piece, model))

    out_grad = dot(o_t, grad_hidden_all, 1, 0).reshape(heads, HEAD_DIM, model)
    qkv_grad = dot(grad_projected, normed_one, 1, 0)
    qkv_grad = qkv_grad.reshape(3, heads, HEAD_DIM, model).transpose(1, 0, 2, 3)
    qkv_grad = qkv_grad.reshape(heads, 3 * HEAD_DIM, model)
    heads_grad = heads_back(jnp.concatenate([qkv_grad, out_grad], axis=1))
    qkv_grad = heads_grad[:, : 3 * HEAD_DIM].reshape(block_heads, 3, HEAD_DIM, rows)
    out_grad = heads_grad[:, 3 * HEAD_DIM :]
    hidden_grad = exchange(total(hidden_grads).astype(bf16)).astype(f32)
    hidden_grad = hidden_grad.reshape(n_context, 3, block_hidden, rows)

    results = spread_line(result, result_near, result_far)
    gains_grad = lax.psum(jnp.stack([gain_one, gain_two]), everyone)
    gains_grad = lax.dynamic_slice_in_dim(gains_grad, lax.axis_index(context) * rows, rows, 1)
    input_pieces[-1] = after(input_pieces[-1], gains_grad)
    input_grad = jnp.concatenate(input_pieces, axis=2).astype(f32)
    return (
        results,
        input_grad.reshape(seqs, local_len, model),
        gains_grad,
        qkv_grad.transpose(1, 3, 0, 2).reshape(qkv_weight.shape),
        out_grad.reshape(out_weight.shape),
        hidden_grad[:, :2].transpose(1, 3, 0, 2).reshape(gateup_weight.shape),
        hidden_grad[:, 2].reshape(down_weight.shape),
    )


def solution(mesh):
    n_context, n_tensor = mesh.shape["context"], mesh.shape["tensor"]
    n_core, n_pair = math.gcd(n_context, 2), math.gcd(n_context, 4) // math.gcd(n_context, 2)
    context, tensor = ("chips", "pair", "core"), ("seq", "extra")

    def program(block_input, *others):
        seqs = block_input.shape[0]
        n_extra = n_tensor // seqs
        assert n_extra * seqs == n_tensor and seqs == 4
        parts = (n_context // (n_pair * n_core), n_pair, n_core, seqs, n_extra)
        split = Mesh(mesh.devices.reshape(parts), (*context, *tensor))
        in_specs = (
            P(None, context, None),
            P(),
            P(None, context),
            P(None, context, tensor),
            P(tensor, context),
            P(None, context, tensor),
            P(tensor, context),
            P(None, context, None),
        )
        out_specs = (
            P(None, context, None),
            P(None, context, None),
            P(None, context),
            P(None, context, tensor),
            P(tensor, context),
            P(None, context, tensor),
            P(tensor, context),
        )
        return jax.shard_map(
            functools.partial(shards, parts),
            mesh=split,
            in_specs=in_specs,
            out_specs=out_specs,
            check_vma=False,
        )(block_input, *others)

    return program
```

time: 2060 us -> 1420 us (0.69)
  waiting for transfers between devices: 1440 us -> 636 us
  starting transfers between devices: 12.2 us -> 135 us
  other arithmetic: 68.6 us -> 137 us
  local copies, waits for them, and re-layouts: 91.3 us -> 147 us
  blocking collectives: 98.2 us -> 56.9 us
  Pallas kernels: 118 us -> 87.4 us
    reduce_scatter x8 -> x0, waiting for transfers between devices: 662 us -> none  [the longest x4 482 us: scatter_plane(): lax.psum_scatter(a.astype(bf16), plane, scatter_dimension=0, tiled=True)]
    ppermute x0 -> x55, waiting for transfers between devices: none -> 522 us  [the longest x30 275 us: send(): return lax.ppermute(a, 'seq', pairs)]
    all_gather x6 -> x2, waiting for transfers between devices: 441 us -> 0.01 us  [shards(): gathered = lax.all_gather(grad_input, ('seq', 'extra'), axis=0, tiled=False)]
    all_gather x4, waiting for transfers between devices: 305 us -> 80.1 us  [gather_plane(): return lax.all_gather(a, plane, axis=0, tiled=True)]
    ppermute x0 -> x55, starting transfers between devices: none -> 116 us  [the longest x30 93.7 us: send(): return lax.ppermute(a, 'seq', pairs)]
    all_to_all x5 -> x0, blocking collectives: 78 us -> none  [exchange(): return lax.all_to_all(a, 'context', split_axis=0, concat_axis=0, tiled=True)]
    convert_element_type x3 -> x22, other arithmetic: 24.7 us -> 66.5 us  [the longest x5 26.8 us: scatter_start(): halve(part.reshape(n_chips, n_pair, n_core, size, model), 'core', 2)]
    squeeze x0 -> x26, local copies, waits for them, and re-layouts: none -> 40.8 us  [the longest x25 37.6 us: halve(): other = lax.dynamic_index_in_dim(a, 1 - index, dim, False)]
  transfers between devices with their start and end apart: 22 -> 66, of which waited for: 19 -> 39; matrix products, arithmetic and copies ran while one was open for 10% -> 21% of each run, Pallas kernels for 0% -> 6%
where the time goes in v2:
time: 1420 us
  waiting for transfers between devices  636 us (45%)
  matrix products  201 us (14%)
  local copies, waits for them, and re-layouts  147 us (10%)
  other arithmetic  137 us (10%)
  starting transfers between devices  135 us (10%)
  Pallas kernels  87.4 us (6%)
  blocking collectives  56.9 us (4%)
  between operations  16.3 us (1%)
    ppermute x30, waiting for transfers between devices, send(): return lax.ppermute(a, 'seq', pairs)  275 us
    ppermute x25, waiting for transfers between devices, swap(): return lax.ppermute(a, axis, [(0, 1), (1, 0)])  247 us
    dot_general x12, matrix products, dot(): lax.dot_general(a, b, (((ca,), (cb,)), ((), ())), preferred_element_type=...  201 us
    ppermute x30, starting transfers between devices, send(): return lax.ppermute(a, 'seq', pairs)  93.7 us
    all_gather x4, waiting for transfers between devices, gather_plane(): return lax.all_gather(a, plane, axis=0, tiled=True)  80.1 us
    pallas_call x1, Pallas kernels, attend_back(): pl.pallas_call(functools.partial(attend_back_kernel, block), out_shape=tu...  54.4 us
    psum x1, blocking collectives, shards(): gains_grad = lax.psum(jnp.stack([gain_one, gain_two]), everyone)  46.4 us
    squeeze x25, local copies, waits for them, and re-layouts, halve(): other = lax.dynamic_index_in_dim(a, 1 - index, dim, False)  37.6 us
  transfers between devices with their start and end apart: 66, of which 39 were waited for; matrix products, arithmetic and copies ran while one was open for 21% of the time, Pallas kernels for 6%

profile of v2, /device:TPU:0, one launch (start us, length us, event | category | flops | bytes accessed | tf_op | source)
XLA Modules:
  0.0 1416.6 jit_solution(12692447054370658679)
XLA Ops:
  9.3 10.5 all_gather.27
  20.4 4.9 convert_multiply_fusion
  33.5 13.8 all-to-all-done
  58.8 5.0 collective-permute-done
  83.4 8.5 collective-permute-done.4
  93.1 9.8 collective-permute-done.2
  112.1 5.6 all-to-all-done.2
  117.7 21.1 %all-gather.9.cloned.1.call-done = bf16[4096,2048]{1,0:T(8,128)(2,1)} async-done(((bf16[512,2048]{1,0:T(8,128)(2,1)}), bf16[4096,2048]{1,0:T(8,128)(2,1)}) %all-gather.9.cloned.1.call-update) | async-done | bytes 16777232 | tf_op jit(solution)/shard_map/all_gather | solution.py:334
  143.6 5.7 collective-permute-start.5
  150.8 20.1 %fusion.48 = f32[768,4096]{1,0:T(8,128)} fusion(bf16[768,2048]{1,0:T(8,128)(2,1)S(1)} %bitcast.391, bf16[4096,2048]{1,0:T(8,128)(2,1)} %all-gather.9.cloned.1.call-done), kind=kOutput, calls=%fused_computation.213 | convolution fusion | flops 12884901888 | bytes 32505856 | tf_op jit(solution)/shard_map/dot_general | solution.py:27
  190.1 8.5 collective-permute-done.11
  206.0 33.0 %attend.1 = (bf16[256,4096]{1,0:T(8,128)(2,1)}, f32[4,4096]{1,0:T(4,128)}) custom-call(s32[8]{0:T(128)} %get-tuple-element.68.lo_ref, s32[8]{0:T(128)} %get-tuple-element.69.full_ref, s32[1,4096]{1,0:T(1,128)} %add_maximum_fusion.low_ref, bf16[256,4096]{1,0:T(8,128)(2,1)} %bitcast.395, bf16[4,4096,64]{2,1,0:T(8,128)(2,1)} %bitcast.378, ...), custom_call_target="tpu_custom_call" | custom-call | flops 51539607552 | bytes 8388608 | tf_op jit(solution)/shard_map/attend/pallas_call | solution.py:156
  240.0 33.7 %collective-permute-done.14 = bf16[8,384,256]{2,1,0:T(8,128)(2,1)S(1)} collective-permute-done((bf16[8,384,256]{2,1,0:T(8,128)(2,1)S(1)}, bf16[8,384,256]{2,1,0:T(8,128)(2,1)S(1)}, u32[]{:S(2)}, u32[]{:S(2)}) %collective-permute-start.14) | collective-permute-done | bytes 1572896 | tf_op jit(solution)/shard_map/ppermute | solution.py:290
  274.9 8.6 convolution_convert_fusion.3
  283.5 8.4 dynamic-slice_bitcast_fusion.2
  291.9 13.5 collective-permute-done.15
  305.4 7.5 fusion.2
  324.8 42.6 %collective-permute-done.16 = bf16[2,256,2048]{2,1,0:T(8,128)(2,1)S(1)} collective-permute-done((bf16[2,256,2048]{2,1,0:T(8,128)(2,1)}, bf16[2,256,2048]{2,1,0:T(8,128)(2,1)S(1)}, u32[]{:S(2)}, u32[]{:S(2)}) %collective-permute-start.16) | collective-permute-done | bytes 2097184 | tf_op jit(solution)/shard_map/ppermute | solution.py:241
  374.9 19.5 %collective-permute-done.17 = bf16[256,2048]{1,0:T(8,128)(2,1)S(1)} collective-permute-done((bf16[256,2048]{1,0:T(8,128)(2,1)S(1)}, bf16[256,2048]{1,0:T(8,128)(2,1)S(1)}, u32[]{:S(2)}, u32[]{:S(2)}) %collective-permute-start.17) | collective-permute-done | bytes 1048608 | tf_op jit(solution)/shard_map/ppermute | solution.py:241
  426.6 11.2 fusion.49
  437.8 54.0 %all-gather.13.cloned.1.call-done = bf16[4096,2048]{1,0:T(8,128)(2,1)} async-done(((bf16[512,2048]{1,0:T(8,128)(2,1)}), bf16[4096,2048]{1,0:T(8,128)(2,1)}) %all-gather.13.cloned.1.call-update) | async-done | bytes 16777232 | tf_op jit(solution)/shard_map/all_gather | solution.py:334
  491.9 22.7 %fusion.50 = f32[4096,1024]{1,0:T(8,128)S(1)} fusion(bf16[4096,2048]{1,0:T(8,128)(2,1)} %all-gather.13.cloned.1.call-done, bf16[1024,2048]{1,0:T(8,128)(2,1)} %bitcast.382), kind=kOutput, calls=%fused_computation.215 | convolution fusion | flops 17179869184 | bytes 37748736 | tf_op jit(solution)/shard_map/dot_general | solution.py:27
  514.6 7.9 multiply_convert_fusion.2
  522.5 23.6 %convolution_convert_fusion.2 = bf16[4096,2048]{1,0:T(8,128)(2,1)} fusion(bf16[1024,2048]{1,0:T(8,128)(2,1)} %bitcast.383, bf16[4096,512]{1,0:T(8,128)(2,1)} %get-tuple-element.171, bf16[4096,512]{1,0:T(8,128)(2,1)} %get-tuple-element.170), kind=kOutput, calls=%fused_computation.8 | convolution fusion | flops 17205035008 | bytes 29360128 | tf_op jit(solution)/shard_map/dot_general | solution.py:27
  546.2 8.6 dynamic-slice_bitcast_fusion.1
  555.0 11.8 convolution_convert_fusion.1
  566.8 8.4 dynamic-slice_bitcast_fusion
  575.5 22.8 %fusion.15 = bf16[1024,2048]{1,0:T(8,128)(2,1)S(1)} fusion(bf16[4096,2048]{1,0:T(8,128)(2,1)} %all-gather.13.cloned.1.call-done, bf16[4096,512]{1,0:T(8,128)(2,1)} %get-tuple-element.171, bf16[4096,512]{1,0:T(8,128)(2,1)} %get-tuple-element.170), kind=kOutput, calls=%fused_computation.58 | convolution fusion | flops 17198743552 | bytes 29360128 | tf_op jit(solution)/shard_map/dot_general | solution.py:27
  599.8 13.0 convolution_convert_fusion.6
  623.7 6.5 fusion.1
  636.8 5.4 fusion
  645.9 36.0 %collective-permute-done.22 = bf16[2,256,2048]{2,1,0:T(8,128)(2,1)} collective-permute-done((bf16[2,256,2048]{2,1,0:T(8,128)(2,1)}, bf16[2,256,2048]{2,1,0:T(8,128)(2,1)}, u32[]{:S(2)}, u32[]{:S(2)}) %collective-permute-start.22) | collective-permute-done | bytes 2097184 | tf_op jit(solution)/shard_map/ppermute | solution.py:241
  694.4 5.1 collective-permute-start.32
  699.7 28.4 %collective-permute-done.26 = bf16[2,256,2048]{2,1,0:T(8,128)(2,1)S(1)} collective-permute-done((bf16[2,256,2048]{2,1,0:T(8,128)(2,1)S(1)}, bf16[2,256,2048]{2,1,0:T(8,128)(2,1)S(1)}, u32[]{:S(2)}, u32[]{:S(2)}) %collective-permute-start.26) | collective-permute-done | bytes 2097184 | tf_op jit(solution)/shard_map/ppermute | solution.py:241
  732.7 19.6 %collective-permute-done.23 = bf16[256,2048]{1,0:T(8,128)(2,1)S(1)} collective-permute-done((bf16[256,2048]{1,0:T(8,128)(2,1)S(1)}, bf16[256,2048]{1,0:T(8,128)(2,1)S(1)}, u32[]{:S(2)}, u32[]{:S(2)}) %collective-permute-start.23) | collective-permute-done | bytes 1048608 | tf_op jit(solution)/shard_map/ppermute | solution.py:241
  756.5 19.0 %collective-permute-done.27 = bf16[256,2048]{1,0:T(8,128)(2,1)S(1)} collective-permute-done((bf16[256,2048]{1,0:T(8,128)(2,1)S(1)}, bf16[256,2048]{1,0:T(8,128)(2,1)S(1)}, u32[]{:S(2)}, u32[]{:S(2)}) %collective-permute-start.27) | collective-permute-done | bytes 1048608 | tf_op jit(solution)/shard_map/ppermute | solution.py:241
  781.6 5.5 fusion.37
  787.2 5.1 collective-permute-start.35
  793.6 6.2 add_convert_fusion.1
  811.4 56.1 %collective-permute-done.33 = bf16[8,384,256]{2,1,0:T(8,128)(2,1)S(1)} collective-permute-done((bf16[8,384,256]{2,1,0:T(8,128)(2,1)}, bf16[8,384,256]{2,1,0:T(8,128)(2,1)S(1)}, u32[]{:S(2)}, u32[]{:S(2)}) %collective-permute-start.33) | collective-permute-done | bytes 1572896 | tf_op jit(solution)/shard_map/ppermute | solution.py:290
  867.5 5.5 collective-permute-done.34
  873.0 4.9 all-gather.15.cloned.1.call-done
  885.9 18.1 %convolution_convert_fusion.4.g_ref = bf16[256,4096]{1,0:T(8,128)(2,1)} fusion(bf16[256,2048]{1,0:T(8,128)(2,1)S(1)} %bitcast.376, bf16[4096,2048]{1,0:T(8,128)(2,1)} %all-gather.15.cloned.1.call-done), kind=kOutput, calls=%fused_computation.31 | convolution fusion | flops 4296015872 | bytes 19922944 | tf_op jit(solution)/shard_map/dot_general | solution.py:27
  904.0 54.4 %attend_back.1 = (f32[256,4096]{1,0:T(8,128)}, f32[256,4096]{1,0:T(8,128)}, f32[256,4096]{1,0:T(8,128)}) custom-call(s32[8]{0:T(128)} %get-tuple-element.68.lo_ref, s32[8]{0:T(128)} %get-tuple-element.69.full_ref, s32[1,4096]{1,0:T(1,128)} %add_maximum_fusion.low_ref, bf16[256,4096]{1,0:T(8,128)(2,1)} %bitcast.396, ...), custom_call_target="tpu_custom_call" | custom-call | flops 103079215104 | bytes 25165824 | tf_op jit(solution)/shard_map/attend_back/pallas_call | solution.py:183
  958.4 22.9 %collective-permute-done.39 = bf16[512,2048]{1,0:T(8,128)(2,1)S(1)} collective-permute-done((bf16[512,2048]{1,0:T(8,128)(2,1)}, bf16[512,2048]{1,0:T(8,128)(2,1)S(1)}, u32[]{:S(2)}, u32[]{:S(2)}) %collective-permute-start.39) | collective-permute-done | bytes 2097184 | tf_op jit(solution)/shard_map/ppermute | solution.py:290
  994.2 19.9 %convolution_convert_fusion = bf16[4096,2048]{1,0:T(8,128)(2,1)} fusion(bf16[768,2048]{1,0:T(8,128)(2,1)S(1)} %bitcast.392, bf16[256,4096]{1,0:T(8,128)(2,1)} %convert.83, bf16[256,4096]{1,0:T(8,128)(2,1)} %bitcast.399, bf16[256,4096]{1,0:T(8,128)(2,1)} %bitcast.397), kind=kOutput, calls=%fused_computation.6 | convolution fusion | flops 12912164864 | bytes 26214400 | tf_op jit(solution)/shard_map/dot_general | solution.py:27
  1014.1 6.7 fusion.38
  1041.5 17.5 %collective-permute-done.46 = bf16[2,128,2048]{2,1,0:T(8,128)(2,1)S(1)} collective-permute-done((bf16[2,128,2048]{2,1,0:T(8,128)(2,1)S(1)}, bf16[2,128,2048]{2,1,0:T(8,128)(2,1)S(1)}, u32[]{:S(2)}, u32[]{:S(2)}) %collective-permute-start.46) | collective-permute-done | bytes 1048608 | tf_op jit(solution)/shard_map/ppermute | solution.py:241
  1062.0 19.4 %collective-permute-done.41 = bf16[2,128,2048]{2,1,0:T(8,128)(2,1)S(1)} collective-permute-done((bf16[2,128,2048]{2,1,0:T(8,128)(2,1)S(1)}, bf16[2,128,2048]{2,1,0:T(8,128)(2,1)S(1)}, u32[]{:S(2)}, u32[]{:S(2)}) %collective-permute-start.41) | collective-permute-done | bytes 1048608 | tf_op jit(solution)/shard_map/ppermute | solution.py:241
  1084.5 9.8 collective-permute-done.47
  1094.7 9.8 collective-permute-done.42
  1116.6 10.9 convolution_convert_fusion.7
  1127.8 9.5 all-to-all-done.4
  1140.9 18.6 %convolution_convert_fusion.5 = bf16[768,2048]{1,0:T(8,128)(2,1)S(1)} fusion(bf16[4096,2048]{1,0:T(8,128)(2,1)} %all-gather.9.cloned.1.call-done, bf16[256,4096]{1,0:T(8,128)(2,1)} %convert.83, bf16[256,4096]{1,0:T(8,128)(2,1)} %bitcast.400, bf16[256,4096]{1,0:T(8,128)(2,1)} %bitcast.398), kind=kOutput, calls=%fused_computation.59 | convolution fusion | flops 12905349120 | bytes 26214400 | tf_op jit(solution)/shard_map/dot_general | solution.py:27
  1161.5 23.1 %collective-permute-start.50 = (bf16[8,256,256]{2,0,1:T(8,128)(2,1)S(1)}, bf16[8,256,256]{2,0,1:T(8,128)(2,1)S(1)}, u32[]{:S(2)}, u32[]{:S(2)}) collective-permute-start(bf16[8,256,256]{2,0,1:T(8,128)(2,1)S(1)} %get-tuple-element.200), channel_id=1, source_target_pairs={{0,1},{1,2},{4,5},{5,6},{8,9},{9,10},{12,13},{13,14},{16,17},{17,1... | collective-permute-start | bytes 3145736 | tf_op jit(solution)/shard_map/ppermute | solution.py:290
  1194.5 32.5 %collective-permute-done.50 = bf16[8,256,256]{2,0,1:T(8,128)(2,1)S(1)} collective-permute-done((bf16[8,256,256]{2,0,1:T(8,128)(2,1)S(1)}, bf16[8,256,256]{2,0,1:T(8,128)(2,1)S(1)}, u32[]{:S(2)}, u32[]{:S(2)}) %collective-permute-start.50) | collective-permute-done | bytes 1048608 | tf_op jit(solution)/shard_map/ppermute | solution.py:290
  1226.9 29.4 %collective-permute-done.51 = bf16[8,256,256]{2,0,1:T(8,128)(2,1)S(1)} collective-permute-done((bf16[8,256,256]{2,0,1:T(8,128)(2,1)S(1)}, bf16[8,256,256]{2,0,1:T(8,128)(2,1)S(1)}, u32[]{:S(2)}, u32[]{:S(2)}) %collective-permute-start.51) | collective-permute-done | bytes 1048608 | tf_op jit(solution)/shard_map/ppermute | solution.py:290
  1257.2 6.4 collective-permute-start.52
  1268.7 39.4 %collective-permute-done.52 = bf16[8,256,256]{2,0,1:T(8,128)(2,1)S(1)} collective-permute-done((bf16[8,256,256]{2,0,1:T(8,128)(2,1)S(1)}, bf16[8,256,256]{2,0,1:T(8,128)(2,1)S(1)}, u32[]{:S(2)}, u32[]{:S(2)}) %collective-permute-start.52) | collective-permute-done | bytes 1048608 | tf_op jit(solution)/shard_map/ppermute | solution.py:290
  1308.0 19.1 %collective-permute-done.54 = bf16[8,256,256]{2,0,1:T(8,128)(2,1)S(1)} collective-permute-done((bf16[8,256,256]{2,0,1:T(8,128)(2,1)S(1)}, bf16[8,256,256]{2,0,1:T(8,128)(2,1)S(1)}, u32[]{:S(2)}, u32[]{:S(2)}) %collective-permute-start.54) | collective-permute-done | bytes 1048608 | tf_op jit(solution)/shard_map/ppermute | solution.py:290
  1333.8 8.4 constant_dynamic-slice_fusion.1
  1342.2 5.5 all-to-all-done.3
  1350.5 46.4 %psum.7 = f32[2,2048]{1,0:T(2,128)S(1)} all-reduce(f32[2,2048]{1,0:T(2,128)S(1)} %pad_maximum_fusion.14), channel_id=1, replica_groups=mesh['chips'=2,'pair'=2,'core'=2,'seq'=4,'extra'=1] {'chips','pair','cor..., use_global_device_ids=true, to_apply=%region_10.11 | all-reduce | flops 4096 | bytes 32768 | tf_op jit(solution)/shard_map/psum | solution.py:527
  1397.4 11.8 maximum_convert_fusion
  (389 shorter events, 293.2 us)
Async XLA Ops:
  7.2 131.7 %all-gather.9.cloned.1.call-start = ((), (), s32[]{:S(2)}) async-start(), calls=%async_computation.5 | async-start | bytes 18874368 | tf_op jit(solution)/shard_map/all_gather | solution.py:334
  26.6 20.8 %all-to-all-start = ((bf16[8,192,256]{2,1,0:T(8,128)(2,1)}), bf16[8,192,256]{2,1,0:T(8,128)(2,1)S(1)}, u32[]{:S(2)}, u32[]{:S(2)}) async-start(bf16[8,192,256]{2,1,0:T(8,128)(2,1)} %bitcast.6), calls=%async_computation | async-start | bytes 1572864 | tf_op jit(solution)/shard_map/all_to_all | solution.py:287
  47.4 16.5 %collective-permute-start = (bf16[8,192,256]{2,1,0:T(8,128)(2,1)S(1)}, bf16[8,192,256]{2,1,0:T(8,128)(2,1)}, u32[]{:S(2)}, u32[]{:S(2)}) collective-permute-start(bf16[8,192,256]{2,1,0:T(8,128)(2,1)S(1)} %all-to-all-done), channel_id=1, source_target_pairs={{0,1},{1,2},{2,3},{4,5},{5,6},{6,7},{8,9},{9,10},{10,11},{12,13},{... | collective-permute-start | bytes 2359304 | tf_op jit(solution)/shard_map/ppermute | solution.py:290
  51.8 17.5 %collective-permute-start.1 = (bf16[8,192,256]{2,1,0:T(8,128)(2,1)S(1)}, bf16[8,192,256]{2,1,0:T(8,128)(2,1)}, u32[]{:S(2)}, u32[]{:S(2)}) collective-permute-start(bf16[8,192,256]{2,1,0:T(8,128)(2,1)S(1)} %all-to-all-done), channel_id=1, source_target_pairs={{1,0},{2,1},{3,2},{5,4},{6,5},{7,6},{9,8},{10,9},{11,10},{13,12},{... | collective-permute-start | bytes 2359304 | tf_op jit(solution)/shard_map/ppermute | solution.py:290
  55.4 19.9 %all-to-all-start.1 = ((bf16[8,64,256]{2,1,0:T(8,128)(2,1)}), bf16[8,64,256]{2,1,0:T(8,128)(2,1)S(1)}, u32[]{:S(2)}, u32[]{:S(2)}) async-start(bf16[8,64,256]{2,1,0:T(8,128)(2,1)} %bitcast.412), calls=%async_computation.1 | async-start | bytes 524288 | tf_op jit(solution)/shard_map/all_to_all | solution.py:287
  63.8 19.6 %collective-permute-start.3 = (bf16[8,192,256]{2,1,0:T(8,128)(2,1)}, bf16[8,192,256]{2,1,0:T(8,128)(2,1)S(1)}, u32[]{:S(2)}, u32[]{:S(2)}) collective-permute-start(bf16[8,192,256]{2,1,0:T(8,128)(2,1)} %collective-permute-done), channel_id=1, source_target_pairs={{1,2},{2,3},{5,6},{6,7},{9,10},{10,11},{13,14},{14,15},{17,18},{18... | collective-permute-start | bytes 2359304 | tf_op jit(solution)/shard_map/ppermute | solution.py:290
  69.3 22.5 %collective-permute-start.4 = (bf16[8,192,256]{2,1,0:T(8,128)(2,1)}, bf16[8,192,256]{2,1,0:T(8,128)(2,1)}, u32[]{:S(2)}, u32[]{:S(2)}) collective-permute-start(bf16[8,192,256]{2,1,0:T(8,128)(2,1)} %collective-permute-done.1), channel_id=1, source_target_pairs={{1,0},{2,1},{5,4},{6,5},{9,8},{10,9},{13,12},{14,13},{17,16},{18,1... | collective-permute-start | bytes 2359304 | tf_op jit(solution)/shard_map/ppermute | solution.py:290
  72.7 30.1 %collective-permute-start.2 = (bf16[8,192,256]{2,1,0:T(8,128)(2,1)}, bf16[8,192,256]{2,1,0:T(8,128)(2,1)}, u32[]{:S(2)}, u32[]{:S(2)}) collective-permute-start(bf16[8,192,256]{2,1,0:T(8,128)(2,1)} %broadcast_select_fusion.6), channel_id=1, source_target_pairs={{1,3},{2,0},{5,7},{6,4},{9,11},{10,8},{13,15},{14,12},{17,19},{18,... | collective-permute-start | bytes 2359304 | tf_op jit(solution)/shard_map/ppermute | solution.py:290
  75.3 42.5 %all-to-all-start.2 = ((bf16[8,384,256]{2,1,0:T(8,128)(2,1)}), bf16[8,384,256]{2,1,0:T(8,128)(2,1)}, u32[]{:S(2)}, u32[]{:S(2)}) async-start(bf16[8,384,256]{2,1,0:T(8,128)(2,1)} %pad_maximum_fusion.13), calls=%async_computation.2 | async-start | bytes 3145728 | tf_op jit(solution)/shard_map/all_to_all | solution.py:287
  79.6 195.3 %all-gather.11.cloned.1.call-start = ((), (), s32[]{:S(2)}) async-start(), calls=%async_computation.6 | async-start | bytes 18874368 | tf_op jit(solution)/shard_map/all_gather | solution.py:334
  138.9 353.0 %all-gather.13.cloned.1.call-start = ((), (), s32[]{:S(2)}) async-start(), calls=%async_computation.7 | async-start | bytes 18874368 | tf_op jit(solution)/shard_map/all_gather | solution.py:334
  138.9 38.8 %collective-permute-start.7 = (bf16[8,64,256]{2,1,0:T(8,128)(2,1)}, bf16[8,64,256]{2,1,0:T(8,128)(2,1)S(1)}, u32[]{:S(2)}, u32[]{:S(2)}) collective-permute-start(bf16[8,64,256]{2,1,0:T(8,128)(2,1)} %copy-done.37), channel_id=1, source_target_pairs={{0,1},{1,2},{2,3},{4,5},{5,6},{6,7},{8,9},{9,10},{10,11},{12,13},{... | collective-permute-start | bytes 786440 | tf_op jit(solution)/shard_map/ppermute | solution.py:290
  142.3 35.4 %collective-permute-start.8 = (bf16[8,64,256]{2,1,0:T(8,128)(2,1)}, bf16[8,64,256]{2,1,0:T(8,128)(2,1)}, u32[]{:S(2)}, u32[]{:S(2)}) collective-permute-start(bf16[8,64,256]{2,1,0:T(8,128)(2,1)} %copy-done.37), channel_id=1, source_target_pairs={{1,0},{2,1},{3,2},{5,4},{6,5},{7,6},{9,8},{10,9},{11,10},{13,12},{... | collective-permute-start | bytes 786440 | tf_op jit(solution)/shard_map/ppermute | solution.py:290
  143.6 56.1 %collective-permute-start.5 = (bf16[8,384,256]{2,1,0:T(8,128)(2,1)}, bf16[8,384,256]{2,1,0:T(8,128)(2,1)}, u32[]{:S(2)}, u32[]{:S(2)}) collective-permute-start(bf16[8,384,256]{2,1,0:T(8,128)(2,1)} %all-to-all-done.2), channel_id=1, source_target_pairs={{0,1},{1,2},{2,3},{4,5},{5,6},{6,7},{8,9},{9,10},{10,11},{12,13},{... | collective-permute-start | bytes 4718600 | tf_op jit(solution)/shard_map/ppermute | solution.py:290
  149.3 50.4 %collective-permute-start.6 = (bf16[8,384,256]{2,1,0:T(8,128)(2,1)}, bf16[8,384,256]{2,1,0:T(8,128)(2,1)}, u32[]{:S(2)}, u32[]{:S(2)}) collective-permute-start(bf16[8,384,256]{2,1,0:T(8,128)(2,1)} %all-to-all-done.2), channel_id=1, source_target_pairs={{1,0},{2,1},{3,2},{5,4},{6,5},{7,6},{9,8},{10,9},{11,10},{13,12},{... | collective-permute-start | bytes 4718600 | tf_op jit(solution)/shard_map/ppermute | solution.py:290
  178.7 19.9 %collective-permute-start.9 = (bf16[8,64,256]{2,1,0:T(8,128)(2,1)S(1)}, bf16[8,64,256]{2,1,0:T(8,128)(2,1)S(1)}, u32[]{:S(2)}, u32[]{:S(2)}) collective-permute-start(bf16[8,64,256]{2,1,0:T(8,128)(2,1)S(1)} %broadcast_select_fusion.9), channel_id=1, source_target_pairs={{1,3},{2,0},{5,7},{6,4},{9,11},{10,8},{13,15},{14,12},{17,19},{18,... | collective-permute-start | bytes 786440 | tf_op jit(solution)/shard_map/ppermute | solution.py:290
  180.7 17.9 %collective-permute-start.11 = (bf16[8,64,256]{2,1,0:T(8,128)(2,1)}, bf16[8,64,256]{2,1,0:T(8,128)(2,1)S(1)}, u32[]{:S(2)}, u32[]{:S(2)}) collective-permute-start(bf16[8,64,256]{2,1,0:T(8,128)(2,1)} %collective-permute-done.8), channel_id=1, source_target_pairs={{1,0},{2,1},{5,4},{6,5},{9,8},{10,9},{13,12},{14,13},{17,16},{18,1... | collective-permute-start | bytes 786440 | tf_op jit(solution)/shard_map/ppermute | solution.py:290
  199.7 75.2 %collective-permute-start.12 = (bf16[8,384,256]{2,1,0:T(8,128)(2,1)}, bf16[8,384,256]{2,1,0:T(8,128)(2,1)}, u32[]{:S(2)}, u32[]{:S(2)}) collective-permute-start(bf16[8,384,256]{2,1,0:T(8,128)(2,1)} %collective-permute-done.5), channel_id=1, source_target_pairs={{1,2},{2,3},{5,6},{6,7},{9,10},{10,11},{13,14},{14,15},{17,18},{18... | collective-permute-start | bytes 4718600 | tf_op jit(solution)/shard_map/ppermute | solution.py:290
  201.6 73.3 %collective-permute-start.13 = (bf16[8,384,256]{2,1,0:T(8,128)(2,1)}, bf16[8,384,256]{2,1,0:T(8,128)(2,1)}, u32[]{:S(2)}, u32[]{:S(2)}) collective-permute-start(bf16[8,384,256]{2,1,0:T(8,128)(2,1)} %collective-permute-done.6), channel_id=1, source_target_pairs={{1,0},{2,1},{5,4},{6,5},{9,8},{10,9},{13,12},{14,13},{17,16},{18,1... | collective-permute-start | bytes 4718600 | tf_op jit(solution)/shard_map/ppermute | solution.py:290
  204.4 69.3 %collective-permute-start.14 = (bf16[8,384,256]{2,1,0:T(8,128)(2,1)S(1)}, bf16[8,384,256]{2,1,0:T(8,128)(2,1)S(1)}, u32[]{:S(2)}, u32[]{:S(2)}) collective-permute-start(bf16[8,384,256]{2,1,0:T(8,128)(2,1)S(1)} %broadcast_select_fusion.5), channel_id=1, source_target_pairs={{1,3},{2,0},{5,7},{6,4},{9,11},{10,8},{13,15},{14,12},{17,19},{18,... | collective-permute-start | bytes 4718600 | tf_op jit(solution)/shard_map/ppermute | solution.py:290
  291.9 13.5 collective-permute-start.15
  319.4 47.9 %collective-permute-start.16 = (bf16[2,256,2048]{2,1,0:T(8,128)(2,1)}, bf16[2,256,2048]{2,1,0:T(8,128)(2,1)S(1)}, u32[]{:S(2)}, u32[]{:S(2)}) collective-permute-start(bf16[2,256,2048]{2,1,0:T(8,128)(2,1)} %dynamic-slice_bitcast_fusion.10), channel_id=1, source_target_pairs={{0,8},{8,0},{1,9},{9,1},{2,10},{10,2},{3,11},{11,3},{4,12},{12,4},... | collective-permute-start | bytes 6291464 | tf_op jit(solution)/shard_map/ppermute | solution.py:241
  324.1 47.7 %collective-permute-start.18 = (bf16[2,256,2048]{2,1,0:T(8,128)(2,1)}, bf16[2,256,2048]{2,1,0:T(8,128)(2,1)}, u32[]{:S(2)}, u32[]{:S(2)}) collective-permute-start(bf16[2,256,2048]{2,1,0:T(8,128)(2,1)} %dynamic-slice_bitcast_fusion.9), channel_id=1, source_target_pairs={{0,16},{16,0},{1,17},{17,1},{2,18},{18,2},{3,19},{19,3},{4,20},{20... | collective-permute-start | bytes 6291464 | tf_op jit(solution)/shard_map/ppermute | solution.py:241
  369.8 24.5 %collective-permute-start.17 = (bf16[256,2048]{1,0:T(8,128)(2,1)S(1)}, bf16[256,2048]{1,0:T(8,128)(2,1)S(1)}, u32[]{:S(2)}, u32[]{:S(2)}) collective-permute-start(bf16[256,2048]{1,0:T(8,128)(2,1)S(1)} %dynamic-slice_bitcast_fusion.21), channel_id=1, source_target_pairs={{0,16},{16,0},{1,17},{17,1},{2,18},{18,2},{3,19},{19,3},{4,20},{20... | collective-permute-start | bytes 3145736 | tf_op jit(solution)/shard_map/ppermute | solution.py:241
  374.3 24.1 %collective-permute-start.19 = (bf16[256,2048]{1,0:T(8,128)(2,1)S(1)}, bf16[256,2048]{1,0:T(8,128)(2,1)S(1)}, u32[]{:S(2)}, u32[]{:S(2)}) collective-permute-start(bf16[256,2048]{1,0:T(8,128)(2,1)S(1)} %dynamic-slice_bitcast_fusion.20), channel_id=1, source_target_pairs={{0,8},{8,0},{1,9},{9,1},{2,10},{10,2},{3,11},{11,3},{4,12},{12,4},... | collective-permute-start | bytes 3145736 | tf_op jit(solution)/shard_map/ppermute | solution.py:241
  404.9 473.0 %all-gather.15.cloned.1.call-start = ((), (), s32[]{:S(2)}) async-start(), calls=%async_computation.8 | async-start | bytes 18874368 | tf_op jit(solution)/shard_map/all_gather | solution.py:334
  554.7 68.9 %collective-permute-start.20 = (bf16[2,2,512,2048]{3,2,1,0:T(8,128)(2,1)}, bf16[2,2,512,2048]{3,2,1,0:T(8,128)(2,1)}, u32[]{:S(2)}, u32[]{:S(2)}) collective-permute-start(bf16[2,2,512,2048]{3,2,1,0:T(8,128)(2,1)} %dynamic-slice_bitcast_fusion.1), channel_id=1, source_target_pairs={{0,4},{4,0},{1,5},{5,1},{2,6},{6,2},{3,7},{7,3},{8,12},{12,8},{9,1... | collective-permute-start | bytes 25165832 | tf_op jit(solution)/shard_map/ppermute | solution.py:241
  575.3 61.5 %collective-permute-start.25 = (bf16[2,2,512,2048]{3,2,1,0:T(8,128)(2,1)}, bf16[2,2,512,2048]{3,2,1,0:T(8,128)(2,1)}, u32[]{:S(2)}, u32[]{:S(2)}) collective-permute-start(bf16[2,2,512,2048]{3,2,1,0:T(8,128)(2,1)} %dynamic-slice_bitcast_fusion), channel_id=1, source_target_pairs={{0,4},{4,0},{1,5},{5,1},{2,6},{6,2},{3,7},{7,3},{8,12},{12,8},{9,1... | collective-permute-start | bytes 25165832 | tf_op jit(solution)/shard_map/ppermute | solution.py:241
  633.1 48.8 %collective-permute-start.22 = (bf16[2,256,2048]{2,1,0:T(8,128)(2,1)}, bf16[2,256,2048]{2,1,0:T(8,128)(2,1)}, u32[]{:S(2)}, u32[]{:S(2)}) collective-permute-start(bf16[2,256,2048]{2,1,0:T(8,128)(2,1)} %dynamic-slice_bitcast_fusion.7), channel_id=1, source_target_pairs={{0,16},{16,0},{1,17},{17,1},{2,18},{18,2},{3,19},{19,3},{4,20},{20... | collective-permute-start | bytes 6291464 | tf_op jit(solution)/shard_map/ppermute | solution.py:241
  635.4 48.8 %collective-permute-start.21 = (bf16[2,256,2048]{2,1,0:T(8,128)(2,1)}, bf16[2,256,2048]{2,1,0:T(8,128)(2,1)}, u32[]{:S(2)}, u32[]{:S(2)}) collective-permute-start(bf16[2,256,2048]{2,1,0:T(8,128)(2,1)} %dynamic-slice_bitcast_fusion.8), channel_id=1, source_target_pairs={{0,8},{8,0},{1,9},{9,1},{2,10},{10,2},{3,11},{11,3},{4,12},{12,4},... | collective-permute-start | bytes 6291464 | tf_op jit(solution)/shard_map/ppermute | solution.py:241
  643.6 84.5 %collective-permute-start.26 = (bf16[2,256,2048]{2,1,0:T(8,128)(2,1)S(1)}, bf16[2,256,2048]{2,1,0:T(8,128)(2,1)S(1)}, u32[]{:S(2)}, u32[]{:S(2)}) collective-permute-start(bf16[2,256,2048]{2,1,0:T(8,128)(2,1)S(1)} %dynamic-slice_bitcast_fusion.6), channel_id=1, source_target_pairs={{0,8},{8,0},{1,9},{9,1},{2,10},{10,2},{3,11},{11,3},{4,12},{12,4},... | collective-permute-start | bytes 6291464 | tf_op jit(solution)/shard_map/ppermute | solution.py:241
  644.5 85.6 %collective-permute-start.28 = (bf16[2,256,2048]{2,1,0:T(8,128)(2,1)S(1)}, bf16[2,256,2048]{2,1,0:T(8,128)(2,1)S(1)}, u32[]{:S(2)}, u32[]{:S(2)}) collective-permute-start(bf16[2,256,2048]{2,1,0:T(8,128)(2,1)S(1)} %dynamic-slice_bitcast_fusion.5), channel_id=1, source_target_pairs={{0,16},{16,0},{1,17},{17,1},{2,18},{18,2},{3,19},{19,3},{4,20},{20... | collective-permute-start | bytes 6291464 | tf_op jit(solution)/shard_map/ppermute | solution.py:241
  686.7 93.4 %collective-permute-start.30 = (bf16[8,384,256]{2,1,0:T(8,128)(2,1)}, bf16[8,384,256]{2,1,0:T(8,128)(2,1)}, u32[]{:S(2)}, u32[]{:S(2)}) collective-permute-start(bf16[8,384,256]{2,1,0:T(8,128)(2,1)} %bitcast.62), channel_id=1, source_target_pairs={{0,1},{1,2},{4,5},{5,6},{8,9},{9,10},{12,13},{13,14},{16,17},{17,1... | collective-permute-start | bytes 4718600 | tf_op jit(solution)/shard_map/ppermute | solution.py:290
  691.2 88.8 %collective-permute-start.31 = (bf16[8,384,256]{2,1,0:T(8,128)(2,1)}, bf16[8,384,256]{2,1,0:T(8,128)(2,1)}, u32[]{:S(2)}, u32[]{:S(2)}) collective-permute-start(bf16[8,384,256]{2,1,0:T(8,128)(2,1)} %bitcast.62), channel_id=1, source_target_pairs={{2,1},{3,2},{6,5},{7,6},{10,9},{11,10},{14,13},{15,14},{18,17},{19... | collective-permute-start | bytes 4718600 | tf_op jit(solution)/shard_map/ppermute | solution.py:290
  694.4 85.7 %collective-permute-start.32 = (bf16[8,384,256]{2,1,0:T(8,128)(2,1)}, bf16[8,384,256]{2,1,0:T(8,128)(2,1)}, u32[]{:S(2)}, u32[]{:S(2)}) collective-permute-start(bf16[8,384,256]{2,1,0:T(8,128)(2,1)} %broadcast_select_fusion.3), channel_id=1, source_target_pairs={{0,2},{3,1},{4,6},{7,5},{8,10},{11,9},{12,14},{15,13},{16,18},{19,... | collective-permute-start | bytes 4718600 | tf_op jit(solution)/shard_map/ppermute | solution.py:290
  728.1 24.2 %collective-permute-start.23 = (bf16[256,2048]{1,0:T(8,128)(2,1)S(1)}, bf16[256,2048]{1,0:T(8,128)(2,1)S(1)}, u32[]{:S(2)}, u32[]{:S(2)}) collective-permute-start(bf16[256,2048]{1,0:T(8,128)(2,1)S(1)} %dynamic-slice_bitcast_fusion.19), channel_id=1, source_target_pairs={{0,16},{16,0},{1,17},{17,1},{2,18},{18,2},{3,19},{19,3},{4,20},{20... | collective-permute-start | bytes 3145736 | tf_op jit(solution)/shard_map/ppermute | solution.py:241
  730.2 24.0 %collective-permute-start.24 = (bf16[256,2048]{1,0:T(8,128)(2,1)S(1)}, bf16[256,2048]{1,0:T(8,128)(2,1)S(1)}, u32[]{:S(2)}, u32[]{:S(2)}) collective-permute-start(bf16[256,2048]{1,0:T(8,128)(2,1)S(1)} %dynamic-slice_bitcast_fusion.18), channel_id=1, source_target_pairs={{0,8},{8,0},{1,9},{9,1},{2,10},{10,2},{3,11},{11,3},{4,12},{12,4},... | collective-permute-start | bytes 3145736 | tf_op jit(solution)/shard_map/ppermute | solution.py:241
  752.3 23.3 %collective-permute-start.27 = (bf16[256,2048]{1,0:T(8,128)(2,1)S(1)}, bf16[256,2048]{1,0:T(8,128)(2,1)S(1)}, u32[]{:S(2)}, u32[]{:S(2)}) collective-permute-start(bf16[256,2048]{1,0:T(8,128)(2,1)S(1)} %dynamic-slice_bitcast_fusion.17), channel_id=1, source_target_pairs={{0,16},{16,0},{1,17},{17,1},{2,18},{18,2},{3,19},{19,3},{4,20},{20... | collective-permute-start | bytes 3145736 | tf_op jit(solution)/shard_map/ppermute | solution.py:241
  754.1 23.0 %collective-permute-start.29 = (bf16[256,2048]{1,0:T(8,128)(2,1)S(1)}, bf16[256,2048]{1,0:T(8,128)(2,1)S(1)}, u32[]{:S(2)}, u32[]{:S(2)}) collective-permute-start(bf16[256,2048]{1,0:T(8,128)(2,1)S(1)} %dynamic-slice_bitcast_fusion.16), channel_id=1, source_target_pairs={{0,8},{8,0},{1,9},{9,1},{2,10},{10,2},{3,11},{11,3},{4,12},{12,4},... | collective-permute-start | bytes 3145736 | tf_op jit(solution)/shard_map/ppermute | solution.py:241
  787.2 610.3 %all-gather.19.cloned.1.call-start = ((), (), s32[]{:S(2)}) async-start(), calls=%async_computation.10 | async-start | bytes 5242880 | tf_op jit(solution)/shard_map/all_gather | solution.py:513
  787.2 85.8 %collective-permute-start.35 = (bf16[512,2048]{1,0:T(8,128)(2,1)}, bf16[512,2048]{1,0:T(8,128)(2,1)}, u32[]{:S(2)}, u32[]{:S(2)}) collective-permute-start(bf16[512,2048]{1,0:T(8,128)(2,1)} %fusion.8), channel_id=1, source_target_pairs={{0,1},{1,2},{2,3},{4,5},{5,6},{6,7},{8,9},{9,10},{10,11},{12,13},{... | collective-permute-start | bytes 6291464 | tf_op jit(solution)/shard_map/ppermute | solution.py:290
  792.3 80.7 %collective-permute-start.36 = (bf16[512,2048]{1,0:T(8,128)(2,1)}, bf16[512,2048]{1,0:T(8,128)(2,1)}, u32[]{:S(2)}, u32[]{:S(2)}) collective-permute-start(bf16[512,2048]{1,0:T(8,128)(2,1)} %fusion.8), channel_id=1, source_target_pairs={{1,0},{2,1},{3,2},{5,4},{6,5},{7,6},{9,8},{10,9},{11,10},{13,12},{... | collective-permute-start | bytes 6291464 | tf_op jit(solution)/shard_map/ppermute | solution.py:290
  799.8 67.6 %collective-permute-start.33 = (bf16[8,384,256]{2,1,0:T(8,128)(2,1)}, bf16[8,384,256]{2,1,0:T(8,128)(2,1)S(1)}, u32[]{:S(2)}, u32[]{:S(2)}) collective-permute-start(bf16[8,384,256]{2,1,0:T(8,128)(2,1)} %get-tuple-element.206), channel_id=1, source_target_pairs={{0,1},{1,2},{2,3},{4,5},{5,6},{6,7},{8,9},{9,10},{10,11},{12,13},{... | collective-permute-start | bytes 4718600 | tf_op jit(solution)/shard_map/ppermute | solution.py:290
  804.4 68.5 %collective-permute-start.34 = (bf16[8,384,256]{2,1,0:T(8,128)(2,1)}, bf16[8,384,256]{2,1,0:T(8,128)(2,1)}, u32[]{:S(2)}, u32[]{:S(2)}) collective-permute-start(bf16[8,384,256]{2,1,0:T(8,128)(2,1)} %get-tuple-element.205), channel_id=1, source_target_pairs={{1,0},{2,1},{3,2},{5,4},{6,5},{7,6},{9,8},{10,9},{11,10},{13,12},{... | collective-permute-start | bytes 4718600 | tf_op jit(solution)/shard_map/ppermute | solution.py:290
  877.9 103.4 %collective-permute-start.37 = (bf16[512,2048]{1,0:T(8,128)(2,1)}, bf16[512,2048]{1,0:T(8,128)(2,1)}, u32[]{:S(2)}, u32[]{:S(2)}) collective-permute-start(bf16[512,2048]{1,0:T(8,128)(2,1)} %collective-permute-done.35), channel_id=1, source_target_pairs={{1,2},{2,3},{5,6},{6,7},{9,10},{10,11},{13,14},{14,15},{17,18},{18... | collective-permute-start | bytes 6291464 | tf_op jit(solution)/shard_map/ppermute | solution.py:290
  883.1 98.2 %collective-permute-start.38 = (bf16[512,2048]{1,0:T(8,128)(2,1)}, bf16[512,2048]{1,0:T(8,128)(2,1)}, u32[]{:S(2)}, u32[]{:S(2)}) collective-permute-start(bf16[512,2048]{1,0:T(8,128)(2,1)} %collective-permute-done.36), channel_id=1, source_target_pairs={{1,0},{2,1},{5,4},{6,5},{9,8},{10,9},{13,12},{14,13},{17,16},{18,1... | collective-permute-start | bytes 6291464 | tf_op jit(solution)/shard_map/ppermute | solution.py:290
  884.3 96.9 %collective-permute-start.39 = (bf16[512,2048]{1,0:T(8,128)(2,1)}, bf16[512,2048]{1,0:T(8,128)(2,1)S(1)}, u32[]{:S(2)}, u32[]{:S(2)}) collective-permute-start(bf16[512,2048]{1,0:T(8,128)(2,1)} %broadcast_select_fusion), channel_id=1, source_target_pairs={{1,3},{2,0},{5,7},{6,4},{9,11},{10,8},{13,15},{14,12},{17,19},{18,... | collective-permute-start | bytes 6291464 | tf_op jit(solution)/shard_map/ppermute | solution.py:290
  1023.6 11.6 collective-permute-start.40
  1032.9 26.1 %collective-permute-start.46 = (bf16[2,128,2048]{2,1,0:T(8,128)(2,1)S(1)}, bf16[2,128,2048]{2,1,0:T(8,128)(2,1)S(1)}, u32[]{:S(2)}, u32[]{:S(2)}) collective-permute-start(bf16[2,128,2048]{2,1,0:T(8,128)(2,1)S(1)} %dynamic-slice_bitcast_fusion.13), channel_id=1, source_target_pairs={{0,8},{8,0},{1,9},{9,1},{2,10},{10,2},{3,11},{11,3},{4,12},{12,4},... | collective-permute-start | bytes 3145736 | tf_op jit(solution)/shard_map/ppermute | solution.py:241
  1034.5 26.1 %collective-permute-start.48 = (bf16[2,128,2048]{2,1,0:T(8,128)(2,1)S(1)}, bf16[2,128,2048]{2,1,0:T(8,128)(2,1)S(1)}, u32[]{:S(2)}, u32[]{:S(2)}) collective-permute-start(bf16[2,128,2048]{2,1,0:T(8,128)(2,1)S(1)} %dynamic-slice_bitcast_fusion.12), channel_id=1, source_target_pairs={{0,16},{16,0},{1,17},{17,1},{2,18},{18,2},{3,19},{19,3},{4,20},{20... | collective-permute-start | bytes 3145736 | tf_op jit(solution)/shard_map/ppermute | solution.py:241
  1039.3 42.2 %collective-permute-start.41 = (bf16[2,128,2048]{2,1,0:T(8,128)(2,1)S(1)}, bf16[2,128,2048]{2,1,0:T(8,128)(2,1)S(1)}, u32[]{:S(2)}, u32[]{:S(2)}) collective-permute-start(bf16[2,128,2048]{2,1,0:T(8,128)(2,1)S(1)} %dynamic-slice_bitcast_fusion.15), channel_id=1, source_target_pairs={{0,8},{8,0},{1,9},{9,1},{2,10},{10,2},{3,11},{11,3},{4,12},{12,4},... | collective-permute-start | bytes 3145736 | tf_op jit(solution)/shard_map/ppermute | solution.py:241
  1040.4 42.7 %collective-permute-start.43 = (bf16[2,128,2048]{2,1,0:T(8,128)(2,1)S(1)}, bf16[2,128,2048]{2,1,0:T(8,128)(2,1)S(1)}, u32[]{:S(2)}, u32[]{:S(2)}) collective-permute-start(bf16[2,128,2048]{2,1,0:T(8,128)(2,1)S(1)} %dynamic-slice_bitcast_fusion.14), channel_id=1, source_target_pairs={{0,16},{16,0},{1,17},{17,1},{2,18},{18,2},{3,19},{19,3},{4,20},{20... | collective-permute-start | bytes 3145736 | tf_op jit(solution)/shard_map/ppermute | solution.py:241
  1059.4 34.9 %collective-permute-start.47 = (bf16[128,2048]{1,0:T(8,128)(2,1)S(1)}, bf16[128,2048]{1,0:T(8,128)(2,1)S(1)}, u32[]{:S(2)}, u32[]{:S(2)}) collective-permute-start(bf16[128,2048]{1,0:T(8,128)(2,1)S(1)} %dynamic-slice_bitcast_fusion.23), channel_id=1, source_target_pairs={{0,16},{16,0},{1,17},{17,1},{2,18},{18,2},{3,19},{19,3},{4,20},{20... | collective-permute-start | bytes 1572872 | tf_op jit(solution)/shard_map/ppermute | solution.py:241
  1061.1 33.4 %collective-permute-start.49 = (bf16[128,2048]{1,0:T(8,128)(2,1)S(1)}, bf16[128,2048]{1,0:T(8,128)(2,1)S(1)}, u32[]{:S(2)}, u32[]{:S(2)}) collective-permute-start(bf16[128,2048]{1,0:T(8,128)(2,1)S(1)} %dynamic-slice_bitcast_fusion.22), channel_id=1, source_target_pairs={{0,8},{8,0},{1,9},{9,1},{2,10},{10,2},{3,11},{11,3},{4,12},{12,4},... | collective-permute-start | bytes 1572872 | tf_op jit(solution)/shard_map/ppermute | solution.py:241
  1081.9 22.6 %collective-permute-start.42 = (bf16[128,2048]{1,0:T(8,128)(2,1)S(1)}, bf16[128,2048]{1,0:T(8,128)(2,1)S(1)}, u32[]{:S(2)}, u32[]{:S(2)}) collective-permute-start(bf16[128,2048]{1,0:T(8,128)(2,1)S(1)} %dynamic-slice_bitcast_fusion.25), channel_id=1, source_target_pairs={{0,16},{16,0},{1,17},{17,1},{2,18},{18,2},{3,19},{19,3},{4,20},{20... | collective-permute-start | bytes 1572872 | tf_op jit(solution)/shard_map/ppermute | solution.py:241
  1083.6 21.0 %collective-permute-start.44 = (bf16[128,2048]{1,0:T(8,128)(2,1)S(1)}, bf16[128,2048]{1,0:T(8,128)(2,1)S(1)}, u32[]{:S(2)}, u32[]{:S(2)}) collective-permute-start(bf16[128,2048]{1,0:T(8,128)(2,1)S(1)} %dynamic-slice_bitcast_fusion.24), channel_id=1, source_target_pairs={{0,8},{8,0},{1,9},{9,1},{2,10},{10,2},{3,11},{11,3},{4,12},{12,4},... | collective-permute-start | bytes 1572872 | tf_op jit(solution)/shard_map/ppermute | solution.py:241
  1112.7 24.5 %all-to-all-start.4 = ((bf16[8,384,256]{2,1,0:T(8,128)(2,1)}), bf16[8,384,256]{2,1,0:T(8,128)(2,1)S(1)}, u32[]{:S(2)}, u32[]{:S(2)}) async-start(bf16[8,384,256]{2,1,0:T(8,128)(2,1)} %add_convert_fusion), calls=%async_computation.4 | async-start | bytes 3145728 | tf_op jit(solution)/shard_map/all_to_all | solution.py:287
  1116.3 281.1 %all-gather.17.cloned.1.call-start = ((), (), s32[]{:S(2)}) async-start(), calls=%async_computation.9 | async-start | bytes 5242880 | tf_op jit(solution)/shard_map/all_gather | solution.py:513
  1161.5 65.5 %collective-permute-start.50 = (bf16[8,256,256]{2,0,1:T(8,128)(2,1)S(1)}, bf16[8,256,256]{2,0,1:T(8,128)(2,1)S(1)}, u32[]{:S(2)}, u32[]{:S(2)}) collective-permute-start(bf16[8,256,256]{2,0,1:T(8,128)(2,1)S(1)} %get-tuple-element.200), channel_id=1, source_target_pairs={{0,1},{1,2},{4,5},{5,6},{8,9},{9,10},{12,13},{13,14},{16,17},{17,1... | collective-permute-start | bytes 3145736 | tf_op jit(solution)/shard_map/ppermute | solution.py:290
  1184.6 71.7 %collective-permute-start.53 = (bf16[8,256,256]{2,0,1:T(8,128)(2,1)S(1)}, bf16[8,256,256]{2,0,1:T(8,128)(2,1)S(1)}, u32[]{:S(2)}, u32[]{:S(2)}) collective-permute-start(bf16[8,256,256]{2,0,1:T(8,128)(2,1)S(1)} %get-tuple-element.200), channel_id=1, source_target_pairs={{2,1},{3,2},{6,5},{7,6},{10,9},{11,10},{14,13},{15,14},{18,17},{19... | collective-permute-start | bytes 3145736 | tf_op jit(solution)/shard_map/ppermute | solution.py:290
  1185.3 71.0 %collective-permute-start.51 = (bf16[8,256,256]{2,0,1:T(8,128)(2,1)S(1)}, bf16[8,256,256]{2,0,1:T(8,128)(2,1)S(1)}, u32[]{:S(2)}, u32[]{:S(2)}) collective-permute-start(bf16[8,256,256]{2,0,1:T(8,128)(2,1)S(1)} %get-tuple-element.199), channel_id=1, source_target_pairs={{0,2},{3,1},{4,6},{7,5},{8,10},{11,9},{12,14},{15,13},{16,18},{19,... | collective-permute-start | bytes 3145736 | tf_op jit(solution)/shard_map/ppermute | solution.py:290
  1257.2 50.8 %collective-permute-start.52 = (bf16[8,256,256]{2,0,1:T(8,128)(2,1)S(1)}, bf16[8,256,256]{2,0,1:T(8,128)(2,1)S(1)}, u32[]{:S(2)}, u32[]{:S(2)}) collective-permute-start(bf16[8,256,256]{2,0,1:T(8,128)(2,1)S(1)} %get-tuple-element.209), channel_id=1, source_target_pairs={{0,1},{1,2},{2,3},{4,5},{5,6},{6,7},{8,9},{9,10},{10,11},{12,13},{... | collective-permute-start | bytes 3145736 | tf_op jit(solution)/shard_map/ppermute | solution.py:290
  1263.7 63.5 %collective-permute-start.54 = (bf16[8,256,256]{2,0,1:T(8,128)(2,1)S(1)}, bf16[8,256,256]{2,0,1:T(8,128)(2,1)S(1)}, u32[]{:S(2)}, u32[]{:S(2)}) collective-permute-start(bf16[8,256,256]{2,0,1:T(8,128)(2,1)S(1)} %get-tuple-element.210), channel_id=1, source_target_pairs={{1,0},{2,1},{3,2},{5,4},{6,5},{7,6},{9,8},{10,9},{11,10},{13,12},{... | collective-permute-start | bytes 3145736 | tf_op jit(solution)/shard_map/ppermute | solution.py:290
  1328.7 19.0 %all-to-all-start.3 = ((bf16[8,256,256]{2,1,0:T(8,128)(2,1)}), bf16[8,256,256]{2,1,0:T(8,128)(2,1)S(1)}, u32[]{:S(2)}, u32[]{:S(2)}) async-start(bf16[8,256,256]{2,1,0:T(8,128)(2,1)} %copy.184), calls=%async_computation.3 | async-start | bytes 2097152 | tf_op jit(solution)/shard_map/all_to_all | solution.py:287
  (65 other events, 784.6 us)
Sparse Core Ops, SparseCore 0:
  25.5 113.2 all-gather.8
  140.7 89.8 all-gather.10
  405.0 86.8 all-gather.12
  787.3 90.5 all-gather.14
  1109.6 113.9 all-gather.18
  1225.0 117.3 all-gather.16

commit v3 on v2

--- a/solution.py
+++ b/solution.py
@@ -12,7 +12,6 @@
 HEAD_DIM = 64
 WINDOW = 2048
 BLOCK = 512
-TAIL_CHUNKS = 2
 
 epsilon = 1e-05
 rope_base = 10000.0
@@ -345,6 +344,27 @@
         one, two = a[:, :, : size // 2], a[:, :, size // 2 :]
         return [halve(one, "pair", 1).astype(bf16), halve(two, "chips", 0).astype(bf16)]
 
+    def scatter_start_by_core(product, a):
+        if not cube:
+            return scatter_start(product(a))
+        core = lax.axis_index("core")
+        a = a.reshape(n_chips * n_pair, n_core, own_len, a.shape[1])
+
+        def part(index):
+            rows_of = lax.dynamic_index_in_dim(a, index, 1, False)
+            return product(rows_of.reshape(-1, a.shape[3]))
+
+        theirs = swap(part(1 - core).astype(bf16), "core")
+        mine = (part(core) + theirs.astype(f32)).astype(bf16)
+        return mine.reshape(n_chips, n_pair, own_len, model)
+
+    def scatter_middle(a):
+        if not cube:
+            return a
+        half = own_len // 2
+        one, two = a[:, :, :half], a[:, :, half:]
+        return [halve(one, "pair", 1).astype(bf16), halve(two, "chips", 0).astype(bf16)]
+
     def scatter_end(halves):
         if not cube:
             return halves[0]
@@ -377,10 +397,6 @@
 
     def heads_back(a):
         m = a.shape[1]
-        if split_heads:
-            blocks = heads_split(a)
-            blocks = collect_near(blocks, collect_far(blocks))
-            return exchange(total(blocks).astype(bf16)).reshape(block_heads, m, rows).astype(f32)
         a = a.astype(bf16).reshape(heads, m, n_context, rows).transpose(2, 0, 1, 3)
         a = exchange(a.reshape(n_context, -1, rows)).reshape(seqs * block_heads, m, rows)
         return lax.psum_scatter(a, "seq", scatter_dimension=0, tiled=True).astype(f32)
@@ -402,26 +418,24 @@
     qkv_t = qkv_t.transpose(1, 0, 2, 3).reshape(3 * width, model)
     out_block = heads_out(out_local.reshape(block_heads, HEAD_DIM, rows))
     gateup_local = gateup_local.reshape(2, rows, n_context, block_hidden).transpose(2, 0, 3, 1)
-    hidden_block = exchange(
-        jnp.concatenate(
-            [
-                gateup_local.reshape(n_context, 2 * block_hidden, rows),
-                down_local.reshape(n_context, block_hidden, rows),
-            ],
-            axis=1,
-        )
+    hidden_local = jnp.concatenate(
+        [
+            gateup_local.reshape(n_context, 2 * block_hidden, rows),
+            down_local.reshape(n_context, block_hidden, rows),
+        ],
+        axis=1,
     )
     cosine, sine = rope_tables(length)
     bounds = attention_bounds(lax.dynamic_slice_in_dim(doc_lengths, seq, 1, 0)[0], length)
-    normed_one, incoming_now, qkv_t, out_block, hidden_block, cosine, sine, bounds = (
+    normed_one, incoming_now, qkv_t, out_block, hidden_local, cosine, sine, bounds = (
         lax.optimization_barrier(
-            (normed_one, incoming, qkv_t, out_block, hidden_block, cosine, sine, bounds)
+            (normed_one, incoming, qkv_t, out_block, hidden_local, cosine, sine, bounds)
         )
     )
 
     incoming_all = gather_plane(incoming_now)
-    hidden_near = spread_near(hidden_block)
-    out_blocks = heads_spread(out_block) if split_heads else [out_block]
+    hidden_block = exchange(hidden_local)
+    out_near = spread_near(out_block) if split_heads else []
     score_scale = HEAD_DIM ** (-0.5)
     projected = dot(qkv_t, normed_one, 1, 1)
     q_t = rotate(projected[:width], cosine, sine).astype(bf16) * bf16(score_scale)
@@ -429,13 +443,19 @@
     v_t = projected[2 * width :].astype(bf16)
     k_h = k_t.reshape(heads, HEAD_DIM, length).transpose(0, 2, 1)
     v_h = v_t.reshape(heads, HEAD_DIM, length).transpose(0, 2, 1)
-    q_t, hidden_near, out_blocks = lax.optimization_barrier((q_t, hidden_near, out_blocks))
+    q_t, hidden_block, out_near = lax.optimization_barrier((q_t, hidden_block, out_near))
+    out_far = spread_far(out_near) if split_heads else []
+    hidden_near = spread_near(hidden_block)
+    o_t, lse = attend(bounds, q_t, k_h, v_t)
+    o_t, incoming_all, hidden_near, out_far = lax.optimization_barrier(
+        (o_t, incoming_all, hidden_near, out_far)
+    )
     hidden_far = spread_far(hidden_near)
-    o_t, lse = attend(bounds, q_t, k_h, v_t)
-    o_t, incoming_all, hidden_far = lax.optimization_barrier((o_t, incoming_all, hidden_far))
-
+
+    out_blocks = spread_blocks(out_block, out_near, out_far) if split_heads else [out_block]
     out_full = heads_whole(out_blocks, HEAD_DIM).reshape(width, model)
-    attention_branch = scatter_rows(dot(o_t, out_full, 0, 0))
+    attention_branch = scatter_plane(dot(o_t, out_full, 0, 0))
+    attention_branch, hidden_far = lax.optimization_barrier((attention_branch, hidden_far))
     hidden = rows_in + attention_branch
     inverse_two = norm_inverse(hidden)
     normal_two = hidden * inverse_two
@@ -457,8 +477,20 @@
     grad_gate = grad_activation * raised * gate_sigmoid * (1.0 + gate * (1.0 - gate_sigmoid))
     grad_up = grad_activation * gate_silu
     grad_gateup = jnp.concatenate([grad_gate, grad_up], axis=1).astype(bf16)
-    feedforward_halves = scatter_start(dot(activation, down_full, 1, 0))
-    second_halves = scatter_start(dot(grad_gateup, gateup_t, 1, 0))
+    feedforward_branch = scatter_plane(dot(activation, down_full, 1, 0))
+    second_sums = scatter_start_by_core(lambda a: dot(a, gateup_t, 1, 0), grad_gateup)
+    grad_normed_two = scatter_end(scatter_middle(second_sums))
+    grad_normed_two, feedforward_branch, activation, grad_gateup = lax.optimization_barrier(
+        (grad_normed_two, feedforward_branch, activation, grad_gateup)
+    )
+
+    result = (hidden + feedforward_branch).astype(bf16)
+    if n_extra > 1:
+        result = lax.all_gather(result, "extra", axis=0, tiled=True)
+    result_near = spread_near(result)
+    grad_rows_two, gain_two = norm_backward(grad_normed_two, normal_two, inverse_two, gains[1])
+    grad_hidden = incoming.astype(f32) + grad_rows_two
+    grad_hidden_all = gather_plane(grad_hidden.astype(bf16))
     down_grad = dot(activation, incoming_all, 0, 0).astype(bf16)
     gateup_grad = dot(grad_gateup, normed_two, 0, 0).astype(bf16)
     hidden_grads = jnp.concatenate(
@@ -469,24 +501,9 @@
         axis=0,
     )
     hidden_grads = list(hidden_grads.transpose(1, 3, 0, 2, 4).reshape(seqs, n_context, -1, rows))
-    second_halves, hidden_grads = lax.optimization_barrier((second_halves, hidden_grads))
     hidden_grads_far = collect_far(hidden_grads)
-    feedforward_branch = scatter_end(feedforward_halves)
-    result = (hidden + feedforward_branch).astype(bf16)
-    if n_extra > 1:
-        result = lax.all_gather(result, "extra", axis=0, tiled=True)
-    grad_normed_two = scatter_end(second_halves)
-    grad_normed_two, result, hidden_grads_far = lax.optimization_barrier(
-        (grad_normed_two, result, hidden_grads_far)
-    )
-
-    hidden_grads = collect_near(hidden_grads, hidden_grads_far)
-    result_near = spread_near(result)
-    grad_rows_two, gain_two = norm_backward(grad_normed_two, normal_two, inverse_two, gains[1])
-    grad_hidden = incoming.astype(f32) + grad_rows_two
-    grad_hidden_all = gather_plane(grad_hidden.astype(bf16))
-    grad_hidden_all, hidden_grads, result_near = lax.optimization_barrier(
-        (grad_hidden_all, hidden_grads, result_near)
+    grad_hidden_all, hidden_grads_far, result_near = lax.optimization_barrier(
+        (grad_hidden_all, hidden_grads_far, result_near)
     )
 
     result_far = spread_far(result_near)
@@ -497,37 +514,44 @@
         [rotate(dq_t * score_scale, cosine, -sine), rotate(dk_t, cosine, -sine), dv_t], axis=0
     ).astype(bf16)
 
-    piece = own_len // TAIL_CHUNKS
     first_part = dot(grad_projected, qkv_t, 0, 0).astype(bf16)
-    first_part = first_part.reshape(n_context * n_extra, own_len, model)
-    input_pieces = []
-    gain_one = jnp.zeros((model,), f32)
-    for i in range(TAIL_CHUNKS):
-        part = slice(i * piece, (i + 1) * piece)
-        grad_normed_one = scatter_rows(first_part[:, part].reshape(-1, model))
-        grad_rows_one, gain_part = norm_backward(
-            grad_normed_one, normal_one[part], inverse_one[part], gains[0]
-        )
-        gain_one = gain_one + gain_part
-        grad_input = (grad_hidden[part] + grad_rows_one).astype(bf16)
-        gathered = lax.all_gather(grad_input, ("seq", "extra"), axis=0, tiled=False)
-        input_pieces.append(gathered.reshape(seqs, n_extra, piece, model))
-
-    out_grad = dot(o_t, grad_hidden_all, 1, 0).reshape(heads, HEAD_DIM, model)
+    first_part, grad_projected = lax.optimization_barrier((first_part, grad_projected))
+    grad_normed_one = scatter_plane(first_part)
+    hidden_grads = collect_near(hidden_grads, hidden_grads_far)
     qkv_grad = dot(grad_projected, normed_one, 1, 0)
     qkv_grad = qkv_grad.reshape(3, heads, HEAD_DIM, model).transpose(1, 0, 2, 3)
     qkv_grad = qkv_grad.reshape(heads, 3 * HEAD_DIM, model)
-    heads_grad = heads_back(jnp.concatenate([qkv_grad, out_grad], axis=1))
+    out_grad = dot(o_t, grad_hidden_all, 1, 0).reshape(heads, HEAD_DIM, model)
+    heads_grad = jnp.concatenate([qkv_grad, out_grad], axis=1)
+    if split_heads:
+        heads_grads = heads_split(heads_grad)
+        heads_grads = collect_near(heads_grads, collect_far(heads_grads))
+    else:
+        heads_grads = []
+    grad_normed_one, hidden_grads, heads_grads = lax.optimization_barrier(
+        (grad_normed_one, hidden_grads, heads_grads)
+    )
+
+    grad_rows_one, gain_one = norm_backward(grad_normed_one, normal_one, inverse_one, gains[0])
+    grad_input = (grad_hidden + grad_rows_one).astype(bf16)
+    input_grad = lax.all_gather(grad_input, ("seq", "extra"), axis=0, tiled=True).astype(f32)
+    if split_heads:
+        heads_grad = exchange(total(heads_grads).astype(bf16)).astype(f32)
+        heads_grad = heads_grad.reshape(block_heads, 4 * HEAD_DIM, rows)
+    else:
+        heads_grad = heads_back(heads_grad)
     qkv_grad = heads_grad[:, : 3 * HEAD_DIM].reshape(block_heads, 3, HEAD_DIM, rows)
     out_grad = heads_grad[:, 3 * HEAD_DIM :]
     hidden_grad = exchange(total(hidden_grads).astype(bf16)).astype(f32)
     hidden_grad = hidden_grad.reshape(n_context, 3, block_hidden, rows)
 
+    gains_grad = jnp.stack([gain_one, gain_two]).reshape(2, n_context, rows).transpose(1, 0, 2)
+    gains_grad = jnp.sum(exchange(gains_grad), axis=0)
+    if n_extra > 1:
+        gains_grad = lax.psum(gains_grad, "extra")
+    gains_near = spread_near(gains_grad)
+    gains_grad = jnp.sum(spread_line(gains_grad, gains_near, spread_far(gains_near)), axis=0)
     results = spread_line(result, result_near, result_far)
-    gains_grad = lax.psum(jnp.stack([gain_one, gain_two]), everyone)
-    gains_grad = lax.dynamic_slice_in_dim(gains_grad, lax.axis_index(context) * rows, rows, 1)
-    input_pieces[-1] = after(input_pieces[-1], gains_grad)
-    input_grad = jnp.concatenate(input_pieces, axis=2).astype(f32)
     return (
         results,
         input_grad.reshape(seqs, local_len, model),

time: 1420 us -> 1330 us (0.937)
  waiting for transfers between devices: 636 us -> 565 us
  Pallas kernels: 87.4 us -> 150 us
  blocking collectives: 56.9 us -> 10.5 us
  starting transfers between devices: 135 us -> 100 us
  local copies, waits for them, and re-layouts: 147 us -> 124 us
    reduce_scatter x0 -> x3, waiting for transfers between devices: none -> 133 us  [scatter_plane(): lax.psum_scatter(a.astype(bf16), plane, scatter_dimension=0, tiled=True)]
    ppermute x30 -> x35, waiting for transfers between devices: 275 us -> 145 us  [send(): return lax.ppermute(a, 'seq', pairs)]
    ppermute x25 -> x5, waiting for transfers between devices: 247 us -> 126 us  [swap(): return lax.ppermute(a, axis, [(0, 1), (1, 0)])]
    all_gather x2 -> x1, waiting for transfers between devices: 0.01 us -> 69.2 us  [shards(): lax.all_gather(grad_input, ('seq', 'extra'), axis=0, tiled=True).astype(f32)]
    psum x1 -> x0, blocking collectives: 46.4 us -> none  [shards(): gains_grad = lax.psum(jnp.stack([gain_one, gain_two]), everyone)]
    pallas_call x1, Pallas kernels: 54.4 us -> 93.1 us  [attend_back(): pl.pallas_call(functools.partial(attend_back_kernel, block), out_shape=tu...]
    convert_element_type x19 -> x9, other arithmetic: 59.7 us -> 27 us  [the longest x3 6.69 us: scatter_plane(): lax.psum_scatter(a.astype(bf16), plane, scatter_dimension=0, tiled=True)]
    squeeze x25 -> x4, local copies, waits for them, and re-layouts: 37.6 us -> 5.42 us  [halve(): other = lax.dynamic_index_in_dim(a, 1 - index, dim, False)]
  transfers between devices with their start and end apart: 66 -> 54, of which waited for: 39 -> 22; matrix products, arithmetic and copies ran while one was open for 21% -> 24% of each run, Pallas kernels for 6% -> 11%
where the time goes in v3:
time: 1330 us; the launch traced here: 1320 us
  waiting for transfers between devices  565 us (42%)
  matrix products  212 us (16%)
  Pallas kernels  150 us (11%)
  other arithmetic  143 us (11%)
  local copies, waits for them, and re-layouts  124 us (9%)
  starting transfers between devices  100 us (8%)
  between operations  15.7 us (1%)
    dot_general x13, matrix products, dot(): lax.dot_general(a, b, (((ca,), (cb,)), ((), ())), preferred_element_type=...  212 us
    ppermute x35, waiting for transfers between devices, send(): return lax.ppermute(a, 'seq', pairs)  145 us
    reduce_scatter x3, waiting for transfers between devices, scatter_plane(): lax.psum_scatter(a.astype(bf16), plane, scatter_dimension=0, tiled=True)  133 us
    ppermute x5, waiting for transfers between devices, swap(): return lax.ppermute(a, axis, [(0, 1), (1, 0)])  126 us
    pallas_call x1, Pallas kernels, attend_back(): pl.pallas_call(functools.partial(attend_back_kernel, block), out_shape=tu...  93.1 us
    ppermute x35, starting transfers between devices, send(): return lax.ppermute(a, 'seq', pairs)  73.5 us
    all_gather x1, waiting for transfers between devices, shards(): lax.all_gather(grad_input, ('seq', 'extra'), axis=0, tiled=True).astype(f32)  69.2 us
    all_gather x4, waiting for transfers between devices, gather_plane(): return lax.all_gather(a, plane, axis=0, tiled=True)  67 us
  transfers between devices with their start and end apart: 54, of which 22 were waited for; matrix products, arithmetic and copies ran while one was open for 24% of the time, Pallas kernels for 11%

profile of v3, /device:TPU:0, one launch (start us, length us, event | category | flops | bytes accessed | tf_op | source)
XLA Modules:
  0.0 1320.9 jit_solution(2800496829098347664)
XLA Ops:
  9.4 10.5 all_gather.18
  24.6 3.5 all-to-all-start
  31.6 13.9 %all-to-all-done = bf16[8,192,256]{2,1,0:T(8,128)(2,1)S(1)} async-done(((bf16[8,192,256]{2,1,0:T(8,128)(2,1)}), bf16[8,192,256]{2,1,0:T(8,128)(2,1)S(1)}, u32[]{:S(2)}, u32[]{:S(2)}) %all-to-all-start) | async-done | bytes 786464 | tf_op jit(solution)/shard_map/all_to_all | solution.py:286
  45.4 4.4 collective-permute-start
  51.8 10.1 collective-permute-done
  63.4 3.7 collective-permute-done.1
  76.4 3.5 all-to-all-start.1
  82.3 7.0 collective-permute-done.4
  90.5 11.2 collective-permute-done.2
  111.0 9.5 all-gather.6.cloned.1.call-done
  125.3 4.3 all-to-all-start.2
  130.2 20.7 %fusion.30 = f32[768,4096]{1,0:T(8,128)} fusion(bf16[768,2048]{1,0:T(8,128)(2,1)S(1)} %bitcast.279, bf16[4096,2048]{1,0:T(8,128)(2,1)} %all-gather.6.cloned.1.call-done), kind=kOutput, calls=%fused_computation.151 | convolution fusion | flops 12884901888 | bytes 32505856 | tf_op jit(solution)/shard_map/dot_general | solution.py:26
  150.8 3.8 slice.174.v_ref
  154.7 6.3 fusion.27
  169.7 4.5 collective-permute-start.7
  179.9 57.2 %attend.1 = (bf16[256,4096]{1,0:T(8,128)(2,1)}, f32[4,4096]{1,0:T(4,128)}) custom-call(s32[8]{0:T(128)} %get-tuple-element.72.lo_ref, s32[8]{0:T(128)} %get-tuple-element.73.full_ref, s32[1,4096]{1,0:T(1,128)} %add_maximum_fusion.low_ref, bf16[256,4096]{1,0:T(8,128)(2,1)} %bitcast.283, bf16[4,4096,64]{2,1,0:T(8,128)(2,1)} %bitcast.265, ...), custom_call_target="tpu_custom_call" | custom-call | flops 51539607552 | bytes 8388608 | tf_op jit(solution)/shard_map/attend/pallas_call | solution.py:155
  243.1 12.6 convolution_convert_fusion.2
  261.4 112.3 %reduce-scatter.4.cloned.1.call-done = bf16[512,2048]{1,0:T(8,128)(2,1)} async-done(((bf16[4096,2048]{1,0:T(8,128)(2,1)}), bf16[512,2048]{1,0:T(8,128)(2,1)}) %reduce-scatter.4.cloned.1.call-update) | async-done | bytes 2097168 | tf_op jit(solution)/shard_map/reduce_scatter | solution.py:336
  395.4 4.4 slice-done
  399.8 3.5 copy.161
  403.3 11.2 fusion.31
  414.5 57.4 %all-gather.10.cloned.1.call-done = bf16[4096,2048]{1,0:T(8,128)(2,1)} async-done(((bf16[512,2048]{1,0:T(8,128)(2,1)}), bf16[4096,2048]{1,0:T(8,128)(2,1)}) %all-gather.10.cloned.1.call-update) | async-done | bytes 16777232 | tf_op jit(solution)/shard_map/all_gather | solution.py:333
  472.0 23.1 %fusion.32 = f32[4096,1024]{1,0:T(8,128)S(1)} fusion(bf16[4096,2048]{1,0:T(8,128)(2,1)} %all-gather.10.cloned.1.call-done, bf16[1024,2048]{1,0:T(8,128)(2,1)} %bitcast.268), kind=kOutput, calls=%fused_computation.153 | convolution fusion | flops 17179869184 | bytes 37748736 | tf_op jit(solution)/shard_map/dot_general | solution.py:26
  495.0 8.0 multiply_convert_fusion.1
  503.1 15.0 %convolution_convert_fusion.1 = bf16[4096,2048]{1,0:T(8,128)(2,1)} fusion(bf16[4096,512]{1,0:T(8,128)(2,1)} %get-tuple-element.102, bf16[512,2048]{1,0:T(8,128)(2,1)} %bitcast.286), kind=kOutput, calls=%fused_computation.2 | convolution fusion | flops 8598323200 | bytes 23068672 | tf_op jit(solution)/shard_map/dot_general | solution.py:26
  518.1 5.6 fusion.13
  524.3 10.9 convolution_convert_fusion.3
  535.5 18.0 %collective-permute-done.15 = bf16[2048,2048]{1,0:T(8,128)(2,1)} collective-permute-done((bf16[2048,2048]{1,0:T(8,128)(2,1)}, bf16[2048,2048]{1,0:T(8,128)(2,1)}, u32[]{:S(2)}, u32[]{:S(2)}) %collective-permute-start.15) | collective-permute-done | bytes 8388640 | tf_op jit(solution)/shard_map/ppermute | solution.py:240
  553.5 13.1 add_convert_fusion
  575.5 80.8 %collective-permute-done.16 = bf16[2,256,2048]{2,1,0:T(8,128)(2,1)} collective-permute-done((bf16[2,256,2048]{2,1,0:T(8,128)(2,1)S(1)}, bf16[2,256,2048]{2,1,0:T(8,128)(2,1)}, u32[]{:S(2)}, u32[]{:S(2)}) %collective-permute-start.16) | collective-permute-done | bytes 2097184 | tf_op jit(solution)/shard_map/ppermute | solution.py:240
  668.0 8.0 pad_maximum_fusion
  676.0 27.5 %collective-permute-done.17 = bf16[256,2048]{1,0:T(8,128)(2,1)S(1)} collective-permute-done((bf16[256,2048]{1,0:T(8,128)(2,1)}, bf16[256,2048]{1,0:T(8,128)(2,1)S(1)}, u32[]{:S(2)}, u32[]{:S(2)}) %collective-permute-start.17) | collective-permute-done | bytes 1048608 | tf_op jit(solution)/shard_map/ppermute | solution.py:240
  710.8 3.9 multiply_reduce_fusion
  714.7 4.2 add_convert_fusion.1
  719.0 4.7 collective-permute-start.23
  725.0 25.0 %convolution_convert_fusion.5 = bf16[1024,2048]{1,0:T(8,128)(2,1)S(1)} fusion(bf16[4096,1024]{1,0:T(8,128)(2,1)} %pad_maximum_fusion, bf16[4096,2048]{1,0:T(8,128)(2,1)} %all-gather.10.cloned.1.call-done), kind=kOutput, calls=%fused_computation.49 | convolution fusion | flops 17181966336 | bytes 29360128 | tf_op jit(solution)/shard_map/dot_general | solution.py:26
  752.3 12.4 convolution_convert_fusion.7
  765.9 3.6 slice_convert_fusion.2
  771.0 5.5 collective-permute-start.20
  779.7 4.1 collective-permute-start.22
  787.8 22.6 %collective-permute-done.20 = bf16[8,384,256]{2,1,0:T(8,128)(2,1)} collective-permute-done((bf16[8,384,256]{2,1,0:T(8,128)(2,1)}, bf16[8,384,256]{2,1,0:T(8,128)(2,1)}, u32[]{:S(2)}, u32[]{:S(2)}) %collective-permute-start.20) | collective-permute-done | bytes 1572896 | tf_op jit(solution)/shard_map/ppermute | solution.py:289
  810.4 32.4 %collective-permute-done.22 = bf16[8,384,256]{2,1,0:T(8,128)(2,1)} collective-permute-done((bf16[8,384,256]{2,1,0:T(8,128)(2,1)}, bf16[8,384,256]{2,1,0:T(8,128)(2,1)}, u32[]{:S(2)}, u32[]{:S(2)}) %collective-permute-start.22) | collective-permute-done | bytes 1572896 | tf_op jit(solution)/shard_map/ppermute | solution.py:289
  850.7 18.1 %convolution_convert_fusion.4.g_ref = bf16[256,4096]{1,0:T(8,128)(2,1)} fusion(bf16[256,2048]{1,0:T(8,128)(2,1)S(1)} %bitcast.263, bf16[4096,2048]{1,0:T(8,128)(2,1)} %all-gather.12.cloned.1.call-done), kind=kOutput, calls=%fused_computation.25 | convolution fusion | flops 4296015872 | bytes 19922944 | tf_op jit(solution)/shard_map/dot_general | solution.py:26
  868.8 93.1 %attend_back.1 = (f32[256,4096]{1,0:T(8,128)}, f32[256,4096]{1,0:T(8,128)}, f32[256,4096]{1,0:T(8,128)}) custom-call(s32[8]{0:T(128)} %get-tuple-element.72.lo_ref, s32[8]{0:T(128)} %get-tuple-element.73.full_ref, s32[1,4096]{1,0:T(1,128)} %add_maximum_fusion.low_ref, bf16[256,4096]{1,0:T(8,128)(2,1)} %bitcast.284, ...), custom_call_target="tpu_custom_call" | custom-call | flops 103079215104 | bytes 25165824 | tf_op jit(solution)/shard_map/attend_back/pallas_call | solution.py:182
  972.4 9.4 pad_maximum_fusion.1
  981.8 19.7 %convolution_convert_fusion = bf16[4096,2048]{1,0:T(8,128)(2,1)} fusion(bf16[768,2048]{1,0:T(8,128)(2,1)} %bitcast.280, bf16[256,4096]{1,0:T(8,128)(2,1)} %copy-done.23, bf16[256,4096]{1,0:T(8,128)(2,1)} %bitcast.254, bf16[256,4096]{1,0:T(8,128)(2,1)S(1)} %bitcast.252), kind=kOutput, calls=%fused_computation.1 | convolution fusion | flops 12912164864 | bytes 26214400 | tf_op jit(solution)/shard_map/dot_general | solution.py:26
  1003.0 9.6 convolution_convert_fusion.8
  1013.0 21.1 %convolution_convert_fusion.6 = bf16[768,2048]{1,0:T(8,128)(2,1)S(1)} fusion(bf16[768,4096]{1,0:T(8,128)(2,1)} %pad_maximum_fusion.1, bf16[4096,2048]{1,0:T(8,128)(2,1)} %all-gather.6.cloned.1.call-done), kind=kOutput, calls=%fused_computation.50 | convolution fusion | flops 12886474752 | bytes 26214400 | tf_op jit(solution)/shard_map/dot_general | solution.py:26
  1050.5 3.9 add_convert_fusion.3
  1058.3 6.8 collective-permute-done.30
  1065.1 22.5 %collective-permute-done.31 = bf16[8,256,256]{2,0,1:T(8,128)(2,1)} collective-permute-done((bf16[8,256,256]{2,0,1:T(8,128)(2,1)}, bf16[8,256,256]{2,0,1:T(8,128)(2,1)}, u32[]{:S(2)}, u32[]{:S(2)}) %collective-permute-start.31) | collective-permute-done | bytes 1048608 | tf_op jit(solution)/shard_map/ppermute | solution.py:289
  1087.6 4.0 fusion.18
  1096.7 21.1 %reduce-scatter.8.cloned.1.call-done = bf16[512,2048]{1,0:T(8,128)(2,1)} async-done(((bf16[4096,2048]{1,0:T(8,128)(2,1)}), bf16[512,2048]{1,0:T(8,128)(2,1)}) %reduce-scatter.8.cloned.1.call-update) | async-done | bytes 2097168 | tf_op jit(solution)/shard_map/reduce_scatter | solution.py:336
  1121.2 20.3 %collective-permute-done.32 = bf16[8,256,256]{2,0,1:T(8,128)(2,1)} collective-permute-done((bf16[8,256,256]{2,0,1:T(8,128)(2,1)}, bf16[8,256,256]{2,0,1:T(8,128)(2,1)}, u32[]{:S(2)}, u32[]{:S(2)}) %collective-permute-start.32) | collective-permute-done | bytes 1048608 | tf_op jit(solution)/shard_map/ppermute | solution.py:289
  1144.2 5.4 fusion.10
  1169.4 3.6 all-to-all-start.4
  1176.2 3.7 add_convert_fusion.2
  1179.9 8.5 all-to-all-done.4
  1188.3 3.6 all-to-all-start.5
  1195.1 4.5 collective-permute-start.35
  1204.1 7.3 collective-permute-done.36
  1214.9 8.5 constant_dynamic-slice_fusion
  1233.0 69.2 %all-gather.14.cloned.1.call-done = bf16[2048,2048]{1,0:T(8,128)(2,1)} async-done(((bf16[512,2048]{1,0:T(8,128)(2,1)}), bf16[2048,2048]{1,0:T(8,128)(2,1)}) %all-gather.14.cloned.1.call-update) | async-done | bytes 8388624 | tf_op jit(solution)/shard_map/all_gather | solution.py:537
  1302.2 11.7 convert.79
  (327 shorter events, 225.8 us)
Async XLA Ops:
  7.2 113.4 %all-gather.6.cloned.1.call-start = ((), (), s32[]{:S(2)}) async-start(), calls=%async_computation.9 | async-start | bytes 18874368 | tf_op jit(solution)/shard_map/all_gather | solution.py:333
  19.9 358.3 %copy-start.44 = (f32[1,2048]{1,0:T(1,128)}, f32[1,2048]{1,0:T(1,128)S(1)}, u32[]{:S(2)}) copy-start(f32[1,2048]{1,0:T(1,128)S(1)} %get-tuple-element.211) | copy-start | bytes 24580
  24.6 20.8 %all-to-all-start = ((bf16[8,192,256]{2,1,0:T(8,128)(2,1)}), bf16[8,192,256]{2,1,0:T(8,128)(2,1)S(1)}, u32[]{:S(2)}, u32[]{:S(2)}) async-start(bf16[8,192,256]{2,1,0:T(8,128)(2,1)} %bitcast.6), calls=%async_computation | async-start | bytes 1572864 | tf_op jit(solution)/shard_map/all_to_all | solution.py:286
  28.2 47.6 %copy-start.38 = (bf16[2,256,1024]{2,1,0:T(8,128)(2,1)S(1)}, bf16[2,256,1024]{2,1,0:T(8,128)(2,1)}, u32[]{:S(2)}) copy-start(bf16[2,256,1024]{2,1,0:T(8,128)(2,1)} %param.13) | copy-start | bytes 3145732
  45.4 16.5 %collective-permute-start = (bf16[8,192,256]{2,1,0:T(8,128)(2,1)S(1)}, bf16[8,192,256]{2,1,0:T(8,128)(2,1)}, u32[]{:S(2)}, u32[]{:S(2)}) collective-permute-start(bf16[8,192,256]{2,1,0:T(8,128)(2,1)S(1)} %all-to-all-done), channel_id=1, source_target_pairs={{0,1},{1,2},{2,3},{4,5},{5,6},{6,7},{8,9},{9,10},{10,11},{12,13},{... | collective-permute-start | bytes 2359304 | tf_op jit(solution)/shard_map/ppermute | solution.py:289
  49.8 17.3 %collective-permute-start.1 = (bf16[8,192,256]{2,1,0:T(8,128)(2,1)S(1)}, bf16[8,192,256]{2,1,0:T(8,128)(2,1)}, u32[]{:S(2)}, u32[]{:S(2)}) collective-permute-start(bf16[8,192,256]{2,1,0:T(8,128)(2,1)S(1)} %all-to-all-done), channel_id=1, source_target_pairs={{1,0},{2,1},{3,2},{5,4},{6,5},{7,6},{9,8},{10,9},{11,10},{13,12},{... | collective-permute-start | bytes 2359304 | tf_op jit(solution)/shard_map/ppermute | solution.py:289
  61.9 20.4 %collective-permute-start.3 = (bf16[8,192,256]{2,1,0:T(8,128)(2,1)}, bf16[8,192,256]{2,1,0:T(8,128)(2,1)}, u32[]{:S(2)}, u32[]{:S(2)}) collective-permute-start(bf16[8,192,256]{2,1,0:T(8,128)(2,1)} %collective-permute-done), channel_id=1, source_target_pairs={{1,2},{2,3},{5,6},{6,7},{9,10},{10,11},{13,14},{14,15},{17,18},{18... | collective-permute-start | bytes 2359304 | tf_op jit(solution)/shard_map/ppermute | solution.py:289
  67.1 22.1 %collective-permute-start.4 = (bf16[8,192,256]{2,1,0:T(8,128)(2,1)}, bf16[8,192,256]{2,1,0:T(8,128)(2,1)}, u32[]{:S(2)}, u32[]{:S(2)}) collective-permute-start(bf16[8,192,256]{2,1,0:T(8,128)(2,1)} %collective-permute-done.1), channel_id=1, source_target_pairs={{1,0},{2,1},{5,4},{6,5},{9,8},{10,9},{13,12},{14,13},{17,16},{18,1... | collective-permute-start | bytes 2359304 | tf_op jit(solution)/shard_map/ppermute | solution.py:289
  70.7 30.9 %collective-permute-start.2 = (bf16[8,192,256]{2,1,0:T(8,128)(2,1)}, bf16[8,192,256]{2,1,0:T(8,128)(2,1)}, u32[]{:S(2)}, u32[]{:S(2)}) collective-permute-start(bf16[8,192,256]{2,1,0:T(8,128)(2,1)} %broadcast_select_fusion.6), channel_id=1, source_target_pairs={{1,3},{2,0},{5,7},{6,4},{9,11},{10,8},{13,15},{14,12},{17,19},{18,... | collective-permute-start | bytes 2359304 | tf_op jit(solution)/shard_map/ppermute | solution.py:289
  76.4 34.6 %all-to-all-start.1 = ((bf16[8,64,256]{2,1,0:T(8,128)(2,1)}), bf16[8,64,256]{2,1,0:T(8,128)(2,1)S(1)}, u32[]{:S(2)}, u32[]{:S(2)}) async-start(bf16[8,64,256]{2,1,0:T(8,128)(2,1)} %bitcast.15), calls=%async_computation.1 | async-start | bytes 524288 | tf_op jit(solution)/shard_map/all_to_all | solution.py:286
  79.9 158.1 %all-gather.8.cloned.1.call-start = ((), (), s32[]{:S(2)}) async-start(), calls=%async_computation.10 | async-start | bytes 18874368 | tf_op jit(solution)/shard_map/all_gather | solution.py:333
  111.0 39.9 %copy-start.34 = (bf16[3,4,64,2048]{3,2,1,0:T(8,128)(2,1)}, bf16[3,4,64,2048]{3,2,1,0:T(8,128)(2,1)S(1)}, u32[]{:S(2)}) copy-start(bf16[3,4,64,2048]{3,2,1,0:T(8,128)(2,1)S(1)} %copy.129) | copy-start | bytes 9437188
  120.6 49.1 %collective-permute-start.5 = (bf16[8,64,256]{2,1,0:T(8,128)(2,1)}, bf16[8,64,256]{2,1,0:T(8,128)(2,1)S(1)}, u32[]{:S(2)}, u32[]{:S(2)}) collective-permute-start(bf16[8,64,256]{2,1,0:T(8,128)(2,1)} %copy-done.39), channel_id=1, source_target_pairs={{0,1},{1,2},{2,3},{4,5},{5,6},{6,7},{8,9},{9,10},{10,11},{12,13},{... | collective-permute-start | bytes 786440 | tf_op jit(solution)/shard_map/ppermute | solution.py:289
  124.0 45.7 %collective-permute-start.6 = (bf16[8,64,256]{2,1,0:T(8,128)(2,1)}, bf16[8,64,256]{2,1,0:T(8,128)(2,1)}, u32[]{:S(2)}, u32[]{:S(2)}) collective-permute-start(bf16[8,64,256]{2,1,0:T(8,128)(2,1)} %copy-done.39), channel_id=1, source_target_pairs={{1,0},{2,1},{3,2},{5,4},{6,5},{7,6},{9,8},{10,9},{11,10},{13,12},{... | collective-permute-start | bytes 786440 | tf_op jit(solution)/shard_map/ppermute | solution.py:289
  125.3 44.4 %all-to-all-start.2 = ((bf16[8,384,256]{2,1,0:T(8,128)(2,1)}), bf16[8,384,256]{2,1,0:T(8,128)(2,1)}, u32[]{:S(2)}, u32[]{:S(2)}) async-start(bf16[8,384,256]{2,1,0:T(8,128)(2,1)} %pad_maximum_fusion.5), calls=%async_computation.2 | async-start | bytes 3145728 | tf_op jit(solution)/shard_map/all_to_all | solution.py:286
  129.6 244.2 %reduce-scatter.4.cloned.1.call-start = ((), (), s32[]{:S(2)}) async-start(), calls=%async_computation.11 | async-start | bytes 18874368 | tf_op jit(solution)/shard_map/reduce_scatter | solution.py:336
  169.7 67.5 %collective-permute-start.7 = (bf16[8,384,256]{2,1,0:T(8,128)(2,1)}, bf16[8,384,256]{2,1,0:T(8,128)(2,1)S(1)}, u32[]{:S(2)}, u32[]{:S(2)}) collective-permute-start(bf16[8,384,256]{2,1,0:T(8,128)(2,1)} %all-to-all-done.2), channel_id=1, source_target_pairs={{0,1},{1,2},{2,3},{4,5},{5,6},{6,7},{8,9},{9,10},{10,11},{12,13},{... | collective-permute-start | bytes 4718600 | tf_op jit(solution)/shard_map/ppermute | solution.py:289
  174.2 63.8 %collective-permute-start.8 = (bf16[8,384,256]{2,1,0:T(8,128)(2,1)}, bf16[8,384,256]{2,1,0:T(8,128)(2,1)S(1)}, u32[]{:S(2)}, u32[]{:S(2)}) collective-permute-start(bf16[8,384,256]{2,1,0:T(8,128)(2,1)} %all-to-all-done.2), channel_id=1, source_target_pairs={{1,0},{2,1},{3,2},{5,4},{6,5},{7,6},{9,8},{10,9},{11,10},{13,12},{... | collective-permute-start | bytes 4718600 | tf_op jit(solution)/shard_map/ppermute | solution.py:289
  175.5 61.6 %collective-permute-start.10 = (bf16[8,64,256]{2,1,0:T(8,128)(2,1)}, bf16[8,64,256]{2,1,0:T(8,128)(2,1)S(1)}, u32[]{:S(2)}, u32[]{:S(2)}) collective-permute-start(bf16[8,64,256]{2,1,0:T(8,128)(2,1)} %collective-permute-done.6), channel_id=1, source_target_pairs={{1,0},{2,1},{5,4},{6,5},{9,8},{10,9},{13,12},{14,13},{17,16},{18,1... | collective-permute-start | bytes 786440 | tf_op jit(solution)/shard_map/ppermute | solution.py:289
  176.8 60.4 %collective-permute-start.9 = (bf16[8,64,256]{2,1,0:T(8,128)(2,1)S(1)}, bf16[8,64,256]{2,1,0:T(8,128)(2,1)S(1)}, u32[]{:S(2)}, u32[]{:S(2)}) collective-permute-start(bf16[8,64,256]{2,1,0:T(8,128)(2,1)S(1)} %collective-permute-done.5), channel_id=1, source_target_pairs={{1,2},{2,3},{5,6},{6,7},{9,10},{10,11},{13,14},{14,15},{17,18},{18... | collective-permute-start | bytes 786440 | tf_op jit(solution)/shard_map/ppermute | solution.py:289
  178.5 58.6 %collective-permute-start.11 = (bf16[8,64,256]{2,1,0:T(8,128)(2,1)S(1)}, bf16[8,64,256]{2,1,0:T(8,128)(2,1)S(1)}, u32[]{:S(2)}, u32[]{:S(2)}) collective-permute-start(bf16[8,64,256]{2,1,0:T(8,128)(2,1)S(1)} %broadcast_select_fusion.7), channel_id=1, source_target_pairs={{1,3},{2,0},{5,7},{6,4},{9,11},{10,8},{13,15},{14,12},{17,19},{18,... | collective-permute-start | bytes 786440 | tf_op jit(solution)/shard_map/ppermute | solution.py:289
  255.7 216.3 %all-gather.10.cloned.1.call-start = ((), (), s32[]{:S(2)}) async-start(), calls=%async_computation.12 | async-start | bytes 18874368 | tf_op jit(solution)/shard_map/all_gather | solution.py:333
  257.0 118.9 %collective-permute-start.14 = (bf16[8,384,256]{2,1,0:T(8,128)(2,1)}, bf16[8,384,256]{2,1,0:T(8,128)(2,1)}, u32[]{:S(2)}, u32[]{:S(2)}) collective-permute-start(bf16[8,384,256]{2,1,0:T(8,128)(2,1)} %broadcast_select_fusion.5), channel_id=1, source_target_pairs={{1,3},{2,0},{5,7},{6,4},{9,11},{10,8},{13,15},{14,12},{17,19},{18,... | collective-permute-start | bytes 4718600 | tf_op jit(solution)/shard_map/ppermute | solution.py:289
  258.3 117.6 %collective-permute-start.12 = (bf16[8,384,256]{2,1,0:T(8,128)(2,1)S(1)}, bf16[8,384,256]{2,1,0:T(8,128)(2,1)}, u32[]{:S(2)}, u32[]{:S(2)}) collective-permute-start(bf16[8,384,256]{2,1,0:T(8,128)(2,1)S(1)} %collective-permute-done.7), channel_id=1, source_target_pairs={{1,2},{2,3},{5,6},{6,7},{9,10},{10,11},{13,14},{14,15},{17,18},{18... | collective-permute-start | bytes 4718600 | tf_op jit(solution)/shard_map/ppermute | solution.py:289
  260.1 115.8 %collective-permute-start.13 = (bf16[8,384,256]{2,1,0:T(8,128)(2,1)S(1)}, bf16[8,384,256]{2,1,0:T(8,128)(2,1)}, u32[]{:S(2)}, u32[]{:S(2)}) collective-permute-start(bf16[8,384,256]{2,1,0:T(8,128)(2,1)S(1)} %collective-permute-done.8), channel_id=1, source_target_pairs={{1,0},{2,1},{5,4},{6,5},{9,8},{10,9},{13,12},{14,13},{17,16},{18,1... | collective-permute-start | bytes 4718600 | tf_op jit(solution)/shard_map/ppermute | solution.py:289
  382.0 326.0 %reduce-scatter.6.cloned.1.call-start = ((), (), s32[]{:S(2)}) async-start(), calls=%async_computation.13 | async-start | bytes 18874368 | tf_op jit(solution)/shard_map/reduce_scatter | solution.py:336
  518.1 324.7 %all-gather.12.cloned.1.call-start = ((), (), s32[]{:S(2)}) async-start(), calls=%async_computation.14 | async-start | bytes 18874368 | tf_op jit(solution)/shard_map/all_gather | solution.py:333
  535.2 18.3 %collective-permute-start.15 = (bf16[2048,2048]{1,0:T(8,128)(2,1)}, bf16[2048,2048]{1,0:T(8,128)(2,1)}, u32[]{:S(2)}, u32[]{:S(2)}) collective-permute-start(bf16[2048,2048]{1,0:T(8,128)(2,1)} %convolution_convert_fusion.3), channel_id=1, source_target_pairs={{0,4},{4,0},{1,5},{5,1},{2,6},{6,2},{3,7},{7,3},{8,12},{12,8},{9,1... | collective-permute-start | bytes 25165832 | tf_op jit(solution)/shard_map/ppermute | solution.py:240
  571.2 85.1 %collective-permute-start.16 = (bf16[2,256,2048]{2,1,0:T(8,128)(2,1)S(1)}, bf16[2,256,2048]{2,1,0:T(8,128)(2,1)}, u32[]{:S(2)}, u32[]{:S(2)}) collective-permute-start(bf16[2,256,2048]{2,1,0:T(8,128)(2,1)S(1)} %dynamic-slice_bitcast_fusion.1), channel_id=1, source_target_pairs={{0,8},{8,0},{1,9},{9,1},{2,10},{10,2},{3,11},{11,3},{4,12},{12,4},... | collective-permute-start | bytes 6291464 | tf_op jit(solution)/shard_map/ppermute | solution.py:240
  574.5 87.9 %collective-permute-start.18 = (bf16[2,256,2048]{2,1,0:T(8,128)(2,1)}, bf16[2,256,2048]{2,1,0:T(8,128)(2,1)}, u32[]{:S(2)}, u32[]{:S(2)}) collective-permute-start(bf16[2,256,2048]{2,1,0:T(8,128)(2,1)} %dynamic-slice_bitcast_fusion), channel_id=1, source_target_pairs={{0,16},{16,0},{1,17},{17,1},{2,18},{18,2},{3,19},{19,3},{4,20},{20... | collective-permute-start | bytes 6291464 | tf_op jit(solution)/shard_map/ppermute | solution.py:240
  575.5 86.9 %copy-start.10 = (bf16[2,2,256,2048]{3,2,1,0:T(8,128)(2,1)S(1)}, bf16[2,2,256,2048]{3,2,1,0:T(8,128)(2,1)}, u32[]{:S(2)}) copy-start(bf16[2,2,256,2048]{3,2,1,0:T(8,128)(2,1)} %get-tuple-element.178) | copy-start | bytes 12582916
  660.7 42.9 %collective-permute-start.17 = (bf16[256,2048]{1,0:T(8,128)(2,1)}, bf16[256,2048]{1,0:T(8,128)(2,1)S(1)}, u32[]{:S(2)}, u32[]{:S(2)}) collective-permute-start(bf16[256,2048]{1,0:T(8,128)(2,1)} %dynamic-slice_bitcast_fusion.4), channel_id=1, source_target_pairs={{0,16},{16,0},{1,17},{17,1},{2,18},{18,2},{3,19},{19,3},{4,20},{20... | collective-permute-start | bytes 3145736 | tf_op jit(solution)/shard_map/ppermute | solution.py:240
  667.4 36.5 %collective-permute-start.19 = (bf16[256,2048]{1,0:T(8,128)(2,1)}, bf16[256,2048]{1,0:T(8,128)(2,1)}, u32[]{:S(2)}, u32[]{:S(2)}) collective-permute-start(bf16[256,2048]{1,0:T(8,128)(2,1)} %dynamic-slice_bitcast_fusion.3), channel_id=1, source_target_pairs={{0,8},{8,0},{1,9},{9,1},{2,10},{10,2},{3,11},{11,3},{4,12},{12,4},... | collective-permute-start | bytes 3145736 | tf_op jit(solution)/shard_map/ppermute | solution.py:240
  676.0 27.9 %copy-start.16 = (bf16[2,256,2048]{2,1,0:T(8,128)(2,1)S(1)}, bf16[2,256,2048]{2,1,0:T(8,128)(2,1)}, u32[]{:S(2)}) copy-start(bf16[2,256,2048]{2,1,0:T(8,128)(2,1)} %copy-done.15) | copy-start | bytes 6291460
  719.0 398.8 %reduce-scatter.8.cloned.1.call-start = ((), (), s32[]{:S(2)}) async-start(), calls=%async_computation.15 | async-start | bytes 18874368 | tf_op jit(solution)/shard_map/reduce_scatter | solution.py:336
  719.0 123.7 %collective-permute-start.23 = (bf16[512,2048]{1,0:T(8,128)(2,1)}, bf16[512,2048]{1,0:T(8,128)(2,1)}, u32[]{:S(2)}, u32[]{:S(2)}) collective-permute-start(bf16[512,2048]{1,0:T(8,128)(2,1)} %get-tuple-element.197), channel_id=1, source_target_pairs={{0,1},{1,2},{2,3},{4,5},{5,6},{6,7},{8,9},{9,10},{10,11},{12,13},{... | collective-permute-start | bytes 6291464 | tf_op jit(solution)/shard_map/ppermute | solution.py:289
  723.7 119.0 %collective-permute-start.24 = (bf16[512,2048]{1,0:T(8,128)(2,1)}, bf16[512,2048]{1,0:T(8,128)(2,1)}, u32[]{:S(2)}, u32[]{:S(2)}) collective-permute-start(bf16[512,2048]{1,0:T(8,128)(2,1)} %get-tuple-element.197), channel_id=1, source_target_pairs={{1,0},{2,1},{3,2},{5,4},{6,5},{7,6},{9,8},{10,9},{11,10},{13,12},{... | collective-permute-start | bytes 6291464 | tf_op jit(solution)/shard_map/ppermute | solution.py:289
  771.0 39.4 %collective-permute-start.20 = (bf16[8,384,256]{2,1,0:T(8,128)(2,1)}, bf16[8,384,256]{2,1,0:T(8,128)(2,1)}, u32[]{:S(2)}, u32[]{:S(2)}) collective-permute-start(bf16[8,384,256]{2,1,0:T(8,128)(2,1)} %bitcast.55), channel_id=1, source_target_pairs={{0,1},{1,2},{4,5},{5,6},{8,9},{9,10},{12,13},{13,14},{16,17},{17,1... | collective-permute-start | bytes 4718600 | tf_op jit(solution)/shard_map/ppermute | solution.py:289
  776.5 33.9 %collective-permute-start.21 = (bf16[8,384,256]{2,1,0:T(8,128)(2,1)}, bf16[8,384,256]{2,1,0:T(8,128)(2,1)}, u32[]{:S(2)}, u32[]{:S(2)}) collective-permute-start(bf16[8,384,256]{2,1,0:T(8,128)(2,1)} %bitcast.55), channel_id=1, source_target_pairs={{2,1},{3,2},{6,5},{7,6},{10,9},{11,10},{14,13},{15,14},{18,17},{19... | collective-permute-start | bytes 4718600 | tf_op jit(solution)/shard_map/ppermute | solution.py:289
  779.7 63.0 %collective-permute-start.22 = (bf16[8,384,256]{2,1,0:T(8,128)(2,1)}, bf16[8,384,256]{2,1,0:T(8,128)(2,1)}, u32[]{:S(2)}, u32[]{:S(2)}) collective-permute-start(bf16[8,384,256]{2,1,0:T(8,128)(2,1)} %bitcast.56), channel_id=1, source_target_pairs={{0,2},{3,1},{4,6},{7,5},{8,10},{11,9},{12,14},{15,13},{16,18},{19,... | collective-permute-start | bytes 4718600 | tf_op jit(solution)/shard_map/ppermute | solution.py:289
  786.9 63.7 %copy-start.29 = (bf16[32,8,8,256]{3,1,2,0:T(8,128)(2,1)S(1)}, bf16[32,8,8,256]{3,1,2,0:T(8,128)(2,1)}, u32[]{:S(2)}) copy-start(bf16[32,8,8,256]{3,1,2,0:T(8,128)(2,1)} %copy.159) | copy-start | bytes 3145732
  842.8 119.1 %collective-permute-start.25 = (bf16[512,2048]{1,0:T(8,128)(2,1)}, bf16[512,2048]{1,0:T(8,128)(2,1)}, u32[]{:S(2)}, u32[]{:S(2)}) collective-permute-start(bf16[512,2048]{1,0:T(8,128)(2,1)} %collective-permute-done.23), channel_id=1, source_target_pairs={{1,2},{2,3},{5,6},{6,7},{9,10},{10,11},{13,14},{14,15},{17,18},{18... | collective-permute-start | bytes 6291464 | tf_op jit(solution)/shard_map/ppermute | solution.py:289
  847.9 114.0 %collective-permute-start.26 = (bf16[512,2048]{1,0:T(8,128)(2,1)}, bf16[512,2048]{1,0:T(8,128)(2,1)}, u32[]{:S(2)}, u32[]{:S(2)}) collective-permute-start(bf16[512,2048]{1,0:T(8,128)(2,1)} %collective-permute-done.24), channel_id=1, source_target_pairs={{1,0},{2,1},{5,4},{6,5},{9,8},{10,9},{13,12},{14,13},{17,16},{18,1... | collective-permute-start | bytes 6291464 | tf_op jit(solution)/shard_map/ppermute | solution.py:289
  849.2 112.7 %collective-permute-start.27 = (bf16[512,2048]{1,0:T(8,128)(2,1)}, bf16[512,2048]{1,0:T(8,128)(2,1)S(1)}, u32[]{:S(2)}, u32[]{:S(2)}) collective-permute-start(bf16[512,2048]{1,0:T(8,128)(2,1)} %broadcast_select_fusion), channel_id=1, source_target_pairs={{1,3},{2,0},{5,7},{6,4},{9,11},{10,8},{13,15},{14,12},{17,19},{18,... | collective-permute-start | bytes 6291464 | tf_op jit(solution)/shard_map/ppermute | solution.py:289
  1001.5 300.7 %all-gather.14.cloned.1.call-start = ((), (), s32[]{:S(2)}) async-start(), calls=%async_computation.16 | async-start | bytes 10485760 | tf_op jit(solution)/shard_map/all_gather | solution.py:537
  1039.6 25.5 %collective-permute-start.30 = (bf16[8,256,256]{2,0,1:T(8,128)(2,1)}, bf16[8,256,256]{2,0,1:T(8,128)(2,1)}, u32[]{:S(2)}, u32[]{:S(2)}) collective-permute-start(bf16[8,256,256]{2,0,1:T(8,128)(2,1)} %get-tuple-element.195), channel_id=1, source_target_pairs={{0,1},{1,2},{4,5},{5,6},{8,9},{9,10},{12,13},{13,14},{16,17},{17,1... | collective-permute-start | bytes 3145736 | tf_op jit(solution)/shard_map/ppermute | solution.py:289
  1042.2 45.4 %collective-permute-start.31 = (bf16[8,256,256]{2,0,1:T(8,128)(2,1)}, bf16[8,256,256]{2,0,1:T(8,128)(2,1)}, u32[]{:S(2)}, u32[]{:S(2)}) collective-permute-start(bf16[8,256,256]{2,0,1:T(8,128)(2,1)} %get-tuple-element.194), channel_id=1, source_target_pairs={{0,2},{3,1},{4,6},{7,5},{8,10},{11,9},{12,14},{15,13},{16,18},{19,... | collective-permute-start | bytes 3145736 | tf_op jit(solution)/shard_map/ppermute | solution.py:289
  1044.5 43.1 %collective-permute-start.33 = (bf16[8,256,256]{2,0,1:T(8,128)(2,1)}, bf16[8,256,256]{2,0,1:T(8,128)(2,1)}, u32[]{:S(2)}, u32[]{:S(2)}) collective-permute-start(bf16[8,256,256]{2,0,1:T(8,128)(2,1)} %get-tuple-element.195), channel_id=1, source_target_pairs={{2,1},{3,2},{6,5},{7,6},{10,9},{11,10},{14,13},{15,14},{18,17},{19... | collective-permute-start | bytes 3145736 | tf_op jit(solution)/shard_map/ppermute | solution.py:289
  1050.5 37.1 %copy-start.9 = (bf16[4,1,256,8,256]{4,3,2,0,1:T(8,128)(2,1)S(1)}, bf16[4,1,256,8,256]{4,3,2,0,1:T(8,128)(2,1)}, u32[]{:S(2)}) copy-start(bf16[4,1,256,8,256]{4,3,2,0,1:T(8,128)(2,1)} %copy-done.8) | copy-start | bytes 12582916
  1054.4 40.8 %copy-start.26 = (bf16[1,8,3,128,256]{4,1,3,0,2:T(8,128)(2,1)S(1)}, bf16[1,8,3,128,256]{4,1,3,0,2:T(8,128)(2,1)}, u32[]{:S(2)}) copy-start(bf16[1,8,3,128,256]{4,1,3,0,2:T(8,128)(2,1)} %get-tuple-element.183) | copy-start | bytes 4718596
  1054.4 66.8 %collective-permute-start.28 = (bf16[8,384,256]{2,1,0:T(8,128)(2,1)S(1)}, bf16[8,384,256]{2,1,0:T(8,128)(2,1)}, u32[]{:S(2)}, u32[]{:S(2)}) collective-permute-start(bf16[8,384,256]{2,1,0:T(8,128)(2,1)S(1)} %get-tuple-element.200), channel_id=1, source_target_pairs={{0,1},{1,2},{2,3},{4,5},{5,6},{6,7},{8,9},{9,10},{10,11},{12,13},{... | collective-permute-start | bytes 4718600 | tf_op jit(solution)/shard_map/ppermute | solution.py:289
  1057.0 64.2 %collective-permute-start.29 = (bf16[8,384,256]{2,1,0:T(8,128)(2,1)S(1)}, bf16[8,384,256]{2,1,0:T(8,128)(2,1)}, u32[]{:S(2)}, u32[]{:S(2)}) collective-permute-start(bf16[8,384,256]{2,1,0:T(8,128)(2,1)S(1)} %get-tuple-element.199), channel_id=1, source_target_pairs={{1,0},{2,1},{3,2},{5,4},{6,5},{7,6},{9,8},{10,9},{11,10},{13,12},{... | collective-permute-start | bytes 4718600 | tf_op jit(solution)/shard_map/ppermute | solution.py:289
  1091.6 49.8 %collective-permute-start.32 = (bf16[8,256,256]{2,0,1:T(8,128)(2,1)}, bf16[8,256,256]{2,0,1:T(8,128)(2,1)}, u32[]{:S(2)}, u32[]{:S(2)}) collective-permute-start(bf16[8,256,256]{2,0,1:T(8,128)(2,1)} %get-tuple-element.204), channel_id=1, source_target_pairs={{0,1},{1,2},{2,3},{4,5},{5,6},{6,7},{8,9},{9,10},{10,11},{12,13},{... | collective-permute-start | bytes 3145736 | tf_op jit(solution)/shard_map/ppermute | solution.py:289
  1093.9 47.5 %collective-permute-start.34 = (bf16[8,256,256]{2,0,1:T(8,128)(2,1)}, bf16[8,256,256]{2,0,1:T(8,128)(2,1)}, u32[]{:S(2)}, u32[]{:S(2)}) collective-permute-start(bf16[8,256,256]{2,0,1:T(8,128)(2,1)} %get-tuple-element.203), channel_id=1, source_target_pairs={{1,0},{2,1},{3,2},{5,4},{6,5},{7,6},{9,8},{10,9},{11,10},{13,12},{... | collective-permute-start | bytes 3145736 | tf_op jit(solution)/shard_map/ppermute | solution.py:289
  1095.2 46.2 %copy-start.48 = (f32[1,2048]{1,0:T(1,128)S(1)}, f32[1,2048]{1,0:T(1,128)}, u32[]{:S(2)}) copy-start(f32[1,2048]{1,0:T(1,128)} %copy-done.47) | copy-start | bytes 24580
  1095.2 46.2 %copy-start.53 = (f32[512]{0:T(512)S(1)}, f32[512]{0:T(512)}, u32[]{:S(2)}) copy-start(f32[512]{0:T(512)} %copy-done.52) | copy-start | bytes 6148
  1161.4 8.0 all-to-all-start.3
  1169.4 18.9 %all-to-all-start.4 = ((bf16[8,256,256]{2,1,0:T(8,128)(2,1)}), bf16[8,256,256]{2,1,0:T(8,128)(2,1)S(1)}, u32[]{:S(2)}, u32[]{:S(2)}) async-start(bf16[8,256,256]{2,1,0:T(8,128)(2,1)} %copy.154), calls=%async_computation.7 | async-start | bytes 2097152 | tf_op jit(solution)/shard_map/all_to_all | solution.py:286
  1188.3 41.1 %all-to-all-start.5 = ((bf16[8,384,256]{2,1,0:T(8,128)(2,1)}), bf16[8,384,256]{2,1,0:T(8,128)(2,1)S(1)}, u32[]{:S(2)}, u32[]{:S(2)}) async-start(bf16[8,384,256]{2,1,0:T(8,128)(2,1)} %add_convert_fusion.2), calls=%async_computation.8 | async-start | bytes 3145728 | tf_op jit(solution)/shard_map/all_to_all | solution.py:286
  1195.1 9.0 collective-permute-start.35
  1199.6 11.8 collective-permute-start.36
  1211.4 12.0 collective-permute-start.37
  1212.7 10.7 collective-permute-start.38
  1213.4 10.0 collective-permute-start.39
  (52 other events, 430.3 us)
Sparse Core Ops, SparseCore 0:
  23.5 96.9 all-gather.5
  122.5 106.5 all-gather.7
  255.8 117.9 reduce-scatter.3
  382.1 89.8 all-gather.9
  518.2 181.6 reduce-scatter.5
  719.1 89.8 all-gather.11
  1001.6 116.1 reduce-scatter.7
  1149.7 152.3 all-gather.13

commit v4 on v3

--- a/solution.py
+++ b/solution.py
@@ -44,7 +44,20 @@
     return carry
 
 
-def attend_kernel(k_block, lo_ref, full_ref, low_ref, q_ref, k_ref, v_ref, o_ref, lse_ref, acc_ref):
+def attend_kernel(
+    k_block,
+    lo_ref,
+    full_ref,
+    low_ref,
+    q_ref,
+    k_ref,
+    v_ref,
+    out_ref,
+    o_ref,
+    lse_ref,
+    part_ref,
+    acc_ref,
+):
     heads = range(k_ref.shape[0])
     q_block = q_ref.shape[1]
     q0 = pl.program_id(0) * q_block
@@ -77,6 +90,10 @@
         top, total = final[h]
         o_ref[rows[h], :] = (acc_ref[rows[h], :] / total).astype(bf16)
         lse_ref[h : h + 1, :] = top + jnp.log(total)
+    attended = o_ref[...]
+    for c in range(0, out_ref.shape[1], k_block):
+        cols = pl.ds(c, k_block)
+        part_ref[:, cols] = dot(attended, out_ref[:, cols], 0, 0).astype(bf16)
 
 
 def attend_back_kernel(
@@ -85,26 +102,43 @@
     full_ref,
     low_ref,
     q_ref,
-    g_ref,
+    hidden_ref,
     o_ref,
     lse_ref,
     k_ref,
     v_ref,
     kt_ref,
+    out_ref,
+    cos_ref,
+    sin_ref,
+    grad_ref,
+    g_ref,
     dq_ref,
     dk_ref,
     dv_ref,
 ):
     heads = range(k_ref.shape[0])
     q_block = q_ref.shape[1]
-    q0 = pl.program_id(0) * q_block
+    q0 = pl.multiple_of(pl.program_id(0) * q_block, q_block)
+    width = q_ref.shape[0]
+    half_dim = HEAD_DIM // 2
     rows = [pl.ds(h * HEAD_DIM, HEAD_DIM) for h in heads]
+
+    def unrotated(ref, here, cols):
+        cosine, sine = cos_ref[:, cols], sin_ref[:, cols]
+        out = []
+        for h in heads:
+            at = h * HEAD_DIM
+            a, b = ref[at : at + half_dim, here], ref[at + half_dim : at + HEAD_DIM, here]
+            out += [a * cosine + b * sine, b * cosine - a * sine]
+        return jnp.concatenate(out, axis=0).T
 
     @pl.when(pl.program_id(0) == 0)
     def _():
         dk_ref[...] = jnp.zeros_like(dk_ref)
         dv_ref[...] = jnp.zeros_like(dv_ref)
 
+    g_ref[...] = dot(out_ref[...], hidden_ref[...], 1, 1).astype(bf16)
     dq_ref[...] = jnp.zeros_like(dq_ref)
     inner = [
         jnp.sum(g_ref[r, :].astype(f32) * o_ref[r, :].astype(f32), axis=0, keepdims=True)
@@ -133,6 +167,16 @@
         return carry
 
     key_loops(lo_ref, full_ref, q_block, k_block, step, 0)
+    here = pl.ds(q0, q_block)
+    dq = unrotated(dq_ref, slice(None), here) * HEAD_DIM ** (-0.5)
+    grad_ref[here, 0:width] = dq.astype(bf16)
+
+    @pl.when(pl.program_id(0) == pl.num_programs(0) - 1)
+    def _():
+        for c in range(0, kt_ref.shape[1], k_block):
+            cols = pl.ds(c, k_block)
+            grad_ref[cols, width : 2 * width] = unrotated(dk_ref, cols, cols).astype(bf16)
+            grad_ref[cols, 2 * width : 3 * width] = dv_ref[:, cols].T.astype(bf16)
 
 
 def attention_specs(heads, length, q_block):
@@ -146,9 +190,9 @@
     return whole_t, whole_h, tile, low, stat
 
 
-def attend(bounds, q_t, k_h, v_t):
+def attend(bounds, q_t, k_h, v_t, out_full):
     heads, length, _ = k_h.shape
-    width = heads * HEAD_DIM
+    width, model = out_full.shape
     block = math.gcd(BLOCK, length)
     whole_t, whole_h, tile, low, stat = attention_specs(heads, length, block)
     pairs = length * WINDOW * heads
@@ -157,43 +201,70 @@
         out_shape=(
             jax.ShapeDtypeStruct((width, length), bf16),
             jax.ShapeDtypeStruct((heads, length), f32),
+            jax.ShapeDtypeStruct((length, model), bf16),
         ),
         grid_spec=pltpu.PrefetchScalarGridSpec(
             num_scalar_prefetch=2,
             grid=(length // block,),
-            in_specs=[low, tile, whole_h, whole_t],
-            out_specs=[tile, stat],
+            in_specs=[
+                low,
+                tile,
+                whole_h,
+                whole_t,
+                pl.BlockSpec((width, model), lambda i, *_: (0, 0), pipeline_mode=pl.Buffered(1)),
+            ],
+            out_specs=[tile, stat, pl.BlockSpec((block, model), lambda i, *_: (i, 0))],
             scratch_shapes=[pltpu.VMEM((width, block), f32)],
         ),
         compiler_params=pltpu.CompilerParams(vmem_limit_bytes=VMEM_BYTES),
         cost_estimate=pl.CostEstimate(
-            flops=pairs * 6 * 256, transcendentals=pairs, bytes_accessed=length * width * 8
+            flops=pairs * 6 * 256, transcendentals=pairs, bytes_accessed=length * model * 2
         ),
         name="attend",
-    )(*bounds, q_t, k_h, v_t)
-
-
-def attend_back(bounds, q_t, g_t, o_t, lse, k_h, v_h, k_t):
+    )(*bounds, q_t, k_h, v_t, out_full)
+
+
+def attend_back(bounds, q_t, grad_hidden, o_t, lse, k_h, v_h, k_t, out_full, cosine, sine):
     heads, length, _ = k_h.shape
-    width = heads * HEAD_DIM
+    width, model = out_full.shape
     block = math.gcd(BLOCK, length)
     whole_t, whole_h, tile, low, stat = attention_specs(heads, length, block)
+    once = pl.Buffered(1)
+    table = pl.BlockSpec((HEAD_DIM // 2, length), lambda i, *_: (0, 0), pipeline_mode=once)
     pairs = length * WINDOW * heads
     return pl.pallas_call(
         functools.partial(attend_back_kernel, block),
-        out_shape=tuple(jax.ShapeDtypeStruct((width, length), f32) for _ in range(3)),
+        out_shape=jax.ShapeDtypeStruct((length, 3 * width), bf16),
         grid_spec=pltpu.PrefetchScalarGridSpec(
             num_scalar_prefetch=2,
             grid=(length // block,),
-            in_specs=[low, tile, tile, tile, stat, whole_h, whole_h, whole_t],
-            out_specs=[tile, whole_t, whole_t],
+            in_specs=[
+                low,
+                tile,
+                pl.BlockSpec((block, model), lambda i, *_: (i, 0)),
+                tile,
+                stat,
+                whole_h,
+                whole_h,
+                whole_t,
+                pl.BlockSpec((width, model), lambda i, *_: (0, 0), pipeline_mode=once),
+                table,
+                table,
+            ],
+            out_specs=pl.BlockSpec((length, 3 * width), lambda i, *_: (0, 0)),
+            scratch_shapes=[
+                pltpu.VMEM((width, block), bf16),
+                pltpu.VMEM((width, block), f32),
+                pltpu.VMEM((width, length), f32),
+                pltpu.VMEM((width, length), f32),
+            ],
         ),
         compiler_params=pltpu.CompilerParams(vmem_limit_bytes=VMEM_BYTES),
         cost_estimate=pl.CostEstimate(
             flops=pairs * 12 * 256, transcendentals=pairs, bytes_accessed=length * width * 24
         ),
         name="attend_back",
-    )(*bounds, q_t, g_t, o_t, lse, k_h, v_h, k_t)
+    )(*bounds, q_t, grad_hidden, o_t, lse, k_h, v_h, k_t, out_full, cosine, sine)
 
 
 def attention_bounds(lengths, length):
@@ -215,7 +286,7 @@
     counter = jnp.arange(half_dim, dtype=f32)
     frequency = jnp.exp(counter * (-2.0 * math.log(rope_base) / HEAD_DIM))
     angles = frequency[:, None] * jnp.arange(length, dtype=f32)[None, :]
-    return jnp.cos(angles)[None], jnp.sin(angles)[None]
+    return jnp.cos(angles), jnp.sin(angles)
 
 
 def rotate(values, cosine, sine):
@@ -335,20 +406,11 @@
     def scatter_plane(a):
         return lax.psum_scatter(a.astype(bf16), plane, scatter_dimension=0, tiled=True).astype(f32)
 
-    def scatter_start(part):
-        part = part.astype(bf16)
+    def scatter_cores(product, a, piece=slice(None)):
+        a = a.reshape(-1, n_core, own_len, a.shape[1])[:, :, piece]
         if not cube:
-            return [scatter_plane(part)]
-        size = part.shape[0] // n_context
-        a = halve(part.reshape(n_chips, n_pair, n_core, size, model), "core", 2).astype(bf16)
-        one, two = a[:, :, : size // 2], a[:, :, size // 2 :]
-        return [halve(one, "pair", 1).astype(bf16), halve(two, "chips", 0).astype(bf16)]
-
-    def scatter_start_by_core(product, a):
-        if not cube:
-            return scatter_start(product(a))
+            return product(a.reshape(-1, a.shape[3]))
         core = lax.axis_index("core")
-        a = a.reshape(n_chips * n_pair, n_core, own_len, a.shape[1])
 
         def part(index):
             rows_of = lax.dynamic_index_in_dim(a, index, 1, False)
@@ -356,12 +418,12 @@
 
         theirs = swap(part(1 - core).astype(bf16), "core")
         mine = (part(core) + theirs.astype(f32)).astype(bf16)
-        return mine.reshape(n_chips, n_pair, own_len, model)
+        return mine.reshape(n_chips, n_pair, a.shape[2], model)
 
     def scatter_middle(a):
         if not cube:
-            return a
-        half = own_len // 2
+            return [scatter_plane(a)]
+        half = a.shape[2] // 2
         one, two = a[:, :, :half], a[:, :, half:]
         return [halve(one, "pair", 1).astype(bf16), halve(two, "chips", 0).astype(bf16)]
 
@@ -369,9 +431,6 @@
         if not cube:
             return halves[0]
         return jnp.concatenate([halve(halves[0], "chips", 0), halve(halves[1], "pair", 0)], axis=0)
-
-    def scatter_rows(part):
-        return scatter_end(scatter_start(part))
 
     def own(a):
         return lax.dynamic_slice(a, (seq, first_row, 0), (1, own_len, model))[0]
@@ -413,10 +472,11 @@
     qkv_block, out_local, gateup_local, down_local = lax.optimization_barrier(
         (qkv_block, out_weight, gateup_weight, down_weight)
     )
+    out_block = heads_out(out_local.reshape(block_heads, HEAD_DIM, rows))
     qkv_blocks = heads_spread(qkv_block) if split_heads else [qkv_block]
+    out_near = spread_near(out_block) if split_heads else []
     qkv_t = heads_whole(qkv_blocks, 3 * HEAD_DIM).reshape(heads, 3, HEAD_DIM, model)
     qkv_t = qkv_t.transpose(1, 0, 2, 3).reshape(3 * width, model)
-    out_block = heads_out(out_local.reshape(block_heads, HEAD_DIM, rows))
     gateup_local = gateup_local.reshape(2, rows, n_context, block_hidden).transpose(2, 0, 3, 1)
     hidden_local = jnp.concatenate(
         [
@@ -427,15 +487,14 @@
     )
     cosine, sine = rope_tables(length)
     bounds = attention_bounds(lax.dynamic_slice_in_dim(doc_lengths, seq, 1, 0)[0], length)
-    normed_one, incoming_now, qkv_t, out_block, hidden_local, cosine, sine, bounds = (
+    normed_one, incoming_now, qkv_t, out_near, hidden_local, cosine, sine, bounds = (
         lax.optimization_barrier(
-            (normed_one, incoming, qkv_t, out_block, hidden_local, cosine, sine, bounds)
+            (normed_one, incoming, qkv_t, out_near, hidden_local, cosine, sine, bounds)
         )
     )
 
     incoming_all = gather_plane(incoming_now)
-    hidden_block = exchange(hidden_local)
-    out_near = spread_near(out_block) if split_heads else []
+    out_far = spread_far(out_near) if split_heads else []
     score_scale = HEAD_DIM ** (-0.5)
     projected = dot(qkv_t, normed_one, 1, 1)
     q_t = rotate(projected[:width], cosine, sine).astype(bf16) * bf16(score_scale)
@@ -443,18 +502,17 @@
     v_t = projected[2 * width :].astype(bf16)
     k_h = k_t.reshape(heads, HEAD_DIM, length).transpose(0, 2, 1)
     v_h = v_t.reshape(heads, HEAD_DIM, length).transpose(0, 2, 1)
-    q_t, hidden_block, out_near = lax.optimization_barrier((q_t, hidden_block, out_near))
-    out_far = spread_far(out_near) if split_heads else []
-    hidden_near = spread_near(hidden_block)
-    o_t, lse = attend(bounds, q_t, k_h, v_t)
-    o_t, incoming_all, hidden_near, out_far = lax.optimization_barrier(
-        (o_t, incoming_all, hidden_near, out_far)
-    )
-    hidden_far = spread_far(hidden_near)
-
+    q_t, out_far = lax.optimization_barrier((q_t, out_far))
     out_blocks = spread_blocks(out_block, out_near, out_far) if split_heads else [out_block]
     out_full = heads_whole(out_blocks, HEAD_DIM).reshape(width, model)
-    attention_branch = scatter_plane(dot(o_t, out_full, 0, 0))
+    hidden_block = exchange(hidden_local)
+    o_t, lse, attention_part = attend(bounds, q_t, k_h, v_t, out_full)
+    attention_part, incoming_all, hidden_block = lax.optimization_barrier(
+        (attention_part, incoming_all, hidden_block)
+    )
+    hidden_near = spread_near(hidden_block)
+    hidden_far = spread_far(hidden_near)
+    attention_branch = scatter_plane(attention_part)
     attention_branch, hidden_far = lax.optimization_barrier((attention_branch, hidden_far))
     hidden = rows_in + attention_branch
     inverse_two = norm_inverse(hidden)
@@ -478,19 +536,7 @@
     grad_up = grad_activation * gate_silu
     grad_gateup = jnp.concatenate([grad_gate, grad_up], axis=1).astype(bf16)
     feedforward_branch = scatter_plane(dot(activation, down_full, 1, 0))
-    second_sums = scatter_start_by_core(lambda a: dot(a, gateup_t, 1, 0), grad_gateup)
-    grad_normed_two = scatter_end(scatter_middle(second_sums))
-    grad_normed_two, feedforward_branch, activation, grad_gateup = lax.optimization_barrier(
-        (grad_normed_two, feedforward_branch, activation, grad_gateup)
-    )
-
-    result = (hidden + feedforward_branch).astype(bf16)
-    if n_extra > 1:
-        result = lax.all_gather(result, "extra", axis=0, tiled=True)
-    result_near = spread_near(result)
-    grad_rows_two, gain_two = norm_backward(grad_normed_two, normal_two, inverse_two, gains[1])
-    grad_hidden = incoming.astype(f32) + grad_rows_two
-    grad_hidden_all = gather_plane(grad_hidden.astype(bf16))
+    second_sums = scatter_cores(lambda a: dot(a, gateup_t, 1, 0), grad_gateup)
     down_grad = dot(activation, incoming_all, 0, 0).astype(bf16)
     gateup_grad = dot(grad_gateup, normed_two, 0, 0).astype(bf16)
     hidden_grads = jnp.concatenate(
@@ -501,36 +547,46 @@
         axis=0,
     )
     hidden_grads = list(hidden_grads.transpose(1, 3, 0, 2, 4).reshape(seqs, n_context, -1, rows))
+    second_sums, hidden_grads = lax.optimization_barrier((second_sums, hidden_grads))
     hidden_grads_far = collect_far(hidden_grads)
-    grad_hidden_all, hidden_grads_far, result_near = lax.optimization_barrier(
-        (grad_hidden_all, hidden_grads_far, result_near)
+    second_halves, hidden_grads_far = lax.optimization_barrier(
+        (scatter_middle(second_sums), hidden_grads_far)
+    )
+    grad_normed_two = scatter_end(second_halves)
+    grad_normed_two, feedforward_branch = lax.optimization_barrier(
+        (grad_normed_two, feedforward_branch)
+    )
+
+    result = (hidden + feedforward_branch).astype(bf16)
+    if n_extra > 1:
+        result = lax.all_gather(result, "extra", axis=0, tiled=True)
+    result_near = spread_near(result)
+    grad_rows_two, gain_two = norm_backward(grad_normed_two, normal_two, inverse_two, gains[1])
+    grad_hidden = incoming.astype(f32) + grad_rows_two
+    grad_hidden_all = gather_plane(grad_hidden.astype(bf16))
+    hidden_grads = collect_near(hidden_grads, hidden_grads_far)
+    grad_hidden_all, hidden_grads, result_near = lax.optimization_barrier(
+        (grad_hidden_all, hidden_grads, result_near)
     )
 
     result_far = spread_far(result_near)
-    g_t = dot(out_full, grad_hidden_all, 1, 1).astype(bf16)
-    dq_t, dk_t, dv_t = attend_back(bounds, q_t, g_t, o_t, lse, k_h, v_h, k_t)
-    dq_t, dk_t, dv_t, result_far = lax.optimization_barrier((dq_t, dk_t, dv_t, result_far))
-    grad_projected = jnp.concatenate(
-        [rotate(dq_t * score_scale, cosine, -sine), rotate(dk_t, cosine, -sine), dv_t], axis=0
-    ).astype(bf16)
-
-    first_part = dot(grad_projected, qkv_t, 0, 0).astype(bf16)
+    grad_projected = attend_back(
+        bounds, q_t, grad_hidden_all, o_t, lse, k_h, v_h, k_t, out_full, cosine, sine
+    )
+    grad_projected, result_far = lax.optimization_barrier((grad_projected, result_far))
+
+    first_part = dot(grad_projected, qkv_t, 1, 0).astype(bf16)
     first_part, grad_projected = lax.optimization_barrier((first_part, grad_projected))
     grad_normed_one = scatter_plane(first_part)
-    hidden_grads = collect_near(hidden_grads, hidden_grads_far)
-    qkv_grad = dot(grad_projected, normed_one, 1, 0)
+    qkv_grad = dot(grad_projected, normed_one, 0, 0)
     qkv_grad = qkv_grad.reshape(3, heads, HEAD_DIM, model).transpose(1, 0, 2, 3)
     qkv_grad = qkv_grad.reshape(heads, 3 * HEAD_DIM, model)
     out_grad = dot(o_t, grad_hidden_all, 1, 0).reshape(heads, HEAD_DIM, model)
     heads_grad = jnp.concatenate([qkv_grad, out_grad], axis=1)
+    heads_grads = heads_split(heads_grad) if split_heads else []
     if split_heads:
-        heads_grads = heads_split(heads_grad)
         heads_grads = collect_near(heads_grads, collect_far(heads_grads))
-    else:
-        heads_grads = []
-    grad_normed_one, hidden_grads, heads_grads = lax.optimization_barrier(
-        (grad_normed_one, hidden_grads, heads_grads)
-    )
+    grad_normed_one, heads_grads = lax.optimization_barrier((grad_normed_one, heads_grads))
 
     grad_rows_one, gain_one = norm_backward(grad_normed_one, normal_one, inverse_one, gains[0])
     grad_input = (grad_hidden + grad_rows_one).astype(bf16)

time: 1330 us -> 1240 us (0.932)
  waiting for transfers between devices: 565 us -> 518 us
  matrix products: 212 us -> 176 us
  other arithmetic: 143 us -> 111 us
  starting transfers between devices: 100 us -> 122 us
  Pallas kernels: 150 us -> 164 us
  local copies, waits for them, and re-layouts: 124 us -> 110 us
    reduce_scatter x3, waiting for transfers between devices: 133 us -> 89.9 us  [scatter_plane(): lax.psum_scatter(a.astype(bf16), plane, scatter_dimension=0, tiled=True)]
    ppermute x5, waiting for transfers between devices: 126 us -> 85.3 us  [swap(): return lax.ppermute(a, axis, [(0, 1), (1, 0)])]
    dot_general x13 -> x11, matrix products: 212 us -> 176 us  [dot(): lax.dot_general(a, b, (((ca,), (cb,)), ((), ())), preferred_element_type=...]
    ppermute x35, waiting for transfers between devices: 145 us -> 170 us  [send(): return lax.ppermute(a, 'seq', pairs)]
    ppermute x35, starting transfers between devices: 73.5 us -> 93.3 us  [send(): return lax.ppermute(a, 'seq', pairs)]
    all_to_all x6, waiting for transfers between devices: 23.7 us -> 40.5 us  [exchange(): return lax.all_to_all(a, context, split_axis=0, concat_axis=0, tiled=True)]
    unnamed x139 -> x117, local copies, waits for them, and re-layouts: 51.8 us -> 40.9 us
  transfers between devices with their start and end apart: 54 -> 54, of which waited for: 22 -> 23; matrix products, arithmetic and copies ran while one was open for 24% -> 22% of each run, Pallas kernels for 11% -> 13%
where the time goes in v4:
time: 1240 us; the launch traced here: 1230 us
  waiting for transfers between devices  518 us (42%)
  matrix products  176 us (14%)
  Pallas kernels  164 us (13%)
  starting transfers between devices  122 us (10%)
  other arithmetic  111 us (9%)
  local copies, waits for them, and re-layouts  110 us (9%)
  between operations  15.7 us (1%)
    dot_general x11, matrix products, dot(): lax.dot_general(a, b, (((ca,), (cb,)), ((), ())), preferred_element_type=...  176 us
    ppermute x35, waiting for transfers between devices, send(): return lax.ppermute(a, 'seq', pairs)  170 us
    pallas_call x1, Pallas kernels, attend_back(): pl.pallas_call(functools.partial(attend_back_kernel, block), out_shape=ja...  102 us
    ppermute x35, starting transfers between devices, send(): return lax.ppermute(a, 'seq', pairs)  93.3 us
    reduce_scatter x3, waiting for transfers between devices, scatter_plane(): lax.psum_scatter(a.astype(bf16), plane, scatter_dimension=0, tiled=True)  89.9 us
    ppermute x5, waiting for transfers between devices, swap(): return lax.ppermute(a, axis, [(0, 1), (1, 0)])  85.3 us
    all_gather x4, waiting for transfers between devices, gather_plane(): return lax.all_gather(a, plane, axis=0, tiled=True)  68.4 us
    all_gather x1, waiting for transfers between devices, shards(): lax.all_gather(grad_input, ('seq', 'extra'), axis=0, tiled=True).astype(f32)  64.2 us
  transfers between devices with their start and end apart: 54, of which 23 were waited for; matrix products, arithmetic and copies ran while one was open for 22% of the time, Pallas kernels for 13%

profile of v4, /device:TPU:0, one launch (start us, length us, event | category | flops | bytes accessed | tf_op | source)
XLA Modules:
  0.0 1227.3 jit_solution(11607706311124003819)
XLA Ops:
  9.4 10.5 all_gather.18
  19.9 3.5 fusion.9
  24.6 3.5 all-to-all-start
  34.5 10.9 all-to-all-done
  45.4 3.6 collective-permute-start
  50.9 10.9 collective-permute-done
  69.8 4.0 all-to-all-start.1
  78.3 5.6 all-to-all-done.1
  83.9 7.2 collective-permute-start.5
  93.7 10.6 collective-permute-done.2
  107.8 3.4 reshape_reshape.6
  113.4 7.2 all-gather.6.cloned.1.call-done
  125.9 19.7 %fusion.39 = f32[768,4096]{1,0:T(8,128)} fusion(bf16[768,2048]{1,0:T(8,128)(2,1)S(1)} %bitcast.255, bf16[4096,2048]{1,0:T(8,128)(2,1)} %all-gather.6.cloned.1.call-done), kind=kOutput, calls=%fused_computation.143 | convolution fusion | flops 12884901888 | bytes 32505856 | tf_op jit(solution)/shard_map/dot_general | solution.py:26
  145.5 3.8 slice.144.v_ref
  149.4 6.3 fusion.35
  156.5 3.4 copy.129
  159.9 4.3 all-to-all-start.2
  174.3 62.4 %attend.1 = (bf16[256,4096]{1,0:T(8,128)(2,1)}, f32[4,4096]{1,0:T(4,128)}, bf16[4096,2048]{1,0:T(8,128)(2,1)}) custom-call(s32[8]{0:T(128)} %get-tuple-element.70.lo_ref, s32[8]{0:T(128)} %get-tuple-element.71.full_ref, s32[1,4096]{1,0:T(1,128)} %add_maximum_fusion.low_ref, bf16[256,4096]{1,0:T(8,128)(2,1)} %bitcast.259, bf16[4,4096,64]{2,1,0:T(8,128)(2,1)} %bitcast.242, ...), custom_call_target="tpu_custom_call" | custom-call | flops 51539607552 | bytes 16777216 | tf_op jit(solution)/shard_map/attend/pallas_call | solution.py:199
  239.5 33.3 %collective-permute-done.10 = bf16[8,384,256]{2,1,0:T(8,128)(2,1)S(1)} collective-permute-done((bf16[8,384,256]{2,1,0:T(8,128)(2,1)}, bf16[8,384,256]{2,1,0:T(8,128)(2,1)S(1)}, u32[]{:S(2)}, u32[]{:S(2)}) %collective-permute-start.10) | collective-permute-done | bytes 1572896 | tf_op jit(solution)/shard_map/ppermute | solution.py:360
  272.8 11.6 collective-permute-done.12
  290.1 69.4 %reduce-scatter.4.cloned.1.call-done = bf16[512,2048]{1,0:T(8,128)(2,1)} async-done(((bf16[4096,2048]{1,0:T(8,128)(2,1)}), bf16[512,2048]{1,0:T(8,128)(2,1)}) %reduce-scatter.4.cloned.1.call-update) | async-done | bytes 2097168 | tf_op jit(solution)/shard_map/reduce_scatter | solution.py:407
  381.0 4.5 slice-done
  385.5 3.5 copy.157
  389.0 11.2 fusion.40
  400.2 57.4 %all-gather.10.cloned.1.call-done = bf16[4096,2048]{1,0:T(8,128)(2,1)} async-done(((bf16[512,2048]{1,0:T(8,128)(2,1)}), bf16[4096,2048]{1,0:T(8,128)(2,1)}) %all-gather.10.cloned.1.call-update) | async-done | bytes 16777232 | tf_op jit(solution)/shard_map/all_gather | solution.py:404
  457.7 22.8 %fusion.41 = f32[4096,1024]{1,0:T(8,128)S(1)} fusion(bf16[4096,2048]{1,0:T(8,128)(2,1)} %all-gather.10.cloned.1.call-done, bf16[1024,2048]{1,0:T(8,128)(2,1)} %bitcast.245), kind=kOutput, calls=%fused_computation.145 | convolution fusion | flops 17179869184 | bytes 37748736 | tf_op jit(solution)/shard_map/dot_general | solution.py:26
  480.4 8.0 multiply_convert_fusion.1
  488.5 15.0 %convolution_convert_fusion.1 = bf16[4096,2048]{1,0:T(8,128)(2,1)} fusion(bf16[4096,512]{1,0:T(8,128)(2,1)} %get-tuple-element.170, bf16[512,2048]{1,0:T(8,128)(2,1)} %bitcast.262), kind=kOutput, calls=%fused_computation.2 | convolution fusion | flops 8598323200 | bytes 23068672 | tf_op jit(solution)/shard_map/dot_general | solution.py:26
  503.5 5.8 fusion.17
  509.4 10.9 convolution_convert_fusion.2
  520.5 23.8 %fusion.21 = bf16[1024,2048]{1,0:T(8,128)(2,1)S(1)} fusion(bf16[4096,2048]{1,0:T(8,128)(2,1)} %all-gather.10.cloned.1.call-done, bf16[4096,512]{1,0:T(8,128)(2,1)} %get-tuple-element.168, bf16[4096,512]{1,0:T(8,128)(2,1)} %get-tuple-element.169), kind=kOutput, calls=%fused_computation.49 | convolution fusion | flops 17198743552 | bytes 29360128 | tf_op jit(solution)/shard_map/dot_general | solution.py:26
  546.5 12.6 %convolution_convert_fusion.4 = bf16[512,2048]{1,0:T(8,128)(2,1)S(1)} fusion(bf16[4096,512]{1,0:T(8,128)(2,1)S(1)} %copy-done.16, bf16[4096,2048]{1,0:T(8,128)(2,1)} %all-gather.8.cloned.1.call-done), kind=kOutput, calls=%fused_computation.55 | convolution fusion | flops 8590983168 | bytes 23068672 | tf_op jit(solution)/shard_map/dot_general | solution.py:26
  566.6 11.5 add_convert_fusion
  591.9 5.5 collective-permute-start.20
  601.8 62.6 %collective-permute-done.17 = bf16[2,256,2048]{2,1,0:T(8,128)(2,1)} collective-permute-done((bf16[2,256,2048]{2,1,0:T(8,128)(2,1)}, bf16[2,256,2048]{2,1,0:T(8,128)(2,1)}, u32[]{:S(2)}, u32[]{:S(2)}) %collective-permute-start.17) | collective-permute-done | bytes 2097184 | tf_op jit(solution)/shard_map/ppermute | solution.py:311
  672.2 22.7 %collective-permute-done.21 = bf16[256,2048]{1,0:T(8,128)(2,1)S(1)} collective-permute-done((bf16[256,2048]{1,0:T(8,128)(2,1)S(1)}, bf16[256,2048]{1,0:T(8,128)(2,1)S(1)}, u32[]{:S(2)}, u32[]{:S(2)}) %collective-permute-start.21) | collective-permute-done | bytes 1048608 | tf_op jit(solution)/shard_map/ppermute | solution.py:311
  700.8 3.9 multiply_reduce_fusion
  704.7 4.2 add_convert_fusion.1
  709.0 4.8 collective-permute-start.25
  715.5 6.2 add_convert_fusion.3
  721.7 4.6 collective-permute-start.23
  727.7 4.8 copy.139
  732.4 57.9 %collective-permute-done.23 = bf16[8,384,256]{2,1,0:T(8,128)(2,1)S(1)} collective-permute-done((bf16[8,384,256]{2,1,0:T(8,128)(2,1)}, bf16[8,384,256]{2,1,0:T(8,128)(2,1)S(1)}, u32[]{:S(2)}, u32[]{:S(2)}) %collective-permute-start.23) | collective-permute-done | bytes 1572896 | tf_op jit(solution)/shard_map/ppermute | solution.py:360
  790.3 5.3 collective-permute-done.24
  795.6 3.8 all-gather.12.cloned.1.call-done.hidden_ref
  805.8 101.6 %attend_back.1 = bf16[4096,768]{1,0:T(8,128)(2,1)} custom-call(s32[8]{0:T(128)} %get-tuple-element.70.lo_ref, s32[8]{0:T(128)} %get-tuple-element.71.full_ref, s32[1,4096]{1,0:T(1,128)} %add_maximum_fusion.low_ref, bf16[256,4096]{1,0:T(8,128)(2,1)} %bitcast.260, bf16[4096,2048]{1,0:T(8,128)(2,1)} %all-gather.12.cloned.1.call-done.hidden_ref, ...), custom_call_target="tpu_custom_call" | custom-call | flops 103079215104 | bytes 25165824 | tf_op jit(solution)/shard_map/attend_back/pallas_call | solution.py:235
  907.4 19.4 %convolution_convert_fusion = bf16[4096,2048]{1,0:T(8,128)(2,1)} fusion(bf16[4096,768]{1,0:T(8,128)(2,1)} %attend_back.1, bf16[768,2048]{1,0:T(8,128)(2,1)S(1)} %bitcast.256), kind=kOutput, calls=%fused_computation.1 | convolution fusion | flops 12893290496 | bytes 26214400 | tf_op jit(solution)/shard_map/dot_general | solution.py:26
  928.4 8.3 convolution_convert_fusion.5
  937.0 20.8 %convolution_convert_fusion.3 = bf16[768,2048]{1,0:T(8,128)(2,1)S(1)} fusion(bf16[4096,768]{1,0:T(8,128)(2,1)} %attend_back.1, bf16[4096,2048]{1,0:T(8,128)(2,1)} %all-gather.6.cloned.1.call-done), kind=kOutput, calls=%fused_computation.50 | convolution fusion | flops 12886474752 | bytes 26214400 | tf_op jit(solution)/shard_map/dot_general | solution.py:26
  961.1 11.5 collective-permute-start.31
  973.4 11.2 collective-permute-done.30
  984.6 22.2 %collective-permute-done.31 = bf16[8,256,256]{2,0,1:T(8,128)(2,1)S(1)} collective-permute-done((bf16[8,256,256]{2,0,1:T(8,128)(2,1)S(1)}, bf16[8,256,256]{2,0,1:T(8,128)(2,1)S(1)}, u32[]{:S(2)}, u32[]{:S(2)}) %collective-permute-start.31) | collective-permute-done | bytes 1048608 | tf_op jit(solution)/shard_map/ppermute | solution.py:360
  1008.9 16.4 %collective-permute-start.32 = (bf16[8,256,256]{2,0,1:T(8,128)(2,1)}, bf16[8,256,256]{2,0,1:T(8,128)(2,1)S(1)}, u32[]{:S(2)}, u32[]{:S(2)}) collective-permute-start(bf16[8,256,256]{2,0,1:T(8,128)(2,1)} %get-tuple-element.195), channel_id=1, source_target_pairs={{0,1},{1,2},{2,3},{4,5},{5,6},{6,7},{8,9},{9,10},{10,11},{12,13},{... | collective-permute-start | bytes 3145736 | tf_op jit(solution)/shard_map/ppermute | solution.py:360
  1026.8 20.5 %reduce-scatter.8.cloned.1.call-done = bf16[512,2048]{1,0:T(8,128)(2,1)} async-done(((bf16[4096,2048]{1,0:T(8,128)(2,1)}), bf16[512,2048]{1,0:T(8,128)(2,1)}) %reduce-scatter.8.cloned.1.call-update) | async-done | bytes 2097168 | tf_op jit(solution)/shard_map/reduce_scatter | solution.py:407
  1055.4 5.3 fusion.14
  1060.7 3.7 add_convert_fusion.2
  1064.4 3.6 all-to-all-start.5
  1068.0 21.0 %all-to-all-done.5 = bf16[8,384,256]{2,1,0:T(8,128)(2,1)S(1)} async-done(((bf16[8,384,256]{2,1,0:T(8,128)(2,1)}), bf16[8,384,256]{2,1,0:T(8,128)(2,1)S(1)}, u32[]{:S(2)}, u32[]{:S(2)}) %all-to-all-start.5) | async-done | bytes 1572896 | tf_op jit(solution)/shard_map/all_to_all | solution.py:357
  1095.7 3.3 bitcast_dynamic-update-slice_fusion.4
  1109.0 3.3 all-to-all-start.3
  1117.1 3.6 all-to-all-start.4
  1132.4 8.5 constant_dynamic-slice_fusion
  1144.4 64.2 %all-gather.14.cloned.1.call-done = bf16[2048,2048]{1,0:T(8,128)(2,1)} async-done(((bf16[512,2048]{1,0:T(8,128)(2,1)}), bf16[2048,2048]{1,0:T(8,128)(2,1)}) %all-gather.14.cloned.1.call-update) | async-done | bytes 8388624 | tf_op jit(solution)/shard_map/all_gather | solution.py:593
  1208.6 11.7 convert.53
  (295 shorter events, 183.2 us)
Async XLA Ops:
  7.2 21.0 %copy-start = (s32[4,8]{1,0:T(4,128)S(1)}, s32[4,8]{1,0:T(4,128)}, u32[]{:S(2)}) copy-start(s32[4,8]{1,0:T(4,128)} %param.9) | copy-start | bytes 388
  7.2 113.4 %all-gather.6.cloned.1.call-start = ((), (), s32[]{:S(2)}) async-start(), calls=%async_computation.9 | async-start | bytes 18874368 | tf_op jit(solution)/shard_map/all_gather | solution.py:404
  7.2 16.2 %copy-start.31 = (bf16[3,256,512]{2,1,0:T(8,128)(2,1)S(1)}, bf16[3,256,512]{2,1,0:T(8,128)(2,1)}, u32[]{:S(2)}) copy-start(bf16[3,256,512]{2,1,0:T(8,128)(2,1)} %param.11) | copy-start | bytes 2359300
  19.9 344.0 %copy-start.32 = (f32[1,2048]{1,0:T(1,128)}, f32[1,2048]{1,0:T(1,128)S(1)}, u32[]{:S(2)}) copy-start(f32[1,2048]{1,0:T(1,128)S(1)} %get-tuple-element.200) | copy-start | bytes 24580
  24.6 20.8 %all-to-all-start = ((bf16[8,192,256]{2,1,0:T(8,128)(2,1)}), bf16[8,192,256]{2,1,0:T(8,128)(2,1)S(1)}, u32[]{:S(2)}, u32[]{:S(2)}) async-start(bf16[8,192,256]{2,1,0:T(8,128)(2,1)} %bitcast.6), calls=%async_computation | async-start | bytes 1572864 | tf_op jit(solution)/shard_map/all_to_all | solution.py:357
  45.4 16.5 %collective-permute-start = (bf16[8,192,256]{2,1,0:T(8,128)(2,1)S(1)}, bf16[8,192,256]{2,1,0:T(8,128)(2,1)S(1)}, u32[]{:S(2)}, u32[]{:S(2)}) collective-permute-start(bf16[8,192,256]{2,1,0:T(8,128)(2,1)S(1)} %all-to-all-done), channel_id=1, source_target_pairs={{0,1},{1,2},{2,3},{4,5},{5,6},{6,7},{8,9},{9,10},{10,11},{12,13},{... | collective-permute-start | bytes 2359304 | tf_op jit(solution)/shard_map/ppermute | solution.py:360
  49.0 17.0 %collective-permute-start.1 = (bf16[8,192,256]{2,1,0:T(8,128)(2,1)S(1)}, bf16[8,192,256]{2,1,0:T(8,128)(2,1)S(1)}, u32[]{:S(2)}, u32[]{:S(2)}) collective-permute-start(bf16[8,192,256]{2,1,0:T(8,128)(2,1)S(1)} %all-to-all-done), channel_id=1, source_target_pairs={{1,0},{2,1},{3,2},{5,4},{6,5},{7,6},{9,8},{10,9},{11,10},{13,12},{... | collective-permute-start | bytes 2359304 | tf_op jit(solution)/shard_map/ppermute | solution.py:360
  61.9 30.5 %collective-permute-start.3 = (bf16[8,192,256]{2,1,0:T(8,128)(2,1)S(1)}, bf16[8,192,256]{2,1,0:T(8,128)(2,1)}, u32[]{:S(2)}, u32[]{:S(2)}) collective-permute-start(bf16[8,192,256]{2,1,0:T(8,128)(2,1)S(1)} %collective-permute-done), channel_id=1, source_target_pairs={{1,2},{2,3},{5,6},{6,7},{9,10},{10,11},{13,14},{14,15},{17,18},{18... | collective-permute-start | bytes 2359304 | tf_op jit(solution)/shard_map/ppermute | solution.py:360
  66.0 26.4 %collective-permute-start.4 = (bf16[8,192,256]{2,1,0:T(8,128)(2,1)S(1)}, bf16[8,192,256]{2,1,0:T(8,128)(2,1)}, u32[]{:S(2)}, u32[]{:S(2)}) collective-permute-start(bf16[8,192,256]{2,1,0:T(8,128)(2,1)S(1)} %collective-permute-done.1), channel_id=1, source_target_pairs={{1,0},{2,1},{5,4},{6,5},{9,8},{10,9},{13,12},{14,13},{17,16},{18,1... | collective-permute-start | bytes 2359304 | tf_op jit(solution)/shard_map/ppermute | solution.py:360
  68.3 36.0 %collective-permute-start.2 = (bf16[8,192,256]{2,1,0:T(8,128)(2,1)}, bf16[8,192,256]{2,1,0:T(8,128)(2,1)}, u32[]{:S(2)}, u32[]{:S(2)}) collective-permute-start(bf16[8,192,256]{2,1,0:T(8,128)(2,1)} %broadcast_select_fusion.6), channel_id=1, source_target_pairs={{1,3},{2,0},{5,7},{6,4},{9,11},{10,8},{13,15},{14,12},{17,19},{18,... | collective-permute-start | bytes 2359304 | tf_op jit(solution)/shard_map/ppermute | solution.py:360
  69.8 14.1 %all-to-all-start.1 = ((bf16[8,64,256]{2,1,0:T(8,128)(2,1)}), bf16[8,64,256]{2,1,0:T(8,128)(2,1)}, u32[]{:S(2)}, u32[]{:S(2)}) async-start(bf16[8,64,256]{2,1,0:T(8,128)(2,1)} %bitcast.15), calls=%async_computation.1 | async-start | bytes 524288 | tf_op jit(solution)/shard_map/all_to_all | solution.py:357
  73.8 162.9 %all-gather.8.cloned.1.call-start = ((), (), s32[]{:S(2)}) async-start(), calls=%async_computation.10 | async-start | bytes 18874368 | tf_op jit(solution)/shard_map/all_gather | solution.py:404
  83.9 29.4 %collective-permute-start.5 = (bf16[8,64,256]{2,1,0:T(8,128)(2,1)}, bf16[8,64,256]{2,1,0:T(8,128)(2,1)}, u32[]{:S(2)}, u32[]{:S(2)}) collective-permute-start(bf16[8,64,256]{2,1,0:T(8,128)(2,1)} %all-to-all-done.1), channel_id=1, source_target_pairs={{0,1},{1,2},{2,3},{4,5},{5,6},{6,7},{8,9},{9,10},{10,11},{12,13},{... | collective-permute-start | bytes 786440 | tf_op jit(solution)/shard_map/ppermute | solution.py:360
  91.1 22.2 %collective-permute-start.6 = (bf16[8,64,256]{2,1,0:T(8,128)(2,1)}, bf16[8,64,256]{2,1,0:T(8,128)(2,1)}, u32[]{:S(2)}, u32[]{:S(2)}) collective-permute-start(bf16[8,64,256]{2,1,0:T(8,128)(2,1)} %all-to-all-done.1), channel_id=1, source_target_pairs={{1,0},{2,1},{3,2},{5,4},{6,5},{7,6},{9,8},{10,9},{11,10},{13,12},{... | collective-permute-start | bytes 786440 | tf_op jit(solution)/shard_map/ppermute | solution.py:360
  113.3 32.2 %copy-start.20 = (bf16[3,4,64,2048]{3,2,1,0:T(8,128)(2,1)}, bf16[3,4,64,2048]{3,2,1,0:T(8,128)(2,1)S(1)}, u32[]{:S(2)}) copy-start(bf16[3,4,64,2048]{3,2,1,0:T(8,128)(2,1)S(1)} %copy.126) | copy-start | bytes 9437188
  120.6 48.7 %collective-permute-start.7 = (bf16[8,64,256]{2,1,0:T(8,128)(2,1)}, bf16[8,64,256]{2,1,0:T(8,128)(2,1)S(1)}, u32[]{:S(2)}, u32[]{:S(2)}) collective-permute-start(bf16[8,64,256]{2,1,0:T(8,128)(2,1)} %collective-permute-done.5), channel_id=1, source_target_pairs={{1,2},{2,3},{5,6},{6,7},{9,10},{10,11},{13,14},{14,15},{17,18},{18... | collective-permute-start | bytes 786440 | tf_op jit(solution)/shard_map/ppermute | solution.py:360
  121.3 48.0 %collective-permute-start.8 = (bf16[8,64,256]{2,1,0:T(8,128)(2,1)}, bf16[8,64,256]{2,1,0:T(8,128)(2,1)}, u32[]{:S(2)}, u32[]{:S(2)}) collective-permute-start(bf16[8,64,256]{2,1,0:T(8,128)(2,1)} %collective-permute-done.6), channel_id=1, source_target_pairs={{1,0},{2,1},{5,4},{6,5},{9,8},{10,9},{13,12},{14,13},{17,16},{18,1... | collective-permute-start | bytes 786440 | tf_op jit(solution)/shard_map/ppermute | solution.py:360
  124.3 45.0 %collective-permute-start.9 = (bf16[8,64,256]{2,1,0:T(8,128)(2,1)}, bf16[8,64,256]{2,1,0:T(8,128)(2,1)}, u32[]{:S(2)}, u32[]{:S(2)}) collective-permute-start(bf16[8,64,256]{2,1,0:T(8,128)(2,1)} %broadcast_select_fusion.7), channel_id=1, source_target_pairs={{1,3},{2,0},{5,7},{6,4},{9,11},{10,8},{13,15},{14,12},{17,19},{18,... | collective-permute-start | bytes 786440 | tf_op jit(solution)/shard_map/ppermute | solution.py:360
  159.9 76.8 %all-to-all-start.2 = ((bf16[8,384,256]{2,1,0:T(8,128)(2,1)}), bf16[8,384,256]{2,1,0:T(8,128)(2,1)}, u32[]{:S(2)}, u32[]{:S(2)}) async-start(bf16[8,384,256]{2,1,0:T(8,128)(2,1)} %pad_maximum_fusion.1), calls=%async_computation.2 | async-start | bytes 3145728 | tf_op jit(solution)/shard_map/all_to_all | solution.py:357
  164.2 195.3 %reduce-scatter.4.cloned.1.call-start = ((), (), s32[]{:S(2)}) async-start(), calls=%async_computation.11 | async-start | bytes 18874368 | tf_op jit(solution)/shard_map/reduce_scatter | solution.py:407
  236.7 220.9 %all-gather.10.cloned.1.call-start = ((), (), s32[]{:S(2)}) async-start(), calls=%async_computation.12 | async-start | bytes 18874368 | tf_op jit(solution)/shard_map/all_gather | solution.py:404
  236.8 36.0 %collective-permute-start.10 = (bf16[8,384,256]{2,1,0:T(8,128)(2,1)}, bf16[8,384,256]{2,1,0:T(8,128)(2,1)S(1)}, u32[]{:S(2)}, u32[]{:S(2)}) collective-permute-start(bf16[8,384,256]{2,1,0:T(8,128)(2,1)} %all-to-all-done.2), channel_id=1, source_target_pairs={{0,1},{1,2},{2,3},{4,5},{5,6},{6,7},{8,9},{9,10},{10,11},{12,13},{... | collective-permute-start | bytes 4718600 | tf_op jit(solution)/shard_map/ppermute | solution.py:360
  238.2 46.2 %collective-permute-start.12 = (bf16[8,384,256]{2,1,0:T(8,128)(2,1)}, bf16[8,384,256]{2,1,0:T(8,128)(2,1)S(1)}, u32[]{:S(2)}, u32[]{:S(2)}) collective-permute-start(bf16[8,384,256]{2,1,0:T(8,128)(2,1)} %all-to-all-done.2), channel_id=1, source_target_pairs={{1,0},{2,1},{3,2},{5,4},{6,5},{7,6},{9,8},{10,9},{11,10},{13,12},{... | collective-permute-start | bytes 4718600 | tf_op jit(solution)/shard_map/ppermute | solution.py:360
  285.7 76.0 %collective-permute-start.14 = (bf16[8,384,256]{2,1,0:T(8,128)(2,1)}, bf16[8,384,256]{2,1,0:T(8,128)(2,1)}, u32[]{:S(2)}, u32[]{:S(2)}) collective-permute-start(bf16[8,384,256]{2,1,0:T(8,128)(2,1)} %broadcast_select_fusion.5), channel_id=1, source_target_pairs={{1,3},{2,0},{5,7},{6,4},{9,11},{10,8},{13,15},{14,12},{17,19},{18,... | collective-permute-start | bytes 4718600 | tf_op jit(solution)/shard_map/ppermute | solution.py:360
  287.0 74.7 %collective-permute-start.11 = (bf16[8,384,256]{2,1,0:T(8,128)(2,1)S(1)}, bf16[8,384,256]{2,1,0:T(8,128)(2,1)}, u32[]{:S(2)}, u32[]{:S(2)}) collective-permute-start(bf16[8,384,256]{2,1,0:T(8,128)(2,1)S(1)} %collective-permute-done.10), channel_id=1, source_target_pairs={{1,2},{2,3},{5,6},{6,7},{9,10},{10,11},{13,14},{14,15},{17,18},{18... | collective-permute-start | bytes 4718600 | tf_op jit(solution)/shard_map/ppermute | solution.py:360
  288.8 72.9 %collective-permute-start.13 = (bf16[8,384,256]{2,1,0:T(8,128)(2,1)S(1)}, bf16[8,384,256]{2,1,0:T(8,128)(2,1)}, u32[]{:S(2)}, u32[]{:S(2)}) collective-permute-start(bf16[8,384,256]{2,1,0:T(8,128)(2,1)S(1)} %collective-permute-done.12), channel_id=1, source_target_pairs={{1,0},{2,1},{5,4},{6,5},{9,8},{10,9},{13,12},{14,13},{17,16},{18,1... | collective-permute-start | bytes 4718600 | tf_op jit(solution)/shard_map/ppermute | solution.py:360
  367.6 330.3 %reduce-scatter.6.cloned.1.call-start = ((), (), s32[]{:S(2)}) async-start(), calls=%async_computation.13 | async-start | bytes 18874368 | tf_op jit(solution)/shard_map/reduce_scatter | solution.py:407
  457.7 22.8 %copy-start.11 = (f32[4096,512]{1,0:T(8,128)S(1)}, f32[4096,512]{1,0:T(8,128)}, u32[]{:S(2)}) copy-start(f32[4096,512]{1,0:T(8,128)} %fusion.40) | copy-start | bytes 25165828
  503.5 295.9 %all-gather.12.cloned.1.call-start = ((), (), s32[]{:S(2)}) async-start(), calls=%async_computation.14 | async-start | bytes 18874368 | tf_op jit(solution)/shard_map/all_gather | solution.py:404
  520.2 44.3 %collective-permute-start.15 = (bf16[2048,2048]{1,0:T(8,128)(2,1)}, bf16[2048,2048]{1,0:T(8,128)(2,1)}, u32[]{:S(2)}, u32[]{:S(2)}) collective-permute-start(bf16[2048,2048]{1,0:T(8,128)(2,1)} %convolution_convert_fusion.2), channel_id=1, source_target_pairs={{0,4},{4,0},{1,5},{5,1},{2,6},{6,2},{3,7},{7,3},{8,12},{12,8},{9,1... | collective-permute-start | bytes 25165832 | tf_op jit(solution)/shard_map/ppermute | solution.py:311
  584.2 80.2 %collective-permute-start.17 = (bf16[2,256,2048]{2,1,0:T(8,128)(2,1)}, bf16[2,256,2048]{2,1,0:T(8,128)(2,1)}, u32[]{:S(2)}, u32[]{:S(2)}) collective-permute-start(bf16[2,256,2048]{2,1,0:T(8,128)(2,1)} %dynamic-slice_bitcast_fusion), channel_id=1, source_target_pairs={{0,16},{16,0},{1,17},{17,1},{2,18},{18,2},{3,19},{19,3},{4,20},{20... | collective-permute-start | bytes 6291464 | tf_op jit(solution)/shard_map/ppermute | solution.py:311
  589.1 78.3 %collective-permute-start.16 = (bf16[2,256,2048]{2,1,0:T(8,128)(2,1)}, bf16[2,256,2048]{2,1,0:T(8,128)(2,1)}, u32[]{:S(2)}, u32[]{:S(2)}) collective-permute-start(bf16[2,256,2048]{2,1,0:T(8,128)(2,1)} %dynamic-slice_bitcast_fusion.1), channel_id=1, source_target_pairs={{0,8},{8,0},{1,9},{9,1},{2,10},{10,2},{3,11},{11,3},{4,12},{12,4},... | collective-permute-start | bytes 6291464 | tf_op jit(solution)/shard_map/ppermute | solution.py:311
  591.9 77.9 %collective-permute-start.20 = (bf16[8,384,256]{2,1,0:T(8,128)(2,1)}, bf16[8,384,256]{2,1,0:T(8,128)(2,1)}, u32[]{:S(2)}, u32[]{:S(2)}) collective-permute-start(bf16[8,384,256]{2,1,0:T(8,128)(2,1)} %broadcast_select_fusion.3), channel_id=1, source_target_pairs={{0,2},{3,1},{4,6},{7,5},{8,10},{11,9},{12,14},{15,13},{16,18},{19,... | collective-permute-start | bytes 4718600 | tf_op jit(solution)/shard_map/ppermute | solution.py:360
  597.4 72.4 %collective-permute-start.18 = (bf16[8,384,256]{2,1,0:T(8,128)(2,1)}, bf16[8,384,256]{2,1,0:T(8,128)(2,1)}, u32[]{:S(2)}, u32[]{:S(2)}) collective-permute-start(bf16[8,384,256]{2,1,0:T(8,128)(2,1)} %bitcast.47), channel_id=1, source_target_pairs={{0,1},{1,2},{4,5},{5,6},{8,9},{9,10},{12,13},{13,14},{16,17},{17,1... | collective-permute-start | bytes 4718600 | tf_op jit(solution)/shard_map/ppermute | solution.py:360
  599.9 70.0 %collective-permute-start.19 = (bf16[8,384,256]{2,1,0:T(8,128)(2,1)}, bf16[8,384,256]{2,1,0:T(8,128)(2,1)}, u32[]{:S(2)}, u32[]{:S(2)}) collective-permute-start(bf16[8,384,256]{2,1,0:T(8,128)(2,1)} %bitcast.47), channel_id=1, source_target_pairs={{2,1},{3,2},{6,5},{7,6},{10,9},{11,10},{14,13},{15,14},{18,17},{19... | collective-permute-start | bytes 4718600 | tf_op jit(solution)/shard_map/ppermute | solution.py:360
  601.8 65.6 %copy-start.8 = (bf16[2,2,256,2048]{3,2,1,0:T(8,128)(2,1)S(1)}, bf16[2,2,256,2048]{3,2,1,0:T(8,128)(2,1)}, u32[]{:S(2)}) copy-start(bf16[2,2,256,2048]{3,2,1,0:T(8,128)(2,1)} %get-tuple-element.174) | copy-start | bytes 12582916
  670.0 25.0 %collective-permute-start.21 = (bf16[256,2048]{1,0:T(8,128)(2,1)S(1)}, bf16[256,2048]{1,0:T(8,128)(2,1)S(1)}, u32[]{:S(2)}, u32[]{:S(2)}) collective-permute-start(bf16[256,2048]{1,0:T(8,128)(2,1)S(1)} %dynamic-slice_bitcast_fusion.4), channel_id=1, source_target_pairs={{0,16},{16,0},{1,17},{17,1},{2,18},{18,2},{3,19},{19,3},{4,20},{20... | collective-permute-start | bytes 3145736 | tf_op jit(solution)/shard_map/ppermute | solution.py:311
  670.5 24.9 %collective-permute-start.22 = (bf16[256,2048]{1,0:T(8,128)(2,1)S(1)}, bf16[256,2048]{1,0:T(8,128)(2,1)S(1)}, u32[]{:S(2)}, u32[]{:S(2)}) collective-permute-start(bf16[256,2048]{1,0:T(8,128)(2,1)S(1)} %dynamic-slice_bitcast_fusion.3), channel_id=1, source_target_pairs={{0,8},{8,0},{1,9},{9,1},{2,10},{10,2},{3,11},{11,3},{4,12},{12,4},... | collective-permute-start | bytes 3145736 | tf_op jit(solution)/shard_map/ppermute | solution.py:311
  709.0 338.4 %reduce-scatter.8.cloned.1.call-start = ((), (), s32[]{:S(2)}) async-start(), calls=%async_computation.15 | async-start | bytes 18874368 | tf_op jit(solution)/shard_map/reduce_scatter | solution.py:407
  709.0 86.6 %collective-permute-start.25 = (bf16[512,2048]{1,0:T(8,128)(2,1)}, bf16[512,2048]{1,0:T(8,128)(2,1)}, u32[]{:S(2)}, u32[]{:S(2)}) collective-permute-start(bf16[512,2048]{1,0:T(8,128)(2,1)} %get-tuple-element.188), channel_id=1, source_target_pairs={{0,1},{1,2},{2,3},{4,5},{5,6},{6,7},{8,9},{9,10},{10,11},{12,13},{... | collective-permute-start | bytes 6291464 | tf_op jit(solution)/shard_map/ppermute | solution.py:360
  713.8 81.8 %collective-permute-start.26 = (bf16[512,2048]{1,0:T(8,128)(2,1)}, bf16[512,2048]{1,0:T(8,128)(2,1)}, u32[]{:S(2)}, u32[]{:S(2)}) collective-permute-start(bf16[512,2048]{1,0:T(8,128)(2,1)} %get-tuple-element.188), channel_id=1, source_target_pairs={{1,0},{2,1},{3,2},{5,4},{6,5},{7,6},{9,8},{10,9},{11,10},{13,12},{... | collective-permute-start | bytes 6291464 | tf_op jit(solution)/shard_map/ppermute | solution.py:360
  721.7 68.6 %collective-permute-start.23 = (bf16[8,384,256]{2,1,0:T(8,128)(2,1)}, bf16[8,384,256]{2,1,0:T(8,128)(2,1)S(1)}, u32[]{:S(2)}, u32[]{:S(2)}) collective-permute-start(bf16[8,384,256]{2,1,0:T(8,128)(2,1)} %get-tuple-element.191), channel_id=1, source_target_pairs={{0,1},{1,2},{2,3},{4,5},{5,6},{6,7},{8,9},{9,10},{10,11},{12,13},{... | collective-permute-start | bytes 4718600 | tf_op jit(solution)/shard_map/ppermute | solution.py:360
  726.4 69.2 %collective-permute-start.24 = (bf16[8,384,256]{2,1,0:T(8,128)(2,1)}, bf16[8,384,256]{2,1,0:T(8,128)(2,1)S(1)}, u32[]{:S(2)}, u32[]{:S(2)}) collective-permute-start(bf16[8,384,256]{2,1,0:T(8,128)(2,1)} %get-tuple-element.190), channel_id=1, source_target_pairs={{1,0},{2,1},{3,2},{5,4},{6,5},{7,6},{9,8},{10,9},{11,10},{13,12},{... | collective-permute-start | bytes 4718600 | tf_op jit(solution)/shard_map/ppermute | solution.py:360
  799.4 108.0 %collective-permute-start.27 = (bf16[512,2048]{1,0:T(8,128)(2,1)}, bf16[512,2048]{1,0:T(8,128)(2,1)}, u32[]{:S(2)}, u32[]{:S(2)}) collective-permute-start(bf16[512,2048]{1,0:T(8,128)(2,1)} %collective-permute-done.25), channel_id=1, source_target_pairs={{1,2},{2,3},{5,6},{6,7},{9,10},{10,11},{13,14},{14,15},{17,18},{18... | collective-permute-start | bytes 6291464 | tf_op jit(solution)/shard_map/ppermute | solution.py:360
  803.2 104.2 %collective-permute-start.28 = (bf16[512,2048]{1,0:T(8,128)(2,1)}, bf16[512,2048]{1,0:T(8,128)(2,1)S(1)}, u32[]{:S(2)}, u32[]{:S(2)}) collective-permute-start(bf16[512,2048]{1,0:T(8,128)(2,1)} %collective-permute-done.26), channel_id=1, source_target_pairs={{1,0},{2,1},{5,4},{6,5},{9,8},{10,9},{13,12},{14,13},{17,16},{18,1... | collective-permute-start | bytes 6291464 | tf_op jit(solution)/shard_map/ppermute | solution.py:360
  804.5 102.9 %collective-permute-start.29 = (bf16[512,2048]{1,0:T(8,128)(2,1)S(1)}, bf16[512,2048]{1,0:T(8,128)(2,1)}, u32[]{:S(2)}, u32[]{:S(2)}) collective-permute-start(bf16[512,2048]{1,0:T(8,128)(2,1)S(1)} %broadcast_select_fusion), channel_id=1, source_target_pairs={{1,3},{2,0},{5,7},{6,4},{9,11},{10,8},{13,15},{14,12},{17,19},{18,... | collective-permute-start | bytes 6291464 | tf_op jit(solution)/shard_map/ppermute | solution.py:360
  805.8 101.6 %copy-start.21 = (bf16[3,4,64,2048]{3,2,1,0:T(8,128)(2,1)S(1)}, bf16[3,4,64,2048]{3,2,1,0:T(8,128)(2,1)}, u32[]{:S(2)}) copy-start(bf16[3,4,64,2048]{3,2,1,0:T(8,128)(2,1)} %copy-done.20) | copy-start | bytes 9437188
  907.4 19.4 %copy-start.22 = (bf16[512,2048]{1,0:T(8,128)(2,1)}, bf16[512,2048]{1,0:T(8,128)(2,1)S(1)}, u32[]{:S(2)}) copy-start(bf16[512,2048]{1,0:T(8,128)(2,1)S(1)} %collective-permute-done.28) | copy-start | bytes 6291460
  926.8 281.8 %all-gather.14.cloned.1.call-start = ((), (), s32[]{:S(2)}) async-start(), calls=%async_computation.16 | async-start | bytes 10485760 | tf_op jit(solution)/shard_map/all_gather | solution.py:593
  959.8 24.8 %collective-permute-start.30 = (bf16[8,256,256]{2,0,1:T(8,128)(2,1)S(1)}, bf16[8,256,256]{2,0,1:T(8,128)(2,1)S(1)}, u32[]{:S(2)}, u32[]{:S(2)}) collective-permute-start(bf16[8,256,256]{2,0,1:T(8,128)(2,1)S(1)} %get-tuple-element.186), channel_id=1, source_target_pairs={{0,1},{1,2},{4,5},{5,6},{8,9},{9,10},{12,13},{13,14},{16,17},{17,1... | collective-permute-start | bytes 3145736 | tf_op jit(solution)/shard_map/ppermute | solution.py:360
  961.1 45.6 %collective-permute-start.31 = (bf16[8,256,256]{2,0,1:T(8,128)(2,1)S(1)}, bf16[8,256,256]{2,0,1:T(8,128)(2,1)S(1)}, u32[]{:S(2)}, u32[]{:S(2)}) collective-permute-start(bf16[8,256,256]{2,0,1:T(8,128)(2,1)S(1)} %get-tuple-element.185), channel_id=1, source_target_pairs={{0,2},{3,1},{4,6},{7,5},{8,10},{11,9},{12,14},{15,13},{16,18},{19,... | collective-permute-start | bytes 3145736 | tf_op jit(solution)/shard_map/ppermute | solution.py:360
  972.6 34.1 %collective-permute-start.33 = (bf16[8,256,256]{2,0,1:T(8,128)(2,1)S(1)}, bf16[8,256,256]{2,0,1:T(8,128)(2,1)S(1)}, u32[]{:S(2)}, u32[]{:S(2)}) collective-permute-start(bf16[8,256,256]{2,0,1:T(8,128)(2,1)S(1)} %get-tuple-element.186), channel_id=1, source_target_pairs={{2,1},{3,2},{6,5},{7,6},{10,9},{11,10},{14,13},{15,14},{18,17},{19... | collective-permute-start | bytes 3145736 | tf_op jit(solution)/shard_map/ppermute | solution.py:360
  1008.9 43.3 %copy-start.36 = (f32[1,2048]{1,0:T(1,128)S(1)}, f32[1,2048]{1,0:T(1,128)}, u32[]{:S(2)}) copy-start(f32[1,2048]{1,0:T(1,128)} %copy-done.35) | copy-start | bytes 24580
  1008.9 43.3 %copy-start.41 = (f32[512]{0:T(512)S(1)}, f32[512]{0:T(512)}, u32[]{:S(2)}) copy-start(f32[512]{0:T(512)} %copy-done.40) | copy-start | bytes 6148
  1008.9 40.8 %collective-permute-start.32 = (bf16[8,256,256]{2,0,1:T(8,128)(2,1)}, bf16[8,256,256]{2,0,1:T(8,128)(2,1)S(1)}, u32[]{:S(2)}, u32[]{:S(2)}) collective-permute-start(bf16[8,256,256]{2,0,1:T(8,128)(2,1)} %get-tuple-element.195), channel_id=1, source_target_pairs={{0,1},{1,2},{2,3},{4,5},{5,6},{6,7},{8,9},{9,10},{10,11},{12,13},{... | collective-permute-start | bytes 3145736 | tf_op jit(solution)/shard_map/ppermute | solution.py:360
  1025.3 26.9 %collective-permute-start.34 = (bf16[8,256,256]{2,0,1:T(8,128)(2,1)}, bf16[8,256,256]{2,0,1:T(8,128)(2,1)S(1)}, u32[]{:S(2)}, u32[]{:S(2)}) collective-permute-start(bf16[8,256,256]{2,0,1:T(8,128)(2,1)} %get-tuple-element.194), channel_id=1, source_target_pairs={{1,0},{2,1},{3,2},{5,4},{6,5},{7,6},{9,8},{10,9},{11,10},{13,12},{... | collective-permute-start | bytes 3145736 | tf_op jit(solution)/shard_map/ppermute | solution.py:360
  1064.4 24.6 %all-to-all-start.5 = ((bf16[8,384,256]{2,1,0:T(8,128)(2,1)}), bf16[8,384,256]{2,1,0:T(8,128)(2,1)S(1)}, u32[]{:S(2)}, u32[]{:S(2)}) async-start(bf16[8,384,256]{2,1,0:T(8,128)(2,1)} %add_convert_fusion.2), calls=%async_computation.8 | async-start | bytes 3145728 | tf_op jit(solution)/shard_map/all_to_all | solution.py:357
  1109.0 8.0 all-to-all-start.3
  1117.1 24.6 %all-to-all-start.4 = ((bf16[8,256,256]{2,1,0:T(8,128)(2,1)}), bf16[8,256,256]{2,1,0:T(8,128)(2,1)S(1)}, u32[]{:S(2)}, u32[]{:S(2)}) async-start(bf16[8,256,256]{2,1,0:T(8,128)(2,1)} %copy.150), calls=%async_computation.7 | async-start | bytes 2097152 | tf_op jit(solution)/shard_map/all_to_all | solution.py:357
  1120.7 6.9 collective-permute-start.35
  1123.1 6.1 collective-permute-start.36
  1129.2 11.8 collective-permute-start.37
  1130.4 10.5 collective-permute-start.38
  1131.1 9.8 collective-permute-start.39
  (41 other events, 243.7 us)
Sparse Core Ops, SparseCore 0:
  23.5 96.9 all-gather.5
  122.5 106.7 all-gather.7
  236.9 122.5 reduce-scatter.3
  367.8 89.8 all-gather.9
  503.6 157.7 reduce-scatter.5
  709.1 90.2 all-gather.11
  926.9 120.4 reduce-scatter.7
  1060.8 147.7 all-gather.13

commit v5 on v4

--- a/solution.py
+++ b/solution.py
@@ -16,6 +16,8 @@
 epsilon = 1e-05
 rope_base = 10000.0
 masked_fill = -1e30
+log2_e = math.log2(math.e)
+query_scale = HEAD_DIM ** (-0.5) * log2_e
 
 f32 = jnp.float32
 bf16 = jnp.bfloat16
@@ -26,26 +28,82 @@
     return lax.dot_general(a, b, (((ca,), (cb,)), ((), ())), preferred_element_type=f32)
 
 
-def visible_block(low_row, q0, k0, q_block, k_block):
-    key = k0 + lax.broadcasted_iota(jnp.int32, (k_block, q_block), 0)
-    query = q0 + lax.broadcasted_iota(jnp.int32, (k_block, q_block), 1)
+def visible_block(low_row, q0, k0, q_rows, k_rows):
+    key = k0 + lax.broadcasted_iota(jnp.int32, (k_rows, q_rows), 0)
+    query = q0 + lax.broadcasted_iota(jnp.int32, (k_rows, q_rows), 1)
     return (key >= low_row) & (key <= query)
 
 
-def key_loops(lo_ref, full_ref, q_block, k_block, step, carry):
+def key_loops(lo_ref, full_ref, block, step, carry):
     qb = pl.program_id(0)
     lo = lo_ref[qb]
-    diagonal = qb * q_block // k_block
-    full = jnp.minimum(jnp.maximum(full_ref[qb], lo), diagonal)
-    carry = lax.fori_loop(lo, full, functools.partial(step, True), carry)
-    carry = lax.fori_loop(full, diagonal, functools.partial(step, False), carry)
-    for extra in range(max(1, q_block // k_block)):
-        carry = step(True, diagonal + extra, carry)
-    return carry
+    full = jnp.minimum(jnp.maximum(full_ref[qb], lo), qb)
+
+    def over(masked, kb, carry):
+        return step(masked, pl.multiple_of(kb * block, block), block, 0, carry)
+
+    carry = lax.fori_loop(lo, full, functools.partial(over, True), carry)
+    return lax.fori_loop(full, qb, functools.partial(over, False), carry)
+
+
+def project_kernel(x_ref, weight_ref, cos_ref, sin_ref, q_ref, k_ref, v_ref, kh_ref, vh_ref):
+    width = q_ref.shape[0]
+    half_dim = HEAD_DIM // 2
+    cosine, sine = cos_ref[...], sin_ref[...]
+    x = x_ref[...]
+
+    def rotated(v):
+        out = []
+        for at in range(0, width, HEAD_DIM):
+            a, b = v[at : at + half_dim], v[at + half_dim : at + HEAD_DIM]
+            out += [a * cosine - b * sine, b * cosine + a * sine]
+        return jnp.concatenate(out, axis=0)
+
+    q_ref[...] = (rotated(dot(weight_ref[:width], x, 1, 1)) * query_scale).astype(bf16)
+    keys = rotated(dot(weight_ref[width : 2 * width], x, 1, 1))
+    values = dot(weight_ref[2 * width :], x, 1, 1)
+    k_ref[...] = keys.astype(bf16)
+    v_ref[...] = values.astype(bf16)
+    keys, values = keys.T.astype(bf16), values.T.astype(bf16)
+    for h in range(kh_ref.shape[0]):
+        cols = slice(h * HEAD_DIM, (h + 1) * HEAD_DIM)
+        kh_ref[h] = keys[:, cols]
+        vh_ref[h] = values[:, cols]
+
+
+def project(x, weight, cosine, sine):
+    length, model = x.shape
+    width = weight.shape[0] // 3
+    heads = width // HEAD_DIM
+    block = math.gcd(BLOCK, length)
+    tile = pl.BlockSpec((width, block), lambda i: (0, i))
+    by_head = pl.BlockSpec((heads, block, HEAD_DIM), lambda i: (0, i, 0))
+    table = pl.BlockSpec((HEAD_DIM // 2, block), lambda i: (0, i))
+    return pl.pallas_call(
+        project_kernel,
+        grid=(length // block,),
+        out_shape=(
+            *(jax.ShapeDtypeStruct((width, length), bf16) for _ in range(3)),
+            *(jax.ShapeDtypeStruct((heads, length, HEAD_DIM), bf16) for _ in range(2)),
+        ),
+        in_specs=[
+            pl.BlockSpec((block, model), lambda i: (i, 0)),
+            pl.BlockSpec((3 * width, model), lambda i: (0, 0), pipeline_mode=pl.Buffered(1)),
+            table,
+            table,
+        ],
+        out_specs=[tile, tile, tile, by_head, by_head],
+        compiler_params=pltpu.CompilerParams(vmem_limit_bytes=VMEM_BYTES),
+        cost_estimate=pl.CostEstimate(
+            flops=6 * length * width * model,
+            transcendentals=0,
+            bytes_accessed=2 * length * (model + 6 * width),
+        ),
+        name="project",
+    )(x, weight, cosine, sine)
 
 
 def attend_kernel(
-    k_block,
     lo_ref,
     full_ref,
     low_ref,
@@ -59,45 +117,48 @@
     acc_ref,
 ):
     heads = range(k_ref.shape[0])
-    q_block = q_ref.shape[1]
-    q0 = pl.program_id(0) * q_block
+    block = q_ref.shape[1]
+    q0 = pl.multiple_of(pl.program_id(0) * block, block)
     rows = [pl.ds(h * HEAD_DIM, HEAD_DIM) for h in heads]
     acc_ref[...] = jnp.zeros_like(acc_ref)
 
-    def step(masked, kb, carry):
-        k0 = pl.multiple_of(kb * k_block, k_block)
-        cols = pl.ds(k0, k_block)
-        scores = [dot(k_ref[h, cols, :], q_ref[rows[h], :], 1, 0) for h in heads]
+    def step(masked, k0, k_rows, q_from, carry):
+        keys, mine = pl.ds(k0, k_rows), slice(q_from, block)
+        scores = [dot(k_ref[h, keys, :], q_ref[rows[h], mine], 1, 0) for h in heads]
         if masked:
-            visible = visible_block(low_ref[...], q0, k0, q_block, k_block)
+            visible = visible_block(low_ref[:, mine], q0 + q_from, k0, block - q_from, k_rows)
             scores = [jnp.where(visible, v, masked_fill) for v in scores]
         top = [jnp.maximum(carry[h][0], jnp.max(scores[h], axis=0, keepdims=True)) for h in heads]
-        weights = [jnp.exp(scores[h] - top[h]) for h in heads]
-        added = [dot(v_ref[rows[h], cols], weights[h].astype(bf16), 1, 0) for h in heads]
+        weights = [jnp.exp2(scores[h] - top[h]) for h in heads]
+        added = [dot(v_ref[rows[h], keys], weights[h].astype(bf16), 1, 0) for h in heads]
         out = []
         for h in heads:
-            fade = jnp.exp(carry[h][0] - top[h])
+            fade = jnp.exp2(carry[h][0] - top[h])
             total = carry[h][1] * fade + jnp.sum(weights[h], axis=0, keepdims=True)
-            acc_ref[rows[h], :] = acc_ref[rows[h], :] * fade + added[h]
+            acc_ref[rows[h], mine] = acc_ref[rows[h], mine] * fade + added[h]
             out.append((top[h], total))
         return tuple(out)
 
     start = tuple(
-        (jnp.full((1, q_block), masked_fill, f32), jnp.zeros((1, q_block), f32)) for _ in heads
-    )
-    final = key_loops(lo_ref, full_ref, q_block, k_block, step, start)
+        (jnp.full((1, block), masked_fill, f32), jnp.zeros((1, block), f32)) for _ in heads
+    )
+    carry = key_loops(lo_ref, full_ref, block, step, start)
+    half = block // 2
+    carry = step(True, q0, half, 0, carry)
+    later = tuple((top[:, half:], total[:, half:]) for top, total in carry)
+    later = step(True, pl.multiple_of(q0 + half, half), half, half, later)
     for h in heads:
-        top, total = final[h]
+        top = jnp.concatenate([carry[h][0][:, :half], later[h][0]], axis=1)
+        total = jnp.concatenate([carry[h][1][:, :half], later[h][1]], axis=1)
         o_ref[rows[h], :] = (acc_ref[rows[h], :] / total).astype(bf16)
-        lse_ref[h : h + 1, :] = top + jnp.log(total)
+        lse_ref[h : h + 1, :] = top + jnp.log(total) * log2_e
     attended = o_ref[...]
-    for c in range(0, out_ref.shape[1], k_block):
-        cols = pl.ds(c, k_block)
+    for c in range(0, out_ref.shape[1], block):
+        cols = pl.ds(c, block)
         part_ref[:, cols] = dot(attended, out_ref[:, cols], 0, 0).astype(bf16)
 
 
 def attend_back_kernel(
-    k_block,
     lo_ref,
     full_ref,
     low_ref,
@@ -118,8 +179,8 @@
     dv_ref,
 ):
     heads = range(k_ref.shape[0])
-    q_block = q_ref.shape[1]
-    q0 = pl.multiple_of(pl.program_id(0) * q_block, q_block)
+    block = q_ref.shape[1]
+    q0 = pl.multiple_of(pl.program_id(0) * block, block)
     width = q_ref.shape[0]
     half_dim = HEAD_DIM // 2
     rows = [pl.ds(h * HEAD_DIM, HEAD_DIM) for h in heads]
@@ -145,37 +206,40 @@
         for r in rows
     ]
 
-    def step(masked, kb, carry):
-        k0 = pl.multiple_of(kb * k_block, k_block)
-        cols = pl.ds(k0, k_block)
+    def step(masked, k0, k_rows, q_from, carry):
+        keys, mine = pl.ds(k0, k_rows), slice(q_from, block)
         if masked:
-            visible = visible_block(low_ref[...], q0, k0, q_block, k_block)
+            visible = visible_block(low_ref[:, mine], q0 + q_from, k0, block - q_from, k_rows)
         for h in heads:
             r = rows[h]
-            scores = dot(k_ref[h, cols, :], q_ref[r, :], 1, 0)
-            grad_probs = dot(v_ref[h, cols, :], g_ref[r, :], 1, 0)
+            scores = dot(k_ref[h, keys, :], q_ref[r, mine], 1, 0)
+            grad_probs = dot(v_ref[h, keys, :], g_ref[r, mine], 1, 0)
             if masked:
                 scores = jnp.where(visible, scores, masked_fill)
-            probs = jnp.exp(scores - lse_ref[h : h + 1, :])
-            grad_scores = (probs * (grad_probs - inner[h])).astype(bf16)
-            dv = dot(g_ref[r, :], probs.astype(bf16), 1, 1)
-            dk = dot(q_ref[r, :], grad_scores, 1, 1)
-            dq = dot(kt_ref[r, cols], grad_scores, 1, 0)
-            dv_ref[r, cols] += dv
-            dk_ref[r, cols] += dk
-            dq_ref[r, :] += dq
+            probs = jnp.exp2(scores - lse_ref[h : h + 1, mine])
+            grad_scores = (probs * (grad_probs - inner[h][:, mine])).astype(bf16)
+            dv = dot(g_ref[r, mine], probs.astype(bf16), 1, 1)
+            dk = dot(q_ref[r, mine], grad_scores, 1, 1)
+            dq = dot(kt_ref[r, keys], grad_scores, 1, 0)
+            dv_ref[r, keys] += dv
+            dk_ref[r, keys] += dk
+            dq_ref[r, mine] += dq
         return carry
 
-    key_loops(lo_ref, full_ref, q_block, k_block, step, 0)
-    here = pl.ds(q0, q_block)
+    key_loops(lo_ref, full_ref, block, step, 0)
+    half = block // 2
+    step(True, q0, half, 0, 0)
+    step(True, pl.multiple_of(q0 + half, half), half, half, 0)
+    here = pl.ds(q0, block)
     dq = unrotated(dq_ref, slice(None), here) * HEAD_DIM ** (-0.5)
     grad_ref[here, 0:width] = dq.astype(bf16)
 
     @pl.when(pl.program_id(0) == pl.num_programs(0) - 1)
     def _():
-        for c in range(0, kt_ref.shape[1], k_block):
-            cols = pl.ds(c, k_block)
-            grad_ref[cols, width : 2 * width] = unrotated(dk_ref, cols, cols).astype(bf16)
+        for c in range(0, kt_ref.shape[1], block):
+            cols = pl.ds(c, block)
+            dk = unrotated(dk_ref, cols, cols) * (1 / log2_e)
+            grad_ref[cols, width : 2 * width] = dk.astype(bf16)
             grad_ref[cols, 2 * width : 3 * width] = dv_ref[:, cols].T.astype(bf16)
 
 
@@ -197,7 +261,7 @@
     whole_t, whole_h, tile, low, stat = attention_specs(heads, length, block)
     pairs = length * WINDOW * heads
     return pl.pallas_call(
-        functools.partial(attend_kernel, block),
+        attend_kernel,
         out_shape=(
             jax.ShapeDtypeStruct((width, length), bf16),
             jax.ShapeDtypeStruct((heads, length), f32),
@@ -233,7 +297,7 @@
     table = pl.BlockSpec((HEAD_DIM // 2, length), lambda i, *_: (0, 0), pipeline_mode=once)
     pairs = length * WINDOW * heads
     return pl.pallas_call(
-        functools.partial(attend_back_kernel, block),
+        attend_back_kernel,
         out_shape=jax.ShapeDtypeStruct((length, 3 * width), bf16),
         grid_spec=pltpu.PrefetchScalarGridSpec(
             num_scalar_prefetch=2,
@@ -267,6 +331,132 @@
     )(*bounds, q_t, grad_hidden, o_t, lse, k_h, v_h, k_t, out_full, cosine, sine)
 
 
+def feedforward_kernel(x_ref, ga_ref, gateup_ref, down_ref, act_ref, grad_ref, branch_ref):
+    block, hidden = act_ref.shape
+    step = math.gcd(hidden, 256)
+    x = x_ref[...]
+    for at in range(0, hidden, step):
+        cols = slice(at, at + step)
+        gate = dot(x, gateup_ref[at : at + step, :], 1, 1)
+        raised = dot(x, gateup_ref[hidden + at : hidden + at + step, :], 1, 1)
+        grad = ga_ref[:, cols]
+        sigmoid = jax.nn.sigmoid(gate)
+        silu = gate * sigmoid
+        act_ref[:, cols] = (silu * raised).astype(bf16)
+        grad_gate = grad * raised * sigmoid * (1.0 + gate * (1.0 - sigmoid))
+        grad_ref[:, cols] = grad_gate.astype(bf16)
+        grad_ref[:, hidden + at : hidden + at + step] = (grad * silu).astype(bf16)
+    act = act_ref[...]
+    for at in range(0, branch_ref.shape[1], block):
+        cols = slice(at, at + block)
+        branch_ref[:, cols] = dot(act, down_ref[:, cols], 1, 0).astype(bf16)
+
+
+def feedforward(x, ga, gateup, down):
+    length, model = x.shape
+    hidden = down.shape[0]
+    block = math.gcd(BLOCK, length)
+    once = pl.Buffered(1)
+
+    def rows_of(width):
+        return pl.BlockSpec((block, width), lambda i: (i, 0))
+
+    return pl.pallas_call(
+        feedforward_kernel,
+        grid=(length // block,),
+        out_shape=tuple(
+            jax.ShapeDtypeStruct((length, width), bf16) for width in (hidden, 2 * hidden, model)
+        ),
+        in_specs=[
+            rows_of(model),
+            rows_of(hidden),
+            pl.BlockSpec((2 * hidden, model), lambda i: (0, 0), pipeline_mode=once),
+            pl.BlockSpec((hidden, model), lambda i: (0, 0), pipeline_mode=once),
+        ],
+        out_specs=[rows_of(hidden), rows_of(2 * hidden), rows_of(model)],
+        compiler_params=pltpu.CompilerParams(vmem_limit_bytes=VMEM_BYTES),
+        cost_estimate=pl.CostEstimate(
+            flops=6 * length * hidden * model,
+            transcendentals=length * hidden,
+            bytes_accessed=length * (4 * model + 10 * hidden),
+        ),
+        name="feedforward",
+    )(x, ga, gateup, down)
+
+
+def halves_kernel(order_ref, a_ref, b_ref, first_ref, second_ref):
+    early = pl.program_id(0) < pl.num_programs(0) // 2
+
+    @pl.when(early)
+    def _():
+        rows_kernel(a_ref, b_ref, first_ref)
+
+    @pl.when(jnp.logical_not(early))
+    def _():
+        rows_kernel(a_ref, b_ref, second_ref)
+
+
+def halves_product(order, a, b):
+    length, inner = a.shape
+    model = b.shape[1]
+    count = order.shape[0]
+    half, block = count // 2, length // count
+    return pl.pallas_call(
+        halves_kernel,
+        out_shape=tuple(jax.ShapeDtypeStruct((length // 2, model), bf16) for _ in range(2)),
+        grid_spec=pltpu.PrefetchScalarGridSpec(
+            num_scalar_prefetch=1,
+            grid=(count,),
+            in_specs=[
+                pl.BlockSpec((block, inner), lambda i, order: (order[i], 0)),
+                pl.BlockSpec((inner, model), lambda i, _: (0, 0), pipeline_mode=pl.Buffered(1)),
+            ],
+            out_specs=[
+                pl.BlockSpec((block, model), lambda i, _: (jnp.minimum(i, half - 1), 0)),
+                pl.BlockSpec((block, model), lambda i, _: (jnp.maximum(i - half, 0), 0)),
+            ],
+        ),
+        compiler_params=pltpu.CompilerParams(vmem_limit_bytes=VMEM_BYTES),
+        cost_estimate=pl.CostEstimate(
+            flops=2 * length * inner * model,
+            transcendentals=0,
+            bytes_accessed=2 * length * (inner + model),
+        ),
+        name="halves_product",
+    )(order, a, b)
+
+
+def rows_kernel(a_ref, b_ref, o_ref):
+    a = a_ref[...]
+    block = a_ref.shape[0]
+    for at in range(0, o_ref.shape[1], block):
+        cols = slice(at, at + block)
+        o_ref[:, cols] = dot(a, b_ref[:, cols], 1, 0).astype(bf16)
+
+
+def rows_product(a, b):
+    length, inner = a.shape
+    model = b.shape[1]
+    block = math.gcd(BLOCK, length)
+    return pl.pallas_call(
+        rows_kernel,
+        grid=(length // block,),
+        out_shape=jax.ShapeDtypeStruct((length, model), bf16),
+        in_specs=[
+            pl.BlockSpec((block, inner), lambda i: (i, 0)),
+            pl.BlockSpec((inner, model), lambda i: (0, 0), pipeline_mode=pl.Buffered(1)),
+        ],
+        out_specs=pl.BlockSpec((block, model), lambda i: (i, 0)),
+        compiler_params=pltpu.CompilerParams(vmem_limit_bytes=VMEM_BYTES),
+        cost_estimate=pl.CostEstimate(
+            flops=2 * length * inner * model,
+            transcendentals=0,
+            bytes_accessed=2 * length * (inner + model),
+        ),
+        name="rows_product",
+    )(a, b)
+
+
 def attention_bounds(lengths, length):
     docs = lengths.shape[0]
     upto = jnp.arange(docs)[:, None] >= jnp.arange(docs)[None, :]
@@ -287,14 +477,6 @@
     frequency = jnp.exp(counter * (-2.0 * math.log(rope_base) / HEAD_DIM))
     angles = frequency[:, None] * jnp.arange(length, dtype=f32)[None, :]
     return jnp.cos(angles), jnp.sin(angles)
-
-
-def rotate(values, cosine, sine):
-    heads = values.shape[0] // HEAD_DIM
-    v = values.reshape(heads, 2, HEAD_DIM // 2, values.shape[1])
-    a, b = v[:, 0], v[:, 1]
-    out = jnp.stack([a * cosine - b * sine, b * cosine + a * sine], axis=1)
-    return out.reshape(values.shape)
 
 
 def norm_inverse(rows):
@@ -406,20 +588,6 @@
     def scatter_plane(a):
         return lax.psum_scatter(a.astype(bf16), plane, scatter_dimension=0, tiled=True).astype(f32)
 
-    def scatter_cores(product, a, piece=slice(None)):
-        a = a.reshape(-1, n_core, own_len, a.shape[1])[:, :, piece]
-        if not cube:
-            return product(a.reshape(-1, a.shape[3]))
-        core = lax.axis_index("core")
-
-        def part(index):
-            rows_of = lax.dynamic_index_in_dim(a, index, 1, False)
-            return product(rows_of.reshape(-1, a.shape[3]))
-
-        theirs = swap(part(1 - core).astype(bf16), "core")
-        mine = (part(core) + theirs.astype(f32)).astype(bf16)
-        return mine.reshape(n_chips, n_pair, a.shape[2], model)
-
     def scatter_middle(a):
         if not cube:
             return [scatter_plane(a)]
@@ -460,23 +628,34 @@
         a = exchange(a.reshape(n_context, -1, rows)).reshape(seqs * block_heads, m, rows)
         return lax.psum_scatter(a, "seq", scatter_dimension=0, tiled=True).astype(f32)
 
-    gains = lax.all_gather(norm_gains, context, axis=1, tiled=True).astype(f32)
     rows_in = own(block_input).astype(f32)
     incoming = own(cotangent)
     inverse_one = norm_inverse(rows_in)
     normal_one = rows_in * inverse_one
-    normed_one = gather_plane((normal_one * gains[0]).astype(bf16))
-
-    qkv_local = qkv_weight.reshape(3, rows, block_heads, HEAD_DIM).transpose(2, 0, 3, 1)
-    qkv_block = heads_out(qkv_local.reshape(block_heads, 3 * HEAD_DIM, rows))
-    qkv_block, out_local, gateup_local, down_local = lax.optimization_barrier(
-        (qkv_block, out_weight, gateup_weight, down_weight)
-    )
-    out_block = heads_out(out_local.reshape(block_heads, HEAD_DIM, rows))
+    normal_own = normal_one.astype(bf16)
+    normal_all = gather_plane(normal_own)
+    gains = lax.all_gather(after(norm_gains, normal_own), context, axis=1, tiled=True).astype(f32)
+
+    qkv_local, out_local, gains = lax.optimization_barrier((qkv_weight, out_weight, gains))
+    heads_local = jnp.concatenate(
+        [
+            qkv_local.reshape(3, rows, block_heads, HEAD_DIM).transpose(2, 0, 3, 1),
+            out_local.reshape(block_heads, 1, HEAD_DIM, rows),
+        ],
+        axis=1,
+    )
+    heads_block = heads_out(heads_local.reshape(block_heads, 4 * HEAD_DIM, rows))
+    heads_block = heads_block.reshape(n_context, -1, 4, HEAD_DIM, rows)
+    qkv_block = heads_block[:, :, :3].reshape(n_context, -1, rows)
+    out_block = heads_block[:, :, 3].reshape(n_context, -1, rows)
     qkv_blocks = heads_spread(qkv_block) if split_heads else [qkv_block]
+    qkv_blocks, out_block, gateup_local, down_local = lax.optimization_barrier(
+        (qkv_blocks, out_block, gateup_weight, down_weight)
+    )
     out_near = spread_near(out_block) if split_heads else []
     qkv_t = heads_whole(qkv_blocks, 3 * HEAD_DIM).reshape(heads, 3, HEAD_DIM, model)
     qkv_t = qkv_t.transpose(1, 0, 2, 3).reshape(3 * width, model)
+    qkv_gained = (qkv_t.astype(f32) * gains[0]).astype(bf16)
     gateup_local = gateup_local.reshape(2, rows, n_context, block_hidden).transpose(2, 0, 3, 1)
     hidden_local = jnp.concatenate(
         [
@@ -487,21 +666,24 @@
     )
     cosine, sine = rope_tables(length)
     bounds = attention_bounds(lax.dynamic_slice_in_dim(doc_lengths, seq, 1, 0)[0], length)
-    normed_one, incoming_now, qkv_t, out_near, hidden_local, cosine, sine, bounds = (
+    incoming_all = gather_plane(after(incoming, normal_all, *qkv_blocks))
+    normal_all, qkv_t, qkv_gained, out_near, hidden_local, cosine, sine, bounds = (
         lax.optimization_barrier(
-            (normed_one, incoming, qkv_t, out_near, hidden_local, cosine, sine, bounds)
+            (
+                normal_all,
+                qkv_t,
+                qkv_gained,
+                out_near,
+                hidden_local,
+                cosine,
+                sine,
+                bounds,
+            )
         )
     )
 
-    incoming_all = gather_plane(incoming_now)
     out_far = spread_far(out_near) if split_heads else []
-    score_scale = HEAD_DIM ** (-0.5)
-    projected = dot(qkv_t, normed_one, 1, 1)
-    q_t = rotate(projected[:width], cosine, sine).astype(bf16) * bf16(score_scale)
-    k_t = rotate(projected[width : 2 * width], cosine, sine).astype(bf16)
-    v_t = projected[2 * width :].astype(bf16)
-    k_h = k_t.reshape(heads, HEAD_DIM, length).transpose(0, 2, 1)
-    v_h = v_t.reshape(heads, HEAD_DIM, length).transpose(0, 2, 1)
+    q_t, k_t, v_t, k_h, v_h = project(normal_all, qkv_gained, cosine, sine)
     q_t, out_far = lax.optimization_barrier((q_t, out_far))
     out_blocks = spread_blocks(out_block, out_near, out_far) if split_heads else [out_block]
     out_full = heads_whole(out_blocks, HEAD_DIM).reshape(width, model)
@@ -527,16 +709,22 @@
     grad_activation = dot(incoming_all, down_full, 1, 1)
     normed_two, grad_activation = lax.optimization_barrier((normed_two, grad_activation))
 
-    gate_up = dot(normed_two, gateup_t, 1, 1)
-    gate, raised = gate_up[:, :hidden_width], gate_up[:, hidden_width:]
-    gate_sigmoid = jax.nn.sigmoid(gate)
-    gate_silu = gate * gate_sigmoid
-    activation = (gate_silu * raised).astype(bf16)
-    grad_gate = grad_activation * raised * gate_sigmoid * (1.0 + gate * (1.0 - gate_sigmoid))
-    grad_up = grad_activation * gate_silu
-    grad_gateup = jnp.concatenate([grad_gate, grad_up], axis=1).astype(bf16)
-    feedforward_branch = scatter_plane(dot(activation, down_full, 1, 0))
-    second_sums = scatter_cores(lambda a: dot(a, gateup_t, 1, 0), grad_gateup)
+    if cube:
+        core = lax.axis_index("core")
+        pairs = n_core * jnp.arange(n_chips * n_pair, dtype=jnp.int32)
+        order = jnp.concatenate([pairs + 1 - core, pairs + core])
+    else:
+        order = jnp.arange(8, dtype=jnp.int32)
+    activation, grad_gateup, feedforward_part = feedforward(
+        normed_two, grad_activation, gateup_t, down_full
+    )
+    theirs, mine = halves_product(order, after(grad_gateup, feedforward_part), gateup_t)
+    feedforward_branch = scatter_plane(feedforward_part)
+    if cube:
+        second_sums = (mine.astype(f32) + swap(theirs, "core").astype(f32)).astype(bf16)
+        second_sums = second_sums.reshape(n_chips, n_pair, own_len, model)
+    else:
+        second_sums = jnp.concatenate([theirs, mine], axis=0)
     down_grad = dot(activation, incoming_all, 0, 0).astype(bf16)
     gateup_grad = dot(grad_gateup, normed_two, 0, 0).astype(bf16)
     hidden_grads = jnp.concatenate(
@@ -575,10 +763,10 @@
     )
     grad_projected, result_far = lax.optimization_barrier((grad_projected, result_far))
 
-    first_part = dot(grad_projected, qkv_t, 1, 0).astype(bf16)
+    first_part = rows_product(grad_projected, qkv_t)
     first_part, grad_projected = lax.optimization_barrier((first_part, grad_projected))
     grad_normed_one = scatter_plane(first_part)
-    qkv_grad = dot(grad_projected, normed_one, 0, 0)
+    qkv_grad = dot(grad_projected, normal_all, 0, 0) * gains[0]
     qkv_grad = qkv_grad.reshape(3, heads, HEAD_DIM, model).transpose(1, 0, 2, 3)
     qkv_grad = qkv_grad.reshape(heads, 3 * HEAD_DIM, model)
     out_grad = dot(o_t, grad_hidden_all, 1, 0).reshape(heads, HEAD_DIM, model)

time: 1240 us -> 1210 us (0.976)
  matrix products: 176 us -> 76.8 us
  waiting for transfers between devices: 518 us -> 554 us
  blocking collectives: 10.5 us -> 39.8 us
  Pallas kernels: 164 us -> 192 us
  local copies, waits for them, and re-layouts: 110 us -> 93.1 us
    dot_general x11 -> x5, matrix products: 176 us -> 76.8 us  [dot(): lax.dot_general(a, b, (((ca,), (cb,)), ((), ())), preferred_element_type=...]
    ppermute x35, waiting for transfers between devices: 170 us -> 234 us  [send(): return lax.ppermute(a, 'seq', pairs)]
    all_to_all x0 -> x1, blocking collectives: none -> 29.5 us  [exchange(): return lax.all_to_all(a, context, split_axis=0, concat_axis=0, tiled=True)]
    pallas_call x2 -> x6, Pallas kernels: 164 us -> 192 us  [the longest x1 58.2 us: attend_back(): pl.pallas_call(attend_back_kernel, out_shape=jax.ShapeDtypeStruct((length...]
    all_to_all x6 -> x4, waiting for transfers between devices: 40.5 us -> 24 us  [exchange(): return lax.all_to_all(a, context, split_axis=0, concat_axis=0, tiled=True)]
    unnamed x117 -> x103, local copies, waits for them, and re-layouts: 40.9 us -> 44.1 us
  transfers between devices with their start and end apart: 54 -> 52, of which waited for: 23 -> 26; matrix products, arithmetic and copies ran while one was open for 22% -> 18% of each run, Pallas kernels for 13% -> 12%
where the time goes in v5:
time: 1210 us; the launch traced here: 1200 us
  waiting for transfers between devices  554 us (46%)
  Pallas kernels  192 us (16%)
  starting transfers between devices  125 us (10%)
  other arithmetic  104 us (9%)
  local copies, waits for them, and re-layouts  93.1 us (8%)
  matrix products  76.8 us (6%)
  blocking collectives  39.8 us (3%)
  between operations  15.8 us (1%)
    ppermute x35, waiting for transfers between devices, send(): return lax.ppermute(a, 'seq', pairs)  234 us
    ppermute x35, starting transfers between devices, send(): return lax.ppermute(a, 'seq', pairs)  105 us
    reduce_scatter x3, waiting for transfers between devices, scatter_plane(): lax.psum_scatter(a.astype(bf16), plane, scatter_dimension=0, tiled=True)  85.7 us
    ppermute x5, waiting for transfers between devices, swap(): return lax.ppermute(a, axis, [(0, 1), (1, 0)])  78.4 us
    dot_general x5, matrix products, dot(): lax.dot_general(a, b, (((ca,), (cb,)), ((), ())), preferred_element_type=...  76.8 us
    all_gather x4, waiting for transfers between devices, gather_plane(): return lax.all_gather(a, plane, axis=0, tiled=True)  69.7 us
    all_gather x1, waiting for transfers between devices, shards(): lax.all_gather(grad_input, ('seq', 'extra'), axis=0, tiled=True).astype(f32)  61.2 us
    pallas_call x1, Pallas kernels, attend_back(): pl.pallas_call(attend_back_kernel, out_shape=jax.ShapeDtypeStruct((length...  58.2 us
  transfers between devices with their start and end apart: 52, of which 26 were waited for; matrix products, arithmetic and copies ran while one was open for 18% of the time, Pallas kernels for 12%

profile of v5, /device:TPU:0, one launch (start us, length us, event | category | flops | bytes accessed | tf_op | source)
XLA Modules:
  0.0 1199.6 jit_solution(4598926428757679312)
XLA Ops:
  9.9 3.4 fusion.3
  13.4 10.3 all_gather.19
  24.2 29.5 %all_to_all.25 = bf16[8,256,256]{2,1,0:T(8,128)(2,1)S(1)} all-to-all(bf16[8,256,256]{2,1,0:T(8,128)(2,1)S(1)} %bitcast.225), channel_id=1, replica_groups=mesh['chips'=2,'pair'=2,'core'=2,'seq'=4,'extra'=1] {'chips','pair','core'}, dimensions={0} | all-to-all | bytes 2097152 | tf_op jit(solution)/shard_map/all_to_all | solution.py:539
  54.2 3.5 collective-permute-start
  59.1 12.8 %collective-permute-done = bf16[8,192,256]{2,0,1:T(8,128)(2,1)S(1)} collective-permute-done((bf16[8,192,256]{2,0,1:T(8,128)(2,1)S(1)}, bf16[8,192,256]{2,0,1:T(8,128)(2,1)S(1)}, u32[]{:S(2)}, u32[]{:S(2)}) %collective-permute-start) | collective-permute-done | bytes 786464 | tf_op jit(solution)/shard_map/ppermute | solution.py:542
  79.6 3.2 dynamic-slice_bitcast_fusion.2
  83.6 14.7 %collective-permute-done.4 = bf16[8,192,256]{2,0,1:T(8,128)(2,1)} collective-permute-done((bf16[8,192,256]{2,0,1:T(8,128)(2,1)S(1)}, bf16[8,192,256]{2,0,1:T(8,128)(2,1)}, u32[]{:S(2)}, u32[]{:S(2)}) %collective-permute-start.4) | collective-permute-done | bytes 786464 | tf_op jit(solution)/shard_map/ppermute | solution.py:542
  100.4 12.1 %collective-permute-done.2 = bf16[8,192,256]{2,0,1:T(8,128)(2,1)} collective-permute-done((bf16[8,192,256]{2,0,1:T(8,128)(2,1)}, bf16[8,192,256]{2,0,1:T(8,128)(2,1)}, u32[]{:S(2)}, u32[]{:S(2)}) %collective-permute-start.2) | collective-permute-done | bytes 786464 | tf_op jit(solution)/shard_map/ppermute | solution.py:542
  121.9 3.4 collective-permute-start.5
  129.2 3.4 reshape_reshape.6
  147.6 3.6 all-to-all-start.1
  151.7 22.0 %project.1 = (bf16[256,4096]{1,0:T(8,128)(2,1)}, bf16[256,4096]{1,0:T(8,128)(2,1)}, bf16[256,4096]{1,0:T(8,128)(2,1)}, bf16[4,4096,64]{2,1,0:T(8,128)(2,1)}, bf16[4,4096,64]{2,1,0:T(8,128)(2,1)}) custom-call(bf16[4096,2048]{1,0:T(8,128)(2,1)} %all-gather.6.cloned.1.call-done.x_ref, bf16[768,2048]{1,0:T(8,128)(2,1)} %multiply_convert_fusion.1.weight_ref, ...), custom_call_target="tpu_custom_call" | custom-call | flops 12884901888 | bytes 29360128 | tf_op jit(solution)/shard_map/project/pallas_call | solution.py:82
  177.2 34.2 %attend.1 = (bf16[256,4096]{1,0:T(8,128)(2,1)}, f32[4,4096]{1,0:T(4,128)}, bf16[4096,2048]{1,0:T(8,128)(2,1)}) custom-call(s32[8]{0:T(128)} %get-tuple-element.96.lo_ref, s32[8]{0:T(128)} %get-tuple-element.97.full_ref, s32[1,4096]{1,0:T(1,128)} %add_maximum_fusion.low_ref, bf16[256,4096]{1,0:T(8,128)(2,1)} %get-tuple-element.106.q_ref, ...), custom_call_target="tpu_custom_call" | custom-call | flops 51539607552 | bytes 16777216 | tf_op jit(solution)/shard_map/attend/pallas_call | solution.py:263
  211.5 7.3 all-gather.8.cloned.1.call-done
  218.8 23.0 %collective-permute-start.10 = (bf16[8,384,256]{2,1,0:T(8,128)(2,1)S(1)}, bf16[8,384,256]{2,1,0:T(8,128)(2,1)S(1)}, u32[]{:S(2)}, u32[]{:S(2)}) collective-permute-start(bf16[8,384,256]{2,1,0:T(8,128)(2,1)S(1)} %all-to-all-done.1), channel_id=1, source_target_pairs={{0,1},{1,2},{2,3},{4,5},{5,6},{6,7},{8,9},{9,10},{10,11},{12,13},{... | collective-permute-start | bytes 4718600 | tf_op jit(solution)/shard_map/ppermute | solution.py:542
  243.1 32.8 %collective-permute-done.10 = bf16[8,384,256]{2,1,0:T(8,128)(2,1)S(1)} collective-permute-done((bf16[8,384,256]{2,1,0:T(8,128)(2,1)S(1)}, bf16[8,384,256]{2,1,0:T(8,128)(2,1)S(1)}, u32[]{:S(2)}, u32[]{:S(2)}) %collective-permute-start.10) | collective-permute-done | bytes 1572896 | tf_op jit(solution)/shard_map/ppermute | solution.py:542
  275.9 4.3 collective-permute-done.12
  287.3 66.4 %reduce-scatter.4.cloned.1.call-done = bf16[512,2048]{1,0:T(8,128)(2,1)} async-done(((bf16[4096,2048]{1,0:T(8,128)(2,1)}), bf16[512,2048]{1,0:T(8,128)(2,1)}) %reduce-scatter.4.cloned.1.call-update) | async-done | bytes 2097168 | tf_op jit(solution)/shard_map/reduce_scatter | solution.py:589
  370.7 3.2 copy-done.7
  374.6 4.4 slice-done
  379.0 3.5 copy.147
  382.5 11.2 fusion.27.ga_ref
  393.8 58.2 %all-gather.10.cloned.1.call-done.x_ref = bf16[4096,2048]{1,0:T(8,128)(2,1)} async-done(((bf16[512,2048]{1,0:T(8,128)(2,1)}), bf16[4096,2048]{1,0:T(8,128)(2,1)}) %all-gather.10.cloned.1.call-update) | async-done | bytes 16777232 | tf_op jit(solution)/shard_map/all_gather | solution.py:586
  451.9 35.0 %feedforward.1 = (bf16[4096,512]{1,0:T(8,128)(2,1)}, bf16[4096,1024]{1,0:T(8,128)(2,1)}, bf16[4096,2048]{1,0:T(8,128)(2,1)}) custom-call(bf16[4096,2048]{1,0:T(8,128)(2,1)} %all-gather.10.cloned.1.call-done.x_ref, f32[4096,512]{1,0:T(8,128)} %fusion.27.ga_ref, bf16[1024,2048]{1,0:T(8,128)(2,1)} %bitcast.218, bf16[512,2048]{1,0:T(8,128)(2,1)} %bitcast.236), custom_call_target="tpu_custom_call" | custom-call | flops 25769803776 | bytes 54525952 | tf_op jit(solution)/shard_map/feedforward/pallas_call | solution.py:364
  487.6 24.7 %halves_product.1 = (bf16[2048,2048]{1,0:T(8,128)(2,1)}, bf16[2048,2048]{1,0:T(8,128)(2,1)}) custom-call(s32[8]{0:T(128)} %pad_add_fusion.order_ref, bf16[4096,1024]{1,0:T(8,128)(2,1)} %get-tuple-element.126.a_ref, bf16[1024,2048]{1,0:T(8,128)(2,1)} %bitcast.219), custom_call_target="tpu_custom_call" | custom-call | flops 17179869184 | bytes 25165824 | tf_op jit(solution)/shard_map/halves_product/pallas_call | solution.py:404
  512.6 23.3 %convolution_convert_fusion = bf16[1024,2048]{1,0:T(8,128)(2,1)S(1)} fusion(bf16[4096,1024]{1,0:T(8,128)(2,1)} %get-tuple-element.126.a_ref, bf16[4096,2048]{1,0:T(8,128)(2,1)} %all-gather.10.cloned.1.call-done.x_ref), kind=kOutput, calls=%fused_computation.30 | convolution fusion | flops 17181966336 | bytes 29360128 | tf_op jit(solution)/shard_map/dot_general | solution.py:28
  538.4 13.1 %convolution_convert_fusion.1 = bf16[512,2048]{1,0:T(8,128)(2,1)S(1)} fusion(bf16[4096,512]{1,0:T(8,128)(2,1)S(1)} %copy-done.35, bf16[4096,2048]{1,0:T(8,128)(2,1)} %all-gather.8.cloned.1.call-done), kind=kOutput, calls=%fused_computation.35 | convolution fusion | flops 8590983168 | bytes 23068672 | tf_op jit(solution)/shard_map/dot_general | solution.py:28
  557.7 5.4 add_convert_fusion
  570.2 3.3 dynamic-slice_bitcast_fusion.1
  576.5 5.5 collective-permute-start.20
  586.2 55.9 %collective-permute-done.17 = bf16[2,256,2048]{2,1,0:T(8,128)(2,1)} collective-permute-done((bf16[2,256,2048]{2,1,0:T(8,128)(2,1)}, bf16[2,256,2048]{2,1,0:T(8,128)(2,1)}, u32[]{:S(2)}, u32[]{:S(2)}) %collective-permute-start.17) | collective-permute-done | bytes 2097184 | tf_op jit(solution)/shard_map/ppermute | solution.py:493
  650.6 22.2 %collective-permute-done.21 = bf16[256,2048]{1,0:T(8,128)(2,1)S(1)} collective-permute-done((bf16[256,2048]{1,0:T(8,128)(2,1)S(1)}, bf16[256,2048]{1,0:T(8,128)(2,1)S(1)}, u32[]{:S(2)}, u32[]{:S(2)}) %collective-permute-start.21) | collective-permute-done | bytes 1048608 | tf_op jit(solution)/shard_map/ppermute | solution.py:493
  678.9 3.9 multiply_reduce_fusion
  682.9 4.2 add_convert_fusion.1
  687.2 6.9 collective-permute-start.25
  695.4 4.5 add_convert_fusion.3
  699.9 5.5 collective-permute-start.23
  706.7 63.9 %collective-permute-done.23 = bf16[8,384,256]{2,1,0:T(8,128)(2,1)} collective-permute-done((bf16[8,384,256]{2,1,0:T(8,128)(2,1)S(1)}, bf16[8,384,256]{2,1,0:T(8,128)(2,1)}, u32[]{:S(2)}, u32[]{:S(2)}) %collective-permute-start.23) | collective-permute-done | bytes 1572896 | tf_op jit(solution)/shard_map/ppermute | solution.py:542
  770.6 5.5 collective-permute-done.24
  784.5 58.2 %attend_back.1.a_ref = bf16[4096,768]{1,0:T(8,128)(2,1)} custom-call(s32[8]{0:T(128)} %get-tuple-element.96.lo_ref, s32[8]{0:T(128)} %get-tuple-element.97.full_ref, s32[1,4096]{1,0:T(1,128)} %add_maximum_fusion.low_ref, bf16[256,4096]{1,0:T(8,128)(2,1)} %get-tuple-element.106.q_ref, bf16[4096,2048]{1,0:T(8,128)(2,1)} %all-gather.12.cloned.1.call-done.hidden_ref, ...), custom_call_target="tpu_custom_call" | custom-call | flops 103079215104 | bytes 25165824 | tf_op jit(solution)/shard_map/attend_back/pallas_call | solution.py:299
  842.7 37.6 %collective-permute-done.29 = bf16[512,2048]{1,0:T(8,128)(2,1)} collective-permute-done((bf16[512,2048]{1,0:T(8,128)(2,1)S(1)}, bf16[512,2048]{1,0:T(8,128)(2,1)}, u32[]{:S(2)}, u32[]{:S(2)}) %collective-permute-start.29) | collective-permute-done | bytes 2097184 | tf_op jit(solution)/shard_map/ppermute | solution.py:542
  880.2 18.0 %rows_product.1 = bf16[4096,2048]{1,0:T(8,128)(2,1)} custom-call(bf16[4096,768]{1,0:T(8,128)(2,1)} %attend_back.1.a_ref, bf16[768,2048]{1,0:T(8,128)(2,1)} %bitcast.198), custom_call_target="tpu_custom_call" | custom-call | flops 12884901888 | bytes 23068672 | tf_op jit(solution)/shard_map/rows_product/pallas_call | solution.py:441
  899.8 8.5 convolution_convert_fusion.2
  908.6 20.7 %multiply_convert_fusion = bf16[768,2048]{1,0:T(8,128)(2,1)S(1)} fusion(bf16[4096,768]{1,0:T(8,128)(2,1)} %attend_back.1.a_ref, bf16[4096,2048]{1,0:T(8,128)(2,1)} %all-gather.6.cloned.1.call-done.x_ref, f32[2048]{0:T(1024)S(1)} %bitcast.251), kind=kOutput, calls=%fused_computation.10 | convolution fusion | flops 12888047616 | bytes 26222592 | tf_op jit(solution)/shard_map/dot_general | solution.py:28
  931.4 12.6 %collective-permute-start.30 = (bf16[8,256,256]{2,0,1:T(8,128)(2,1)S(1)}, bf16[8,256,256]{2,0,1:T(8,128)(2,1)S(1)}, u32[]{:S(2)}, u32[]{:S(2)}) collective-permute-start(bf16[8,256,256]{2,0,1:T(8,128)(2,1)S(1)} %get-tuple-element.213), channel_id=1, source_target_pairs={{0,1},{1,2},{4,5},{5,6},{8,9},{9,10},{12,13},{13,14},{16,17},{17,1... | collective-permute-start | bytes 3145736 | tf_op jit(solution)/shard_map/ppermute | solution.py:542
  946.0 21.4 %collective-permute-done.30 = bf16[8,256,256]{2,0,1:T(8,128)(2,1)S(1)} collective-permute-done((bf16[8,256,256]{2,0,1:T(8,128)(2,1)S(1)}, bf16[8,256,256]{2,0,1:T(8,128)(2,1)S(1)}, u32[]{:S(2)}, u32[]{:S(2)}) %collective-permute-start.30) | collective-permute-done | bytes 1048608 | tf_op jit(solution)/shard_map/ppermute | solution.py:542
  967.4 21.3 %collective-permute-done.31 = bf16[8,256,256]{2,0,1:T(8,128)(2,1)S(1)} collective-permute-done((bf16[8,256,256]{2,0,1:T(8,128)(2,1)S(1)}, bf16[8,256,256]{2,0,1:T(8,128)(2,1)S(1)}, u32[]{:S(2)}, u32[]{:S(2)}) %collective-permute-start.31) | collective-permute-done | bytes 1048608 | tf_op jit(solution)/shard_map/ppermute | solution.py:542
  990.9 7.3 collective-permute-start.32
  999.7 19.4 %reduce-scatter.8.cloned.1.call-done = bf16[512,2048]{1,0:T(8,128)(2,1)} async-done(((bf16[4096,2048]{1,0:T(8,128)(2,1)}), bf16[512,2048]{1,0:T(8,128)(2,1)}) %reduce-scatter.8.cloned.1.call-update) | async-done | bytes 2097168 | tf_op jit(solution)/shard_map/reduce_scatter | solution.py:589
  1021.4 3.7 collective-permute-done.34
  1028.3 5.1 fusion.8
  1034.8 3.6 add_convert_fusion.2
  1038.5 3.6 all-to-all-start.4
  1042.1 21.0 %all-to-all-done.4 = bf16[8,384,256]{2,1,0:T(8,128)(2,1)S(1)} async-done(((bf16[8,384,256]{2,1,0:T(8,128)(2,1)}), bf16[8,384,256]{2,1,0:T(8,128)(2,1)S(1)}, u32[]{:S(2)}, u32[]{:S(2)}) %all-to-all-start.4) | async-done | bytes 1572896 | tf_op jit(solution)/shard_map/all_to_all | solution.py:539
  1066.6 3.2 bitcast_dynamic-update-slice_fusion.5
  1069.8 3.2 bitcast_dynamic-update-slice_fusion.4
  1073.0 3.3 bitcast_dynamic-update-slice_fusion.3
  1080.9 3.3 bitcast_dynamic-update-slice_fusion
  1084.9 3.3 all-to-all-start.2
  1092.9 3.6 all-to-all-start.3
  1099.9 3.2 bitcast_dynamic-update-slice_fusion.6
  1107.4 8.5 constant_dynamic-slice_fusion
  1119.4 61.2 %all-gather.14.cloned.1.call-done = bf16[2048,2048]{1,0:T(8,128)(2,1)} async-done(((bf16[512,2048]{1,0:T(8,128)(2,1)}), bf16[2048,2048]{1,0:T(8,128)(2,1)}) %all-gather.14.cloned.1.call-update) | async-done | bytes 8388624 | tf_op jit(solution)/shard_map/all_gather | solution.py:781
  1180.6 11.7 convert.29
  (275 shorter events, 164.3 us)
Async XLA Ops:
  7.2 110.1 %copy-start = (s32[4,8]{1,0:T(4,128)S(1)}, s32[4,8]{1,0:T(4,128)}, u32[]{:S(2)}) copy-start(s32[4,8]{1,0:T(4,128)} %param.9) | copy-start | bytes 388
  7.2 110.1 %all-gather.6.cloned.1.call-start = ((), (), s32[]{:S(2)}) async-start(), calls=%async_computation.8 | async-start | bytes 18874368 | tf_op jit(solution)/shard_map/all_gather | solution.py:586
  9.9 13.9 %copy-start.19 = (bf16[3,256,512]{2,1,0:T(8,128)(2,1)S(1)}, bf16[3,256,512]{2,1,0:T(8,128)(2,1)}, u32[]{:S(2)}) copy-start(bf16[3,256,512]{2,1,0:T(8,128)(2,1)} %param.11) | copy-start | bytes 2359300
  9.9 14.1 %copy-start.20 = (bf16[512,256]{1,0:T(8,128)(2,1)S(1)}, bf16[512,256]{1,0:T(8,128)(2,1)}, u32[]{:S(2)}) copy-start(bf16[512,256]{1,0:T(8,128)(2,1)} %param.12) | copy-start | bytes 786436
  13.3 205.4 %all-gather.8.cloned.1.call-start = ((), (), s32[]{:S(2)}) async-start(), calls=%async_computation.9 | async-start | bytes 18874368 | tf_op jit(solution)/shard_map/all_gather | solution.py:586
  54.2 28.6 %copy-start.13 = (bf16[8,1,3,64,256]{4,0,3,2,1:T(8,128)(2,1)}, bf16[8,1,3,64,256]{4,0,3,2,1:T(8,128)(2,1)S(1)}, u32[]{:S(2)}) copy-start(bf16[8,1,3,64,256]{4,0,3,2,1:T(8,128)(2,1)S(1)} %copy.116) | copy-start | bytes 2359300
  54.2 17.7 %collective-permute-start = (bf16[8,192,256]{2,0,1:T(8,128)(2,1)S(1)}, bf16[8,192,256]{2,0,1:T(8,128)(2,1)S(1)}, u32[]{:S(2)}, u32[]{:S(2)}) collective-permute-start(bf16[8,192,256]{2,0,1:T(8,128)(2,1)S(1)} %bitcast.228), channel_id=1, source_target_pairs={{0,1},{1,2},{2,3},{4,5},{5,6},{6,7},{8,9},{9,10},{10,11},{12,13},{... | collective-permute-start | bytes 2359304 | tf_op jit(solution)/shard_map/ppermute | solution.py:542
  57.8 18.3 %collective-permute-start.1 = (bf16[8,192,256]{2,0,1:T(8,128)(2,1)S(1)}, bf16[8,192,256]{2,0,1:T(8,128)(2,1)S(1)}, u32[]{:S(2)}, u32[]{:S(2)}) collective-permute-start(bf16[8,192,256]{2,0,1:T(8,128)(2,1)S(1)} %bitcast.229), channel_id=1, source_target_pairs={{1,0},{2,1},{3,2},{5,4},{6,5},{7,6},{9,8},{10,9},{11,10},{13,12},{... | collective-permute-start | bytes 2359304 | tf_op jit(solution)/shard_map/ppermute | solution.py:542
  71.9 11.7 collective-permute-start.3
  76.0 22.3 %collective-permute-start.4 = (bf16[8,192,256]{2,0,1:T(8,128)(2,1)S(1)}, bf16[8,192,256]{2,0,1:T(8,128)(2,1)}, u32[]{:S(2)}, u32[]{:S(2)}) collective-permute-start(bf16[8,192,256]{2,0,1:T(8,128)(2,1)S(1)} %collective-permute-done.1), channel_id=1, source_target_pairs={{1,0},{2,1},{5,4},{6,5},{9,8},{10,9},{13,12},{14,13},{17,16},{18,1... | collective-permute-start | bytes 2359304 | tf_op jit(solution)/shard_map/ppermute | solution.py:542
  78.3 34.2 %collective-permute-start.2 = (bf16[8,192,256]{2,0,1:T(8,128)(2,1)}, bf16[8,192,256]{2,0,1:T(8,128)(2,1)}, u32[]{:S(2)}, u32[]{:S(2)}) collective-permute-start(bf16[8,192,256]{2,0,1:T(8,128)(2,1)} %broadcast_select_fusion.8), channel_id=1, source_target_pairs={{1,3},{2,0},{5,7},{6,4},{9,11},{10,8},{13,15},{14,12},{17,19},{18,... | collective-permute-start | bytes 2359304 | tf_op jit(solution)/shard_map/ppermute | solution.py:542
  118.4 16.3 %copy-start.24 = (f32[1,2048]{1,0:T(1,128)}, f32[1,2048]{1,0:T(1,128)S(1)}, u32[]{:S(2)}) copy-start(f32[1,2048]{1,0:T(1,128)S(1)} %get-tuple-element.228) | copy-start | bytes 24580
  118.4 239.7 %copy-start.21 = (f32[1,2048]{1,0:T(1,128)}, f32[1,2048]{1,0:T(1,128)S(1)}, u32[]{:S(2)}) copy-start(f32[1,2048]{1,0:T(1,128)S(1)} %get-tuple-element.227) | copy-start | bytes 24580
  121.9 21.5 %collective-permute-start.5 = (bf16[8,64,256]{2,0,1:T(8,128)(2,1)}, bf16[8,64,256]{2,0,1:T(8,128)(2,1)S(1)}, u32[]{:S(2)}, u32[]{:S(2)}) collective-permute-start(bf16[8,64,256]{2,0,1:T(8,128)(2,1)} %bitcast.186), channel_id=1, source_target_pairs={{0,1},{1,2},{2,3},{4,5},{5,6},{6,7},{8,9},{9,10},{10,11},{12,13},{... | collective-permute-start | bytes 786440 | tf_op jit(solution)/shard_map/ppermute | solution.py:542
  125.3 18.1 %collective-permute-start.6 = (bf16[8,64,256]{2,0,1:T(8,128)(2,1)}, bf16[8,64,256]{2,0,1:T(8,128)(2,1)}, u32[]{:S(2)}, u32[]{:S(2)}) collective-permute-start(bf16[8,64,256]{2,0,1:T(8,128)(2,1)} %bitcast.186), channel_id=1, source_target_pairs={{1,0},{2,1},{3,2},{5,4},{6,5},{7,6},{9,8},{10,9},{11,10},{13,12},{... | collective-permute-start | bytes 786440 | tf_op jit(solution)/shard_map/ppermute | solution.py:542
  143.4 30.4 %collective-permute-start.7 = (bf16[8,64,256]{2,0,1:T(8,128)(2,1)S(1)}, bf16[8,64,256]{2,0,1:T(8,128)(2,1)S(1)}, u32[]{:S(2)}, u32[]{:S(2)}) collective-permute-start(bf16[8,64,256]{2,0,1:T(8,128)(2,1)S(1)} %collective-permute-done.5), channel_id=1, source_target_pairs={{1,2},{2,3},{5,6},{6,7},{9,10},{10,11},{13,14},{14,15},{17,18},{18... | collective-permute-start | bytes 786440 | tf_op jit(solution)/shard_map/ppermute | solution.py:542
  144.0 29.7 %collective-permute-start.8 = (bf16[8,64,256]{2,0,1:T(8,128)(2,1)}, bf16[8,64,256]{2,0,1:T(8,128)(2,1)S(1)}, u32[]{:S(2)}, u32[]{:S(2)}) collective-permute-start(bf16[8,64,256]{2,0,1:T(8,128)(2,1)} %collective-permute-done.6), channel_id=1, source_target_pairs={{1,0},{2,1},{5,4},{6,5},{9,8},{10,9},{13,12},{14,13},{17,16},{18,1... | collective-permute-start | bytes 786440 | tf_op jit(solution)/shard_map/ppermute | solution.py:542
  146.3 27.4 %collective-permute-start.9 = (bf16[8,64,256]{2,0,1:T(8,128)(2,1)S(1)}, bf16[8,64,256]{2,0,1:T(8,128)(2,1)S(1)}, u32[]{:S(2)}, u32[]{:S(2)}) collective-permute-start(bf16[8,64,256]{2,0,1:T(8,128)(2,1)S(1)} %broadcast_select_fusion.10), channel_id=1, source_target_pairs={{1,3},{2,0},{5,7},{6,4},{9,11},{10,8},{13,15},{14,12},{17,19},{18,... | collective-permute-start | bytes 786440 | tf_op jit(solution)/shard_map/ppermute | solution.py:542
  147.6 63.8 %all-to-all-start.1 = ((bf16[8,384,256]{2,1,0:T(8,128)(2,1)}), bf16[8,384,256]{2,1,0:T(8,128)(2,1)S(1)}, u32[]{:S(2)}, u32[]{:S(2)}) async-start(bf16[8,384,256]{2,1,0:T(8,128)(2,1)} %pad_maximum_fusion.1), calls=%async_computation.1 | async-start | bytes 3145728 | tf_op jit(solution)/shard_map/all_to_all | solution.py:539
  151.2 202.5 %reduce-scatter.4.cloned.1.call-start = ((), (), s32[]{:S(2)}) async-start(), calls=%async_computation.10 | async-start | bytes 18874368 | tf_op jit(solution)/shard_map/reduce_scatter | solution.py:589
  218.8 233.2 %all-gather.10.cloned.1.call-start = ((), (), s32[]{:S(2)}) async-start(), calls=%async_computation.11 | async-start | bytes 18874368 | tf_op jit(solution)/shard_map/all_gather | solution.py:586
  218.8 57.0 %collective-permute-start.10 = (bf16[8,384,256]{2,1,0:T(8,128)(2,1)S(1)}, bf16[8,384,256]{2,1,0:T(8,128)(2,1)S(1)}, u32[]{:S(2)}, u32[]{:S(2)}) collective-permute-start(bf16[8,384,256]{2,1,0:T(8,128)(2,1)S(1)} %all-to-all-done.1), channel_id=1, source_target_pairs={{0,1},{1,2},{2,3},{4,5},{5,6},{6,7},{8,9},{9,10},{10,11},{12,13},{... | collective-permute-start | bytes 4718600 | tf_op jit(solution)/shard_map/ppermute | solution.py:542
  241.8 38.4 %collective-permute-start.12 = (bf16[8,384,256]{2,1,0:T(8,128)(2,1)S(1)}, bf16[8,384,256]{2,1,0:T(8,128)(2,1)}, u32[]{:S(2)}, u32[]{:S(2)}) collective-permute-start(bf16[8,384,256]{2,1,0:T(8,128)(2,1)S(1)} %all-to-all-done.1), channel_id=1, source_target_pairs={{1,0},{2,1},{3,2},{5,4},{6,5},{7,6},{9,8},{10,9},{11,10},{13,12},{... | collective-permute-start | bytes 4718600 | tf_op jit(solution)/shard_map/ppermute | solution.py:542
  283.0 72.9 %collective-permute-start.14 = (bf16[8,384,256]{2,1,0:T(8,128)(2,1)}, bf16[8,384,256]{2,1,0:T(8,128)(2,1)}, u32[]{:S(2)}, u32[]{:S(2)}) collective-permute-start(bf16[8,384,256]{2,1,0:T(8,128)(2,1)} %broadcast_select_fusion.5), channel_id=1, source_target_pairs={{1,3},{2,0},{5,7},{6,4},{9,11},{10,8},{13,15},{14,12},{17,19},{18,... | collective-permute-start | bytes 4718600 | tf_op jit(solution)/shard_map/ppermute | solution.py:542
  284.2 71.6 %collective-permute-start.11 = (bf16[8,384,256]{2,1,0:T(8,128)(2,1)S(1)}, bf16[8,384,256]{2,1,0:T(8,128)(2,1)}, u32[]{:S(2)}, u32[]{:S(2)}) collective-permute-start(bf16[8,384,256]{2,1,0:T(8,128)(2,1)S(1)} %collective-permute-done.10), channel_id=1, source_target_pairs={{1,2},{2,3},{5,6},{6,7},{9,10},{10,11},{13,14},{14,15},{17,18},{18... | collective-permute-start | bytes 4718600 | tf_op jit(solution)/shard_map/ppermute | solution.py:542
  286.1 69.8 %collective-permute-start.13 = (bf16[8,384,256]{2,1,0:T(8,128)(2,1)}, bf16[8,384,256]{2,1,0:T(8,128)(2,1)}, u32[]{:S(2)}, u32[]{:S(2)}) collective-permute-start(bf16[8,384,256]{2,1,0:T(8,128)(2,1)} %collective-permute-done.12), channel_id=1, source_target_pairs={{1,0},{2,1},{5,4},{6,5},{9,8},{10,9},{13,12},{14,13},{17,16},{18,1... | collective-permute-start | bytes 4718600 | tf_op jit(solution)/shard_map/ppermute | solution.py:542
  361.9 314.2 %reduce-scatter.6.cloned.1.call-start = ((), (), s32[]{:S(2)}) async-start(), calls=%async_computation.12 | async-start | bytes 18874368 | tf_op jit(solution)/shard_map/reduce_scatter | solution.py:589
  369.5 13.0 %slice-start.3 = ((s8[16777216]{0:T(1024)(128)(4,1)}), s8[4194304]{0:T(1024)(128)(4,1)S(1)}, s32[]{:S(2)}) async-start(s8[16777216]{0:T(1024)(128)(4,1)} %bitcast.261), calls=%async_computation.19 | async-start | bytes 8388608
  369.5 13.0 %slice-start.4 = ((s8[16777216]{0:T(1024)(128)(4,1)}), s8[4194304]{0:T(1024)(128)(4,1)S(1)}, s32[]{:S(2)}) async-start(s8[16777216]{0:T(1024)(128)(4,1)} %bitcast.261), calls=%async_computation.20 | async-start | bytes 8388608
  370.7 11.8 slice-start.5
  487.0 291.1 %all-gather.12.cloned.1.call-start = ((), (), s32[]{:S(2)}) async-start(), calls=%async_computation.13 | async-start | bytes 18874368 | tf_op jit(solution)/shard_map/all_gather | solution.py:586
  512.3 44.6 %collective-permute-start.15 = (bf16[2048,2048]{1,0:T(8,128)(2,1)}, bf16[2048,2048]{1,0:T(8,128)(2,1)}, u32[]{:S(2)}, u32[]{:S(2)}) collective-permute-start(bf16[2048,2048]{1,0:T(8,128)(2,1)} %get-tuple-element.128), channel_id=1, source_target_pairs={{0,4},{4,0},{1,5},{5,1},{2,6},{6,2},{3,7},{7,3},{8,12},{12,8},{9,1... | collective-permute-start | bytes 25165832 | tf_op jit(solution)/shard_map/ppermute | solution.py:493
  569.4 72.7 %collective-permute-start.17 = (bf16[2,256,2048]{2,1,0:T(8,128)(2,1)}, bf16[2,256,2048]{2,1,0:T(8,128)(2,1)}, u32[]{:S(2)}, u32[]{:S(2)}) collective-permute-start(bf16[2,256,2048]{2,1,0:T(8,128)(2,1)} %dynamic-slice_bitcast_fusion), channel_id=1, source_target_pairs={{0,16},{16,0},{1,17},{17,1},{2,18},{18,2},{3,19},{19,3},{4,20},{20... | collective-permute-start | bytes 6291464 | tf_op jit(solution)/shard_map/ppermute | solution.py:493
  573.4 71.7 %collective-permute-start.16 = (bf16[2,256,2048]{2,1,0:T(8,128)(2,1)}, bf16[2,256,2048]{2,1,0:T(8,128)(2,1)}, u32[]{:S(2)}, u32[]{:S(2)}) collective-permute-start(bf16[2,256,2048]{2,1,0:T(8,128)(2,1)} %dynamic-slice_bitcast_fusion.1), channel_id=1, source_target_pairs={{0,8},{8,0},{1,9},{9,1},{2,10},{10,2},{3,11},{11,3},{4,12},{12,4},... | collective-permute-start | bytes 6291464 | tf_op jit(solution)/shard_map/ppermute | solution.py:493
  576.5 71.1 %collective-permute-start.20 = (bf16[8,384,256]{2,1,0:T(8,128)(2,1)}, bf16[8,384,256]{2,1,0:T(8,128)(2,1)}, u32[]{:S(2)}, u32[]{:S(2)}) collective-permute-start(bf16[8,384,256]{2,1,0:T(8,128)(2,1)} %broadcast_select_fusion.3), channel_id=1, source_target_pairs={{0,2},{3,1},{4,6},{7,5},{8,10},{11,9},{12,14},{15,13},{16,18},{19,... | collective-permute-start | bytes 4718600 | tf_op jit(solution)/shard_map/ppermute | solution.py:542
  582.0 66.3 %collective-permute-start.18 = (bf16[8,384,256]{2,1,0:T(8,128)(2,1)}, bf16[8,384,256]{2,1,0:T(8,128)(2,1)}, u32[]{:S(2)}, u32[]{:S(2)}) collective-permute-start(bf16[8,384,256]{2,1,0:T(8,128)(2,1)} %bitcast.41), channel_id=1, source_target_pairs={{0,1},{1,2},{4,5},{5,6},{8,9},{9,10},{12,13},{13,14},{16,17},{17,1... | collective-permute-start | bytes 4718600 | tf_op jit(solution)/shard_map/ppermute | solution.py:542
  584.4 63.9 %collective-permute-start.19 = (bf16[8,384,256]{2,1,0:T(8,128)(2,1)}, bf16[8,384,256]{2,1,0:T(8,128)(2,1)}, u32[]{:S(2)}, u32[]{:S(2)}) collective-permute-start(bf16[8,384,256]{2,1,0:T(8,128)(2,1)} %bitcast.41), channel_id=1, source_target_pairs={{2,1},{3,2},{6,5},{7,6},{10,9},{11,10},{14,13},{15,14},{18,17},{19... | collective-permute-start | bytes 4718600 | tf_op jit(solution)/shard_map/ppermute | solution.py:542
  586.2 58.9 %copy-start.8 = (bf16[2,2,256,2048]{3,2,1,0:T(8,128)(2,1)S(1)}, bf16[2,2,256,2048]{3,2,1,0:T(8,128)(2,1)}, u32[]{:S(2)}) copy-start(bf16[2,2,256,2048]{3,2,1,0:T(8,128)(2,1)} %get-tuple-element.207) | copy-start | bytes 12582916
  648.4 24.4 %collective-permute-start.21 = (bf16[256,2048]{1,0:T(8,128)(2,1)S(1)}, bf16[256,2048]{1,0:T(8,128)(2,1)S(1)}, u32[]{:S(2)}, u32[]{:S(2)}) collective-permute-start(bf16[256,2048]{1,0:T(8,128)(2,1)S(1)} %dynamic-slice_bitcast_fusion.4), channel_id=1, source_target_pairs={{0,16},{16,0},{1,17},{17,1},{2,18},{18,2},{3,19},{19,3},{4,20},{20... | collective-permute-start | bytes 3145736 | tf_op jit(solution)/shard_map/ppermute | solution.py:493
  649.9 23.6 %collective-permute-start.22 = (bf16[256,2048]{1,0:T(8,128)(2,1)S(1)}, bf16[256,2048]{1,0:T(8,128)(2,1)S(1)}, u32[]{:S(2)}, u32[]{:S(2)}) collective-permute-start(bf16[256,2048]{1,0:T(8,128)(2,1)S(1)} %dynamic-slice_bitcast_fusion.3), channel_id=1, source_target_pairs={{0,8},{8,0},{1,9},{9,1},{2,10},{10,2},{3,11},{11,3},{4,12},{12,4},... | collective-permute-start | bytes 3145736 | tf_op jit(solution)/shard_map/ppermute | solution.py:493
  687.1 331.9 %reduce-scatter.8.cloned.1.call-start = ((), (), s32[]{:S(2)}) async-start(), calls=%async_computation.14 | async-start | bytes 18874368 | tf_op jit(solution)/shard_map/reduce_scatter | solution.py:589
  687.2 88.9 %collective-permute-start.25 = (bf16[512,2048]{1,0:T(8,128)(2,1)}, bf16[512,2048]{1,0:T(8,128)(2,1)}, u32[]{:S(2)}, u32[]{:S(2)}) collective-permute-start(bf16[512,2048]{1,0:T(8,128)(2,1)} %get-tuple-element.215), channel_id=1, source_target_pairs={{0,1},{1,2},{2,3},{4,5},{5,6},{6,7},{8,9},{9,10},{10,11},{12,13},{... | collective-permute-start | bytes 6291464 | tf_op jit(solution)/shard_map/ppermute | solution.py:542
  694.1 82.0 %collective-permute-start.26 = (bf16[512,2048]{1,0:T(8,128)(2,1)}, bf16[512,2048]{1,0:T(8,128)(2,1)}, u32[]{:S(2)}, u32[]{:S(2)}) collective-permute-start(bf16[512,2048]{1,0:T(8,128)(2,1)} %get-tuple-element.215), channel_id=1, source_target_pairs={{1,0},{2,1},{3,2},{5,4},{6,5},{7,6},{9,8},{10,9},{11,10},{13,12},{... | collective-permute-start | bytes 6291464 | tf_op jit(solution)/shard_map/ppermute | solution.py:542
  699.9 70.7 %collective-permute-start.23 = (bf16[8,384,256]{2,1,0:T(8,128)(2,1)S(1)}, bf16[8,384,256]{2,1,0:T(8,128)(2,1)}, u32[]{:S(2)}, u32[]{:S(2)}) collective-permute-start(bf16[8,384,256]{2,1,0:T(8,128)(2,1)S(1)} %get-tuple-element.218), channel_id=1, source_target_pairs={{0,1},{1,2},{2,3},{4,5},{5,6},{6,7},{8,9},{9,10},{10,11},{12,13},{... | collective-permute-start | bytes 4718600 | tf_op jit(solution)/shard_map/ppermute | solution.py:542
  705.4 70.7 %collective-permute-start.24 = (bf16[8,384,256]{2,1,0:T(8,128)(2,1)S(1)}, bf16[8,384,256]{2,1,0:T(8,128)(2,1)}, u32[]{:S(2)}, u32[]{:S(2)}) collective-permute-start(bf16[8,384,256]{2,1,0:T(8,128)(2,1)S(1)} %get-tuple-element.217), channel_id=1, source_target_pairs={{1,0},{2,1},{3,2},{5,4},{6,5},{7,6},{9,8},{10,9},{11,10},{13,12},{... | collective-permute-start | bytes 4718600 | tf_op jit(solution)/shard_map/ppermute | solution.py:542
  778.1 102.2 %collective-permute-start.27 = (bf16[512,2048]{1,0:T(8,128)(2,1)}, bf16[512,2048]{1,0:T(8,128)(2,1)}, u32[]{:S(2)}, u32[]{:S(2)}) collective-permute-start(bf16[512,2048]{1,0:T(8,128)(2,1)} %collective-permute-done.25), channel_id=1, source_target_pairs={{1,2},{2,3},{5,6},{6,7},{9,10},{10,11},{13,14},{14,15},{17,18},{18... | collective-permute-start | bytes 6291464 | tf_op jit(solution)/shard_map/ppermute | solution.py:542
  781.9 98.3 %collective-permute-start.28 = (bf16[512,2048]{1,0:T(8,128)(2,1)}, bf16[512,2048]{1,0:T(8,128)(2,1)}, u32[]{:S(2)}, u32[]{:S(2)}) collective-permute-start(bf16[512,2048]{1,0:T(8,128)(2,1)} %collective-permute-done.26), channel_id=1, source_target_pairs={{1,0},{2,1},{5,4},{6,5},{9,8},{10,9},{13,12},{14,13},{17,16},{18,1... | collective-permute-start | bytes 6291464 | tf_op jit(solution)/shard_map/ppermute | solution.py:542
  783.2 97.0 %collective-permute-start.29 = (bf16[512,2048]{1,0:T(8,128)(2,1)S(1)}, bf16[512,2048]{1,0:T(8,128)(2,1)}, u32[]{:S(2)}, u32[]{:S(2)}) collective-permute-start(bf16[512,2048]{1,0:T(8,128)(2,1)S(1)} %broadcast_select_fusion), channel_id=1, source_target_pairs={{1,3},{2,0},{5,7},{6,4},{9,11},{10,8},{13,15},{14,12},{17,19},{18,... | collective-permute-start | bytes 6291464 | tf_op jit(solution)/shard_map/ppermute | solution.py:542
  898.2 282.4 %all-gather.14.cloned.1.call-start = ((), (), s32[]{:S(2)}) async-start(), calls=%async_computation.15 | async-start | bytes 10485760 | tf_op jit(solution)/shard_map/all_gather | solution.py:781
  931.4 36.1 %collective-permute-start.30 = (bf16[8,256,256]{2,0,1:T(8,128)(2,1)S(1)}, bf16[8,256,256]{2,0,1:T(8,128)(2,1)S(1)}, u32[]{:S(2)}, u32[]{:S(2)}) collective-permute-start(bf16[8,256,256]{2,0,1:T(8,128)(2,1)S(1)} %get-tuple-element.213), channel_id=1, source_target_pairs={{0,1},{1,2},{4,5},{5,6},{8,9},{9,10},{12,13},{13,14},{16,17},{17,1... | collective-permute-start | bytes 3145736 | tf_op jit(solution)/shard_map/ppermute | solution.py:542
  943.9 44.8 %collective-permute-start.31 = (bf16[8,256,256]{2,0,1:T(8,128)(2,1)S(1)}, bf16[8,256,256]{2,0,1:T(8,128)(2,1)S(1)}, u32[]{:S(2)}, u32[]{:S(2)}) collective-permute-start(bf16[8,256,256]{2,0,1:T(8,128)(2,1)S(1)} %get-tuple-element.212), channel_id=1, source_target_pairs={{0,2},{3,1},{4,6},{7,5},{8,10},{11,9},{12,14},{15,13},{16,18},{19,... | collective-permute-start | bytes 3145736 | tf_op jit(solution)/shard_map/ppermute | solution.py:542
  945.3 43.4 %collective-permute-start.33 = (bf16[8,256,256]{2,0,1:T(8,128)(2,1)S(1)}, bf16[8,256,256]{2,0,1:T(8,128)(2,1)S(1)}, u32[]{:S(2)}, u32[]{:S(2)}) collective-permute-start(bf16[8,256,256]{2,0,1:T(8,128)(2,1)S(1)} %get-tuple-element.213), channel_id=1, source_target_pairs={{2,1},{3,2},{6,5},{7,6},{10,9},{11,10},{14,13},{15,14},{18,17},{19... | collective-permute-start | bytes 3145736 | tf_op jit(solution)/shard_map/ppermute | solution.py:542
  990.9 30.5 %collective-permute-start.32 = (bf16[8,256,256]{2,0,1:T(8,128)(2,1)}, bf16[8,256,256]{2,0,1:T(8,128)(2,1)S(1)}, u32[]{:S(2)}, u32[]{:S(2)}) collective-permute-start(bf16[8,256,256]{2,0,1:T(8,128)(2,1)} %get-tuple-element.222), channel_id=1, source_target_pairs={{0,1},{1,2},{2,3},{4,5},{5,6},{6,7},{8,9},{9,10},{10,11},{12,13},{... | collective-permute-start | bytes 3145736 | tf_op jit(solution)/shard_map/ppermute | solution.py:542
  998.1 26.9 %copy-start.30 = (f32[512]{0:T(512)S(1)}, f32[512]{0:T(512)}, u32[]{:S(2)}) copy-start(f32[512]{0:T(512)} %copy-done.29) | copy-start | bytes 6148
  998.1 26.9 %collective-permute-start.34 = (bf16[8,256,256]{2,0,1:T(8,128)(2,1)}, bf16[8,256,256]{2,0,1:T(8,128)(2,1)S(1)}, u32[]{:S(2)}, u32[]{:S(2)}) collective-permute-start(bf16[8,256,256]{2,0,1:T(8,128)(2,1)} %get-tuple-element.221), channel_id=1, source_target_pairs={{1,0},{2,1},{3,2},{5,4},{6,5},{7,6},{9,8},{10,9},{11,10},{13,12},{... | collective-permute-start | bytes 3145736 | tf_op jit(solution)/shard_map/ppermute | solution.py:542
  1038.5 24.6 %all-to-all-start.4 = ((bf16[8,384,256]{2,1,0:T(8,128)(2,1)}), bf16[8,384,256]{2,1,0:T(8,128)(2,1)S(1)}, u32[]{:S(2)}, u32[]{:S(2)}) async-start(bf16[8,384,256]{2,1,0:T(8,128)(2,1)} %add_convert_fusion.2), calls=%async_computation.7 | async-start | bytes 3145728 | tf_op jit(solution)/shard_map/all_to_all | solution.py:539
  1084.9 8.0 all-to-all-start.2
  1092.9 23.7 %all-to-all-start.3 = ((bf16[8,256,256]{2,1,0:T(8,128)(2,1)}), bf16[8,256,256]{2,1,0:T(8,128)(2,1)S(1)}, u32[]{:S(2)}, u32[]{:S(2)}) async-start(bf16[8,256,256]{2,1,0:T(8,128)(2,1)} %copy.139), calls=%async_computation.6 | async-start | bytes 2097152 | tf_op jit(solution)/shard_map/all_to_all | solution.py:539
  1096.5 6.6 collective-permute-start.35
  1098.6 5.5 collective-permute-start.36
  1104.1 11.8 collective-permute-start.37
  1105.4 10.5 collective-permute-start.38
  1106.1 9.8 collective-permute-start.39
  1180.6 11.7 copy-start.1
  (32 other events, 133.3 us)
Sparse Core Ops, SparseCore 0:
  13.4 103.7 all-gather.5
  119.1 99.5 all-gather.7
  222.9 130.7 reduce-scatter.3
  362.0 89.8 all-gather.9
  487.1 144.6 reduce-scatter.5
  687.3 90.7 all-gather.11
  898.4 120.6 reduce-scatter.7
  1033.6 146.9 all-gather.13

commit v6 on v5

--- a/solution.py
+++ b/solution.py
@@ -493,11 +493,12 @@
     return lax.ppermute(a, axis, [(0, 1), (1, 0)])
 
 
-def halve(a, axis, dim):
+def halve(terms, axis, dim):
+    def part(index):
+        return sum(lax.dynamic_index_in_dim(a, index, dim, False).astype(f32) for a in terms)
+
     index = lax.axis_index(axis)
-    mine = lax.dynamic_index_in_dim(a, index, dim, False)
-    other = lax.dynamic_index_in_dim(a, 1 - index, dim, False)
-    return mine.astype(f32) + swap(other, axis).astype(f32)
+    return part(index) + swap(part(1 - index).astype(bf16), axis).astype(f32)
 
 
 def after(a, *others):
@@ -588,17 +589,15 @@
     def scatter_plane(a):
         return lax.psum_scatter(a.astype(bf16), plane, scatter_dimension=0, tiled=True).astype(f32)
 
-    def scatter_middle(a):
-        if not cube:
-            return [scatter_plane(a)]
-        half = a.shape[2] // 2
-        one, two = a[:, :, :half], a[:, :, half:]
+    def scatter_middle(terms):
+        half = own_len // 2
+        one, two = [a[:, :, :half] for a in terms], [a[:, :, half:] for a in terms]
         return [halve(one, "pair", 1).astype(bf16), halve(two, "chips", 0).astype(bf16)]
 
     def scatter_end(halves):
-        if not cube:
-            return halves[0]
-        return jnp.concatenate([halve(halves[0], "chips", 0), halve(halves[1], "pair", 0)], axis=0)
+        return jnp.concatenate(
+            [halve(halves[:1], "chips", 0), halve(halves[1:], "pair", 0)], axis=0
+        )
 
     def own(a):
         return lax.dynamic_slice(a, (seq, first_row, 0), (1, own_len, model))[0]
@@ -610,10 +609,6 @@
         a = lax.all_gather(a, "seq", axis=0, tiled=True)
         return exchange(a.reshape(n_context, heads * m, rows))
 
-    def heads_spread(a):
-        near = spread_near(a)
-        return spread_blocks(a, near, spread_far(near))
-
     def heads_whole(blocks, m):
         a = jnp.stack(blocks).reshape(len(blocks), n_context, heads // len(blocks), m, rows)
         return a.transpose(0, 2, 3, 1, 4).reshape(heads, m, model)
@@ -634,9 +629,8 @@
     normal_one = rows_in * inverse_one
     normal_own = normal_one.astype(bf16)
     normal_all = gather_plane(normal_own)
-    gains = lax.all_gather(after(norm_gains, normal_own), context, axis=1, tiled=True).astype(f32)
-
-    qkv_local, out_local, gains = lax.optimization_barrier((qkv_weight, out_weight, gains))
+
+    qkv_local, out_local, _ = lax.optimization_barrier((qkv_weight, out_weight, normal_own))
     heads_local = jnp.concatenate(
         [
             qkv_local.reshape(3, rows, block_heads, HEAD_DIM).transpose(2, 0, 3, 1),
@@ -648,14 +642,10 @@
     heads_block = heads_block.reshape(n_context, -1, 4, HEAD_DIM, rows)
     qkv_block = heads_block[:, :, :3].reshape(n_context, -1, rows)
     out_block = heads_block[:, :, 3].reshape(n_context, -1, rows)
-    qkv_blocks = heads_spread(qkv_block) if split_heads else [qkv_block]
-    qkv_blocks, out_block, gateup_local, down_local = lax.optimization_barrier(
-        (qkv_blocks, out_block, gateup_weight, down_weight)
-    )
-    out_near = spread_near(out_block) if split_heads else []
-    qkv_t = heads_whole(qkv_blocks, 3 * HEAD_DIM).reshape(heads, 3, HEAD_DIM, model)
-    qkv_t = qkv_t.transpose(1, 0, 2, 3).reshape(3 * width, model)
-    qkv_gained = (qkv_t.astype(f32) * gains[0]).astype(bf16)
+    gains_local, gateup_local, down_local, qkv_block, out_block = lax.optimization_barrier(
+        (norm_gains, gateup_weight, down_weight, qkv_block, out_block)
+    )
+    qkv_near = spread_near(qkv_block) if split_heads else []
     gateup_local = gateup_local.reshape(2, rows, n_context, block_hidden).transpose(2, 0, 3, 1)
     hidden_local = jnp.concatenate(
         [
@@ -664,6 +654,20 @@
         ],
         axis=1,
     )
+    qkv_near, hidden_local, qkv_block, out_block = lax.optimization_barrier(
+        (qkv_near, hidden_local, qkv_block, out_block)
+    )
+    if split_heads:
+        qkv_blocks = spread_blocks(qkv_block, qkv_near, spread_far(qkv_near))
+    else:
+        qkv_blocks = [qkv_block]
+    gains = lax.all_gather(gains_local, context, axis=1, tiled=True).astype(f32)
+    out_near = spread_near(out_block) if split_heads else []
+    qkv_blocks, out_near, gains = lax.optimization_barrier((qkv_blocks, out_near, gains))
+    qkv_t = jnp.stack(qkv_blocks)
+    qkv_t = qkv_t.reshape(len(qkv_blocks), n_context, -1, 3, HEAD_DIM, rows)
+    qkv_t = qkv_t.transpose(3, 0, 2, 4, 1, 5).reshape(3 * width, model)
+    qkv_gained = (qkv_t.astype(f32) * gains[0]).astype(bf16)
     cosine, sine = rope_tables(length)
     bounds = attention_bounds(lax.dynamic_slice_in_dim(doc_lengths, seq, 1, 0)[0], length)
     incoming_all = gather_plane(after(incoming, normal_all, *qkv_blocks))
@@ -722,9 +726,9 @@
     feedforward_branch = scatter_plane(feedforward_part)
     if cube:
         second_sums = (mine.astype(f32) + swap(theirs, "core").astype(f32)).astype(bf16)
-        second_sums = second_sums.reshape(n_chips, n_pair, own_len, model)
+        second_sums = [second_sums.reshape(n_chips, n_pair, own_len, model)]
     else:
-        second_sums = jnp.concatenate([theirs, mine], axis=0)
+        second_sums = [jnp.concatenate([theirs, mine], axis=0)]
     down_grad = dot(activation, incoming_all, 0, 0).astype(bf16)
     gateup_grad = dot(grad_gateup, normed_two, 0, 0).astype(bf16)
     hidden_grads = jnp.concatenate(
@@ -738,9 +742,9 @@
     second_sums, hidden_grads = lax.optimization_barrier((second_sums, hidden_grads))
     hidden_grads_far = collect_far(hidden_grads)
     second_halves, hidden_grads_far = lax.optimization_barrier(
-        (scatter_middle(second_sums), hidden_grads_far)
-    )
-    grad_normed_two = scatter_end(second_halves)
+        (scatter_middle(second_sums) if cube else scatter_plane(*second_sums), hidden_grads_far)
+    )
+    grad_normed_two = scatter_end(second_halves) if cube else second_halves
     grad_normed_two, feedforward_branch = lax.optimization_barrier(
         (grad_normed_two, feedforward_branch)
     )

time: 1210 us -> 1190 us (0.983)
  waiting for transfers between devices: 554 us -> 570 us
  starting transfers between devices: 125 us -> 110 us
    all_gather x4, waiting for transfers between devices: 69.7 us -> 94.2 us  [gather_plane(): return lax.all_gather(a, plane, axis=0, tiled=True)]
    ppermute x35, starting transfers between devices: 105 us -> 90.8 us  [send(): return lax.ppermute(a, 'seq', pairs)]
    ppermute x35, waiting for transfers between devices: 234 us -> 222 us  [send(): return lax.ppermute(a, 'seq', pairs)]
    unnamed x103 -> x108, local copies, waits for them, and re-layouts: 44.1 us -> 46.4 us
  transfers between devices with their start and end apart: 52 -> 52, of which waited for: 26 -> 26; matrix products, arithmetic and copies ran while one was open for 18% -> 17% of each run, Pallas kernels for 12% -> 12%
where the time goes in v6:
time: 1190 us
  waiting for transfers between devices  570 us (48%)
  Pallas kernels  191 us (16%)
  starting transfers between devices  110 us (9%)
  other arithmetic  98.7 us (8%)
  local copies, waits for them, and re-layouts  88.2 us (7%)
  matrix products  76.9 us (6%)
  blocking collectives  34.3 us (3%)
  between operations  15.8 us (1%)
    ppermute x35, waiting for transfers between devices, send(): return lax.ppermute(a, 'seq', pairs)  222 us
    all_gather x4, waiting for transfers between devices, gather_plane(): return lax.all_gather(a, plane, axis=0, tiled=True)  94.2 us
    ppermute x35, starting transfers between devices, send(): return lax.ppermute(a, 'seq', pairs)  90.8 us
    reduce_scatter x3, waiting for transfers between devices, scatter_plane(): lax.psum_scatter(a.astype(bf16), plane, scatter_dimension=0, tiled=True)  90.6 us
    ppermute x5, waiting for transfers between devices, swap(): return lax.ppermute(a, axis, [(0, 1), (1, 0)])  78.4 us
    dot_general x5, matrix products, dot(): lax.dot_general(a, b, (((ca,), (cb,)), ((), ())), preferred_element_type=...  76.9 us
    all_gather x1, waiting for transfers between devices, shards(): lax.all_gather(grad_input, ('seq', 'extra'), axis=0, tiled=True).astype(f32)  61.3 us
    pallas_call x1, Pallas kernels, attend_back(): pl.pallas_call(attend_back_kernel, out_shape=jax.ShapeDtypeStruct((length...  58 us
  transfers between devices with their start and end apart: 52, of which 26 were waited for; matrix products, arithmetic and copies ran while one was open for 17% of the time, Pallas kernels for 12%

profile of v6, /device:TPU:0, one launch (start us, length us, event | category | flops | bytes accessed | tf_op | source)
XLA Modules:
  0.0 1185.9 jit_solution(665470244644237500)
XLA Ops:
  9.9 3.4 fusion.3
  13.9 26.3 %all_to_all.25 = bf16[8,256,256]{2,1,0:T(8,128)(2,1)S(1)} all-to-all(bf16[8,256,256]{2,1,0:T(8,128)(2,1)S(1)} %bitcast.222), channel_id=1, replica_groups=mesh['chips'=2,'pair'=2,'core'=2,'seq'=4,'extra'=1] {'chips','pair','core'}, dimensions={0} | all-to-all | bytes 2097152 | tf_op jit(solution)/shard_map/all_to_all | solution.py:540
  42.5 4.5 collective-permute-start
  50.2 11.0 collective-permute-done
  61.1 5.0 collective-permute-done.1
  73.8 7.9 all_gather.19
  81.8 8.8 collective-permute-start.5
  94.3 9.2 collective-permute-done.4
  104.7 4.3 collective-permute-done.6
  125.2 3.6 all-to-all-start.1
  129.3 21.4 %project.1 = (bf16[256,4096]{1,0:T(8,128)(2,1)}, bf16[256,4096]{1,0:T(8,128)(2,1)}, bf16[256,4096]{1,0:T(8,128)(2,1)}, bf16[4,4096,64]{2,1,0:T(8,128)(2,1)}, bf16[4,4096,64]{2,1,0:T(8,128)(2,1)}) custom-call(bf16[4096,2048]{1,0:T(8,128)(2,1)} %all-gather.6.cloned.1.call-done.x_ref, bf16[768,2048]{1,0:T(8,128)(2,1)} %multiply_convert_fusion.1.weight_ref, ...), custom_call_target="tpu_custom_call" | custom-call | flops 12884901888 | bytes 29360128 | tf_op jit(solution)/shard_map/project/pallas_call | solution.py:82
  154.2 34.3 %attend.1 = (bf16[256,4096]{1,0:T(8,128)(2,1)}, f32[4,4096]{1,0:T(4,128)}, bf16[4096,2048]{1,0:T(8,128)(2,1)}) custom-call(s32[8]{0:T(128)} %get-tuple-element.112.lo_ref, s32[8]{0:T(128)} %get-tuple-element.113.full_ref, s32[1,4096]{1,0:T(1,128)} %add_maximum_fusion.low_ref, bf16[256,4096]{1,0:T(8,128)(2,1)} %get-tuple-element.122.q_ref, ...), custom_call_target="tpu_custom_call" | custom-call | flops 51539607552 | bytes 16777216 | tf_op jit(solution)/shard_map/attend/pallas_call | solution.py:263
  188.5 31.6 %all-gather.8.cloned.1.call-done = bf16[4096,2048]{1,0:T(8,128)(2,1)} async-done(((bf16[512,2048]{1,0:T(8,128)(2,1)}), bf16[4096,2048]{1,0:T(8,128)(2,1)}) %all-gather.8.cloned.1.call-update) | async-done | bytes 16777232 | tf_op jit(solution)/shard_map/all_gather | solution.py:587
  220.1 3.5 collective-permute-start.10
  224.9 32.7 %collective-permute-done.10 = bf16[8,384,256]{2,1,0:T(8,128)(2,1)S(1)} collective-permute-done((bf16[8,384,256]{2,1,0:T(8,128)(2,1)S(1)}, bf16[8,384,256]{2,1,0:T(8,128)(2,1)S(1)}, u32[]{:S(2)}, u32[]{:S(2)}) %collective-permute-start.10) | collective-permute-done | bytes 1572896 | tf_op jit(solution)/shard_map/ppermute | solution.py:543
  257.6 4.3 collective-permute-done.12
  269.0 71.2 %reduce-scatter.4.cloned.1.call-done = bf16[512,2048]{1,0:T(8,128)(2,1)} async-done(((bf16[4096,2048]{1,0:T(8,128)(2,1)}), bf16[512,2048]{1,0:T(8,128)(2,1)}) %reduce-scatter.4.cloned.1.call-update) | async-done | bytes 2097168 | tf_op jit(solution)/shard_map/reduce_scatter | solution.py:590
  357.2 3.2 copy-done.7
  361.1 4.4 slice-done
  365.5 3.5 copy.153
  369.0 11.2 fusion.27.ga_ref
  380.3 58.2 %all-gather.10.cloned.1.call-done.x_ref = bf16[4096,2048]{1,0:T(8,128)(2,1)} async-done(((bf16[512,2048]{1,0:T(8,128)(2,1)}), bf16[4096,2048]{1,0:T(8,128)(2,1)}) %all-gather.10.cloned.1.call-update) | async-done | bytes 16777232 | tf_op jit(solution)/shard_map/all_gather | solution.py:587
  438.5 35.0 %feedforward.1 = (bf16[4096,512]{1,0:T(8,128)(2,1)}, bf16[4096,1024]{1,0:T(8,128)(2,1)}, bf16[4096,2048]{1,0:T(8,128)(2,1)}) custom-call(bf16[4096,2048]{1,0:T(8,128)(2,1)} %all-gather.10.cloned.1.call-done.x_ref, f32[4096,512]{1,0:T(8,128)} %fusion.27.ga_ref, bf16[1024,2048]{1,0:T(8,128)(2,1)} %bitcast.215, bf16[512,2048]{1,0:T(8,128)(2,1)} %bitcast.231), custom_call_target="tpu_custom_call" | custom-call | flops 25769803776 | bytes 54525952 | tf_op jit(solution)/shard_map/feedforward/pallas_call | solution.py:364
  474.2 24.7 %halves_product.1 = (bf16[2048,2048]{1,0:T(8,128)(2,1)}, bf16[2048,2048]{1,0:T(8,128)(2,1)}) custom-call(s32[8]{0:T(128)} %pad_add_fusion.order_ref, bf16[4096,1024]{1,0:T(8,128)(2,1)} %get-tuple-element.142.a_ref, bf16[1024,2048]{1,0:T(8,128)(2,1)} %bitcast.216), custom_call_target="tpu_custom_call" | custom-call | flops 17179869184 | bytes 25165824 | tf_op jit(solution)/shard_map/halves_product/pallas_call | solution.py:404
  499.1 23.3 %convolution_convert_fusion = bf16[1024,2048]{1,0:T(8,128)(2,1)S(1)} fusion(bf16[4096,1024]{1,0:T(8,128)(2,1)} %get-tuple-element.142.a_ref, bf16[4096,2048]{1,0:T(8,128)(2,1)} %all-gather.10.cloned.1.call-done.x_ref), kind=kOutput, calls=%fused_computation.30 | convolution fusion | flops 17181966336 | bytes 29360128 | tf_op jit(solution)/shard_map/dot_general | solution.py:28
  524.9 13.1 %convolution_convert_fusion.1 = bf16[512,2048]{1,0:T(8,128)(2,1)S(1)} fusion(bf16[4096,512]{1,0:T(8,128)(2,1)S(1)} %copy-done.37, bf16[4096,2048]{1,0:T(8,128)(2,1)} %all-gather.8.cloned.1.call-done), kind=kOutput, calls=%fused_computation.35 | convolution fusion | flops 8590983168 | bytes 23068672 | tf_op jit(solution)/shard_map/dot_general | solution.py:28
  544.2 5.5 add_convert_fusion
  556.7 3.3 dynamic-slice_bitcast_fusion.1
  563.0 5.5 collective-permute-start.20
  572.7 55.9 %collective-permute-done.17 = bf16[2,256,2048]{2,1,0:T(8,128)(2,1)} collective-permute-done((bf16[2,256,2048]{2,1,0:T(8,128)(2,1)}, bf16[2,256,2048]{2,1,0:T(8,128)(2,1)}, u32[]{:S(2)}, u32[]{:S(2)}) %collective-permute-start.17) | collective-permute-done | bytes 2097184 | tf_op jit(solution)/shard_map/ppermute | solution.py:493
  637.1 22.2 %collective-permute-done.21 = bf16[256,2048]{1,0:T(8,128)(2,1)S(1)} collective-permute-done((bf16[256,2048]{1,0:T(8,128)(2,1)S(1)}, bf16[256,2048]{1,0:T(8,128)(2,1)S(1)}, u32[]{:S(2)}, u32[]{:S(2)}) %collective-permute-start.21) | collective-permute-done | bytes 1048608 | tf_op jit(solution)/shard_map/ppermute | solution.py:493
  665.3 3.9 multiply_reduce_fusion
  669.3 4.2 add_convert_fusion.1
  673.6 7.0 collective-permute-start.25
  681.9 4.5 add_convert_fusion.3
  686.4 5.5 collective-permute-start.23
  693.2 63.9 %collective-permute-done.23 = bf16[8,384,256]{2,1,0:T(8,128)(2,1)} collective-permute-done((bf16[8,384,256]{2,1,0:T(8,128)(2,1)S(1)}, bf16[8,384,256]{2,1,0:T(8,128)(2,1)}, u32[]{:S(2)}, u32[]{:S(2)}) %collective-permute-start.23) | collective-permute-done | bytes 1572896 | tf_op jit(solution)/shard_map/ppermute | solution.py:543
  757.1 5.5 collective-permute-done.24
  771.0 58.0 %attend_back.1.a_ref = bf16[4096,768]{1,0:T(8,128)(2,1)} custom-call(s32[8]{0:T(128)} %get-tuple-element.112.lo_ref, s32[8]{0:T(128)} %get-tuple-element.113.full_ref, s32[1,4096]{1,0:T(1,128)} %add_maximum_fusion.low_ref, bf16[256,4096]{1,0:T(8,128)(2,1)} %get-tuple-element.122.q_ref, bf16[4096,2048]{1,0:T(8,128)(2,1)} %all-gather.12.cloned.1.call-done.hidden_ref, ...), custom_call_target="tpu_custom_call" | custom-call | flops 103079215104 | bytes 25165824 | tf_op jit(solution)/shard_map/attend_back/pallas_call | solution.py:299
  829.1 37.7 %collective-permute-done.29 = bf16[512,2048]{1,0:T(8,128)(2,1)} collective-permute-done((bf16[512,2048]{1,0:T(8,128)(2,1)S(1)}, bf16[512,2048]{1,0:T(8,128)(2,1)}, u32[]{:S(2)}, u32[]{:S(2)}) %collective-permute-start.29) | collective-permute-done | bytes 2097184 | tf_op jit(solution)/shard_map/ppermute | solution.py:543
  866.8 18.0 %rows_product.1 = bf16[4096,2048]{1,0:T(8,128)(2,1)} custom-call(bf16[4096,768]{1,0:T(8,128)(2,1)} %attend_back.1.a_ref, bf16[768,2048]{1,0:T(8,128)(2,1)} %bitcast.193), custom_call_target="tpu_custom_call" | custom-call | flops 12884901888 | bytes 23068672 | tf_op jit(solution)/shard_map/rows_product/pallas_call | solution.py:441
  886.3 8.5 convolution_convert_fusion.2
  895.1 20.8 %multiply_convert_fusion = bf16[768,2048]{1,0:T(8,128)(2,1)S(1)} fusion(bf16[4096,768]{1,0:T(8,128)(2,1)} %attend_back.1.a_ref, bf16[4096,2048]{1,0:T(8,128)(2,1)} %all-gather.6.cloned.1.call-done.x_ref, f32[2048]{0:T(1024)S(1)} %bitcast.246), kind=kOutput, calls=%fused_computation.10 | convolution fusion | flops 12888047616 | bytes 26222592 | tf_op jit(solution)/shard_map/dot_general | solution.py:28
  918.0 12.3 %collective-permute-start.30 = (bf16[8,256,256]{2,0,1:T(8,128)(2,1)S(1)}, bf16[8,256,256]{2,0,1:T(8,128)(2,1)S(1)}, u32[]{:S(2)}, u32[]{:S(2)}) collective-permute-start(bf16[8,256,256]{2,0,1:T(8,128)(2,1)S(1)} %get-tuple-element.229), channel_id=1, source_target_pairs={{0,1},{1,2},{4,5},{5,6},{8,9},{9,10},{12,13},{13,14},{16,17},{17,1... | collective-permute-start | bytes 3145736 | tf_op jit(solution)/shard_map/ppermute | solution.py:543
  932.4 21.4 %collective-permute-done.30 = bf16[8,256,256]{2,0,1:T(8,128)(2,1)S(1)} collective-permute-done((bf16[8,256,256]{2,0,1:T(8,128)(2,1)S(1)}, bf16[8,256,256]{2,0,1:T(8,128)(2,1)S(1)}, u32[]{:S(2)}, u32[]{:S(2)}) %collective-permute-start.30) | collective-permute-done | bytes 1048608 | tf_op jit(solution)/shard_map/ppermute | solution.py:543
  953.8 21.2 %collective-permute-done.31 = bf16[8,256,256]{2,0,1:T(8,128)(2,1)S(1)} collective-permute-done((bf16[8,256,256]{2,0,1:T(8,128)(2,1)S(1)}, bf16[8,256,256]{2,0,1:T(8,128)(2,1)S(1)}, u32[]{:S(2)}, u32[]{:S(2)}) %collective-permute-start.31) | collective-permute-done | bytes 1048608 | tf_op jit(solution)/shard_map/ppermute | solution.py:543
  977.2 7.3 collective-permute-start.32
  986.0 19.4 %reduce-scatter.8.cloned.1.call-done = bf16[512,2048]{1,0:T(8,128)(2,1)} async-done(((bf16[4096,2048]{1,0:T(8,128)(2,1)}), bf16[512,2048]{1,0:T(8,128)(2,1)}) %reduce-scatter.8.cloned.1.call-update) | async-done | bytes 2097168 | tf_op jit(solution)/shard_map/reduce_scatter | solution.py:590
  1007.7 3.7 collective-permute-done.34
  1014.6 5.1 fusion.8
  1021.2 3.6 add_convert_fusion.2
  1024.8 3.6 all-to-all-start.4
  1028.4 21.0 %all-to-all-done.4 = bf16[8,384,256]{2,1,0:T(8,128)(2,1)S(1)} async-done(((bf16[8,384,256]{2,1,0:T(8,128)(2,1)}), bf16[8,384,256]{2,1,0:T(8,128)(2,1)S(1)}, u32[]{:S(2)}, u32[]{:S(2)}) %all-to-all-start.4) | async-done | bytes 1572896 | tf_op jit(solution)/shard_map/all_to_all | solution.py:540
  1053.0 3.2 bitcast_dynamic-update-slice_fusion.5
  1056.1 3.2 bitcast_dynamic-update-slice_fusion.4
  1059.3 3.3 bitcast_dynamic-update-slice_fusion.3
  1064.1 3.2 bitcast_dynamic-update-slice_fusion.1
  1067.3 3.3 bitcast_dynamic-update-slice_fusion
  1071.2 3.3 all-to-all-start.2
  1079.3 3.6 all-to-all-start.3
  1086.3 3.2 bitcast_dynamic-update-slice_fusion.6
  1093.7 8.5 constant_dynamic-slice_fusion
  1105.7 61.3 %all-gather.14.cloned.1.call-done = bf16[2048,2048]{1,0:T(8,128)(2,1)} async-done(((bf16[512,2048]{1,0:T(8,128)(2,1)}), bf16[2048,2048]{1,0:T(8,128)(2,1)}) %all-gather.14.cloned.1.call-update) | async-done | bytes 8388624 | tf_op jit(solution)/shard_map/all_gather | solution.py:785
  1167.0 11.7 convert.29
  (279 shorter events, 154.4 us)
Async XLA Ops:
  7.2 104.3 %copy-start = (s32[4,8]{1,0:T(4,128)S(1)}, s32[4,8]{1,0:T(4,128)}, u32[]{:S(2)}) copy-start(s32[4,8]{1,0:T(4,128)} %param.9) | copy-start | bytes 388
  7.2 104.3 %all-gather.6.cloned.1.call-start = ((), (), s32[]{:S(2)}) async-start(), calls=%async_computation.8 | async-start | bytes 18874368 | tf_op jit(solution)/shard_map/all_gather | solution.py:587
  13.3 206.7 %all-gather.8.cloned.1.call-start = ((), (), s32[]{:S(2)}) async-start(), calls=%async_computation.9 | async-start | bytes 18874368 | tf_op jit(solution)/shard_map/all_gather | solution.py:587
  13.9 34.4 %copy-start.14 = (bf16[2,256,1024]{2,1,0:T(8,128)(2,1)S(1)}, bf16[2,256,1024]{2,1,0:T(8,128)(2,1)}, u32[]{:S(2)}) copy-start(bf16[2,256,1024]{2,1,0:T(8,128)(2,1)} %param.13) | copy-start | bytes 3145732
  42.5 18.6 %collective-permute-start = (bf16[8,192,256]{2,0,1:T(8,128)(2,1)}, bf16[8,192,256]{2,0,1:T(8,128)(2,1)}, u32[]{:S(2)}, u32[]{:S(2)}) collective-permute-start(bf16[8,192,256]{2,0,1:T(8,128)(2,1)} %copy.121), channel_id=1, source_target_pairs={{0,1},{1,2},{2,3},{4,5},{5,6},{6,7},{8,9},{9,10},{10,11},{12,13},{... | collective-permute-start | bytes 2359304 | tf_op jit(solution)/shard_map/ppermute | solution.py:543
  47.0 19.1 %collective-permute-start.1 = (bf16[8,192,256]{2,0,1:T(8,128)(2,1)}, bf16[8,192,256]{2,0,1:T(8,128)(2,1)}, u32[]{:S(2)}, u32[]{:S(2)}) collective-permute-start(bf16[8,192,256]{2,0,1:T(8,128)(2,1)} %copy.121), channel_id=1, source_target_pairs={{1,0},{2,1},{3,2},{5,4},{6,5},{7,6},{9,8},{10,9},{11,10},{13,12},{... | collective-permute-start | bytes 2359304 | tf_op jit(solution)/shard_map/ppermute | solution.py:543
  50.2 23.7 %copy-start.36 = (bf16[2,256]{1,0:T(2,128)(2,1)S(1)}, bf16[2,256]{1,0:T(2,128)(2,1)}, u32[]{:S(2)}) copy-start(bf16[2,256]{1,0:T(2,128)(2,1)} %param.10) | copy-start | bytes 3076
  67.3 24.5 %collective-permute-start.2 = (bf16[8,192,256]{2,0,1:T(8,128)(2,1)S(1)}, bf16[8,192,256]{2,0,1:T(8,128)(2,1)}, u32[]{:S(2)}, u32[]{:S(2)}) collective-permute-start(bf16[8,192,256]{2,0,1:T(8,128)(2,1)S(1)} %broadcast_select_fusion.8), channel_id=1, source_target_pairs={{1,3},{2,0},{5,7},{6,4},{9,11},{10,8},{13,15},{14,12},{17,19},{18,... | collective-permute-start | bytes 2359304 | tf_op jit(solution)/shard_map/ppermute | solution.py:543
  68.6 24.8 %collective-permute-start.3 = (bf16[8,192,256]{2,0,1:T(8,128)(2,1)}, bf16[8,192,256]{2,0,1:T(8,128)(2,1)S(1)}, u32[]{:S(2)}, u32[]{:S(2)}) collective-permute-start(bf16[8,192,256]{2,0,1:T(8,128)(2,1)} %collective-permute-done), channel_id=1, source_target_pairs={{1,2},{2,3},{5,6},{6,7},{9,10},{10,11},{13,14},{14,15},{17,18},{18... | collective-permute-start | bytes 2359304 | tf_op jit(solution)/shard_map/ppermute | solution.py:543
  69.4 34.1 %collective-permute-start.4 = (bf16[8,192,256]{2,0,1:T(8,128)(2,1)}, bf16[8,192,256]{2,0,1:T(8,128)(2,1)}, u32[]{:S(2)}, u32[]{:S(2)}) collective-permute-start(bf16[8,192,256]{2,0,1:T(8,128)(2,1)} %collective-permute-done.1), channel_id=1, source_target_pairs={{1,0},{2,1},{5,4},{6,5},{9,8},{10,9},{13,12},{14,13},{17,16},{18,1... | collective-permute-start | bytes 2359304 | tf_op jit(solution)/shard_map/ppermute | solution.py:543
  81.8 22.9 %collective-permute-start.5 = (bf16[8,64,256]{2,0,1:T(8,128)(2,1)}, bf16[8,64,256]{2,0,1:T(8,128)(2,1)S(1)}, u32[]{:S(2)}, u32[]{:S(2)}) collective-permute-start(bf16[8,64,256]{2,0,1:T(8,128)(2,1)} %bitcast.180), channel_id=1, source_target_pairs={{0,1},{1,2},{2,3},{4,5},{5,6},{6,7},{8,9},{9,10},{10,11},{12,13},{... | collective-permute-start | bytes 786440 | tf_op jit(solution)/shard_map/ppermute | solution.py:543
  90.6 18.4 %collective-permute-start.6 = (bf16[8,64,256]{2,0,1:T(8,128)(2,1)}, bf16[8,64,256]{2,0,1:T(8,128)(2,1)}, u32[]{:S(2)}, u32[]{:S(2)}) collective-permute-start(bf16[8,64,256]{2,0,1:T(8,128)(2,1)} %bitcast.180), channel_id=1, source_target_pairs={{1,0},{2,1},{3,2},{5,4},{6,5},{7,6},{9,8},{10,9},{11,10},{13,12},{... | collective-permute-start | bytes 786440 | tf_op jit(solution)/shard_map/ppermute | solution.py:543
  118.1 226.6 %copy-start.23 = (f32[1,2048]{1,0:T(1,128)}, f32[1,2048]{1,0:T(1,128)S(1)}, u32[]{:S(2)}) copy-start(f32[1,2048]{1,0:T(1,128)S(1)} %get-tuple-element.243) | copy-start | bytes 24580
  120.9 29.9 %collective-permute-start.7 = (bf16[8,64,256]{2,0,1:T(8,128)(2,1)S(1)}, bf16[8,64,256]{2,0,1:T(8,128)(2,1)S(1)}, u32[]{:S(2)}, u32[]{:S(2)}) collective-permute-start(bf16[8,64,256]{2,0,1:T(8,128)(2,1)S(1)} %collective-permute-done.5), channel_id=1, source_target_pairs={{1,2},{2,3},{5,6},{6,7},{9,10},{10,11},{13,14},{14,15},{17,18},{18... | collective-permute-start | bytes 786440 | tf_op jit(solution)/shard_map/ppermute | solution.py:543
  121.6 29.2 %collective-permute-start.8 = (bf16[8,64,256]{2,0,1:T(8,128)(2,1)}, bf16[8,64,256]{2,0,1:T(8,128)(2,1)S(1)}, u32[]{:S(2)}, u32[]{:S(2)}) collective-permute-start(bf16[8,64,256]{2,0,1:T(8,128)(2,1)} %collective-permute-done.6), channel_id=1, source_target_pairs={{1,0},{2,1},{5,4},{6,5},{9,8},{10,9},{13,12},{14,13},{17,16},{18,1... | collective-permute-start | bytes 786440 | tf_op jit(solution)/shard_map/ppermute | solution.py:543
  123.9 26.9 %collective-permute-start.9 = (bf16[8,64,256]{2,0,1:T(8,128)(2,1)S(1)}, bf16[8,64,256]{2,0,1:T(8,128)(2,1)S(1)}, u32[]{:S(2)}, u32[]{:S(2)}) collective-permute-start(bf16[8,64,256]{2,0,1:T(8,128)(2,1)S(1)} %broadcast_select_fusion.10), channel_id=1, source_target_pairs={{1,3},{2,0},{5,7},{6,4},{9,11},{10,8},{13,15},{14,12},{17,19},{18,... | collective-permute-start | bytes 786440 | tf_op jit(solution)/shard_map/ppermute | solution.py:543
  125.2 63.3 %all-to-all-start.1 = ((bf16[8,384,256]{2,1,0:T(8,128)(2,1)}), bf16[8,384,256]{2,1,0:T(8,128)(2,1)S(1)}, u32[]{:S(2)}, u32[]{:S(2)}) async-start(bf16[8,384,256]{2,1,0:T(8,128)(2,1)} %pad_maximum_fusion.2), calls=%async_computation.1 | async-start | bytes 3145728 | tf_op jit(solution)/shard_map/all_to_all | solution.py:540
  128.8 211.4 %reduce-scatter.4.cloned.1.call-start = ((), (), s32[]{:S(2)}) async-start(), calls=%async_computation.10 | async-start | bytes 18874368 | tf_op jit(solution)/shard_map/reduce_scatter | solution.py:590
  220.1 218.3 %all-gather.10.cloned.1.call-start = ((), (), s32[]{:S(2)}) async-start(), calls=%async_computation.11 | async-start | bytes 18874368 | tf_op jit(solution)/shard_map/all_gather | solution.py:587
  220.1 37.4 %collective-permute-start.10 = (bf16[8,384,256]{2,1,0:T(8,128)(2,1)S(1)}, bf16[8,384,256]{2,1,0:T(8,128)(2,1)S(1)}, u32[]{:S(2)}, u32[]{:S(2)}) collective-permute-start(bf16[8,384,256]{2,1,0:T(8,128)(2,1)S(1)} %all-to-all-done.1), channel_id=1, source_target_pairs={{0,1},{1,2},{2,3},{4,5},{5,6},{6,7},{8,9},{9,10},{10,11},{12,13},{... | collective-permute-start | bytes 4718600 | tf_op jit(solution)/shard_map/ppermute | solution.py:543
  223.6 38.3 %collective-permute-start.12 = (bf16[8,384,256]{2,1,0:T(8,128)(2,1)S(1)}, bf16[8,384,256]{2,1,0:T(8,128)(2,1)}, u32[]{:S(2)}, u32[]{:S(2)}) collective-permute-start(bf16[8,384,256]{2,1,0:T(8,128)(2,1)S(1)} %all-to-all-done.1), channel_id=1, source_target_pairs={{1,0},{2,1},{3,2},{5,4},{6,5},{7,6},{9,8},{10,9},{11,10},{13,12},{... | collective-permute-start | bytes 4718600 | tf_op jit(solution)/shard_map/ppermute | solution.py:543
  264.6 77.7 %collective-permute-start.14 = (bf16[8,384,256]{2,1,0:T(8,128)(2,1)}, bf16[8,384,256]{2,1,0:T(8,128)(2,1)}, u32[]{:S(2)}, u32[]{:S(2)}) collective-permute-start(bf16[8,384,256]{2,1,0:T(8,128)(2,1)} %broadcast_select_fusion.5), channel_id=1, source_target_pairs={{1,3},{2,0},{5,7},{6,4},{9,11},{10,8},{13,15},{14,12},{17,19},{18,... | collective-permute-start | bytes 4718600 | tf_op jit(solution)/shard_map/ppermute | solution.py:543
  265.9 76.4 %collective-permute-start.11 = (bf16[8,384,256]{2,1,0:T(8,128)(2,1)S(1)}, bf16[8,384,256]{2,1,0:T(8,128)(2,1)}, u32[]{:S(2)}, u32[]{:S(2)}) collective-permute-start(bf16[8,384,256]{2,1,0:T(8,128)(2,1)S(1)} %collective-permute-done.10), channel_id=1, source_target_pairs={{1,2},{2,3},{5,6},{6,7},{9,10},{10,11},{13,14},{14,15},{17,18},{18... | collective-permute-start | bytes 4718600 | tf_op jit(solution)/shard_map/ppermute | solution.py:543
  267.7 74.7 %collective-permute-start.13 = (bf16[8,384,256]{2,1,0:T(8,128)(2,1)}, bf16[8,384,256]{2,1,0:T(8,128)(2,1)}, u32[]{:S(2)}, u32[]{:S(2)}) collective-permute-start(bf16[8,384,256]{2,1,0:T(8,128)(2,1)} %collective-permute-done.12), channel_id=1, source_target_pairs={{1,0},{2,1},{5,4},{6,5},{9,8},{10,9},{13,12},{14,13},{17,16},{18,1... | collective-permute-start | bytes 4718600 | tf_op jit(solution)/shard_map/ppermute | solution.py:543
  348.4 314.1 %reduce-scatter.6.cloned.1.call-start = ((), (), s32[]{:S(2)}) async-start(), calls=%async_computation.12 | async-start | bytes 18874368 | tf_op jit(solution)/shard_map/reduce_scatter | solution.py:590
  356.0 13.0 %slice-start.3 = ((s8[16777216]{0:T(1024)(128)(4,1)}), s8[4194304]{0:T(1024)(128)(4,1)S(1)}, s32[]{:S(2)}) async-start(s8[16777216]{0:T(1024)(128)(4,1)} %bitcast.256), calls=%async_computation.19 | async-start | bytes 8388608
  356.0 13.0 %slice-start.4 = ((s8[16777216]{0:T(1024)(128)(4,1)}), s8[4194304]{0:T(1024)(128)(4,1)S(1)}, s32[]{:S(2)}) async-start(s8[16777216]{0:T(1024)(128)(4,1)} %bitcast.256), calls=%async_computation.20 | async-start | bytes 8388608
  357.2 11.8 slice-start.5
  473.5 291.1 %all-gather.12.cloned.1.call-start = ((), (), s32[]{:S(2)}) async-start(), calls=%async_computation.13 | async-start | bytes 18874368 | tf_op jit(solution)/shard_map/all_gather | solution.py:587
  498.9 44.6 %collective-permute-start.15 = (bf16[2048,2048]{1,0:T(8,128)(2,1)}, bf16[2048,2048]{1,0:T(8,128)(2,1)}, u32[]{:S(2)}, u32[]{:S(2)}) collective-permute-start(bf16[2048,2048]{1,0:T(8,128)(2,1)} %get-tuple-element.144), channel_id=1, source_target_pairs={{0,4},{4,0},{1,5},{5,1},{2,6},{6,2},{3,7},{7,3},{8,12},{12,8},{9,1... | collective-permute-start | bytes 25165832 | tf_op jit(solution)/shard_map/ppermute | solution.py:493
  556.0 72.6 %collective-permute-start.17 = (bf16[2,256,2048]{2,1,0:T(8,128)(2,1)}, bf16[2,256,2048]{2,1,0:T(8,128)(2,1)}, u32[]{:S(2)}, u32[]{:S(2)}) collective-permute-start(bf16[2,256,2048]{2,1,0:T(8,128)(2,1)} %dynamic-slice_bitcast_fusion), channel_id=1, source_target_pairs={{0,16},{16,0},{1,17},{17,1},{2,18},{18,2},{3,19},{19,3},{4,20},{20... | collective-permute-start | bytes 6291464 | tf_op jit(solution)/shard_map/ppermute | solution.py:493
  560.0 71.7 %collective-permute-start.16 = (bf16[2,256,2048]{2,1,0:T(8,128)(2,1)}, bf16[2,256,2048]{2,1,0:T(8,128)(2,1)}, u32[]{:S(2)}, u32[]{:S(2)}) collective-permute-start(bf16[2,256,2048]{2,1,0:T(8,128)(2,1)} %dynamic-slice_bitcast_fusion.1), channel_id=1, source_target_pairs={{0,8},{8,0},{1,9},{9,1},{2,10},{10,2},{3,11},{11,3},{4,12},{12,4},... | collective-permute-start | bytes 6291464 | tf_op jit(solution)/shard_map/ppermute | solution.py:493
  563.0 71.1 %collective-permute-start.20 = (bf16[8,384,256]{2,1,0:T(8,128)(2,1)}, bf16[8,384,256]{2,1,0:T(8,128)(2,1)}, u32[]{:S(2)}, u32[]{:S(2)}) collective-permute-start(bf16[8,384,256]{2,1,0:T(8,128)(2,1)} %broadcast_select_fusion.3), channel_id=1, source_target_pairs={{0,2},{3,1},{4,6},{7,5},{8,10},{11,9},{12,14},{15,13},{16,18},{19,... | collective-permute-start | bytes 4718600 | tf_op jit(solution)/shard_map/ppermute | solution.py:543
  568.5 66.2 %collective-permute-start.18 = (bf16[8,384,256]{2,1,0:T(8,128)(2,1)}, bf16[8,384,256]{2,1,0:T(8,128)(2,1)}, u32[]{:S(2)}, u32[]{:S(2)}) collective-permute-start(bf16[8,384,256]{2,1,0:T(8,128)(2,1)} %bitcast.38), channel_id=1, source_target_pairs={{0,1},{1,2},{4,5},{5,6},{8,9},{9,10},{12,13},{13,14},{16,17},{17,1... | collective-permute-start | bytes 4718600 | tf_op jit(solution)/shard_map/ppermute | solution.py:543
  570.9 63.8 %collective-permute-start.19 = (bf16[8,384,256]{2,1,0:T(8,128)(2,1)}, bf16[8,384,256]{2,1,0:T(8,128)(2,1)}, u32[]{:S(2)}, u32[]{:S(2)}) collective-permute-start(bf16[8,384,256]{2,1,0:T(8,128)(2,1)} %bitcast.38), channel_id=1, source_target_pairs={{2,1},{3,2},{6,5},{7,6},{10,9},{11,10},{14,13},{15,14},{18,17},{19... | collective-permute-start | bytes 4718600 | tf_op jit(solution)/shard_map/ppermute | solution.py:543
  572.7 58.9 %copy-start.8 = (bf16[2,2,256,2048]{3,2,1,0:T(8,128)(2,1)S(1)}, bf16[2,2,256,2048]{3,2,1,0:T(8,128)(2,1)}, u32[]{:S(2)}) copy-start(bf16[2,2,256,2048]{3,2,1,0:T(8,128)(2,1)} %get-tuple-element.223) | copy-start | bytes 12582916
  634.8 24.4 %collective-permute-start.21 = (bf16[256,2048]{1,0:T(8,128)(2,1)S(1)}, bf16[256,2048]{1,0:T(8,128)(2,1)S(1)}, u32[]{:S(2)}, u32[]{:S(2)}) collective-permute-start(bf16[256,2048]{1,0:T(8,128)(2,1)S(1)} %dynamic-slice_bitcast_fusion.4), channel_id=1, source_target_pairs={{0,16},{16,0},{1,17},{17,1},{2,18},{18,2},{3,19},{19,3},{4,20},{20... | collective-permute-start | bytes 3145736 | tf_op jit(solution)/shard_map/ppermute | solution.py:493
  636.4 23.5 %collective-permute-start.22 = (bf16[256,2048]{1,0:T(8,128)(2,1)S(1)}, bf16[256,2048]{1,0:T(8,128)(2,1)S(1)}, u32[]{:S(2)}, u32[]{:S(2)}) collective-permute-start(bf16[256,2048]{1,0:T(8,128)(2,1)S(1)} %dynamic-slice_bitcast_fusion.3), channel_id=1, source_target_pairs={{0,8},{8,0},{1,9},{9,1},{2,10},{10,2},{3,11},{11,3},{4,12},{12,4},... | collective-permute-start | bytes 3145736 | tf_op jit(solution)/shard_map/ppermute | solution.py:493
  673.6 331.8 %reduce-scatter.8.cloned.1.call-start = ((), (), s32[]{:S(2)}) async-start(), calls=%async_computation.14 | async-start | bytes 18874368 | tf_op jit(solution)/shard_map/reduce_scatter | solution.py:590
  673.6 89.0 %collective-permute-start.25 = (bf16[512,2048]{1,0:T(8,128)(2,1)}, bf16[512,2048]{1,0:T(8,128)(2,1)}, u32[]{:S(2)}, u32[]{:S(2)}) collective-permute-start(bf16[512,2048]{1,0:T(8,128)(2,1)} %get-tuple-element.231), channel_id=1, source_target_pairs={{0,1},{1,2},{2,3},{4,5},{5,6},{6,7},{8,9},{9,10},{10,11},{12,13},{... | collective-permute-start | bytes 6291464 | tf_op jit(solution)/shard_map/ppermute | solution.py:543
  680.6 82.0 %collective-permute-start.26 = (bf16[512,2048]{1,0:T(8,128)(2,1)}, bf16[512,2048]{1,0:T(8,128)(2,1)}, u32[]{:S(2)}, u32[]{:S(2)}) collective-permute-start(bf16[512,2048]{1,0:T(8,128)(2,1)} %get-tuple-element.231), channel_id=1, source_target_pairs={{1,0},{2,1},{3,2},{5,4},{6,5},{7,6},{9,8},{10,9},{11,10},{13,12},{... | collective-permute-start | bytes 6291464 | tf_op jit(solution)/shard_map/ppermute | solution.py:543
  686.4 70.7 %collective-permute-start.23 = (bf16[8,384,256]{2,1,0:T(8,128)(2,1)S(1)}, bf16[8,384,256]{2,1,0:T(8,128)(2,1)}, u32[]{:S(2)}, u32[]{:S(2)}) collective-permute-start(bf16[8,384,256]{2,1,0:T(8,128)(2,1)S(1)} %get-tuple-element.234), channel_id=1, source_target_pairs={{0,1},{1,2},{2,3},{4,5},{5,6},{6,7},{8,9},{9,10},{10,11},{12,13},{... | collective-permute-start | bytes 4718600 | tf_op jit(solution)/shard_map/ppermute | solution.py:543
  691.9 70.7 %collective-permute-start.24 = (bf16[8,384,256]{2,1,0:T(8,128)(2,1)S(1)}, bf16[8,384,256]{2,1,0:T(8,128)(2,1)}, u32[]{:S(2)}, u32[]{:S(2)}) collective-permute-start(bf16[8,384,256]{2,1,0:T(8,128)(2,1)S(1)} %get-tuple-element.233), channel_id=1, source_target_pairs={{1,0},{2,1},{3,2},{5,4},{6,5},{7,6},{9,8},{10,9},{11,10},{13,12},{... | collective-permute-start | bytes 4718600 | tf_op jit(solution)/shard_map/ppermute | solution.py:543
  764.6 102.2 %collective-permute-start.27 = (bf16[512,2048]{1,0:T(8,128)(2,1)}, bf16[512,2048]{1,0:T(8,128)(2,1)}, u32[]{:S(2)}, u32[]{:S(2)}) collective-permute-start(bf16[512,2048]{1,0:T(8,128)(2,1)} %collective-permute-done.25), channel_id=1, source_target_pairs={{1,2},{2,3},{5,6},{6,7},{9,10},{10,11},{13,14},{14,15},{17,18},{18... | collective-permute-start | bytes 6291464 | tf_op jit(solution)/shard_map/ppermute | solution.py:543
  768.4 98.3 %collective-permute-start.28 = (bf16[512,2048]{1,0:T(8,128)(2,1)}, bf16[512,2048]{1,0:T(8,128)(2,1)}, u32[]{:S(2)}, u32[]{:S(2)}) collective-permute-start(bf16[512,2048]{1,0:T(8,128)(2,1)} %collective-permute-done.26), channel_id=1, source_target_pairs={{1,0},{2,1},{5,4},{6,5},{9,8},{10,9},{13,12},{14,13},{17,16},{18,1... | collective-permute-start | bytes 6291464 | tf_op jit(solution)/shard_map/ppermute | solution.py:543
  769.7 97.0 %collective-permute-start.29 = (bf16[512,2048]{1,0:T(8,128)(2,1)S(1)}, bf16[512,2048]{1,0:T(8,128)(2,1)}, u32[]{:S(2)}, u32[]{:S(2)}) collective-permute-start(bf16[512,2048]{1,0:T(8,128)(2,1)S(1)} %broadcast_select_fusion), channel_id=1, source_target_pairs={{1,3},{2,0},{5,7},{6,4},{9,11},{10,8},{13,15},{14,12},{17,19},{18,... | collective-permute-start | bytes 6291464 | tf_op jit(solution)/shard_map/ppermute | solution.py:543
  884.7 10.4 copy-start.27
  884.8 282.2 %all-gather.14.cloned.1.call-start = ((), (), s32[]{:S(2)}) async-start(), calls=%async_computation.15 | async-start | bytes 10485760 | tf_op jit(solution)/shard_map/all_gather | solution.py:785
  918.0 35.8 %collective-permute-start.30 = (bf16[8,256,256]{2,0,1:T(8,128)(2,1)S(1)}, bf16[8,256,256]{2,0,1:T(8,128)(2,1)S(1)}, u32[]{:S(2)}, u32[]{:S(2)}) collective-permute-start(bf16[8,256,256]{2,0,1:T(8,128)(2,1)S(1)} %get-tuple-element.229), channel_id=1, source_target_pairs={{0,1},{1,2},{4,5},{5,6},{8,9},{9,10},{12,13},{13,14},{16,17},{17,1... | collective-permute-start | bytes 3145736 | tf_op jit(solution)/shard_map/ppermute | solution.py:543
  930.3 44.7 %collective-permute-start.31 = (bf16[8,256,256]{2,0,1:T(8,128)(2,1)S(1)}, bf16[8,256,256]{2,0,1:T(8,128)(2,1)S(1)}, u32[]{:S(2)}, u32[]{:S(2)}) collective-permute-start(bf16[8,256,256]{2,0,1:T(8,128)(2,1)S(1)} %get-tuple-element.228), channel_id=1, source_target_pairs={{0,2},{3,1},{4,6},{7,5},{8,10},{11,9},{12,14},{15,13},{16,18},{19,... | collective-permute-start | bytes 3145736 | tf_op jit(solution)/shard_map/ppermute | solution.py:543
  931.7 43.4 %collective-permute-start.33 = (bf16[8,256,256]{2,0,1:T(8,128)(2,1)S(1)}, bf16[8,256,256]{2,0,1:T(8,128)(2,1)S(1)}, u32[]{:S(2)}, u32[]{:S(2)}) collective-permute-start(bf16[8,256,256]{2,0,1:T(8,128)(2,1)S(1)} %get-tuple-element.229), channel_id=1, source_target_pairs={{2,1},{3,2},{6,5},{7,6},{10,9},{11,10},{14,13},{15,14},{18,17},{19... | collective-permute-start | bytes 3145736 | tf_op jit(solution)/shard_map/ppermute | solution.py:543
  977.2 30.5 %collective-permute-start.32 = (bf16[8,256,256]{2,0,1:T(8,128)(2,1)}, bf16[8,256,256]{2,0,1:T(8,128)(2,1)S(1)}, u32[]{:S(2)}, u32[]{:S(2)}) collective-permute-start(bf16[8,256,256]{2,0,1:T(8,128)(2,1)} %get-tuple-element.238), channel_id=1, source_target_pairs={{0,1},{1,2},{2,3},{4,5},{5,6},{6,7},{8,9},{9,10},{10,11},{12,13},{... | collective-permute-start | bytes 3145736 | tf_op jit(solution)/shard_map/ppermute | solution.py:543
  984.5 26.9 %copy-start.32 = (f32[512]{0:T(512)S(1)}, f32[512]{0:T(512)}, u32[]{:S(2)}) copy-start(f32[512]{0:T(512)} %copy-done.31) | copy-start | bytes 6148
  984.5 26.9 %collective-permute-start.34 = (bf16[8,256,256]{2,0,1:T(8,128)(2,1)}, bf16[8,256,256]{2,0,1:T(8,128)(2,1)S(1)}, u32[]{:S(2)}, u32[]{:S(2)}) collective-permute-start(bf16[8,256,256]{2,0,1:T(8,128)(2,1)} %get-tuple-element.237), channel_id=1, source_target_pairs={{1,0},{2,1},{3,2},{5,4},{6,5},{7,6},{9,8},{10,9},{11,10},{13,12},{... | collective-permute-start | bytes 3145736 | tf_op jit(solution)/shard_map/ppermute | solution.py:543
  1005.4 9.2 copy-start.6
  1024.8 24.6 %all-to-all-start.4 = ((bf16[8,384,256]{2,1,0:T(8,128)(2,1)}), bf16[8,384,256]{2,1,0:T(8,128)(2,1)S(1)}, u32[]{:S(2)}, u32[]{:S(2)}) async-start(bf16[8,384,256]{2,1,0:T(8,128)(2,1)} %add_convert_fusion.2), calls=%async_computation.7 | async-start | bytes 3145728 | tf_op jit(solution)/shard_map/all_to_all | solution.py:540
  1071.2 8.0 all-to-all-start.2
  1079.3 23.7 %all-to-all-start.3 = ((bf16[8,256,256]{2,1,0:T(8,128)(2,1)}), bf16[8,256,256]{2,1,0:T(8,128)(2,1)S(1)}, u32[]{:S(2)}, u32[]{:S(2)}) async-start(bf16[8,256,256]{2,1,0:T(8,128)(2,1)} %copy.144), calls=%async_computation.6 | async-start | bytes 2097152 | tf_op jit(solution)/shard_map/all_to_all | solution.py:540
  1082.9 6.6 collective-permute-start.35
  1085.0 5.5 collective-permute-start.36
  1090.5 11.8 collective-permute-start.37
  1091.8 10.5 collective-permute-start.38
  1092.4 9.8 collective-permute-start.39
  1167.0 11.7 copy-start.1
  (34 other events, 129.9 us)
Sparse Core Ops, SparseCore 0:
  13.5 97.9 all-gather.5
  113.3 106.7 all-gather.7
  224.2 115.9 reduce-scatter.3
  348.5 89.8 all-gather.9
  473.6 144.6 reduce-scatter.5
  673.7 90.8 all-gather.11
  884.9 120.4 reduce-scatter.7
  1019.9 147.0 all-gather.13

commit v7 on v6

--- a/solution.py
+++ b/solution.py
@@ -483,10 +483,66 @@
     return lax.rsqrt(jnp.mean(rows * rows, axis=-1, keepdims=True) + epsilon)
 
 
-def norm_backward(grad_normed, normal, inverse, gain):
-    grad_normal = grad_normed * gain
+def norm_kernel(x_ref, branch_ref, gain_ref, hidden_ref, normed_ref):
+    hidden = x_ref[...].astype(f32) + branch_ref[...].astype(f32)
+    hidden_ref[...] = hidden
+    normed_ref[...] = (hidden * norm_inverse(hidden) * gain_ref[...]).astype(bf16)
+
+
+def norm_back_kernel(grad_ref, x_ref, base_ref, gain_ref, gain_grad_ref, *out_refs):
+    @pl.when(pl.program_id(0) == 0)
+    def _():
+        gain_grad_ref[...] = jnp.zeros_like(gain_grad_ref)
+
+    x, grad = x_ref[...].astype(f32), grad_ref[...].astype(f32)
+    inverse = norm_inverse(x)
+    normal = x * inverse
+    grad_normal = grad * gain_ref[...]
     inner = jnp.mean(grad_normal * normal, axis=-1, keepdims=True)
-    return inverse * (grad_normal - normal * inner), jnp.sum(grad_normed * normal, axis=0)
+    out = base_ref[...].astype(f32) + inverse * (grad_normal - normal * inner)
+    for ref in out_refs:
+        ref[...] = out.astype(ref.dtype)
+    gain_grad_ref[...] += jnp.sum(grad * normal, axis=0, keepdims=True)
+
+
+def cast_kernel(a_ref, o_ref):
+    o_ref[...] = a_ref[...].astype(o_ref.dtype)
+
+
+def by_rows(kernel, name, arrays, tables, outs, block):
+    length, model = arrays[0].shape
+    block = math.gcd(block, length)
+
+    def spec(a):
+        return pl.BlockSpec((min(block, a.shape[0]), model), lambda i: (i * (a.shape[0] > 1), 0))
+
+    return pl.pallas_call(
+        kernel,
+        grid=(length // block,),
+        out_shape=tuple(outs),
+        in_specs=[spec(a) for a in (*arrays, *tables)],
+        out_specs=tuple(spec(a) for a in outs),
+        compiler_params=pltpu.CompilerParams(vmem_limit_bytes=VMEM_BYTES),
+        cost_estimate=pl.CostEstimate(
+            flops=8 * length * model, transcendentals=length, bytes_accessed=12 * length * model
+        ),
+        name=name,
+    )(*arrays, *tables)
+
+
+def add_and_norm(x, branch, gain):
+    outs = [jax.ShapeDtypeStruct(x.shape, f32), jax.ShapeDtypeStruct(x.shape, bf16)]
+    return by_rows(norm_kernel, "add_and_norm", (x, branch), (gain,), outs, 128)
+
+
+def norm_backward(grad_normed, x, base, gain, dtypes):
+    outs = [jax.ShapeDtypeStruct(gain.shape, f32)]
+    outs += [jax.ShapeDtypeStruct(x.shape, dtype) for dtype in dtypes]
+    return by_rows(norm_back_kernel, "norm_backward", (grad_normed, x, base), (gain,), outs, 128)
+
+
+def widen(a):
+    return by_rows(cast_kernel, "widen", (a,), (), [jax.ShapeDtypeStruct(a.shape, f32)], 512)[0]
 
 
 def swap(a, axis):
@@ -587,7 +643,7 @@
         return lax.all_gather(a, plane, axis=0, tiled=True)
 
     def scatter_plane(a):
-        return lax.psum_scatter(a.astype(bf16), plane, scatter_dimension=0, tiled=True).astype(f32)
+        return lax.psum_scatter(a.astype(bf16), plane, scatter_dimension=0, tiled=True)
 
     def scatter_middle(terms):
         half = own_len // 2
@@ -623,11 +679,10 @@
         a = exchange(a.reshape(n_context, -1, rows)).reshape(seqs * block_heads, m, rows)
         return lax.psum_scatter(a, "seq", scatter_dimension=0, tiled=True).astype(f32)
 
-    rows_in = own(block_input).astype(f32)
+    rows_in = own(block_input)
     incoming = own(cotangent)
-    inverse_one = norm_inverse(rows_in)
-    normal_one = rows_in * inverse_one
-    normal_own = normal_one.astype(bf16)
+    wide = rows_in.astype(f32)
+    normal_own = (wide * norm_inverse(wide)).astype(bf16)
     normal_all = gather_plane(normal_own)
 
     qkv_local, out_local, _ = lax.optimization_barrier((qkv_weight, out_weight, normal_own))
@@ -700,10 +755,8 @@
     hidden_far = spread_far(hidden_near)
     attention_branch = scatter_plane(attention_part)
     attention_branch, hidden_far = lax.optimization_barrier((attention_branch, hidden_far))
-    hidden = rows_in + attention_branch
-    inverse_two = norm_inverse(hidden)
-    normal_two = hidden * inverse_two
-    normed_two = gather_plane((normal_two * gains[1]).astype(bf16))
+    hidden, normed_own = add_and_norm(rows_in, attention_branch, gains[1:2])
+    normed_two = gather_plane(normed_own)
 
     hidden_full = jnp.stack(spread_blocks(hidden_block, hidden_near, hidden_far))
     hidden_full = hidden_full.reshape(seqs, n_context, 3, block_hidden, rows)
@@ -749,13 +802,14 @@
         (grad_normed_two, feedforward_branch)
     )
 
-    result = (hidden + feedforward_branch).astype(bf16)
+    result = (hidden + feedforward_branch.astype(f32)).astype(bf16)
     if n_extra > 1:
         result = lax.all_gather(result, "extra", axis=0, tiled=True)
     result_near = spread_near(result)
-    grad_rows_two, gain_two = norm_backward(grad_normed_two, normal_two, inverse_two, gains[1])
-    grad_hidden = incoming.astype(f32) + grad_rows_two
-    grad_hidden_all = gather_plane(grad_hidden.astype(bf16))
+    gain_two, grad_hidden, grad_hidden_low = norm_backward(
+        grad_normed_two, hidden, incoming, gains[1:2], (f32, bf16)
+    )
+    grad_hidden_all = gather_plane(grad_hidden_low)
     hidden_grads = collect_near(hidden_grads, hidden_grads_far)
     grad_hidden_all, hidden_grads, result_near = lax.optimization_barrier(
         (grad_hidden_all, hidden_grads, result_near)
@@ -780,9 +834,10 @@
         heads_grads = collect_near(heads_grads, collect_far(heads_grads))
     grad_normed_one, heads_grads = lax.optimization_barrier((grad_normed_one, heads_grads))
 
-    grad_rows_one, gain_one = norm_backward(grad_normed_one, normal_one, inverse_one, gains[0])
-    grad_input = (grad_hidden + grad_rows_one).astype(bf16)
-    input_grad = lax.all_gather(grad_input, ("seq", "extra"), axis=0, tiled=True).astype(f32)
+    gain_one, grad_input = norm_backward(
+        grad_normed_one, rows_in, grad_hidden, gains[0:1], (bf16,)
+    )
+    input_grad = widen(lax.all_gather(grad_input, ("seq", "extra"), axis=0, tiled=True))
     if split_heads:
         heads_grad = exchange(total(heads_grads).astype(bf16)).astype(f32)
         heads_grad = heads_grad.reshape(block_heads, 4 * HEAD_DIM, rows)

time: 1190 us -> 1180 us (level)
  other arithmetic: 98.7 us -> 57.5 us
  Pallas kernels: 191 us -> 226 us
    reduce_scatter x3, waiting for transfers between devices: 90.6 us -> 6.18 us  [scatter_plane(): lax.psum_scatter(a.astype(bf16), plane, scatter_dimension=0, tiled=True)]
    ppermute x35, waiting for transfers between devices: 222 us -> 303 us  [send(): return lax.ppermute(a, 'seq', pairs)]
    pallas_call x0 -> x4, Pallas kernels: none -> 29.8 us  [by_rows(): pl.pallas_call(kernel, grid=(length // block,), out_shape=tuple(outs), in...]
    convert_element_type x7 -> x2, other arithmetic: 21.2 us -> 5.27 us  [the longest x1 3.55 us: shards(): result = (hidden + feedforward_branch.astype(f32)).astype(bf16)]
    unnamed x108 -> x92, local copies, waits for them, and re-layouts: 46.4 us -> 46.9 us
  transfers between devices with their start and end apart: 52 -> 52, of which waited for: 26 -> 27; matrix products, arithmetic and copies ran while one was open for 17% -> 17% of each run, Pallas kernels for 12% -> 12%
where the time goes in v7:
time: 1180 us
  waiting for transfers between devices  562 us (48%)
  Pallas kernels  226 us (19%)
  starting transfers between devices  115 us (10%)
  local copies, waits for them, and re-layouts  89.4 us (8%)
  matrix products  76.8 us (7%)
  other arithmetic  57.5 us (5%)
  blocking collectives  34.5 us (3%)
  between operations  15.7 us (1%)
    ppermute x35, waiting for transfers between devices, send(): return lax.ppermute(a, 'seq', pairs)  303 us
    ppermute x35, starting transfers between devices, send(): return lax.ppermute(a, 'seq', pairs)  94.9 us
    all_gather x4, waiting for transfers between devices, gather_plane(): return lax.all_gather(a, plane, axis=0, tiled=True)  90.4 us
    ppermute x5, waiting for transfers between devices, swap(): return lax.ppermute(a, axis, [(0, 1), (1, 0)])  77.6 us
    dot_general x5, matrix products, dot(): lax.dot_general(a, b, (((ca,), (cb,)), ((), ())), preferred_element_type=...  76.8 us
    all_gather x1, waiting for transfers between devices, shards(): lax.all_gather(grad_input, ('seq', 'extra'), axis=0, tiled=True)  62.2 us
    pallas_call x1, Pallas kernels, attend_back(): pl.pallas_call(attend_back_kernel, out_shape=jax.ShapeDtypeStruct((length...  60.6 us
    unnamed x92, local copies, waits for them, and re-layouts  46.9 us
  transfers between devices with their start and end apart: 52, of which 27 were waited for; matrix products, arithmetic and copies ran while one was open for 17% of the time, Pallas kernels for 12%

profile of v7, /device:TPU:0, one launch (start us, length us, event | category | flops | bytes accessed | tf_op | source)
XLA Modules:
  0.0 1176.1 jit_solution(9474980858718037981)
XLA Ops:
  11.8 26.5 %all_to_all.25 = bf16[8,256,256]{2,1,0:T(8,128)(2,1)S(1)} all-to-all(bf16[8,256,256]{2,1,0:T(8,128)(2,1)S(1)} %bitcast.210), channel_id=1, replica_groups=mesh['chips'=2,'pair'=2,'core'=2,'seq'=4,'extra'=1] {'chips','pair','core'}, dimensions={0} | all-to-all | bytes 2097152 | tf_op jit(solution)/shard_map/all_to_all | solution.py:596
  40.6 4.4 collective-permute-start
  48.2 11.0 collective-permute-done
  59.2 5.0 collective-permute-done.1
  71.9 8.0 all_gather.19
  79.9 8.8 collective-permute-start.5
  92.4 9.1 collective-permute-done.4
  102.8 4.3 collective-permute-done.6
  123.5 3.6 all-to-all-start.1
  127.6 21.5 %project.1 = (bf16[256,4096]{1,0:T(8,128)(2,1)}, bf16[256,4096]{1,0:T(8,128)(2,1)}, bf16[256,4096]{1,0:T(8,128)(2,1)}, bf16[4,4096,64]{2,1,0:T(8,128)(2,1)}, bf16[4,4096,64]{2,1,0:T(8,128)(2,1)}) custom-call(bf16[4096,2048]{1,0:T(8,128)(2,1)} %all-gather.6.cloned.1.call-done.x_ref, bf16[768,2048]{1,0:T(8,128)(2,1)} %multiply_convert_fusion.1.weight_ref, ...), custom_call_target="tpu_custom_call" | custom-call | flops 12884901888 | bytes 29360128 | tf_op jit(solution)/shard_map/project/pallas_call | solution.py:82
  152.5 36.1 %attend.1 = (bf16[256,4096]{1,0:T(8,128)(2,1)}, f32[4,4096]{1,0:T(4,128)}, bf16[4096,2048]{1,0:T(8,128)(2,1)}) custom-call(s32[8]{0:T(128)} %get-tuple-element.119.lo_ref, s32[8]{0:T(128)} %get-tuple-element.120.full_ref, s32[1,4096]{1,0:T(1,128)} %add_maximum_fusion.low_ref, bf16[256,4096]{1,0:T(8,128)(2,1)} %get-tuple-element.129.q_ref, ...), custom_call_target="tpu_custom_call" | custom-call | flops 51539607552 | bytes 16777216 | tf_op jit(solution)/shard_map/attend/pallas_call | solution.py:263
  188.6 29.4 %all-gather.8.cloned.1.call-done = bf16[4096,2048]{1,0:T(8,128)(2,1)} async-done(((bf16[512,2048]{1,0:T(8,128)(2,1)}), bf16[4096,2048]{1,0:T(8,128)(2,1)}) %all-gather.8.cloned.1.call-update) | async-done | bytes 16777232 | tf_op jit(solution)/shard_map/all_gather | solution.py:643
  218.1 3.5 collective-permute-start.10
  222.9 32.7 %collective-permute-done.10 = bf16[8,384,256]{2,1,0:T(8,128)(2,1)S(1)} collective-permute-done((bf16[8,384,256]{2,1,0:T(8,128)(2,1)S(1)}, bf16[8,384,256]{2,1,0:T(8,128)(2,1)S(1)}, u32[]{:S(2)}, u32[]{:S(2)}) %collective-permute-start.10) | collective-permute-done | bytes 1572896 | tf_op jit(solution)/shard_map/ppermute | solution.py:599
  255.5 4.2 collective-permute-done.12
  263.3 36.8 %collective-permute-done.14 = bf16[8,384,256]{2,1,0:T(8,128)(2,1)S(1)} collective-permute-done((bf16[8,384,256]{2,1,0:T(8,128)(2,1)S(1)}, bf16[8,384,256]{2,1,0:T(8,128)(2,1)S(1)}, u32[]{:S(2)}, u32[]{:S(2)}) %collective-permute-start.14) | collective-permute-done | bytes 1572896 | tf_op jit(solution)/shard_map/ppermute | solution.py:599
  302.4 29.6 %collective-permute-done.13 = bf16[8,384,256]{2,1,0:T(8,128)(2,1)} collective-permute-done((bf16[8,384,256]{2,1,0:T(8,128)(2,1)S(1)}, bf16[8,384,256]{2,1,0:T(8,128)(2,1)}, u32[]{:S(2)}, u32[]{:S(2)}) %collective-permute-start.13) | collective-permute-done | bytes 1572896 | tf_op jit(solution)/shard_map/ppermute | solution.py:599
  332.0 6.2 reduce-scatter.4.cloned.1.call-done.branch_ref
  338.1 5.5 add_and_norm.1
  351.1 3.3 copy-done.3
  355.1 4.6 slice-done
  359.7 3.5 copy.159
  363.3 11.8 %fusion.17.ga_ref = f32[4096,512]{1,0:T(8,128)} fusion(bf16[4096,2048]{1,0:T(8,128)(2,1)S(1)} %bitcast.239, bf16[512,2048]{1,0:T(8,128)(2,1)S(1)} %bitcast.218), kind=kOutput, calls=%fused_computation.104 | convolution fusion | flops 8589934592 | bytes 27262976 | tf_op jit(solution)/shard_map/dot_general | solution.py:28
  375.1 58.7 %all-gather.10.cloned.1.call-done.x_ref = bf16[4096,2048]{1,0:T(8,128)(2,1)} async-done(((bf16[512,2048]{1,0:T(8,128)(2,1)}), bf16[4096,2048]{1,0:T(8,128)(2,1)}) %all-gather.10.cloned.1.call-update) | async-done | bytes 16777232 | tf_op jit(solution)/shard_map/all_gather | solution.py:643
  433.7 35.0 %feedforward.1 = (bf16[4096,512]{1,0:T(8,128)(2,1)}, bf16[4096,1024]{1,0:T(8,128)(2,1)}, bf16[4096,2048]{1,0:T(8,128)(2,1)}) custom-call(bf16[4096,2048]{1,0:T(8,128)(2,1)} %all-gather.10.cloned.1.call-done.x_ref, f32[4096,512]{1,0:T(8,128)} %fusion.17.ga_ref, bf16[1024,2048]{1,0:T(8,128)(2,1)} %bitcast.203, bf16[512,2048]{1,0:T(8,128)(2,1)} %bitcast.219), custom_call_target="tpu_custom_call" | custom-call | flops 25769803776 | bytes 54525952 | tf_op jit(solution)/shard_map/feedforward/pallas_call | solution.py:364
  469.4 24.7 %halves_product.1 = (bf16[2048,2048]{1,0:T(8,128)(2,1)}, bf16[2048,2048]{1,0:T(8,128)(2,1)}) custom-call(s32[8]{0:T(128)} %pad_add_fusion.order_ref, bf16[4096,1024]{1,0:T(8,128)(2,1)} %get-tuple-element.150.a_ref, bf16[1024,2048]{1,0:T(8,128)(2,1)} %bitcast.204), custom_call_target="tpu_custom_call" | custom-call | flops 17179869184 | bytes 25165824 | tf_op jit(solution)/shard_map/halves_product/pallas_call | solution.py:404
  494.4 23.3 %convolution_convert_fusion = bf16[1024,2048]{1,0:T(8,128)(2,1)S(1)} fusion(bf16[4096,1024]{1,0:T(8,128)(2,1)} %get-tuple-element.150.a_ref, bf16[4096,2048]{1,0:T(8,128)(2,1)} %all-gather.10.cloned.1.call-done.x_ref), kind=kOutput, calls=%fused_computation.15 | convolution fusion | flops 17181966336 | bytes 29360128 | tf_op jit(solution)/shard_map/dot_general | solution.py:28
  520.2 13.4 %convolution_convert_fusion.1 = bf16[512,2048]{1,0:T(8,128)(2,1)S(1)} fusion(bf16[4096,512]{1,0:T(8,128)(2,1)S(1)} %copy-done.29, bf16[4096,2048]{1,0:T(8,128)(2,1)} %all-gather.8.cloned.1.call-done), kind=kOutput, calls=%fused_computation.20 | convolution fusion | flops 8590983168 | bytes 23068672 | tf_op jit(solution)/shard_map/dot_general | solution.py:28
  539.9 6.1 add_convert_fusion
  552.8 3.2 dynamic-slice_bitcast_fusion.1
  558.9 5.5 collective-permute-start.20
  568.7 55.2 %collective-permute-done.17 = bf16[2,256,2048]{2,1,0:T(8,128)(2,1)} collective-permute-done((bf16[2,256,2048]{2,1,0:T(8,128)(2,1)}, bf16[2,256,2048]{2,1,0:T(8,128)(2,1)}, u32[]{:S(2)}, u32[]{:S(2)}) %collective-permute-start.17) | collective-permute-done | bytes 2097184 | tf_op jit(solution)/shard_map/ppermute | solution.py:549
  632.8 21.6 %collective-permute-done.21 = bf16[256,2048]{1,0:T(8,128)(2,1)S(1)} collective-permute-done((bf16[256,2048]{1,0:T(8,128)(2,1)S(1)}, bf16[256,2048]{1,0:T(8,128)(2,1)S(1)}, u32[]{:S(2)}, u32[]{:S(2)}) %collective-permute-start.21) | collective-permute-done | bytes 1048608 | tf_op jit(solution)/shard_map/ppermute | solution.py:549
  658.2 8.3 norm_backward.2
  666.6 3.5 add_convert_fusion.1
  670.1 7.1 collective-permute-start.25
  678.5 4.0 add_convert_fusion.3
  682.5 4.3 collective-permute-start.23
  688.2 65.3 %collective-permute-done.23 = bf16[8,384,256]{2,1,0:T(8,128)(2,1)S(1)} collective-permute-done((bf16[8,384,256]{2,1,0:T(8,128)(2,1)S(1)}, bf16[8,384,256]{2,1,0:T(8,128)(2,1)S(1)}, u32[]{:S(2)}, u32[]{:S(2)}) %collective-permute-start.23) | collective-permute-done | bytes 1572896 | tf_op jit(solution)/shard_map/ppermute | solution.py:599
  753.4 5.4 collective-permute-done.24
  766.6 60.6 %attend_back.1.a_ref = bf16[4096,768]{1,0:T(8,128)(2,1)} custom-call(s32[8]{0:T(128)} %get-tuple-element.119.lo_ref, s32[8]{0:T(128)} %get-tuple-element.120.full_ref, s32[1,4096]{1,0:T(1,128)} %add_maximum_fusion.low_ref, bf16[256,4096]{1,0:T(8,128)(2,1)} %get-tuple-element.129.q_ref, bf16[4096,2048]{1,0:T(8,128)(2,1)} %all-gather.12.cloned.1.call-done.hidden_ref, ...), custom_call_target="tpu_custom_call" | custom-call | flops 103079215104 | bytes 25165824 | tf_op jit(solution)/shard_map/attend_back/pallas_call | solution.py:299
  827.2 32.8 %collective-permute-done.29 = bf16[512,2048]{1,0:T(8,128)(2,1)} collective-permute-done((bf16[512,2048]{1,0:T(8,128)(2,1)S(1)}, bf16[512,2048]{1,0:T(8,128)(2,1)}, u32[]{:S(2)}, u32[]{:S(2)}) %collective-permute-start.29) | collective-permute-done | bytes 2097184 | tf_op jit(solution)/shard_map/ppermute | solution.py:599
  860.0 18.0 %rows_product.1 = bf16[4096,2048]{1,0:T(8,128)(2,1)} custom-call(bf16[4096,768]{1,0:T(8,128)(2,1)} %attend_back.1.a_ref, bf16[768,2048]{1,0:T(8,128)(2,1)} %bitcast.182), custom_call_target="tpu_custom_call" | custom-call | flops 12884901888 | bytes 23068672 | tf_op jit(solution)/shard_map/rows_product/pallas_call | solution.py:441
  879.5 8.3 convolution_convert_fusion.2
  888.1 20.0 %multiply_convert_fusion = bf16[768,2048]{1,0:T(8,128)(2,1)S(1)} fusion(bf16[4096,768]{1,0:T(8,128)(2,1)} %attend_back.1.a_ref, bf16[4096,2048]{1,0:T(8,128)(2,1)} %all-gather.6.cloned.1.call-done.x_ref, f32[2048]{0:T(1024)S(1)} %bitcast.230), kind=kOutput, calls=%fused_computation.3 | convolution fusion | flops 12888047616 | bytes 26222592 | tf_op jit(solution)/shard_map/dot_general | solution.py:28
  910.2 11.9 %collective-permute-start.30 = (bf16[8,256,256]{2,0,1:T(8,128)(2,1)S(1)}, bf16[8,256,256]{2,0,1:T(8,128)(2,1)S(1)}, u32[]{:S(2)}, u32[]{:S(2)}) collective-permute-start(bf16[8,256,256]{2,0,1:T(8,128)(2,1)S(1)} %get-tuple-element.239), channel_id=1, source_target_pairs={{0,1},{1,2},{4,5},{5,6},{8,9},{9,10},{12,13},{13,14},{16,17},{17,1... | collective-permute-start | bytes 3145736 | tf_op jit(solution)/shard_map/ppermute | solution.py:599
  922.1 4.5 collective-permute-start.31
  927.4 18.3 %collective-permute-done.30 = bf16[8,256,256]{2,0,1:T(8,128)(2,1)S(1)} collective-permute-done((bf16[8,256,256]{2,0,1:T(8,128)(2,1)S(1)}, bf16[8,256,256]{2,0,1:T(8,128)(2,1)S(1)}, u32[]{:S(2)}, u32[]{:S(2)}) %collective-permute-start.30) | collective-permute-done | bytes 1048608 | tf_op jit(solution)/shard_map/ppermute | solution.py:599
  945.6 21.0 %collective-permute-done.31 = bf16[8,256,256]{2,0,1:T(8,128)(2,1)S(1)} collective-permute-done((bf16[8,256,256]{2,0,1:T(8,128)(2,1)S(1)}, bf16[8,256,256]{2,0,1:T(8,128)(2,1)S(1)}, u32[]{:S(2)}, u32[]{:S(2)}) %collective-permute-start.31) | collective-permute-done | bytes 1048608 | tf_op jit(solution)/shard_map/ppermute | solution.py:599
  967.5 11.3 collective-permute-start.32
  980.4 20.1 %collective-permute-done.32 = bf16[8,256,256]{2,0,1:T(8,128)(2,1)} collective-permute-done((bf16[8,256,256]{2,0,1:T(8,128)(2,1)S(1)}, bf16[8,256,256]{2,0,1:T(8,128)(2,1)}, u32[]{:S(2)}, u32[]{:S(2)}) %collective-permute-start.32) | collective-permute-done | bytes 1048608 | tf_op jit(solution)/shard_map/ppermute | solution.py:599
  1000.5 5.2 collective-permute-done.34
  1005.7 6.4 norm_backward.3
  1013.5 3.6 add_convert_fusion.2
  1017.1 3.6 all-to-all-start.4
  1020.7 21.0 %all-to-all-done.4 = bf16[8,384,256]{2,1,0:T(8,128)(2,1)S(1)} async-done(((bf16[8,384,256]{2,1,0:T(8,128)(2,1)}), bf16[8,384,256]{2,1,0:T(8,128)(2,1)S(1)}, u32[]{:S(2)}, u32[]{:S(2)}) %all-to-all-start.4) | async-done | bytes 1572896 | tf_op jit(solution)/shard_map/all_to_all | solution.py:596
  1048.5 3.2 bitcast_dynamic-update-slice_fusion.4
  1051.6 3.3 bitcast_dynamic-update-slice_fusion.3
  1059.6 3.2 bitcast_dynamic-update-slice_fusion
  1063.4 3.3 all-to-all-start.2
  1071.5 3.6 all-to-all-start.3
  1085.1 8.5 constant_dynamic-slice_fusion
  1097.1 62.2 %all-gather.14.cloned.1.call-done.a_ref = bf16[2048,2048]{1,0:T(8,128)(2,1)} async-done(((bf16[512,2048]{1,0:T(8,128)(2,1)}), bf16[2048,2048]{1,0:T(8,128)(2,1)}) %all-gather.14.cloned.1.call-update) | async-done | bytes 8388624 | tf_op jit(solution)/shard_map/all_gather | solution.py:840
  1159.3 9.5 widen.1
  (255 shorter events, 143.1 us)
Async XLA Ops:
  7.2 102.2 %copy-start = (s32[4,8]{1,0:T(4,128)S(1)}, s32[4,8]{1,0:T(4,128)}, u32[]{:S(2)}) copy-start(s32[4,8]{1,0:T(4,128)} %param.9) | copy-start | bytes 388
  7.2 102.2 %all-gather.6.cloned.1.call-start = ((), (), s32[]{:S(2)}) async-start(), calls=%async_computation.8 | async-start | bytes 18874368 | tf_op jit(solution)/shard_map/all_gather | solution.py:643
  11.3 206.7 %all-gather.8.cloned.1.call-start = ((), (), s32[]{:S(2)}) async-start(), calls=%async_computation.9 | async-start | bytes 18874368 | tf_op jit(solution)/shard_map/all_gather | solution.py:643
  11.8 34.5 %copy-start.19 = (bf16[2,256,1024]{2,1,0:T(8,128)(2,1)S(1)}, bf16[2,256,1024]{2,1,0:T(8,128)(2,1)}, u32[]{:S(2)}) copy-start(bf16[2,256,1024]{2,1,0:T(8,128)(2,1)} %param.13) | copy-start | bytes 3145732
  40.6 18.6 %collective-permute-start = (bf16[8,192,256]{2,0,1:T(8,128)(2,1)}, bf16[8,192,256]{2,0,1:T(8,128)(2,1)}, u32[]{:S(2)}, u32[]{:S(2)}) collective-permute-start(bf16[8,192,256]{2,0,1:T(8,128)(2,1)} %copy.125), channel_id=1, source_target_pairs={{0,1},{1,2},{2,3},{4,5},{5,6},{6,7},{8,9},{9,10},{10,11},{12,13},{... | collective-permute-start | bytes 2359304 | tf_op jit(solution)/shard_map/ppermute | solution.py:599
  45.1 19.1 %collective-permute-start.1 = (bf16[8,192,256]{2,0,1:T(8,128)(2,1)}, bf16[8,192,256]{2,0,1:T(8,128)(2,1)}, u32[]{:S(2)}, u32[]{:S(2)}) collective-permute-start(bf16[8,192,256]{2,0,1:T(8,128)(2,1)} %copy.125), channel_id=1, source_target_pairs={{1,0},{2,1},{3,2},{5,4},{6,5},{7,6},{9,8},{10,9},{11,10},{13,12},{... | collective-permute-start | bytes 2359304 | tf_op jit(solution)/shard_map/ppermute | solution.py:599
  48.2 23.7 %copy-start.28 = (bf16[2,256]{1,0:T(2,128)(2,1)S(1)}, bf16[2,256]{1,0:T(2,128)(2,1)}, u32[]{:S(2)}) copy-start(bf16[2,256]{1,0:T(2,128)(2,1)} %param.10) | copy-start | bytes 3076
  65.4 24.6 %collective-permute-start.2 = (bf16[8,192,256]{2,0,1:T(8,128)(2,1)S(1)}, bf16[8,192,256]{2,0,1:T(8,128)(2,1)}, u32[]{:S(2)}, u32[]{:S(2)}) collective-permute-start(bf16[8,192,256]{2,0,1:T(8,128)(2,1)S(1)} %broadcast_select_fusion.8), channel_id=1, source_target_pairs={{1,3},{2,0},{5,7},{6,4},{9,11},{10,8},{13,15},{14,12},{17,19},{18,... | collective-permute-start | bytes 2359304 | tf_op jit(solution)/shard_map/ppermute | solution.py:599
  66.7 24.8 %collective-permute-start.3 = (bf16[8,192,256]{2,0,1:T(8,128)(2,1)}, bf16[8,192,256]{2,0,1:T(8,128)(2,1)S(1)}, u32[]{:S(2)}, u32[]{:S(2)}) collective-permute-start(bf16[8,192,256]{2,0,1:T(8,128)(2,1)} %collective-permute-done), channel_id=1, source_target_pairs={{1,2},{2,3},{5,6},{6,7},{9,10},{10,11},{13,14},{14,15},{17,18},{18... | collective-permute-start | bytes 2359304 | tf_op jit(solution)/shard_map/ppermute | solution.py:599
  67.4 34.1 %collective-permute-start.4 = (bf16[8,192,256]{2,0,1:T(8,128)(2,1)}, bf16[8,192,256]{2,0,1:T(8,128)(2,1)}, u32[]{:S(2)}, u32[]{:S(2)}) collective-permute-start(bf16[8,192,256]{2,0,1:T(8,128)(2,1)} %collective-permute-done.1), channel_id=1, source_target_pairs={{1,0},{2,1},{5,4},{6,5},{9,8},{10,9},{13,12},{14,13},{17,16},{18,1... | collective-permute-start | bytes 2359304 | tf_op jit(solution)/shard_map/ppermute | solution.py:599
  79.9 22.9 %collective-permute-start.5 = (bf16[8,64,256]{2,0,1:T(8,128)(2,1)}, bf16[8,64,256]{2,0,1:T(8,128)(2,1)S(1)}, u32[]{:S(2)}, u32[]{:S(2)}) collective-permute-start(bf16[8,64,256]{2,0,1:T(8,128)(2,1)} %bitcast.168), channel_id=1, source_target_pairs={{0,1},{1,2},{2,3},{4,5},{5,6},{6,7},{8,9},{9,10},{10,11},{12,13},{... | collective-permute-start | bytes 786440 | tf_op jit(solution)/shard_map/ppermute | solution.py:599
  88.7 18.4 %collective-permute-start.6 = (bf16[8,64,256]{2,0,1:T(8,128)(2,1)}, bf16[8,64,256]{2,0,1:T(8,128)(2,1)}, u32[]{:S(2)}, u32[]{:S(2)}) collective-permute-start(bf16[8,64,256]{2,0,1:T(8,128)(2,1)} %bitcast.168), channel_id=1, source_target_pairs={{1,0},{2,1},{3,2},{5,4},{6,5},{7,6},{9,8},{10,9},{11,10},{13,12},{... | collective-permute-start | bytes 786440 | tf_op jit(solution)/shard_map/ppermute | solution.py:599
  119.2 29.9 %collective-permute-start.7 = (bf16[8,64,256]{2,0,1:T(8,128)(2,1)S(1)}, bf16[8,64,256]{2,0,1:T(8,128)(2,1)S(1)}, u32[]{:S(2)}, u32[]{:S(2)}) collective-permute-start(bf16[8,64,256]{2,0,1:T(8,128)(2,1)S(1)} %collective-permute-done.5), channel_id=1, source_target_pairs={{1,2},{2,3},{5,6},{6,7},{9,10},{10,11},{13,14},{14,15},{17,18},{18... | collective-permute-start | bytes 786440 | tf_op jit(solution)/shard_map/ppermute | solution.py:599
  119.8 29.2 %collective-permute-start.8 = (bf16[8,64,256]{2,0,1:T(8,128)(2,1)}, bf16[8,64,256]{2,0,1:T(8,128)(2,1)S(1)}, u32[]{:S(2)}, u32[]{:S(2)}) collective-permute-start(bf16[8,64,256]{2,0,1:T(8,128)(2,1)} %collective-permute-done.6), channel_id=1, source_target_pairs={{1,0},{2,1},{5,4},{6,5},{9,8},{10,9},{13,12},{14,13},{17,16},{18,1... | collective-permute-start | bytes 786440 | tf_op jit(solution)/shard_map/ppermute | solution.py:599
  122.2 26.9 %collective-permute-start.9 = (bf16[8,64,256]{2,0,1:T(8,128)(2,1)S(1)}, bf16[8,64,256]{2,0,1:T(8,128)(2,1)S(1)}, u32[]{:S(2)}, u32[]{:S(2)}) collective-permute-start(bf16[8,64,256]{2,0,1:T(8,128)(2,1)S(1)} %broadcast_select_fusion.10), channel_id=1, source_target_pairs={{1,3},{2,0},{5,7},{6,4},{9,11},{10,8},{13,15},{14,12},{17,19},{18,... | collective-permute-start | bytes 786440 | tf_op jit(solution)/shard_map/ppermute | solution.py:599
  123.5 65.1 %all-to-all-start.1 = ((bf16[8,384,256]{2,1,0:T(8,128)(2,1)}), bf16[8,384,256]{2,1,0:T(8,128)(2,1)S(1)}, u32[]{:S(2)}, u32[]{:S(2)}) async-start(bf16[8,384,256]{2,1,0:T(8,128)(2,1)} %pad_maximum_fusion.2), calls=%async_computation.1 | async-start | bytes 3145728 | tf_op jit(solution)/shard_map/all_to_all | solution.py:596
  127.1 211.1 %reduce-scatter.4.cloned.1.call-start = ((), (), s32[]{:S(2)}) async-start(), calls=%async_computation.10 | async-start | bytes 18874368 | tf_op jit(solution)/shard_map/reduce_scatter | solution.py:646
  218.0 215.7 %all-gather.10.cloned.1.call-start = ((), (), s32[]{:S(2)}) async-start(), calls=%async_computation.11 | async-start | bytes 18874368 | tf_op jit(solution)/shard_map/all_gather | solution.py:643
  218.1 37.5 %collective-permute-start.10 = (bf16[8,384,256]{2,1,0:T(8,128)(2,1)S(1)}, bf16[8,384,256]{2,1,0:T(8,128)(2,1)S(1)}, u32[]{:S(2)}, u32[]{:S(2)}) collective-permute-start(bf16[8,384,256]{2,1,0:T(8,128)(2,1)S(1)} %all-to-all-done.1), channel_id=1, source_target_pairs={{0,1},{1,2},{2,3},{4,5},{5,6},{6,7},{8,9},{9,10},{10,11},{12,13},{... | collective-permute-start | bytes 4718600 | tf_op jit(solution)/shard_map/ppermute | solution.py:599
  221.6 38.2 %collective-permute-start.12 = (bf16[8,384,256]{2,1,0:T(8,128)(2,1)S(1)}, bf16[8,384,256]{2,1,0:T(8,128)(2,1)S(1)}, u32[]{:S(2)}, u32[]{:S(2)}) collective-permute-start(bf16[8,384,256]{2,1,0:T(8,128)(2,1)S(1)} %all-to-all-done.1), channel_id=1, source_target_pairs={{1,0},{2,1},{3,2},{5,4},{6,5},{7,6},{9,8},{10,9},{11,10},{13,12},{... | collective-permute-start | bytes 4718600 | tf_op jit(solution)/shard_map/ppermute | solution.py:599
  259.7 40.4 %copy-start.9 = (bf16[8,384,256]{2,1,0:T(8,128)(2,1)}, bf16[8,384,256]{2,1,0:T(8,128)(2,1)S(1)}, u32[]{:S(2)}) copy-start(bf16[8,384,256]{2,1,0:T(8,128)(2,1)S(1)} %collective-permute-done.12) | copy-start | bytes 4718596
  259.9 40.2 %collective-permute-start.14 = (bf16[8,384,256]{2,1,0:T(8,128)(2,1)S(1)}, bf16[8,384,256]{2,1,0:T(8,128)(2,1)S(1)}, u32[]{:S(2)}, u32[]{:S(2)}) collective-permute-start(bf16[8,384,256]{2,1,0:T(8,128)(2,1)S(1)} %broadcast_select_fusion.5), channel_id=1, source_target_pairs={{1,3},{2,0},{5,7},{6,4},{9,11},{10,8},{13,15},{14,12},{17,19},{18,... | collective-permute-start | bytes 4718600 | tf_op jit(solution)/shard_map/ppermute | solution.py:599
  261.2 38.9 %collective-permute-start.11 = (bf16[8,384,256]{2,1,0:T(8,128)(2,1)S(1)}, bf16[8,384,256]{2,1,0:T(8,128)(2,1)S(1)}, u32[]{:S(2)}, u32[]{:S(2)}) collective-permute-start(bf16[8,384,256]{2,1,0:T(8,128)(2,1)S(1)} %collective-permute-done.10), channel_id=1, source_target_pairs={{1,2},{2,3},{5,6},{6,7},{9,10},{10,11},{13,14},{14,15},{17,18},{18... | collective-permute-start | bytes 4718600 | tf_op jit(solution)/shard_map/ppermute | solution.py:599
  262.0 70.0 %collective-permute-start.13 = (bf16[8,384,256]{2,1,0:T(8,128)(2,1)S(1)}, bf16[8,384,256]{2,1,0:T(8,128)(2,1)}, u32[]{:S(2)}, u32[]{:S(2)}) collective-permute-start(bf16[8,384,256]{2,1,0:T(8,128)(2,1)S(1)} %collective-permute-done.12), channel_id=1, source_target_pairs={{1,0},{2,1},{5,4},{6,5},{9,8},{10,9},{13,12},{14,13},{17,16},{18,1... | collective-permute-start | bytes 4718600 | tf_op jit(solution)/shard_map/ppermute | solution.py:599
  343.7 314.5 %reduce-scatter.6.cloned.1.call-start = ((), (), s32[]{:S(2)}) async-start(), calls=%async_computation.12 | async-start | bytes 18874368 | tf_op jit(solution)/shard_map/reduce_scatter | solution.py:646
  349.9 13.3 %slice-start.3 = ((s8[16777216]{0:T(1024)(128)(4,1)}), s8[4194304]{0:T(1024)(128)(4,1)S(1)}, s32[]{:S(2)}) async-start(s8[16777216]{0:T(1024)(128)(4,1)} %bitcast.238), calls=%async_computation.19 | async-start | bytes 8388608
  349.9 13.3 %slice-start.4 = ((s8[16777216]{0:T(1024)(128)(4,1)}), s8[4194304]{0:T(1024)(128)(4,1)S(1)}, s32[]{:S(2)}) async-start(s8[16777216]{0:T(1024)(128)(4,1)} %bitcast.238), calls=%async_computation.20 | async-start | bytes 8388608
  351.1 12.1 %slice-start.5 = ((s8[16777216]{0:T(1024)(128)(4,1)}), s8[4194304]{0:T(1024)(128)(4,1)S(1)}, s32[]{:S(2)}) async-start(s8[16777216]{0:T(1024)(128)(4,1)} %bitcast.238), calls=%async_computation.21 | async-start | bytes 8388608
  354.4 8.9 slice-start.6
  468.8 291.2 %all-gather.12.cloned.1.call-start = ((), (), s32[]{:S(2)}) async-start(), calls=%async_computation.13 | async-start | bytes 18874368 | tf_op jit(solution)/shard_map/all_gather | solution.py:643
  494.2 44.9 %collective-permute-start.15 = (bf16[2048,2048]{1,0:T(8,128)(2,1)}, bf16[2048,2048]{1,0:T(8,128)(2,1)}, u32[]{:S(2)}, u32[]{:S(2)}) collective-permute-start(bf16[2048,2048]{1,0:T(8,128)(2,1)} %get-tuple-element.152), channel_id=1, source_target_pairs={{0,4},{4,0},{1,5},{5,1},{2,6},{6,2},{3,7},{7,3},{8,12},{12,8},{9,1... | collective-permute-start | bytes 25165832 | tf_op jit(solution)/shard_map/ppermute | solution.py:549
  552.2 71.7 %collective-permute-start.17 = (bf16[2,256,2048]{2,1,0:T(8,128)(2,1)}, bf16[2,256,2048]{2,1,0:T(8,128)(2,1)}, u32[]{:S(2)}, u32[]{:S(2)}) collective-permute-start(bf16[2,256,2048]{2,1,0:T(8,128)(2,1)} %dynamic-slice_bitcast_fusion), channel_id=1, source_target_pairs={{0,16},{16,0},{1,17},{17,1},{2,18},{18,2},{3,19},{19,3},{4,20},{20... | collective-permute-start | bytes 6291464 | tf_op jit(solution)/shard_map/ppermute | solution.py:549
  556.0 70.9 %collective-permute-start.16 = (bf16[2,256,2048]{2,1,0:T(8,128)(2,1)}, bf16[2,256,2048]{2,1,0:T(8,128)(2,1)}, u32[]{:S(2)}, u32[]{:S(2)}) collective-permute-start(bf16[2,256,2048]{2,1,0:T(8,128)(2,1)} %dynamic-slice_bitcast_fusion.1), channel_id=1, source_target_pairs={{0,8},{8,0},{1,9},{9,1},{2,10},{10,2},{3,11},{11,3},{4,12},{12,4},... | collective-permute-start | bytes 6291464 | tf_op jit(solution)/shard_map/ppermute | solution.py:549
  558.9 70.4 %collective-permute-start.20 = (bf16[8,384,256]{2,1,0:T(8,128)(2,1)}, bf16[8,384,256]{2,1,0:T(8,128)(2,1)}, u32[]{:S(2)}, u32[]{:S(2)}) collective-permute-start(bf16[8,384,256]{2,1,0:T(8,128)(2,1)} %broadcast_select_fusion.3), channel_id=1, source_target_pairs={{0,2},{3,1},{4,6},{7,5},{8,10},{11,9},{12,14},{15,13},{16,18},{19,... | collective-permute-start | bytes 4718600 | tf_op jit(solution)/shard_map/ppermute | solution.py:599
  564.4 66.1 %collective-permute-start.18 = (bf16[8,384,256]{2,1,0:T(8,128)(2,1)}, bf16[8,384,256]{2,1,0:T(8,128)(2,1)}, u32[]{:S(2)}, u32[]{:S(2)}) collective-permute-start(bf16[8,384,256]{2,1,0:T(8,128)(2,1)} %bitcast.36), channel_id=1, source_target_pairs={{0,1},{1,2},{4,5},{5,6},{8,9},{9,10},{12,13},{13,14},{16,17},{17,1... | collective-permute-start | bytes 4718600 | tf_op jit(solution)/shard_map/ppermute | solution.py:599
  566.9 63.6 %collective-permute-start.19 = (bf16[8,384,256]{2,1,0:T(8,128)(2,1)}, bf16[8,384,256]{2,1,0:T(8,128)(2,1)}, u32[]{:S(2)}, u32[]{:S(2)}) collective-permute-start(bf16[8,384,256]{2,1,0:T(8,128)(2,1)} %bitcast.36), channel_id=1, source_target_pairs={{2,1},{3,2},{6,5},{7,6},{10,9},{11,10},{14,13},{15,14},{18,17},{19... | collective-permute-start | bytes 4718600 | tf_op jit(solution)/shard_map/ppermute | solution.py:599
  568.7 58.2 %copy-start.4 = (bf16[2,2,256,2048]{3,2,1,0:T(8,128)(2,1)S(1)}, bf16[2,2,256,2048]{3,2,1,0:T(8,128)(2,1)}, u32[]{:S(2)}) copy-start(bf16[2,2,256,2048]{3,2,1,0:T(8,128)(2,1)} %get-tuple-element.233) | copy-start | bytes 12582916
  630.6 23.8 %collective-permute-start.21 = (bf16[256,2048]{1,0:T(8,128)(2,1)S(1)}, bf16[256,2048]{1,0:T(8,128)(2,1)S(1)}, u32[]{:S(2)}, u32[]{:S(2)}) collective-permute-start(bf16[256,2048]{1,0:T(8,128)(2,1)S(1)} %dynamic-slice_bitcast_fusion.5), channel_id=1, source_target_pairs={{0,16},{16,0},{1,17},{17,1},{2,18},{18,2},{3,19},{19,3},{4,20},{20... | collective-permute-start | bytes 3145736 | tf_op jit(solution)/shard_map/ppermute | solution.py:549
  632.2 23.4 %collective-permute-start.22 = (bf16[256,2048]{1,0:T(8,128)(2,1)S(1)}, bf16[256,2048]{1,0:T(8,128)(2,1)S(1)}, u32[]{:S(2)}, u32[]{:S(2)}) collective-permute-start(bf16[256,2048]{1,0:T(8,128)(2,1)S(1)} %dynamic-slice_bitcast_fusion.4), channel_id=1, source_target_pairs={{0,8},{8,0},{1,9},{9,1},{2,10},{10,2},{3,11},{11,3},{4,12},{12,4},... | collective-permute-start | bytes 3145736 | tf_op jit(solution)/shard_map/ppermute | solution.py:549
  666.5 339.1 %reduce-scatter.8.cloned.1.call-start = ((), (), s32[]{:S(2)}) async-start(), calls=%async_computation.14 | async-start | bytes 18874368 | tf_op jit(solution)/shard_map/reduce_scatter | solution.py:646
  670.1 12.4 %copy-start.7 = (bf16[512,2048]{1,0:T(8,128)(2,1)}, bf16[512,2048]{1,0:T(8,128)(2,1)S(1)}, u32[]{:S(2)}) copy-start(bf16[512,2048]{1,0:T(8,128)(2,1)S(1)} %add_convert_fusion.1) | copy-start | bytes 6291460
  670.1 88.7 %collective-permute-start.25 = (bf16[512,2048]{1,0:T(8,128)(2,1)S(1)}, bf16[512,2048]{1,0:T(8,128)(2,1)}, u32[]{:S(2)}, u32[]{:S(2)}) collective-permute-start(bf16[512,2048]{1,0:T(8,128)(2,1)S(1)} %add_convert_fusion.1), channel_id=1, source_target_pairs={{0,1},{1,2},{2,3},{4,5},{5,6},{6,7},{8,9},{9,10},{10,11},{12,13},{... | collective-permute-start | bytes 6291464 | tf_op jit(solution)/shard_map/ppermute | solution.py:599
  677.3 82.8 %collective-permute-start.26 = (bf16[512,2048]{1,0:T(8,128)(2,1)S(1)}, bf16[512,2048]{1,0:T(8,128)(2,1)}, u32[]{:S(2)}, u32[]{:S(2)}) collective-permute-start(bf16[512,2048]{1,0:T(8,128)(2,1)S(1)} %add_convert_fusion.1), channel_id=1, source_target_pairs={{1,0},{2,1},{3,2},{5,4},{6,5},{7,6},{9,8},{10,9},{11,10},{13,12},{... | collective-permute-start | bytes 6291464 | tf_op jit(solution)/shard_map/ppermute | solution.py:599
  682.5 70.9 %collective-permute-start.23 = (bf16[8,384,256]{2,1,0:T(8,128)(2,1)S(1)}, bf16[8,384,256]{2,1,0:T(8,128)(2,1)S(1)}, u32[]{:S(2)}, u32[]{:S(2)}) collective-permute-start(bf16[8,384,256]{2,1,0:T(8,128)(2,1)S(1)} %get-tuple-element.242), channel_id=1, source_target_pairs={{0,1},{1,2},{2,3},{4,5},{5,6},{6,7},{8,9},{9,10},{10,11},{12,13},{... | collective-permute-start | bytes 4718600 | tf_op jit(solution)/shard_map/ppermute | solution.py:599
  686.9 72.0 %collective-permute-start.24 = (bf16[8,384,256]{2,1,0:T(8,128)(2,1)S(1)}, bf16[8,384,256]{2,1,0:T(8,128)(2,1)S(1)}, u32[]{:S(2)}, u32[]{:S(2)}) collective-permute-start(bf16[8,384,256]{2,1,0:T(8,128)(2,1)S(1)} %get-tuple-element.241), channel_id=1, source_target_pairs={{1,0},{2,1},{3,2},{5,4},{6,5},{7,6},{9,8},{10,9},{11,10},{13,12},{... | collective-permute-start | bytes 4718600 | tf_op jit(solution)/shard_map/ppermute | solution.py:599
  760.0 100.0 %collective-permute-start.27 = (bf16[512,2048]{1,0:T(8,128)(2,1)}, bf16[512,2048]{1,0:T(8,128)(2,1)}, u32[]{:S(2)}, u32[]{:S(2)}) collective-permute-start(bf16[512,2048]{1,0:T(8,128)(2,1)} %collective-permute-done.25), channel_id=1, source_target_pairs={{1,2},{2,3},{5,6},{6,7},{9,10},{10,11},{13,14},{14,15},{17,18},{18... | collective-permute-start | bytes 6291464 | tf_op jit(solution)/shard_map/ppermute | solution.py:599
  763.8 96.2 %collective-permute-start.28 = (bf16[512,2048]{1,0:T(8,128)(2,1)}, bf16[512,2048]{1,0:T(8,128)(2,1)}, u32[]{:S(2)}, u32[]{:S(2)}) collective-permute-start(bf16[512,2048]{1,0:T(8,128)(2,1)} %collective-permute-done.26), channel_id=1, source_target_pairs={{1,0},{2,1},{5,4},{6,5},{9,8},{10,9},{13,12},{14,13},{17,16},{18,1... | collective-permute-start | bytes 6291464 | tf_op jit(solution)/shard_map/ppermute | solution.py:599
  765.3 94.7 %collective-permute-start.29 = (bf16[512,2048]{1,0:T(8,128)(2,1)S(1)}, bf16[512,2048]{1,0:T(8,128)(2,1)}, u32[]{:S(2)}, u32[]{:S(2)}) collective-permute-start(bf16[512,2048]{1,0:T(8,128)(2,1)S(1)} %broadcast_select_fusion), channel_id=1, source_target_pairs={{1,3},{2,0},{5,7},{6,4},{9,11},{10,8},{13,15},{14,12},{17,19},{18,... | collective-permute-start | bytes 6291464 | tf_op jit(solution)/shard_map/ppermute | solution.py:599
  878.0 10.2 copy-start.25
  878.0 281.3 %all-gather.14.cloned.1.call-start = ((), (), s32[]{:S(2)}) async-start(), calls=%async_computation.15 | async-start | bytes 10485760 | tf_op jit(solution)/shard_map/all_gather | solution.py:840
  910.2 35.4 %collective-permute-start.30 = (bf16[8,256,256]{2,0,1:T(8,128)(2,1)S(1)}, bf16[8,256,256]{2,0,1:T(8,128)(2,1)S(1)}, u32[]{:S(2)}, u32[]{:S(2)}) collective-permute-start(bf16[8,256,256]{2,0,1:T(8,128)(2,1)S(1)} %get-tuple-element.239), channel_id=1, source_target_pairs={{0,1},{1,2},{4,5},{5,6},{8,9},{9,10},{12,13},{13,14},{16,17},{17,1... | collective-permute-start | bytes 3145736 | tf_op jit(solution)/shard_map/ppermute | solution.py:599
  922.1 44.5 %collective-permute-start.31 = (bf16[8,256,256]{2,0,1:T(8,128)(2,1)S(1)}, bf16[8,256,256]{2,0,1:T(8,128)(2,1)S(1)}, u32[]{:S(2)}, u32[]{:S(2)}) collective-permute-start(bf16[8,256,256]{2,0,1:T(8,128)(2,1)S(1)} %get-tuple-element.238), channel_id=1, source_target_pairs={{0,2},{3,1},{4,6},{7,5},{8,10},{11,9},{12,14},{15,13},{16,18},{19,... | collective-permute-start | bytes 3145736 | tf_op jit(solution)/shard_map/ppermute | solution.py:599
  926.6 40.0 %collective-permute-start.33 = (bf16[8,256,256]{2,0,1:T(8,128)(2,1)S(1)}, bf16[8,256,256]{2,0,1:T(8,128)(2,1)S(1)}, u32[]{:S(2)}, u32[]{:S(2)}) collective-permute-start(bf16[8,256,256]{2,0,1:T(8,128)(2,1)S(1)} %get-tuple-element.239), channel_id=1, source_target_pairs={{2,1},{3,2},{6,5},{7,6},{10,9},{11,10},{14,13},{15,14},{18,17},{19... | collective-permute-start | bytes 3145736 | tf_op jit(solution)/shard_map/ppermute | solution.py:599
  967.5 33.0 %collective-permute-start.32 = (bf16[8,256,256]{2,0,1:T(8,128)(2,1)S(1)}, bf16[8,256,256]{2,0,1:T(8,128)(2,1)}, u32[]{:S(2)}, u32[]{:S(2)}) collective-permute-start(bf16[8,256,256]{2,0,1:T(8,128)(2,1)S(1)} %get-tuple-element.246), channel_id=1, source_target_pairs={{0,1},{1,2},{2,3},{4,5},{5,6},{6,7},{8,9},{9,10},{10,11},{12,13},{... | collective-permute-start | bytes 3145736 | tf_op jit(solution)/shard_map/ppermute | solution.py:599
  978.9 26.8 %collective-permute-start.34 = (bf16[8,256,256]{2,0,1:T(8,128)(2,1)S(1)}, bf16[8,256,256]{2,0,1:T(8,128)(2,1)}, u32[]{:S(2)}, u32[]{:S(2)}) collective-permute-start(bf16[8,256,256]{2,0,1:T(8,128)(2,1)S(1)} %get-tuple-element.245), channel_id=1, source_target_pairs={{1,0},{2,1},{3,2},{5,4},{6,5},{7,6},{9,8},{10,9},{11,10},{13,12},{... | collective-permute-start | bytes 3145736 | tf_op jit(solution)/shard_map/ppermute | solution.py:599
  1017.1 24.6 %all-to-all-start.4 = ((bf16[8,384,256]{2,1,0:T(8,128)(2,1)}), bf16[8,384,256]{2,1,0:T(8,128)(2,1)S(1)}, u32[]{:S(2)}, u32[]{:S(2)}) async-start(bf16[8,384,256]{2,1,0:T(8,128)(2,1)} %add_convert_fusion.2), calls=%async_computation.7 | async-start | bytes 3145728 | tf_op jit(solution)/shard_map/all_to_all | solution.py:596
  1063.4 8.0 all-to-all-start.2
  1071.5 22.9 %all-to-all-start.3 = ((bf16[8,256,256]{2,1,0:T(8,128)(2,1)}), bf16[8,256,256]{2,1,0:T(8,128)(2,1)S(1)}, u32[]{:S(2)}, u32[]{:S(2)}) async-start(bf16[8,256,256]{2,1,0:T(8,128)(2,1)} %copy.150), calls=%async_computation.6 | async-start | bytes 2097152 | tf_op jit(solution)/shard_map/all_to_all | solution.py:596
  1075.0 5.8 collective-permute-start.35
  1076.4 5.5 collective-permute-start.36
  1081.9 11.8 %collective-permute-start.37 = (f32[2,256]{1,0:T(2,128)S(1)}, f32[2,256]{1,0:T(2,128)S(1)}, u32[]{:S(2)}, u32[]{:S(2)}) collective-permute-start(f32[2,256]{1,0:T(2,128)S(1)} %broadcast_select_fusion.11), channel_id=1, source_target_pairs={{1,3},{2,0},{5,7},{6,4},{9,11},{10,8},{13,15},{14,12},{17,19},{18,... | collective-permute-start | bytes 6152 | tf_op jit(solution)/shard_map/ppermute | solution.py:599
  1083.2 10.5 collective-permute-start.38
  1083.8 9.8 collective-permute-start.39
  1159.3 9.5 copy-start.1
  (26 other events, 80.1 us)
Sparse Core Ops, SparseCore 0:
  11.2 98.0 all-gather.5
  111.2 106.7 all-gather.7
  222.1 115.9 reduce-scatter.3
  343.8 89.8 all-gather.9
  468.9 144.0 reduce-scatter.5
  666.7 91.0 all-gather.11
  878.1 123.2 reduce-scatter.7
  1012.3 146.9 all-gather.13

commit v8 on v7

--- a/solution.py
+++ b/solution.py
@@ -821,9 +821,15 @@
     )
     grad_projected, result_far = lax.optimization_barrier((grad_projected, result_far))
 
-    first_part = rows_product(grad_projected, qkv_t)
-    first_part, grad_projected = lax.optimization_barrier((first_part, grad_projected))
-    grad_normed_one = scatter_plane(first_part)
+    owners = 2 * jnp.arange(n_context * n_extra, dtype=jnp.int32)
+    first_half, second_half = halves_product(
+        jnp.concatenate([owners, owners + 1]), grad_projected, qkv_t
+    )
+    first_half, second_half, grad_projected = lax.optimization_barrier(
+        (first_half, second_half, grad_projected)
+    )
+    grad_one = scatter_plane(first_half)
+    grad_two = scatter_plane(after(second_half, grad_one))
     qkv_grad = dot(grad_projected, normal_all, 0, 0) * gains[0]
     qkv_grad = qkv_grad.reshape(3, heads, HEAD_DIM, model).transpose(1, 0, 2, 3)
     qkv_grad = qkv_grad.reshape(heads, 3 * HEAD_DIM, model)
@@ -832,12 +838,22 @@
     heads_grads = heads_split(heads_grad) if split_heads else []
     if split_heads:
         heads_grads = collect_near(heads_grads, collect_far(heads_grads))
-    grad_normed_one, heads_grads = lax.optimization_barrier((grad_normed_one, heads_grads))
-
-    gain_one, grad_input = norm_backward(
-        grad_normed_one, rows_in, grad_hidden, gains[0:1], (bf16,)
-    )
-    input_grad = widen(lax.all_gather(grad_input, ("seq", "extra"), axis=0, tiled=True))
+    grad_two, heads_grads = lax.optimization_barrier((grad_two, heads_grads))
+
+    half = own_len // 2
+    gain_one = 0
+    gathered = None
+    input_grad = jnp.zeros((seqs * n_extra, own_len, model), f32)
+    for at, grad_normed in ((0, grad_one), (half, grad_two)):
+        part = slice(at, at + half)
+        gain_part, grad_input = norm_backward(
+            grad_normed, rows_in[part], grad_hidden[part], gains[0:1], (bf16,)
+        )
+        gain_one = gain_one + gain_part
+        if at:
+            grad_input = after(grad_input, gathered)
+        gathered = lax.all_gather(grad_input, ("seq", "extra"), axis=0, tiled=False)
+        input_grad = lax.dynamic_update_slice_in_dim(input_grad, gathered.astype(f32), at, 1)
     if split_heads:
         heads_grad = exchange(total(heads_grads).astype(bf16)).astype(f32)
         heads_grad = heads_grad.reshape(block_heads, 4 * HEAD_DIM, rows)

time: 1180 us -> 1260 us (1.068)
  waiting for transfers between devices: 562 us -> 620 us
  other arithmetic: 57.5 us -> 70.4 us
    reduce_scatter x3 -> x4, waiting for transfers between devices: 6.18 us -> 82.5 us  [scatter_plane(): lax.psum_scatter(a.astype(bf16), plane, scatter_dimension=0, tiled=True)]
    ppermute x35, waiting for transfers between devices: 303 us -> 339 us  [send(): return lax.ppermute(a, 'seq', pairs)]
    all_gather x1 -> x2, waiting for transfers between devices: 62.2 us -> 28.9 us  [shards(): gathered = lax.all_gather(grad_input, ('seq', 'extra'), axis=0, tiled=False)]
    pallas_call x1 -> x2, Pallas kernels: 24.7 us -> 47.9 us  [halves_product(): pl.pallas_call(halves_kernel, out_shape=tuple((jax.ShapeDtypeStruct((leng...]
    all_to_all x4, waiting for transfers between devices: 22.6 us -> 1.59 us  [exchange(): return lax.all_to_all(a, context, split_axis=0, concat_axis=0, tiled=True)]
    pallas_call x1 -> x0, Pallas kernels: 18 us -> none  [rows_product(): pl.pallas_call(rows_kernel, grid=(length // block,), out_shape=jax.ShapeD...]
    unnamed x92 -> x112, local copies, waits for them, and re-layouts: 46.9 us -> 42.5 us
  transfers between devices with their start and end apart: 52 -> 54, of which waited for: 27 -> 28; matrix products, arithmetic and copies ran while one was open for 17% -> 17% of each run, Pallas kernels for 12% -> 12%
where the time goes in v8:
time: 1260 us; the launch traced here: 1250 us
  waiting for transfers between devices  620 us (49%)
  Pallas kernels  223 us (18%)
  starting transfers between devices  117 us (9%)
  local copies, waits for them, and re-layouts  90.3 us (7%)
  matrix products  78.1 us (6%)
  other arithmetic  70.4 us (6%)
  blocking collectives  34.5 us (3%)
  between operations  15.9 us (1%)
    ppermute x35, waiting for transfers between devices, send(): return lax.ppermute(a, 'seq', pairs)  339 us
    ppermute x35, starting transfers between devices, send(): return lax.ppermute(a, 'seq', pairs)  97.1 us
    all_gather x4, waiting for transfers between devices, gather_plane(): return lax.all_gather(a, plane, axis=0, tiled=True)  90.2 us
    reduce_scatter x4, waiting for transfers between devices, scatter_plane(): lax.psum_scatter(a.astype(bf16), plane, scatter_dimension=0, tiled=True)  82.5 us
    dot_general x5, matrix products, dot(): lax.dot_general(a, b, (((ca,), (cb,)), ((), ())), preferred_element_type=...  78.1 us
    ppermute x5, waiting for transfers between devices, swap(): return lax.ppermute(a, axis, [(0, 1), (1, 0)])  77.7 us
    pallas_call x1, Pallas kernels, attend_back(): pl.pallas_call(attend_back_kernel, out_shape=jax.ShapeDtypeStruct((length...  60.6 us
    pallas_call x2, Pallas kernels, halves_product(): pl.pallas_call(halves_kernel, out_shape=tuple((jax.ShapeDtypeStruct((leng...  47.9 us
  transfers between devices with their start and end apart: 54, of which 28 were waited for; matrix products, arithmetic and copies ran while one was open for 17% of the time, Pallas kernels for 12%

profile of v8, /device:TPU:0, one launch (start us, length us, event | category | flops | bytes accessed | tf_op | source)
XLA Modules:
  0.0 1248.7 jit_solution(1323163775383059654)
XLA Ops:
  11.8 26.5 %all_to_all.25 = bf16[8,256,256]{2,1,0:T(8,128)(2,1)S(1)} all-to-all(bf16[8,256,256]{2,1,0:T(8,128)(2,1)S(1)} %bitcast.214), channel_id=1, replica_groups=mesh['chips'=2,'pair'=2,'core'=2,'seq'=4,'extra'=1] {'chips','pair','core'}, dimensions={0} | all-to-all | bytes 2097152 | tf_op jit(solution)/shard_map/all_to_all | solution.py:596
  40.6 4.5 collective-permute-start
  48.3 11.0 collective-permute-done
  59.2 5.0 collective-permute-done.1
  71.9 8.0 all_gather.28
  79.9 8.8 collective-permute-start.5
  92.5 9.1 collective-permute-done.4
  102.8 4.3 collective-permute-done.6
  123.5 3.6 all-to-all-start.1
  127.6 21.5 %project.1 = (bf16[256,4096]{1,0:T(8,128)(2,1)}, bf16[256,4096]{1,0:T(8,128)(2,1)}, bf16[256,4096]{1,0:T(8,128)(2,1)}, bf16[4,4096,64]{2,1,0:T(8,128)(2,1)}, bf16[4,4096,64]{2,1,0:T(8,128)(2,1)}) custom-call(bf16[4096,2048]{1,0:T(8,128)(2,1)} %all-gather.9.cloned.1.call-done.x_ref, bf16[768,2048]{1,0:T(8,128)(2,1)} %multiply_convert_fusion.1.weight_ref, ...), custom_call_target="tpu_custom_call" | custom-call | flops 12884901888 | bytes 29360128 | tf_op jit(solution)/shard_map/project/pallas_call | solution.py:82
  152.6 36.0 %attend.1 = (bf16[256,4096]{1,0:T(8,128)(2,1)}, f32[4,4096]{1,0:T(4,128)}, bf16[4096,2048]{1,0:T(8,128)(2,1)}) custom-call(s32[8]{0:T(128)} %get-tuple-element.126.lo_ref, s32[8]{0:T(128)} %get-tuple-element.127.full_ref, s32[1,4096]{1,0:T(1,128)} %add_maximum_fusion.low_ref, bf16[256,4096]{1,0:T(8,128)(2,1)} %get-tuple-element.136.q_ref, ...), custom_call_target="tpu_custom_call" | custom-call | flops 51539607552 | bytes 16777216 | tf_op jit(solution)/shard_map/attend/pallas_call | solution.py:263
  188.7 29.3 %all-gather.11.cloned.1.call-done = bf16[4096,2048]{1,0:T(8,128)(2,1)} async-done(((bf16[512,2048]{1,0:T(8,128)(2,1)}), bf16[4096,2048]{1,0:T(8,128)(2,1)}) %all-gather.11.cloned.1.call-update) | async-done | bytes 16777232 | tf_op jit(solution)/shard_map/all_gather | solution.py:643
  218.1 3.5 collective-permute-start.10
  222.9 32.7 %collective-permute-done.10 = bf16[8,384,256]{2,1,0:T(8,128)(2,1)S(1)} collective-permute-done((bf16[8,384,256]{2,1,0:T(8,128)(2,1)S(1)}, bf16[8,384,256]{2,1,0:T(8,128)(2,1)S(1)}, u32[]{:S(2)}, u32[]{:S(2)}) %collective-permute-start.10) | collective-permute-done | bytes 1572896 | tf_op jit(solution)/shard_map/ppermute | solution.py:599
  255.5 4.2 collective-permute-done.12
  263.3 36.8 %collective-permute-done.14 = bf16[8,384,256]{2,1,0:T(8,128)(2,1)S(1)} collective-permute-done((bf16[8,384,256]{2,1,0:T(8,128)(2,1)S(1)}, bf16[8,384,256]{2,1,0:T(8,128)(2,1)S(1)}, u32[]{:S(2)}, u32[]{:S(2)}) %collective-permute-start.14) | collective-permute-done | bytes 1572896 | tf_op jit(solution)/shard_map/ppermute | solution.py:599
  302.4 29.6 %collective-permute-done.13 = bf16[8,384,256]{2,1,0:T(8,128)(2,1)} collective-permute-done((bf16[8,384,256]{2,1,0:T(8,128)(2,1)S(1)}, bf16[8,384,256]{2,1,0:T(8,128)(2,1)}, u32[]{:S(2)}, u32[]{:S(2)}) %collective-permute-start.13) | collective-permute-done | bytes 1572896 | tf_op jit(solution)/shard_map/ppermute | solution.py:599
  332.0 6.2 reduce-scatter.5.cloned.1.call-done.branch_ref
  338.1 5.5 add_and_norm.1
  355.1 4.6 slice-done
  359.7 3.5 copy.159
  363.3 11.8 fusion.18.ga_ref
  375.1 58.6 %all-gather.13.cloned.1.call-done.x_ref = bf16[4096,2048]{1,0:T(8,128)(2,1)} async-done(((bf16[512,2048]{1,0:T(8,128)(2,1)}), bf16[4096,2048]{1,0:T(8,128)(2,1)}) %all-gather.13.cloned.1.call-update) | async-done | bytes 16777232 | tf_op jit(solution)/shard_map/all_gather | solution.py:643
  433.7 35.0 %feedforward.1 = (bf16[4096,512]{1,0:T(8,128)(2,1)}, bf16[4096,1024]{1,0:T(8,128)(2,1)}, bf16[4096,2048]{1,0:T(8,128)(2,1)}) custom-call(bf16[4096,2048]{1,0:T(8,128)(2,1)} %all-gather.13.cloned.1.call-done.x_ref, f32[4096,512]{1,0:T(8,128)} %fusion.18.ga_ref, bf16[1024,2048]{1,0:T(8,128)(2,1)} %bitcast.207, bf16[512,2048]{1,0:T(8,128)(2,1)} %bitcast.225), custom_call_target="tpu_custom_call" | custom-call | flops 25769803776 | bytes 54525952 | tf_op jit(solution)/shard_map/feedforward/pallas_call | solution.py:364
  469.4 24.7 %halves_product.2 = (bf16[2048,2048]{1,0:T(8,128)(2,1)}, bf16[2048,2048]{1,0:T(8,128)(2,1)}) custom-call(s32[8]{0:T(128)} %pad_add_fusion.order_ref, bf16[4096,1024]{1,0:T(8,128)(2,1)} %get-tuple-element.157.a_ref, bf16[1024,2048]{1,0:T(8,128)(2,1)} %bitcast.208), custom_call_target="tpu_custom_call" | custom-call | flops 17179869184 | bytes 25165824 | tf_op jit(solution)/shard_map/halves_product/pallas_call | solution.py:404
  494.4 23.3 %convolution_convert_fusion = bf16[1024,2048]{1,0:T(8,128)(2,1)S(1)} fusion(bf16[4096,1024]{1,0:T(8,128)(2,1)} %get-tuple-element.157.a_ref, bf16[4096,2048]{1,0:T(8,128)(2,1)} %all-gather.13.cloned.1.call-done.x_ref), kind=kOutput, calls=%fused_computation.16 | convolution fusion | flops 17181966336 | bytes 29360128 | tf_op jit(solution)/shard_map/dot_general | solution.py:28
  520.1 13.4 %convolution_convert_fusion.1 = bf16[512,2048]{1,0:T(8,128)(2,1)S(1)} fusion(bf16[4096,512]{1,0:T(8,128)(2,1)S(1)} %copy-done.39, bf16[4096,2048]{1,0:T(8,128)(2,1)} %all-gather.11.cloned.1.call-done), kind=kOutput, calls=%fused_computation.21 | convolution fusion | flops 8590983168 | bytes 23068672 | tf_op jit(solution)/shard_map/dot_general | solution.py:28
  539.8 6.1 add_convert_fusion
  558.9 5.5 collective-permute-start.20
  568.6 55.3 %collective-permute-done.17 = bf16[2,256,2048]{2,1,0:T(8,128)(2,1)} collective-permute-done((bf16[2,256,2048]{2,1,0:T(8,128)(2,1)}, bf16[2,256,2048]{2,1,0:T(8,128)(2,1)}, u32[]{:S(2)}, u32[]{:S(2)}) %collective-permute-start.17) | collective-permute-done | bytes 2097184 | tf_op jit(solution)/shard_map/ppermute | solution.py:549
  632.8 21.6 %collective-permute-done.21 = bf16[256,2048]{1,0:T(8,128)(2,1)S(1)} collective-permute-done((bf16[256,2048]{1,0:T(8,128)(2,1)S(1)}, bf16[256,2048]{1,0:T(8,128)(2,1)S(1)}, u32[]{:S(2)}, u32[]{:S(2)}) %collective-permute-start.21) | collective-permute-done | bytes 1048608 | tf_op jit(solution)/shard_map/ppermute | solution.py:549
  658.2 8.3 norm_backward.3
  666.6 3.5 add_convert_fusion.1
  670.1 7.1 collective-permute-start.25
  678.5 4.0 add_convert_fusion.3
  682.5 4.3 collective-permute-start.23
  688.8 64.7 %collective-permute-done.23 = bf16[8,384,256]{2,1,0:T(8,128)(2,1)S(1)} collective-permute-done((bf16[8,384,256]{2,1,0:T(8,128)(2,1)S(1)}, bf16[8,384,256]{2,1,0:T(8,128)(2,1)S(1)}, u32[]{:S(2)}, u32[]{:S(2)}) %collective-permute-start.23) | collective-permute-done | bytes 1572896 | tf_op jit(solution)/shard_map/ppermute | solution.py:599
  753.5 5.4 collective-permute-done.24
  766.6 60.6 %attend_back.1.a_ref = bf16[4096,768]{1,0:T(8,128)(2,1)} custom-call(s32[8]{0:T(128)} %get-tuple-element.126.lo_ref, s32[8]{0:T(128)} %get-tuple-element.127.full_ref, s32[1,4096]{1,0:T(1,128)} %add_maximum_fusion.low_ref, bf16[256,4096]{1,0:T(8,128)(2,1)} %get-tuple-element.136.q_ref, bf16[4096,2048]{1,0:T(8,128)(2,1)} %all-gather.15.cloned.1.call-done.hidden_ref, ...), custom_call_target="tpu_custom_call" | custom-call | flops 103079215104 | bytes 25165824 | tf_op jit(solution)/shard_map/attend_back/pallas_call | solution.py:299
  827.2 32.7 %collective-permute-done.29 = bf16[512,2048]{1,0:T(8,128)(2,1)S(1)} collective-permute-done((bf16[512,2048]{1,0:T(8,128)(2,1)S(1)}, bf16[512,2048]{1,0:T(8,128)(2,1)S(1)}, u32[]{:S(2)}, u32[]{:S(2)}) %collective-permute-start.29) | collective-permute-done | bytes 2097184 | tf_op jit(solution)/shard_map/ppermute | solution.py:599
  859.9 23.1 %halves_product.3 = (bf16[2048,2048]{1,0:T(8,128)(2,1)}, bf16[2048,2048]{1,0:T(8,128)(2,1)}) custom-call(s32[16]{0:T(128)} %pad_add_fusion.1.order_ref, bf16[4096,768]{1,0:T(8,128)(2,1)} %attend_back.1.a_ref, bf16[768,2048]{1,0:T(8,128)(2,1)} %bitcast.186), custom_call_target="tpu_custom_call" | custom-call | flops 12884901888 | bytes 23068672 | tf_op jit(solution)/shard_map/halves_product/pallas_call | solution.py:404
  883.1 76.3 %reduce-scatter.9.cloned.1.call-done.grad_ref = bf16[256,2048]{1,0:T(8,128)(2,1)} async-done(((bf16[2048,2048]{1,0:T(8,128)(2,1)}), bf16[256,2048]{1,0:T(8,128)(2,1)}) %reduce-scatter.9.cloned.1.call-update) | async-done | bytes 1048592 | tf_op jit(solution)/shard_map/reduce_scatter | solution.py:646
  959.8 3.3 dynamic-slice_bitcast_fusion.5
  965.4 4.2 norm_backward.4
  969.6 10.8 convolution_convert_fusion.2
  980.7 18.8 %multiply_convert_fusion = bf16[768,2048]{1,0:T(8,128)(2,1)S(1)} fusion(bf16[4096,768]{1,0:T(8,128)(2,1)} %attend_back.1.a_ref, bf16[4096,2048]{1,0:T(8,128)(2,1)} %all-gather.9.cloned.1.call-done.x_ref, f32[2048]{0:T(1024)S(1)} %bitcast.236), kind=kOutput, calls=%fused_computation.4 | convolution fusion | flops 12888047616 | bytes 26222592 | tf_op jit(solution)/shard_map/dot_general | solution.py:28
  1002.5 3.4 collective-permute-start.30
  1009.4 20.0 %collective-permute-done.30 = bf16[8,256,256]{2,0,1:T(8,128)(2,1)S(1)} collective-permute-done((bf16[8,256,256]{2,0,1:T(8,128)(2,1)S(1)}, bf16[8,256,256]{2,0,1:T(8,128)(2,1)S(1)}, u32[]{:S(2)}, u32[]{:S(2)}) %collective-permute-start.30) | collective-permute-done | bytes 1048608 | tf_op jit(solution)/shard_map/ppermute | solution.py:599
  1029.4 27.5 %collective-permute-done.31 = bf16[8,256,256]{2,0,1:T(8,128)(2,1)S(1)} collective-permute-done((bf16[8,256,256]{2,0,1:T(8,128)(2,1)S(1)}, bf16[8,256,256]{2,0,1:T(8,128)(2,1)S(1)}, u32[]{:S(2)}, u32[]{:S(2)}) %collective-permute-start.31) | collective-permute-done | bytes 1048608 | tf_op jit(solution)/shard_map/ppermute | solution.py:599
  1059.0 18.6 %collective-permute-start.32 = (bf16[8,256,256]{2,0,1:T(8,128)(2,1)}, bf16[8,256,256]{2,0,1:T(8,128)(2,1)S(1)}, u32[]{:S(2)}, u32[]{:S(2)}) collective-permute-start(bf16[8,256,256]{2,0,1:T(8,128)(2,1)} %get-tuple-element.264), channel_id=1, source_target_pairs={{0,1},{1,2},{2,3},{4,5},{5,6},{6,7},{8,9},{9,10},{10,11},{12,13},{... | collective-permute-start | bytes 3145736 | tf_op jit(solution)/shard_map/ppermute | solution.py:599
  1080.7 3.6 all-to-all-start.4
  1084.4 39.2 %collective-permute-done.32 = bf16[8,256,256]{2,0,1:T(8,128)(2,1)S(1)} collective-permute-done((bf16[8,256,256]{2,0,1:T(8,128)(2,1)}, bf16[8,256,256]{2,0,1:T(8,128)(2,1)S(1)}, u32[]{:S(2)}, u32[]{:S(2)}) %collective-permute-start.32) | collective-permute-done | bytes 1048608 | tf_op jit(solution)/shard_map/ppermute | solution.py:599
  1123.5 12.7 %collective-permute-done.34 = bf16[8,256,256]{2,0,1:T(8,128)(2,1)} collective-permute-done((bf16[8,256,256]{2,0,1:T(8,128)(2,1)}, bf16[8,256,256]{2,0,1:T(8,128)(2,1)}, u32[]{:S(2)}, u32[]{:S(2)}) %collective-permute-start.34) | collective-permute-done | bytes 1048608 | tf_op jit(solution)/shard_map/ppermute | solution.py:599
  1136.2 4.0 norm_backward.5
  1140.2 6.3 all-gather.17.cloned.1.call-done
  1154.2 3.3 bitcast_dynamic-update-slice_fusion.4
  1157.5 3.5 bitcast_dynamic-update-slice_fusion.3
  1162.5 3.3 bitcast_dynamic-update-slice_fusion.1
  1167.9 3.3 all-to-all-start.2
  1176.0 3.6 all-to-all-start.3
  1179.5 6.7 collective-permute-start.35
  1195.0 8.5 constant_dynamic-slice_fusion
  1207.0 22.6 %all-gather.19.cloned.1.call-done = bf16[1024,2048]{1,0:T(8,128)(2,1)} async-done(((bf16[256,2048]{1,0:T(8,128)(2,1)}), bf16[1024,2048]{1,0:T(8,128)(2,1)}) %all-gather.19.cloned.1.call-update) | async-done | bytes 4194320 | tf_op jit(solution)/shard_map/all_gather | solution.py:855
  1229.6 11.8 maximum_convert_fusion
  (287 shorter events, 154.2 us)
Async XLA Ops:
  7.2 102.2 %copy-start = (s32[4,8]{1,0:T(4,128)S(1)}, s32[4,8]{1,0:T(4,128)}, u32[]{:S(2)}) copy-start(s32[4,8]{1,0:T(4,128)} %param.9) | copy-start | bytes 388
  7.2 102.2 %all-gather.9.cloned.1.call-start = ((), (), s32[]{:S(2)}) async-start(), calls=%async_computation.9 | async-start | bytes 18874368 | tf_op jit(solution)/shard_map/all_gather | solution.py:643
  11.3 206.7 %all-gather.11.cloned.1.call-start = ((), (), s32[]{:S(2)}) async-start(), calls=%async_computation.10 | async-start | bytes 18874368 | tf_op jit(solution)/shard_map/all_gather | solution.py:643
  11.8 34.5 %copy-start.27 = (bf16[2,256,1024]{2,1,0:T(8,128)(2,1)S(1)}, bf16[2,256,1024]{2,1,0:T(8,128)(2,1)}, u32[]{:S(2)}) copy-start(bf16[2,256,1024]{2,1,0:T(8,128)(2,1)} %param.13) | copy-start | bytes 3145732
  40.6 18.6 %collective-permute-start = (bf16[8,192,256]{2,0,1:T(8,128)(2,1)}, bf16[8,192,256]{2,0,1:T(8,128)(2,1)}, u32[]{:S(2)}, u32[]{:S(2)}) collective-permute-start(bf16[8,192,256]{2,0,1:T(8,128)(2,1)} %copy.125), channel_id=1, source_target_pairs={{0,1},{1,2},{2,3},{4,5},{5,6},{6,7},{8,9},{9,10},{10,11},{12,13},{... | collective-permute-start | bytes 2359304 | tf_op jit(solution)/shard_map/ppermute | solution.py:599
  45.1 19.1 %collective-permute-start.1 = (bf16[8,192,256]{2,0,1:T(8,128)(2,1)}, bf16[8,192,256]{2,0,1:T(8,128)(2,1)}, u32[]{:S(2)}, u32[]{:S(2)}) collective-permute-start(bf16[8,192,256]{2,0,1:T(8,128)(2,1)} %copy.125), channel_id=1, source_target_pairs={{1,0},{2,1},{3,2},{5,4},{6,5},{7,6},{9,8},{10,9},{11,10},{13,12},{... | collective-permute-start | bytes 2359304 | tf_op jit(solution)/shard_map/ppermute | solution.py:599
  48.3 23.7 %copy-start.38 = (bf16[2,256]{1,0:T(2,128)(2,1)S(1)}, bf16[2,256]{1,0:T(2,128)(2,1)}, u32[]{:S(2)}) copy-start(bf16[2,256]{1,0:T(2,128)(2,1)} %param.10) | copy-start | bytes 3076
  65.4 24.6 %collective-permute-start.2 = (bf16[8,192,256]{2,0,1:T(8,128)(2,1)S(1)}, bf16[8,192,256]{2,0,1:T(8,128)(2,1)}, u32[]{:S(2)}, u32[]{:S(2)}) collective-permute-start(bf16[8,192,256]{2,0,1:T(8,128)(2,1)S(1)} %broadcast_select_fusion.8), channel_id=1, source_target_pairs={{1,3},{2,0},{5,7},{6,4},{9,11},{10,8},{13,15},{14,12},{17,19},{18,... | collective-permute-start | bytes 2359304 | tf_op jit(solution)/shard_map/ppermute | solution.py:599
  66.7 24.8 %collective-permute-start.3 = (bf16[8,192,256]{2,0,1:T(8,128)(2,1)}, bf16[8,192,256]{2,0,1:T(8,128)(2,1)S(1)}, u32[]{:S(2)}, u32[]{:S(2)}) collective-permute-start(bf16[8,192,256]{2,0,1:T(8,128)(2,1)} %collective-permute-done), channel_id=1, source_target_pairs={{1,2},{2,3},{5,6},{6,7},{9,10},{10,11},{13,14},{14,15},{17,18},{18... | collective-permute-start | bytes 2359304 | tf_op jit(solution)/shard_map/ppermute | solution.py:599
  67.5 34.1 %collective-permute-start.4 = (bf16[8,192,256]{2,0,1:T(8,128)(2,1)}, bf16[8,192,256]{2,0,1:T(8,128)(2,1)}, u32[]{:S(2)}, u32[]{:S(2)}) collective-permute-start(bf16[8,192,256]{2,0,1:T(8,128)(2,1)} %collective-permute-done.1), channel_id=1, source_target_pairs={{1,0},{2,1},{5,4},{6,5},{9,8},{10,9},{13,12},{14,13},{17,16},{18,1... | collective-permute-start | bytes 2359304 | tf_op jit(solution)/shard_map/ppermute | solution.py:599
  79.9 22.9 %collective-permute-start.5 = (bf16[8,64,256]{2,0,1:T(8,128)(2,1)}, bf16[8,64,256]{2,0,1:T(8,128)(2,1)S(1)}, u32[]{:S(2)}, u32[]{:S(2)}) collective-permute-start(bf16[8,64,256]{2,0,1:T(8,128)(2,1)} %bitcast.173), channel_id=1, source_target_pairs={{0,1},{1,2},{2,3},{4,5},{5,6},{6,7},{8,9},{9,10},{10,11},{12,13},{... | collective-permute-start | bytes 786440 | tf_op jit(solution)/shard_map/ppermute | solution.py:599
  88.7 18.3 %collective-permute-start.6 = (bf16[8,64,256]{2,0,1:T(8,128)(2,1)}, bf16[8,64,256]{2,0,1:T(8,128)(2,1)}, u32[]{:S(2)}, u32[]{:S(2)}) collective-permute-start(bf16[8,64,256]{2,0,1:T(8,128)(2,1)} %bitcast.173), channel_id=1, source_target_pairs={{1,0},{2,1},{3,2},{5,4},{6,5},{7,6},{9,8},{10,9},{11,10},{13,12},{... | collective-permute-start | bytes 786440 | tf_op jit(solution)/shard_map/ppermute | solution.py:599
  119.2 29.9 %collective-permute-start.7 = (bf16[8,64,256]{2,0,1:T(8,128)(2,1)S(1)}, bf16[8,64,256]{2,0,1:T(8,128)(2,1)S(1)}, u32[]{:S(2)}, u32[]{:S(2)}) collective-permute-start(bf16[8,64,256]{2,0,1:T(8,128)(2,1)S(1)} %collective-permute-done.5), channel_id=1, source_target_pairs={{1,2},{2,3},{5,6},{6,7},{9,10},{10,11},{13,14},{14,15},{17,18},{18... | collective-permute-start | bytes 786440 | tf_op jit(solution)/shard_map/ppermute | solution.py:599
  119.9 29.3 %collective-permute-start.8 = (bf16[8,64,256]{2,0,1:T(8,128)(2,1)}, bf16[8,64,256]{2,0,1:T(8,128)(2,1)S(1)}, u32[]{:S(2)}, u32[]{:S(2)}) collective-permute-start(bf16[8,64,256]{2,0,1:T(8,128)(2,1)} %collective-permute-done.6), channel_id=1, source_target_pairs={{1,0},{2,1},{5,4},{6,5},{9,8},{10,9},{13,12},{14,13},{17,16},{18,1... | collective-permute-start | bytes 786440 | tf_op jit(solution)/shard_map/ppermute | solution.py:599
  122.2 26.9 %collective-permute-start.9 = (bf16[8,64,256]{2,0,1:T(8,128)(2,1)S(1)}, bf16[8,64,256]{2,0,1:T(8,128)(2,1)S(1)}, u32[]{:S(2)}, u32[]{:S(2)}) collective-permute-start(bf16[8,64,256]{2,0,1:T(8,128)(2,1)S(1)} %broadcast_select_fusion.10), channel_id=1, source_target_pairs={{1,3},{2,0},{5,7},{6,4},{9,11},{10,8},{13,15},{14,12},{17,19},{18,... | collective-permute-start | bytes 786440 | tf_op jit(solution)/shard_map/ppermute | solution.py:599
  123.5 65.1 %all-to-all-start.1 = ((bf16[8,384,256]{2,1,0:T(8,128)(2,1)}), bf16[8,384,256]{2,1,0:T(8,128)(2,1)S(1)}, u32[]{:S(2)}, u32[]{:S(2)}) async-start(bf16[8,384,256]{2,1,0:T(8,128)(2,1)} %pad_maximum_fusion.2), calls=%async_computation.1 | async-start | bytes 3145728 | tf_op jit(solution)/shard_map/all_to_all | solution.py:596
  127.1 211.0 %reduce-scatter.5.cloned.1.call-start = ((), (), s32[]{:S(2)}) async-start(), calls=%async_computation.11 | async-start | bytes 18874368 | tf_op jit(solution)/shard_map/reduce_scatter | solution.py:646
  218.0 215.7 %all-gather.13.cloned.1.call-start = ((), (), s32[]{:S(2)}) async-start(), calls=%async_computation.12 | async-start | bytes 18874368 | tf_op jit(solution)/shard_map/all_gather | solution.py:643
  218.1 37.5 %collective-permute-start.10 = (bf16[8,384,256]{2,1,0:T(8,128)(2,1)S(1)}, bf16[8,384,256]{2,1,0:T(8,128)(2,1)S(1)}, u32[]{:S(2)}, u32[]{:S(2)}) collective-permute-start(bf16[8,384,256]{2,1,0:T(8,128)(2,1)S(1)} %all-to-all-done.1), channel_id=1, source_target_pairs={{0,1},{1,2},{2,3},{4,5},{5,6},{6,7},{8,9},{9,10},{10,11},{12,13},{... | collective-permute-start | bytes 4718600 | tf_op jit(solution)/shard_map/ppermute | solution.py:599
  221.6 38.2 %collective-permute-start.12 = (bf16[8,384,256]{2,1,0:T(8,128)(2,1)S(1)}, bf16[8,384,256]{2,1,0:T(8,128)(2,1)S(1)}, u32[]{:S(2)}, u32[]{:S(2)}) collective-permute-start(bf16[8,384,256]{2,1,0:T(8,128)(2,1)S(1)} %all-to-all-done.1), channel_id=1, source_target_pairs={{1,0},{2,1},{3,2},{5,4},{6,5},{7,6},{9,8},{10,9},{11,10},{13,12},{... | collective-permute-start | bytes 4718600 | tf_op jit(solution)/shard_map/ppermute | solution.py:599
  259.7 40.4 %copy-start.11 = (bf16[8,384,256]{2,1,0:T(8,128)(2,1)}, bf16[8,384,256]{2,1,0:T(8,128)(2,1)S(1)}, u32[]{:S(2)}) copy-start(bf16[8,384,256]{2,1,0:T(8,128)(2,1)S(1)} %collective-permute-done.12) | copy-start | bytes 4718596
  259.9 40.2 %collective-permute-start.14 = (bf16[8,384,256]{2,1,0:T(8,128)(2,1)S(1)}, bf16[8,384,256]{2,1,0:T(8,128)(2,1)S(1)}, u32[]{:S(2)}, u32[]{:S(2)}) collective-permute-start(bf16[8,384,256]{2,1,0:T(8,128)(2,1)S(1)} %broadcast_select_fusion.5), channel_id=1, source_target_pairs={{1,3},{2,0},{5,7},{6,4},{9,11},{10,8},{13,15},{14,12},{17,19},{18,... | collective-permute-start | bytes 4718600 | tf_op jit(solution)/shard_map/ppermute | solution.py:599
  261.2 38.9 %collective-permute-start.11 = (bf16[8,384,256]{2,1,0:T(8,128)(2,1)S(1)}, bf16[8,384,256]{2,1,0:T(8,128)(2,1)S(1)}, u32[]{:S(2)}, u32[]{:S(2)}) collective-permute-start(bf16[8,384,256]{2,1,0:T(8,128)(2,1)S(1)} %collective-permute-done.10), channel_id=1, source_target_pairs={{1,2},{2,3},{5,6},{6,7},{9,10},{10,11},{13,14},{14,15},{17,18},{18... | collective-permute-start | bytes 4718600 | tf_op jit(solution)/shard_map/ppermute | solution.py:599
  262.0 70.0 %collective-permute-start.13 = (bf16[8,384,256]{2,1,0:T(8,128)(2,1)S(1)}, bf16[8,384,256]{2,1,0:T(8,128)(2,1)}, u32[]{:S(2)}, u32[]{:S(2)}) collective-permute-start(bf16[8,384,256]{2,1,0:T(8,128)(2,1)S(1)} %collective-permute-done.12), channel_id=1, source_target_pairs={{1,0},{2,1},{5,4},{6,5},{9,8},{10,9},{13,12},{14,13},{17,16},{18,1... | collective-permute-start | bytes 4718600 | tf_op jit(solution)/shard_map/ppermute | solution.py:599
  343.7 314.5 %reduce-scatter.7.cloned.1.call-start = ((), (), s32[]{:S(2)}) async-start(), calls=%async_computation.13 | async-start | bytes 18874368 | tf_op jit(solution)/shard_map/reduce_scatter | solution.py:646
  468.8 291.3 %all-gather.15.cloned.1.call-start = ((), (), s32[]{:S(2)}) async-start(), calls=%async_computation.14 | async-start | bytes 18874368 | tf_op jit(solution)/shard_map/all_gather | solution.py:643
  494.1 44.9 %collective-permute-start.15 = (bf16[2048,2048]{1,0:T(8,128)(2,1)}, bf16[2048,2048]{1,0:T(8,128)(2,1)}, u32[]{:S(2)}, u32[]{:S(2)}) collective-permute-start(bf16[2048,2048]{1,0:T(8,128)(2,1)} %get-tuple-element.159), channel_id=1, source_target_pairs={{0,4},{4,0},{1,5},{5,1},{2,6},{6,2},{3,7},{7,3},{8,12},{12,8},{9,1... | collective-permute-start | bytes 25165832 | tf_op jit(solution)/shard_map/ppermute | solution.py:549
  552.1 71.8 %collective-permute-start.17 = (bf16[2,256,2048]{2,1,0:T(8,128)(2,1)}, bf16[2,256,2048]{2,1,0:T(8,128)(2,1)}, u32[]{:S(2)}, u32[]{:S(2)}) collective-permute-start(bf16[2,256,2048]{2,1,0:T(8,128)(2,1)} %dynamic-slice_bitcast_fusion), channel_id=1, source_target_pairs={{0,16},{16,0},{1,17},{17,1},{2,18},{18,2},{3,19},{19,3},{4,20},{20... | collective-permute-start | bytes 6291464 | tf_op jit(solution)/shard_map/ppermute | solution.py:549
  555.9 71.0 %collective-permute-start.16 = (bf16[2,256,2048]{2,1,0:T(8,128)(2,1)}, bf16[2,256,2048]{2,1,0:T(8,128)(2,1)}, u32[]{:S(2)}, u32[]{:S(2)}) collective-permute-start(bf16[2,256,2048]{2,1,0:T(8,128)(2,1)} %dynamic-slice_bitcast_fusion.1), channel_id=1, source_target_pairs={{0,8},{8,0},{1,9},{9,1},{2,10},{10,2},{3,11},{11,3},{4,12},{12,4},... | collective-permute-start | bytes 6291464 | tf_op jit(solution)/shard_map/ppermute | solution.py:549
  558.9 70.5 %collective-permute-start.20 = (bf16[8,384,256]{2,1,0:T(8,128)(2,1)}, bf16[8,384,256]{2,1,0:T(8,128)(2,1)}, u32[]{:S(2)}, u32[]{:S(2)}) collective-permute-start(bf16[8,384,256]{2,1,0:T(8,128)(2,1)} %broadcast_select_fusion.3), channel_id=1, source_target_pairs={{0,2},{3,1},{4,6},{7,5},{8,10},{11,9},{12,14},{15,13},{16,18},{19,... | collective-permute-start | bytes 4718600 | tf_op jit(solution)/shard_map/ppermute | solution.py:599
  564.3 66.2 %collective-permute-start.18 = (bf16[8,384,256]{2,1,0:T(8,128)(2,1)}, bf16[8,384,256]{2,1,0:T(8,128)(2,1)}, u32[]{:S(2)}, u32[]{:S(2)}) collective-permute-start(bf16[8,384,256]{2,1,0:T(8,128)(2,1)} %bitcast.36), channel_id=1, source_target_pairs={{0,1},{1,2},{4,5},{5,6},{8,9},{9,10},{12,13},{13,14},{16,17},{17,1... | collective-permute-start | bytes 4718600 | tf_op jit(solution)/shard_map/ppermute | solution.py:599
  566.8 63.7 %collective-permute-start.19 = (bf16[8,384,256]{2,1,0:T(8,128)(2,1)}, bf16[8,384,256]{2,1,0:T(8,128)(2,1)}, u32[]{:S(2)}, u32[]{:S(2)}) collective-permute-start(bf16[8,384,256]{2,1,0:T(8,128)(2,1)} %bitcast.36), channel_id=1, source_target_pairs={{2,1},{3,2},{6,5},{7,6},{10,9},{11,10},{14,13},{15,14},{18,17},{19... | collective-permute-start | bytes 4718600 | tf_op jit(solution)/shard_map/ppermute | solution.py:599
  568.6 58.3 %copy-start.4 = (bf16[2,2,256,2048]{3,2,1,0:T(8,128)(2,1)S(1)}, bf16[2,2,256,2048]{3,2,1,0:T(8,128)(2,1)}, u32[]{:S(2)}) copy-start(bf16[2,2,256,2048]{3,2,1,0:T(8,128)(2,1)} %get-tuple-element.249) | copy-start | bytes 12582916
  630.6 23.8 %collective-permute-start.21 = (bf16[256,2048]{1,0:T(8,128)(2,1)S(1)}, bf16[256,2048]{1,0:T(8,128)(2,1)S(1)}, u32[]{:S(2)}, u32[]{:S(2)}) collective-permute-start(bf16[256,2048]{1,0:T(8,128)(2,1)S(1)} %dynamic-slice_bitcast_fusion.7), channel_id=1, source_target_pairs={{0,16},{16,0},{1,17},{17,1},{2,18},{18,2},{3,19},{19,3},{4,20},{20... | collective-permute-start | bytes 3145736 | tf_op jit(solution)/shard_map/ppermute | solution.py:549
  632.2 23.4 %collective-permute-start.22 = (bf16[256,2048]{1,0:T(8,128)(2,1)S(1)}, bf16[256,2048]{1,0:T(8,128)(2,1)S(1)}, u32[]{:S(2)}, u32[]{:S(2)}) collective-permute-start(bf16[256,2048]{1,0:T(8,128)(2,1)S(1)} %dynamic-slice_bitcast_fusion.6), channel_id=1, source_target_pairs={{0,8},{8,0},{1,9},{9,1},{2,10},{10,2},{3,11},{11,3},{4,12},{12,4},... | collective-permute-start | bytes 3145736 | tf_op jit(solution)/shard_map/ppermute | solution.py:549
  666.5 293.0 %reduce-scatter.9.cloned.1.call-start = ((), (), s32[]{:S(2)}) async-start(), calls=%async_computation.15 | async-start | bytes 9437184 | tf_op jit(solution)/shard_map/reduce_scatter | solution.py:646
  670.1 88.7 %collective-permute-start.25 = (bf16[512,2048]{1,0:T(8,128)(2,1)S(1)}, bf16[512,2048]{1,0:T(8,128)(2,1)}, u32[]{:S(2)}, u32[]{:S(2)}) collective-permute-start(bf16[512,2048]{1,0:T(8,128)(2,1)S(1)} %add_convert_fusion.1), channel_id=1, source_target_pairs={{0,1},{1,2},{2,3},{4,5},{5,6},{6,7},{8,9},{9,10},{10,11},{12,13},{... | collective-permute-start | bytes 6291464 | tf_op jit(solution)/shard_map/ppermute | solution.py:599
  677.2 82.8 %collective-permute-start.26 = (bf16[512,2048]{1,0:T(8,128)(2,1)S(1)}, bf16[512,2048]{1,0:T(8,128)(2,1)}, u32[]{:S(2)}, u32[]{:S(2)}) collective-permute-start(bf16[512,2048]{1,0:T(8,128)(2,1)S(1)} %add_convert_fusion.1), channel_id=1, source_target_pairs={{1,0},{2,1},{3,2},{5,4},{6,5},{7,6},{9,8},{10,9},{11,10},{13,12},{... | collective-permute-start | bytes 6291464 | tf_op jit(solution)/shard_map/ppermute | solution.py:599
  682.5 70.9 %collective-permute-start.23 = (bf16[8,384,256]{2,1,0:T(8,128)(2,1)S(1)}, bf16[8,384,256]{2,1,0:T(8,128)(2,1)S(1)}, u32[]{:S(2)}, u32[]{:S(2)}) collective-permute-start(bf16[8,384,256]{2,1,0:T(8,128)(2,1)S(1)} %get-tuple-element.260), channel_id=1, source_target_pairs={{0,1},{1,2},{2,3},{4,5},{5,6},{6,7},{8,9},{9,10},{10,11},{12,13},{... | collective-permute-start | bytes 4718600 | tf_op jit(solution)/shard_map/ppermute | solution.py:599
  686.9 72.0 %collective-permute-start.24 = (bf16[8,384,256]{2,1,0:T(8,128)(2,1)S(1)}, bf16[8,384,256]{2,1,0:T(8,128)(2,1)S(1)}, u32[]{:S(2)}, u32[]{:S(2)}) collective-permute-start(bf16[8,384,256]{2,1,0:T(8,128)(2,1)S(1)} %get-tuple-element.259), channel_id=1, source_target_pairs={{1,0},{2,1},{3,2},{5,4},{6,5},{7,6},{9,8},{10,9},{11,10},{13,12},{... | collective-permute-start | bytes 4718600 | tf_op jit(solution)/shard_map/ppermute | solution.py:599
  760.0 99.9 %collective-permute-start.27 = (bf16[512,2048]{1,0:T(8,128)(2,1)}, bf16[512,2048]{1,0:T(8,128)(2,1)}, u32[]{:S(2)}, u32[]{:S(2)}) collective-permute-start(bf16[512,2048]{1,0:T(8,128)(2,1)} %collective-permute-done.25), channel_id=1, source_target_pairs={{1,2},{2,3},{5,6},{6,7},{9,10},{10,11},{13,14},{14,15},{17,18},{18... | collective-permute-start | bytes 6291464 | tf_op jit(solution)/shard_map/ppermute | solution.py:599
  763.9 96.0 %collective-permute-start.28 = (bf16[512,2048]{1,0:T(8,128)(2,1)}, bf16[512,2048]{1,0:T(8,128)(2,1)S(1)}, u32[]{:S(2)}, u32[]{:S(2)}) collective-permute-start(bf16[512,2048]{1,0:T(8,128)(2,1)} %collective-permute-done.26), channel_id=1, source_target_pairs={{1,0},{2,1},{5,4},{6,5},{9,8},{10,9},{13,12},{14,13},{17,16},{18,1... | collective-permute-start | bytes 6291464 | tf_op jit(solution)/shard_map/ppermute | solution.py:599
  765.3 94.6 %collective-permute-start.29 = (bf16[512,2048]{1,0:T(8,128)(2,1)S(1)}, bf16[512,2048]{1,0:T(8,128)(2,1)S(1)}, u32[]{:S(2)}, u32[]{:S(2)}) collective-permute-start(bf16[512,2048]{1,0:T(8,128)(2,1)S(1)} %broadcast_select_fusion), channel_id=1, source_target_pairs={{1,3},{2,0},{5,7},{6,4},{9,11},{10,8},{13,15},{14,12},{17,19},{18,... | collective-permute-start | bytes 6291464 | tf_op jit(solution)/shard_map/ppermute | solution.py:599
  859.9 23.2 %copy-start.7 = (bf16[512,2048]{1,0:T(8,128)(2,1)}, bf16[512,2048]{1,0:T(8,128)(2,1)S(1)}, u32[]{:S(2)}) copy-start(bf16[512,2048]{1,0:T(8,128)(2,1)S(1)} %collective-permute-done.29) | copy-start | bytes 6291460
  883.1 253.1 %reduce-scatter.11.cloned.1.call-start = ((), (), s32[]{:S(2)}) async-start(), calls=%async_computation.16 | async-start | bytes 9437184 | tf_op jit(solution)/shard_map/reduce_scatter | solution.py:646
  959.5 187.0 %all-gather.17.cloned.1.call-start = ((), (), s32[]{:S(2)}) async-start(), calls=%async_computation.17 | async-start | bytes 5242880 | tf_op jit(solution)/shard_map/all_gather | solution.py:855
  1002.5 26.9 %collective-permute-start.30 = (bf16[8,256,256]{2,0,1:T(8,128)(2,1)S(1)}, bf16[8,256,256]{2,0,1:T(8,128)(2,1)S(1)}, u32[]{:S(2)}, u32[]{:S(2)}) collective-permute-start(bf16[8,256,256]{2,0,1:T(8,128)(2,1)S(1)} %get-tuple-element.257), channel_id=1, source_target_pairs={{0,1},{1,2},{4,5},{5,6},{8,9},{9,10},{12,13},{13,14},{16,17},{17,1... | collective-permute-start | bytes 3145736 | tf_op jit(solution)/shard_map/ppermute | solution.py:599
  1005.9 73.0 %copy-start.13 = (bf16[1,8,3,128,256]{4,3,2,1,0:T(8,128)(2,1)S(1)}, bf16[1,8,3,128,256]{4,3,2,1,0:T(8,128)(2,1)}, u32[]{:S(2)}) copy-start(bf16[1,8,3,128,256]{4,3,2,1,0:T(8,128)(2,1)} %copy.134) | copy-start | bytes 4718596
  1005.9 73.0 %copy-start.22 = (bf16[8,384,256]{2,1,0:T(8,128)(2,1)S(1)}, bf16[8,384,256]{2,1,0:T(8,128)(2,1)}, u32[]{:S(2)}) copy-start(bf16[8,384,256]{2,1,0:T(8,128)(2,1)} %copy-done.21) | copy-start | bytes 4718596
  1005.9 73.0 %copy-start.24 = (bf16[8,384,256]{2,1,0:T(8,128)(2,1)S(1)}, bf16[8,384,256]{2,1,0:T(8,128)(2,1)}, u32[]{:S(2)}) copy-start(bf16[8,384,256]{2,1,0:T(8,128)(2,1)} %copy-done.23) | copy-start | bytes 4718596
  1006.0 50.9 %collective-permute-start.31 = (bf16[8,256,256]{2,0,1:T(8,128)(2,1)S(1)}, bf16[8,256,256]{2,0,1:T(8,128)(2,1)S(1)}, u32[]{:S(2)}, u32[]{:S(2)}) collective-permute-start(bf16[8,256,256]{2,0,1:T(8,128)(2,1)S(1)} %get-tuple-element.256), channel_id=1, source_target_pairs={{0,2},{3,1},{4,6},{7,5},{8,10},{11,9},{12,14},{15,13},{16,18},{19,... | collective-permute-start | bytes 3145736 | tf_op jit(solution)/shard_map/ppermute | solution.py:599
  1008.4 48.5 %collective-permute-start.33 = (bf16[8,256,256]{2,0,1:T(8,128)(2,1)S(1)}, bf16[8,256,256]{2,0,1:T(8,128)(2,1)S(1)}, u32[]{:S(2)}, u32[]{:S(2)}) collective-permute-start(bf16[8,256,256]{2,0,1:T(8,128)(2,1)S(1)} %get-tuple-element.257), channel_id=1, source_target_pairs={{2,1},{3,2},{6,5},{7,6},{10,9},{11,10},{14,13},{15,14},{18,17},{19... | collective-permute-start | bytes 3145736 | tf_op jit(solution)/shard_map/ppermute | solution.py:599
  1059.0 64.5 %collective-permute-start.32 = (bf16[8,256,256]{2,0,1:T(8,128)(2,1)}, bf16[8,256,256]{2,0,1:T(8,128)(2,1)S(1)}, u32[]{:S(2)}, u32[]{:S(2)}) collective-permute-start(bf16[8,256,256]{2,0,1:T(8,128)(2,1)} %get-tuple-element.264), channel_id=1, source_target_pairs={{0,1},{1,2},{2,3},{4,5},{5,6},{6,7},{8,9},{9,10},{10,11},{12,13},{... | collective-permute-start | bytes 3145736 | tf_op jit(solution)/shard_map/ppermute | solution.py:599
  1077.7 58.6 %collective-permute-start.34 = (bf16[8,256,256]{2,0,1:T(8,128)(2,1)}, bf16[8,256,256]{2,0,1:T(8,128)(2,1)}, u32[]{:S(2)}, u32[]{:S(2)}) collective-permute-start(bf16[8,256,256]{2,0,1:T(8,128)(2,1)} %get-tuple-element.263), channel_id=1, source_target_pairs={{1,0},{2,1},{3,2},{5,4},{6,5},{7,6},{9,8},{10,9},{11,10},{13,12},{... | collective-permute-start | bytes 3145736 | tf_op jit(solution)/shard_map/ppermute | solution.py:599
  1080.7 65.8 %all-to-all-start.4 = ((bf16[8,384,256]{2,1,0:T(8,128)(2,1)}), bf16[8,384,256]{2,1,0:T(8,128)(2,1)S(1)}, u32[]{:S(2)}, u32[]{:S(2)}) async-start(bf16[8,384,256]{2,1,0:T(8,128)(2,1)} %add_convert_fusion.2), calls=%async_computation.8 | async-start | bytes 3145728 | tf_op jit(solution)/shard_map/all_to_all | solution.py:596
  1084.3 145.3 %all-gather.19.cloned.1.call-start = ((), (), s32[]{:S(2)}) async-start(), calls=%async_computation.18 | async-start | bytes 5242880 | tf_op jit(solution)/shard_map/all_gather | solution.py:855
  1123.5 23.4 %copy-start.28 = (bf16[8,256,256]{2,0,1:T(8,128)(2,1)}, bf16[8,256,256]{2,0,1:T(8,128)(2,1)S(1)}, u32[]{:S(2)}) copy-start(bf16[8,256,256]{2,0,1:T(8,128)(2,1)S(1)} %collective-permute-done.32) | copy-start | bytes 3145732
  1167.9 8.0 all-to-all-start.2
  1176.0 28.3 %all-to-all-start.3 = ((bf16[8,256,256]{2,1,0:T(8,128)(2,1)}), bf16[8,256,256]{2,1,0:T(8,128)(2,1)S(1)}, u32[]{:S(2)}, u32[]{:S(2)}) async-start(bf16[8,256,256]{2,1,0:T(8,128)(2,1)} %copy.150), calls=%async_computation.7 | async-start | bytes 2097152 | tf_op jit(solution)/shard_map/all_to_all | solution.py:596
  1179.5 9.5 collective-permute-start.35
  1186.3 5.5 collective-permute-start.36
  1191.8 11.8 collective-permute-start.37
  1193.1 10.5 collective-permute-start.38
  1193.7 9.8 collective-permute-start.39
  (38 other events, 200.9 us)
Sparse Core Ops, SparseCore 0:
  11.2 98.0 all-gather.8
  111.2 106.7 all-gather.10
  222.1 115.9 reduce-scatter.4
  343.8 89.8 all-gather.12
  468.9 144.1 reduce-scatter.6
  666.6 90.9 all-gather.14
  883.2 76.2 reduce-scatter.8
  963.9 71.2 reduce-scatter.10
  1036.8 109.6 all-gather.16
  1147.9 81.5 all-gather.18
